TPU v7x, 32 devices: a whole 2x2x4 slice. The times are simulated.
32 devices in a mesh: groups: 2 (over x), section: 16 (over z, y, core).
Axes of the slice: x: 2, y: 2, z: 4, core: 2. Of those that a mesh axis runs over, the one named last changes fastest.
Arguments:
- hidden_in: bfloat16 [512, 3072], P(('groups', 'section')), parts along dimension 0, may hold values from -0.59765625 to 0.59765625
- latent_in: bfloat16 [512, 64], P(('groups', 'section')), parts along dimension 0, may hold values from -6 to 6
- w_qkv: bfloat16 [3, 3072, 6144], P(None, None, 'section'), may hold values from -0.109375 to 0.109375
- w_out: bfloat16 [6144, 3072], P('section'), may hold values from -0.109375 to 0.109375
- stale_kv: bfloat16 [4, 256, 6144], P('groups', None, 'section'), parts along dimension 0, may hold values from -3 to 3
- qk_gain: float32 [2, 2, 128], replicated, may hold values from 0.6 to 2.4
- block_mod: float32 [4, 3, 3072], P('groups'), parts along dimension 0, may hold values from -4 to 4
- final_mod: float32 [4, 3072], P('groups'), parts along dimension 0, may hold values from -3 to 3
- w_final: bfloat16 [3072, 64], replicated, may hold values from -0.109375 to 0.109375
- w_embed: bfloat16 [64, 3072], replicated, may hold values from -0.75 to 0.75
- patch_flow: int32 [6, 2], replicated, may hold values from 0 to 1, as said below
Outputs:
- hidden_out: bfloat16 [512, 3072], P(('groups', 'section')), parts along dimension 0
- latent_out: bfloat16 [512, 64], P(('groups', 'section')), parts along dimension 0
There are 2 independent parts, one for each index of `groups`. A program takes and returns all parts, laid end to end along the dimension named above; an argument that names none is the same for every part. Nothing has to cross between parts.
Inputs may be any that keep to these rules, and one draw needn't show every extreme that they name: `patch_flow`: each row holds each of 0 to 1 once.
All inputs are finite; a program needn't handle non-finite values.
Results may differ from a plain program's by a relative error of at most 0.03.
Values may be sent and summed in bfloat16 or wider, within the bound.
No kernel may reach another device: no remote copies, remote signals or barrier semaphores. Data moves between devices by JAX's collectives and lax.ppermute only.
A program may use at most 128 MiB of HBM per device.

v0:
```python
import math

import jax
import jax.numpy as jnp
from jax import lax
from jax.sharding import PartitionSpec as P

HS = 128
GROUP = 8
TICKS = 6


def for_sending(value):

    def short(part):
        return part.astype(jnp.bfloat16) if part.dtype == jnp.float32 else part

    return jax.tree.map(short, value)


def partner(block, axis, apart):
    count = lax.axis_size(axis)
    route = []
    for low in range(count):
        high = low | 1 << apart
        if high != low and high < count:
            route += [(low, high), (high, low)]
    return lax.ppermute(block, axis, route)


def from_behind(value, axis, by):
    size = lax.axis_size(axis)
    return lax.ppermute(value, axis, [(i, (i + by) % size) for i in range(size)])


def layer_norm(tokens, offset_row, scale_row):
    average = jnp.mean(tokens, axis=-1, keepdims=True)
    centred = tokens - average
    variance = jnp.mean(centred * centred, axis=-1, keepdims=True)
    return (centred * lax.rsqrt(variance + 1e-06) * (1.0 + scale_row) + offset_row).astype(
        jnp.bfloat16
    )


def head_norm(values, gain_row):
    return (
        values * lax.rsqrt(jnp.mean(values * values, axis=-1, keepdims=True) + 1e-06) * gain_row
    ).astype(jnp.bfloat16)


def head_terms_of(
    hidden, w_qkv, w_out, key_cache, value_cache, modulation, norm_gains, patch_index
):
    token_count = hidden.shape[0]
    total_rows = key_cache.shape[0]
    head_count = w_qkv.shape[2] // HS
    normed = layer_norm(hidden.astype(jnp.float32), modulation[0], modulation[1])
    queries = jnp.dot(normed, w_qkv[0], preferred_element_type=jnp.float32).reshape(
        token_count, head_count, HS
    )
    fresh_keys = jnp.dot(normed, w_qkv[1], preferred_element_type=jnp.float32).reshape(
        token_count, head_count, HS
    )
    fresh_values = jnp.dot(normed, w_qkv[2], preferred_element_type=jnp.float32)
    query_norm = head_norm(queries, norm_gains[0])
    key_norm = head_norm(fresh_keys, norm_gains[1]).reshape(token_count, head_count * HS)
    offset = patch_index * token_count
    key_cache = lax.dynamic_update_slice(key_cache, key_norm, (offset, jnp.int32(0)))
    value_cache = lax.dynamic_update_slice(
        value_cache, fresh_values.astype(jnp.bfloat16), (offset, jnp.int32(0))
    )
    scores = jnp.einsum(
        "qhd,khd->hqk",
        query_norm,
        key_cache.reshape(total_rows, head_count, HS),
        preferred_element_type=jnp.float32,
    ) / math.sqrt(HS)
    exp_scores = jnp.exp(scores)
    totals = jnp.sum(exp_scores, axis=-1)
    attended = jnp.einsum(
        "hqk,khd->qhd",
        exp_scores.astype(jnp.bfloat16),
        value_cache.reshape(total_rows, head_count, HS),
        preferred_element_type=jnp.float32,
    )
    attended = (
        (attended / jnp.transpose(totals)[:, :, None])
        .astype(jnp.bfloat16)
        .reshape(token_count, head_count * HS)
    )
    return (jnp.dot(attended, w_out, preferred_element_type=jnp.float32), key_cache, value_cache)


def restart(hidden, latent, final_mod, w_final, w_embed, at_start):
    normed = layer_norm(hidden.astype(jnp.float32), final_mod[0], final_mod[1])
    velocity = jnp.dot(normed, w_final, preferred_element_type=jnp.float32)
    renewed = (latent.astype(jnp.float32) + velocity).astype(jnp.bfloat16)
    embedded = jnp.dot(renewed, w_embed, preferred_element_type=jnp.float32).astype(jnp.bfloat16)
    return (jnp.where(at_start, embedded, hidden), jnp.where(at_start, renewed, latent))


def collect(pieces, position, levels, fetcher):
    for bit_number in range(levels):
        others = fetcher(pieces, bit_number)
        lower_half = position >> bit_number & 1 == 0
        pieces = tuple(
            (
                jnp.where(
                    lower_half,
                    jnp.concatenate([own_piece, other_piece], 0),
                    jnp.concatenate([other_piece, own_piece], 0),
                )
                for own_piece, other_piece in zip(pieces, others)
            )
        )
    return pieces


def body(
    hidden_in,
    latent_in,
    w_qkv,
    w_out,
    stale_kv,
    qk_gain,
    block_mod,
    final_mod,
    w_final,
    w_embed,
    patch_flow,
):
    device_index = lax.axis_index("section")
    section_index = device_index // GROUP
    position = device_index % GROUP
    levels = GROUP.bit_length() - 1
    modulation = lax.dynamic_index_in_dim(block_mod, section_index, 0, keepdims=False)
    norm_gains = lax.dynamic_index_in_dim(qk_gain, section_index, 0, keepdims=False)
    key_cache = stale_kv[0]
    value_cache = stale_kv[1]
    at_start = section_index == 0

    def fetch_rows(payload, bit_number):
        return jax.tree.map(
            lambda part, own: part.astype(own.dtype),
            partner(for_sending(payload), "section", bit_number),
            payload,
        )

    hidden_out, latent_out = (hidden_in, latent_in)
    for tick_index in range(TICKS):
        (hidden,) = collect((hidden_out,), position, levels, fetch_rows)
        patch_index = lax.dynamic_index_in_dim(
            patch_flow[tick_index], section_index, 0, keepdims=False
        )
        partial_value, key_cache, value_cache = head_terms_of(
            hidden, w_qkv, w_out, key_cache, value_cache, modulation, norm_gains, patch_index
        )
        for bit_number in reversed(range(levels)):
            half_rows = partial_value.shape[0] // 2
            lower_half = position >> bit_number & 1 == 0
            kept_part = jnp.where(lower_half, partial_value[:half_rows], partial_value[half_rows:])
            sent_part = jnp.where(lower_half, partial_value[half_rows:], partial_value[:half_rows])
            partial_value = kept_part + partner(
                sent_part.astype(jnp.bfloat16), "section", bit_number
            ).astype(sent_part.dtype)
        result = (hidden_out.astype(jnp.float32) + modulation[2] * partial_value).astype(
            jnp.bfloat16
        )
        hidden_out, latent_out = from_behind((result, latent_out), "section", GROUP)
        hidden_out, latent_out = restart(
            hidden_out, latent_out, final_mod, w_final, w_embed, at_start
        )
    return (hidden_out, latent_out)


def solution(mesh):
    in_specs = (
        P(("groups", "section"), None),
        P(("groups", "section"), None),
        P(None, None, "section"),
        P("section", None),
        P("groups", None, "section"),
        P(),
        P("groups", None, None),
        P("groups", None),
        P(),
        P(),
        P(),
    )
    out_specs = (P(("groups", "section"), None), P(("groups", "section"), None))
    return jax.shard_map(body, mesh=mesh, in_specs=in_specs, out_specs=out_specs, check_vma=False)
```

profile of v0, /device:TPU:0, one launch (start us, length us, event | category | flops | bytes accessed | tf_op | source)
XLA Modules:
  0.0 390.2 jit_solution(14024831218794991269)
XLA Ops:
  1.2 5.1 %slice_bitcast_fusion.1 = (bf16[384,3072]{0,1:T(8,128)(2,1)}, bf16[384,3072]{0,1:T(8,128)(2,1)}) fusion(bf16[3,3072,384]{2,1,0:T(8,128)(2,1)} %param.13), kind=kLoop, calls=%fused_computation.25 | loop fusion | bytes 9437184 | tf_op jit(solution)/shard_map/dot_general | solution.py:58
  6.5 2.7 collective-permute-start.2
  9.8 4.7 %collective-permute-done.2 = bf16[32,3072]{1,0:T(8,128)(2,1)S(1)} collective-permute-done((bf16[32,3072]{1,0:T(8,128)(2,1)S(1)}, bf16[32,3072]{1,0:T(8,128)(2,1)S(1)}, u32[]{:S(2)}, u32[]{:S(2)}) %collective-permute-start.2) | collective-permute-done | bytes 196640 | tf_op jit(solution)/shard_map/ppermute | solution.py:28
  17.1 4.3 %copy.41 = bf16[384,3072]{1,0:T(8,128)(2,1)} copy(bf16[384,3072]{0,1:T(8,128)(2,1)} %get-tuple-element.2) | data formatting | bytes 4718592 | tf_op jit(solution)/shard_map/dot_general | solution.py:58
  21.3 4.3 %copy.43 = bf16[384,3072]{1,0:T(8,128)(2,1)} copy(bf16[384,3072]{0,1:T(8,128)(2,1)} %get-tuple-element.3) | data formatting | bytes 4718592 | tf_op jit(solution)/shard_map/dot_general | solution.py:61
  30.6 3.3 multiply_reduce_fusion.11
  36.9 2.7 multiply_reduce_fusion.10
  41.5 10.0 %collective-permute-done.4 = bf16[64,3072]{1,0:T(8,128)(2,1)S(1)} collective-permute-done((bf16[64,3072]{1,0:T(8,128)(2,1)S(1)}, bf16[64,3072]{1,0:T(8,128)(2,1)S(1)}, u32[]{:S(2)}, u32[]{:S(2)}) %collective-permute-start.4) | collective-permute-done | bytes 393248 | tf_op jit(solution)/shard_map/ppermute | solution.py:28
  53.3 4.1 %collective-permute-done.5 = bf16[32,3072]{1,0:T(8,128)(2,1)S(1)} collective-permute-done((bf16[32,3072]{1,0:T(8,128)(2,1)S(1)}, bf16[32,3072]{1,0:T(8,128)(2,1)S(1)}, u32[]{:S(2)}, u32[]{:S(2)}) %collective-permute-start.5) | collective-permute-done | bytes 196640 | tf_op jit(solution)/shard_map/ppermute | solution.py:28
  57.6 2.7 collective-permute-start
  61.7 6.5 %collective-permute-done.7 = bf16[16,3072]{1,0:T(8,128)(2,1)S(1)} collective-permute-done((bf16[16,3072]{1,0:T(8,128)(2,1)S(1)}, bf16[16,3072]{1,0:T(8,128)(2,1)S(1)}, u32[]{:S(2)}, u32[]{:S(2)}) %collective-permute-start.7) | collective-permute-done | bytes 98336 | tf_op jit(solution)/shard_map/ppermute | solution.py:33
  73.6 5.4 %collective-permute-done.10 = bf16[32,3072]{1,0:T(8,128)(2,1)S(1)} collective-permute-done((bf16[32,3072]{1,0:T(8,128)(2,1)S(1)}, bf16[32,3072]{1,0:T(8,128)(2,1)S(1)}, u32[]{:S(2)}, u32[]{:S(2)}) %collective-permute-start.10) | collective-permute-done | bytes 196640 | tf_op jit(solution)/shard_map/ppermute | solution.py:28
  81.3 8.3 %collective-permute-done.11 = bf16[64,3072]{1,0:T(8,128)(2,1)} collective-permute-done((bf16[64,3072]{1,0:T(8,128)(2,1)S(1)}, bf16[64,3072]{1,0:T(8,128)(2,1)}, u32[]{:S(2)}, u32[]{:S(2)}) %collective-permute-start.11) | collective-permute-done | bytes 393248 | tf_op jit(solution)/shard_map/ppermute | solution.py:28
  92.5 3.7 multiply_reduce_fusion.9
  96.8 2.8 multiply_reduce_fusion.8
  108.1 9.2 %collective-permute-done.12 = bf16[64,3072]{1,0:T(8,128)(2,1)S(1)} collective-permute-done((bf16[64,3072]{1,0:T(8,128)(2,1)S(1)}, bf16[64,3072]{1,0:T(8,128)(2,1)S(1)}, u32[]{:S(2)}, u32[]{:S(2)}) %collective-permute-start.12) | collective-permute-done | bytes 393248 | tf_op jit(solution)/shard_map/ppermute | solution.py:28
  119.1 4.2 %collective-permute-done.13 = bf16[32,3072]{1,0:T(8,128)(2,1)S(1)} collective-permute-done((bf16[32,3072]{1,0:T(8,128)(2,1)S(1)}, bf16[32,3072]{1,0:T(8,128)(2,1)S(1)}, u32[]{:S(2)}, u32[]{:S(2)}) %collective-permute-start.13) | collective-permute-done | bytes 196640 | tf_op jit(solution)/shard_map/ppermute | solution.py:28
  125.2 2.6 collective-permute-start.8
  127.8 5.1 %collective-permute-done.15 = bf16[16,3072]{1,0:T(8,128)(2,1)S(1)} collective-permute-done((bf16[16,3072]{1,0:T(8,128)(2,1)S(1)}, bf16[16,3072]{1,0:T(8,128)(2,1)S(1)}, u32[]{:S(2)}, u32[]{:S(2)}) %collective-permute-start.15) | collective-permute-done | bytes 98336 | tf_op jit(solution)/shard_map/ppermute | solution.py:33
  137.3 5.4 %collective-permute-done.18 = bf16[32,3072]{1,0:T(8,128)(2,1)S(1)} collective-permute-done((bf16[32,3072]{1,0:T(8,128)(2,1)S(1)}, bf16[32,3072]{1,0:T(8,128)(2,1)S(1)}, u32[]{:S(2)}, u32[]{:S(2)}) %collective-permute-start.18) | collective-permute-done | bytes 196640 | tf_op jit(solution)/shard_map/ppermute | solution.py:28
  145.3 8.0 %collective-permute-done.19 = bf16[64,3072]{1,0:T(8,128)(2,1)} collective-permute-done((bf16[64,3072]{1,0:T(8,128)(2,1)S(1)}, bf16[64,3072]{1,0:T(8,128)(2,1)}, u32[]{:S(2)}, u32[]{:S(2)}) %collective-permute-start.19) | collective-permute-done | bytes 393248 | tf_op jit(solution)/shard_map/ppermute | solution.py:28
  156.2 3.8 multiply_reduce_fusion.7
  160.7 2.8 multiply_reduce_fusion.6
  172.1 9.2 %collective-permute-done.20 = bf16[64,3072]{1,0:T(8,128)(2,1)S(1)} collective-permute-done((bf16[64,3072]{1,0:T(8,128)(2,1)S(1)}, bf16[64,3072]{1,0:T(8,128)(2,1)S(1)}, u32[]{:S(2)}, u32[]{:S(2)}) %collective-permute-start.20) | collective-permute-done | bytes 393248 | tf_op jit(solution)/shard_map/ppermute | solution.py:28
  183.0 4.2 %collective-permute-done.21 = bf16[32,3072]{1,0:T(8,128)(2,1)S(1)} collective-permute-done((bf16[32,3072]{1,0:T(8,128)(2,1)S(1)}, bf16[32,3072]{1,0:T(8,128)(2,1)S(1)}, u32[]{:S(2)}, u32[]{:S(2)}) %collective-permute-start.21) | collective-permute-done | bytes 196640 | tf_op jit(solution)/shard_map/ppermute | solution.py:28
  189.1 2.6 collective-permute-start.16
  191.7 5.1 %collective-permute-done.23 = bf16[16,3072]{1,0:T(8,128)(2,1)S(1)} collective-permute-done((bf16[16,3072]{1,0:T(8,128)(2,1)S(1)}, bf16[16,3072]{1,0:T(8,128)(2,1)S(1)}, u32[]{:S(2)}, u32[]{:S(2)}) %collective-permute-start.23) | collective-permute-done | bytes 98336 | tf_op jit(solution)/shard_map/ppermute | solution.py:33
  201.2 5.4 %collective-permute-done.26 = bf16[32,3072]{1,0:T(8,128)(2,1)S(1)} collective-permute-done((bf16[32,3072]{1,0:T(8,128)(2,1)S(1)}, bf16[32,3072]{1,0:T(8,128)(2,1)S(1)}, u32[]{:S(2)}, u32[]{:S(2)}) %collective-permute-start.26) | collective-permute-done | bytes 196640 | tf_op jit(solution)/shard_map/ppermute | solution.py:28
  209.4 7.8 %collective-permute-done.27 = bf16[64,3072]{1,0:T(8,128)(2,1)} collective-permute-done((bf16[64,3072]{1,0:T(8,128)(2,1)S(1)}, bf16[64,3072]{1,0:T(8,128)(2,1)}, u32[]{:S(2)}, u32[]{:S(2)}) %collective-permute-start.27) | collective-permute-done | bytes 393248 | tf_op jit(solution)/shard_map/ppermute | solution.py:28
  220.1 3.7 multiply_reduce_fusion.5
  224.4 2.8 multiply_reduce_fusion.4
  235.8 9.2 %collective-permute-done.28 = bf16[64,3072]{1,0:T(8,128)(2,1)S(1)} collective-permute-done((bf16[64,3072]{1,0:T(8,128)(2,1)S(1)}, bf16[64,3072]{1,0:T(8,128)(2,1)S(1)}, u32[]{:S(2)}, u32[]{:S(2)}) %collective-permute-start.28) | collective-permute-done | bytes 393248 | tf_op jit(solution)/shard_map/ppermute | solution.py:28
  246.7 4.2 %collective-permute-done.29 = bf16[32,3072]{1,0:T(8,128)(2,1)S(1)} collective-permute-done((bf16[32,3072]{1,0:T(8,128)(2,1)S(1)}, bf16[32,3072]{1,0:T(8,128)(2,1)S(1)}, u32[]{:S(2)}, u32[]{:S(2)}) %collective-permute-start.29) | collective-permute-done | bytes 196640 | tf_op jit(solution)/shard_map/ppermute | solution.py:28
  255.4 5.0 %collective-permute-done.31 = bf16[16,3072]{1,0:T(8,128)(2,1)S(1)} collective-permute-done((bf16[16,3072]{1,0:T(8,128)(2,1)S(1)}, bf16[16,3072]{1,0:T(8,128)(2,1)S(1)}, u32[]{:S(2)}, u32[]{:S(2)}) %collective-permute-start.31) | collective-permute-done | bytes 98336 | tf_op jit(solution)/shard_map/ppermute | solution.py:33
  264.9 5.4 %collective-permute-done.34 = bf16[32,3072]{1,0:T(8,128)(2,1)S(1)} collective-permute-done((bf16[32,3072]{1,0:T(8,128)(2,1)S(1)}, bf16[32,3072]{1,0:T(8,128)(2,1)S(1)}, u32[]{:S(2)}, u32[]{:S(2)}) %collective-permute-start.34) | collective-permute-done | bytes 196640 | tf_op jit(solution)/shard_map/ppermute | solution.py:28
  272.7 8.2 %collective-permute-done.35 = bf16[64,3072]{1,0:T(8,128)(2,1)} collective-permute-done((bf16[64,3072]{1,0:T(8,128)(2,1)S(1)}, bf16[64,3072]{1,0:T(8,128)(2,1)}, u32[]{:S(2)}, u32[]{:S(2)}) %collective-permute-start.35) | collective-permute-done | bytes 393248 | tf_op jit(solution)/shard_map/ppermute | solution.py:28
  283.8 3.6 multiply_reduce_fusion.3
  288.1 3.0 multiply_reduce_fusion.2
  299.7 9.2 %collective-permute-done.36 = bf16[64,3072]{1,0:T(8,128)(2,1)S(1)} collective-permute-done((bf16[64,3072]{1,0:T(8,128)(2,1)S(1)}, bf16[64,3072]{1,0:T(8,128)(2,1)S(1)}, u32[]{:S(2)}, u32[]{:S(2)}) %collective-permute-start.36) | collective-permute-done | bytes 393248 | tf_op jit(solution)/shard_map/ppermute | solution.py:28
  310.7 4.2 %collective-permute-done.37 = bf16[32,3072]{1,0:T(8,128)(2,1)S(1)} collective-permute-done((bf16[32,3072]{1,0:T(8,128)(2,1)S(1)}, bf16[32,3072]{1,0:T(8,128)(2,1)S(1)}, u32[]{:S(2)}, u32[]{:S(2)}) %collective-permute-start.37) | collective-permute-done | bytes 196640 | tf_op jit(solution)/shard_map/ppermute | solution.py:28
  319.4 5.0 %collective-permute-done.39 = bf16[16,3072]{1,0:T(8,128)(2,1)S(1)} collective-permute-done((bf16[16,3072]{1,0:T(8,128)(2,1)S(1)}, bf16[16,3072]{1,0:T(8,128)(2,1)S(1)}, u32[]{:S(2)}, u32[]{:S(2)}) %collective-permute-start.39) | collective-permute-done | bytes 98336 | tf_op jit(solution)/shard_map/ppermute | solution.py:33
  328.9 5.4 %collective-permute-done.42 = bf16[32,3072]{1,0:T(8,128)(2,1)S(1)} collective-permute-done((bf16[32,3072]{1,0:T(8,128)(2,1)S(1)}, bf16[32,3072]{1,0:T(8,128)(2,1)S(1)}, u32[]{:S(2)}, u32[]{:S(2)}) %collective-permute-start.42) | collective-permute-done | bytes 196640 | tf_op jit(solution)/shard_map/ppermute | solution.py:28
  336.9 8.0 %collective-permute-done.43 = bf16[64,3072]{1,0:T(8,128)(2,1)} collective-permute-done((bf16[64,3072]{1,0:T(8,128)(2,1)S(1)}, bf16[64,3072]{1,0:T(8,128)(2,1)}, u32[]{:S(2)}, u32[]{:S(2)}) %collective-permute-start.43) | collective-permute-done | bytes 393248 | tf_op jit(solution)/shard_map/ppermute | solution.py:28
  347.8 3.6 multiply_reduce_fusion.1
  352.0 2.8 multiply_reduce_fusion
  363.4 9.2 %collective-permute-done.44 = bf16[64,3072]{1,0:T(8,128)(2,1)S(1)} collective-permute-done((bf16[64,3072]{1,0:T(8,128)(2,1)S(1)}, bf16[64,3072]{1,0:T(8,128)(2,1)S(1)}, u32[]{:S(2)}, u32[]{:S(2)}) %collective-permute-start.44) | collective-permute-done | bytes 393248 | tf_op jit(solution)/shard_map/ppermute | solution.py:28
  374.4 4.2 %collective-permute-done.45 = bf16[32,3072]{1,0:T(8,128)(2,1)S(1)} collective-permute-done((bf16[32,3072]{1,0:T(8,128)(2,1)S(1)}, bf16[32,3072]{1,0:T(8,128)(2,1)S(1)}, u32[]{:S(2)}, u32[]{:S(2)}) %collective-permute-start.45) | collective-permute-done | bytes 196640 | tf_op jit(solution)/shard_map/ppermute | solution.py:28
  383.0 5.1 %collective-permute-done.47 = bf16[16,3072]{1,0:T(8,128)(2,1)S(1)} collective-permute-done((bf16[16,3072]{1,0:T(8,128)(2,1)S(1)}, bf16[16,3072]{1,0:T(8,128)(2,1)S(1)}, u32[]{:S(2)}, u32[]{:S(2)}) %collective-permute-start.47) | collective-permute-done | bytes 98336 | tf_op jit(solution)/shard_map/ppermute | solution.py:33
  (384 shorter events, 129.6 us)
Async XLA Ops:
  0.6 5.8 %collective-permute-start.1 = (bf16[16,3072]{1,0:T(8,128)(2,1)}, bf16[16,3072]{1,0:T(8,128)(2,1)S(1)}, u32[]{:S(2)}, u32[]{:S(2)}) collective-permute-start(bf16[16,3072]{1,0:T(8,128)(2,1)} %param.11), channel_id=1, source_target_pairs={{0,1},{1,0},{2,3},{3,2},{4,5},{5,4},{6,7},{7,6},{8,9},{9,8},{10,11... | collective-permute-start | bytes 294920 | tf_op jit(solution)/shard_map/ppermute | solution.py:28
  6.5 8.1 %collective-permute-start.2 = (bf16[32,3072]{1,0:T(8,128)(2,1)S(1)}, bf16[32,3072]{1,0:T(8,128)(2,1)S(1)}, u32[]{:S(2)}, u32[]{:S(2)}) collective-permute-start(bf16[32,3072]{1,0:T(8,128)(2,1)S(1)} %maximum_select_fusion.12), channel_id=1, source_target_pairs={{0,2},{2,0},{1,3},{3,1},{4,6},{6,4},{5,7},{7,5},{8,10},{10,8},{9,1... | collective-permute-start | bytes 589832 | tf_op jit(solution)/shard_map/ppermute | solution.py:28
  14.6 15.3 %collective-permute-start.3 = (bf16[64,3072]{1,0:T(8,128)(2,1)S(1)}, bf16[64,3072]{1,0:T(8,128)(2,1)S(1)}, u32[]{:S(2)}, u32[]{:S(2)}) collective-permute-start(bf16[64,3072]{1,0:T(8,128)(2,1)S(1)} %maximum_select_fusion.6), channel_id=1, source_target_pairs={{0,4},{4,0},{1,5},{5,1},{2,6},{6,2},{3,7},{7,3},{8,12},{12,8},{9,1... | collective-permute-start | bytes 1179656 | tf_op jit(solution)/shard_map/ppermute | solution.py:28
  41.2 10.3 %collective-permute-start.4 = (bf16[64,3072]{1,0:T(8,128)(2,1)S(1)}, bf16[64,3072]{1,0:T(8,128)(2,1)S(1)}, u32[]{:S(2)}, u32[]{:S(2)}) collective-permute-start(bf16[64,3072]{1,0:T(8,128)(2,1)S(1)} %select_convert_fusion.5), channel_id=1, source_target_pairs={{0,4},{4,0},{1,5},{5,1},{2,6},{6,2},{3,7},{7,3},{8,12},{12,8},{9,1... | collective-permute-start | bytes 1179656 | tf_op jit(solution)/shard_map/ppermute | solution.py:28
  51.7 5.7 %collective-permute-start.5 = (bf16[32,3072]{1,0:T(8,128)(2,1)S(1)}, bf16[32,3072]{1,0:T(8,128)(2,1)S(1)}, u32[]{:S(2)}, u32[]{:S(2)}) collective-permute-start(bf16[32,3072]{1,0:T(8,128)(2,1)S(1)} %select_convert_fusion.11), channel_id=1, source_target_pairs={{0,2},{2,0},{1,3},{3,1},{4,6},{6,4},{5,7},{7,5},{8,10},{10,8},{9,1... | collective-permute-start | bytes 589832 | tf_op jit(solution)/shard_map/ppermute | solution.py:28
  57.5 2.8 collective-permute-start.6
  57.6 10.9 %collective-permute-start = (bf16[16,64]{1,0:T(8,128)(2,1)S(1)}, bf16[16,64]{1,0:T(8,128)(2,1)S(1)}, u32[]{:S(2)}, u32[]{:S(2)}) collective-permute-start(bf16[16,64]{1,0:T(8,128)(2,1)S(1)} %copy-done.63), channel_id=1, source_target_pairs={{0,8},{1,9},{2,10},{3,11},{4,12},{5,13},{6,14},{7,15},{8,0},{9,1},... | collective-permute-start | bytes 6152 | tf_op jit(solution)/shard_map/ppermute | solution.py:33
  60.3 7.8 %collective-permute-start.7 = (bf16[16,3072]{1,0:T(8,128)(2,1)S(1)}, bf16[16,3072]{1,0:T(8,128)(2,1)S(1)}, u32[]{:S(2)}, u32[]{:S(2)}) collective-permute-start(bf16[16,3072]{1,0:T(8,128)(2,1)S(1)} %add_convert_fusion.5), channel_id=1, source_target_pairs={{0,8},{1,9},{2,10},{3,11},{4,12},{5,13},{6,14},{7,15},{8,0},{9,1},... | collective-permute-start | bytes 294920 | tf_op jit(solution)/shard_map/ppermute | solution.py:33
  70.6 1.4 collective-permute-start.9
  72.0 7.0 %collective-permute-start.10 = (bf16[32,3072]{1,0:T(8,128)(2,1)S(1)}, bf16[32,3072]{1,0:T(8,128)(2,1)S(1)}, u32[]{:S(2)}, u32[]{:S(2)}) collective-permute-start(bf16[32,3072]{1,0:T(8,128)(2,1)S(1)} %maximum_select_fusion.13), channel_id=1, source_target_pairs={{0,2},{2,0},{1,3},{3,1},{4,6},{6,4},{5,7},{7,5},{8,10},{10,8},{9,1... | collective-permute-start | bytes 589832 | tf_op jit(solution)/shard_map/ppermute | solution.py:28
  79.1 10.5 %collective-permute-start.11 = (bf16[64,3072]{1,0:T(8,128)(2,1)S(1)}, bf16[64,3072]{1,0:T(8,128)(2,1)}, u32[]{:S(2)}, u32[]{:S(2)}) collective-permute-start(bf16[64,3072]{1,0:T(8,128)(2,1)S(1)} %maximum_select_fusion.7), channel_id=1, source_target_pairs={{0,4},{4,0},{1,5},{5,1},{2,6},{6,2},{3,7},{7,3},{8,12},{12,8},{9,1... | collective-permute-start | bytes 1179656 | tf_op jit(solution)/shard_map/ppermute | solution.py:28
  107.8 9.5 %collective-permute-start.12 = (bf16[64,3072]{1,0:T(8,128)(2,1)S(1)}, bf16[64,3072]{1,0:T(8,128)(2,1)S(1)}, u32[]{:S(2)}, u32[]{:S(2)}) collective-permute-start(bf16[64,3072]{1,0:T(8,128)(2,1)S(1)} %select_convert_fusion.4), channel_id=1, source_target_pairs={{0,4},{4,0},{1,5},{5,1},{2,6},{6,2},{3,7},{7,3},{8,12},{12,8},{9,1... | collective-permute-start | bytes 1179656 | tf_op jit(solution)/shard_map/ppermute | solution.py:28
  117.5 5.7 %collective-permute-start.13 = (bf16[32,3072]{1,0:T(8,128)(2,1)S(1)}, bf16[32,3072]{1,0:T(8,128)(2,1)S(1)}, u32[]{:S(2)}, u32[]{:S(2)}) collective-permute-start(bf16[32,3072]{1,0:T(8,128)(2,1)S(1)} %select_convert_fusion.10), channel_id=1, source_target_pairs={{0,2},{2,0},{1,3},{3,1},{4,6},{6,4},{5,7},{7,5},{8,10},{10,8},{9,1... | collective-permute-start | bytes 589832 | tf_op jit(solution)/shard_map/ppermute | solution.py:28
  123.4 1.4 collective-permute-start.14
  124.8 8.1 %collective-permute-start.15 = (bf16[16,3072]{1,0:T(8,128)(2,1)S(1)}, bf16[16,3072]{1,0:T(8,128)(2,1)S(1)}, u32[]{:S(2)}, u32[]{:S(2)}) collective-permute-start(bf16[16,3072]{1,0:T(8,128)(2,1)S(1)} %add_convert_fusion.4), channel_id=1, source_target_pairs={{0,8},{1,9},{2,10},{3,11},{4,12},{5,13},{6,14},{7,15},{8,0},{9,1},... | collective-permute-start | bytes 294920 | tf_op jit(solution)/shard_map/ppermute | solution.py:33
  125.2 8.0 %collective-permute-start.8 = (bf16[16,64]{1,0:T(8,128)(2,1)S(1)}, bf16[16,64]{1,0:T(8,128)(2,1)S(1)}, u32[]{:S(2)}, u32[]{:S(2)}) collective-permute-start(bf16[16,64]{1,0:T(8,128)(2,1)S(1)} %copy-done.65), channel_id=1, source_target_pairs={{0,8},{1,9},{2,10},{3,11},{4,12},{5,13},{6,14},{7,15},{8,0},{9,1},... | collective-permute-start | bytes 6152 | tf_op jit(solution)/shard_map/ppermute | solution.py:33
  134.3 1.4 collective-permute-start.17
  135.7 7.0 %collective-permute-start.18 = (bf16[32,3072]{1,0:T(8,128)(2,1)S(1)}, bf16[32,3072]{1,0:T(8,128)(2,1)S(1)}, u32[]{:S(2)}, u32[]{:S(2)}) collective-permute-start(bf16[32,3072]{1,0:T(8,128)(2,1)S(1)} %maximum_select_fusion.14), channel_id=1, source_target_pairs={{0,2},{2,0},{1,3},{3,1},{4,6},{6,4},{5,7},{7,5},{8,10},{10,8},{9,1... | collective-permute-start | bytes 589832 | tf_op jit(solution)/shard_map/ppermute | solution.py:28
  142.8 10.5 %collective-permute-start.19 = (bf16[64,3072]{1,0:T(8,128)(2,1)S(1)}, bf16[64,3072]{1,0:T(8,128)(2,1)}, u32[]{:S(2)}, u32[]{:S(2)}) collective-permute-start(bf16[64,3072]{1,0:T(8,128)(2,1)S(1)} %maximum_select_fusion.8), channel_id=1, source_target_pairs={{0,4},{4,0},{1,5},{5,1},{2,6},{6,2},{3,7},{7,3},{8,12},{12,8},{9,1... | collective-permute-start | bytes 1179656 | tf_op jit(solution)/shard_map/ppermute | solution.py:28
  171.7 9.5 %collective-permute-start.20 = (bf16[64,3072]{1,0:T(8,128)(2,1)S(1)}, bf16[64,3072]{1,0:T(8,128)(2,1)S(1)}, u32[]{:S(2)}, u32[]{:S(2)}) collective-permute-start(bf16[64,3072]{1,0:T(8,128)(2,1)S(1)} %select_convert_fusion.3), channel_id=1, source_target_pairs={{0,4},{4,0},{1,5},{5,1},{2,6},{6,2},{3,7},{7,3},{8,12},{12,8},{9,1... | collective-permute-start | bytes 1179656 | tf_op jit(solution)/shard_map/ppermute | solution.py:28
  181.4 5.7 %collective-permute-start.21 = (bf16[32,3072]{1,0:T(8,128)(2,1)S(1)}, bf16[32,3072]{1,0:T(8,128)(2,1)S(1)}, u32[]{:S(2)}, u32[]{:S(2)}) collective-permute-start(bf16[32,3072]{1,0:T(8,128)(2,1)S(1)} %select_convert_fusion.9), channel_id=1, source_target_pairs={{0,2},{2,0},{1,3},{3,1},{4,6},{6,4},{5,7},{7,5},{8,10},{10,8},{9,1... | collective-permute-start | bytes 589832 | tf_op jit(solution)/shard_map/ppermute | solution.py:28
  187.3 1.4 collective-permute-start.22
  188.7 8.1 %collective-permute-start.23 = (bf16[16,3072]{1,0:T(8,128)(2,1)S(1)}, bf16[16,3072]{1,0:T(8,128)(2,1)S(1)}, u32[]{:S(2)}, u32[]{:S(2)}) collective-permute-start(bf16[16,3072]{1,0:T(8,128)(2,1)S(1)} %add_convert_fusion.3), channel_id=1, source_target_pairs={{0,8},{1,9},{2,10},{3,11},{4,12},{5,13},{6,14},{7,15},{8,0},{9,1},... | collective-permute-start | bytes 294920 | tf_op jit(solution)/shard_map/ppermute | solution.py:33
  189.1 8.0 %collective-permute-start.16 = (bf16[16,64]{1,0:T(8,128)(2,1)S(1)}, bf16[16,64]{1,0:T(8,128)(2,1)S(1)}, u32[]{:S(2)}, u32[]{:S(2)}) collective-permute-start(bf16[16,64]{1,0:T(8,128)(2,1)S(1)} %copy-done.66), channel_id=1, source_target_pairs={{0,8},{1,9},{2,10},{3,11},{4,12},{5,13},{6,14},{7,15},{8,0},{9,1},... | collective-permute-start | bytes 6152 | tf_op jit(solution)/shard_map/ppermute | solution.py:33
  198.2 1.4 collective-permute-start.25
  199.6 7.0 %collective-permute-start.26 = (bf16[32,3072]{1,0:T(8,128)(2,1)S(1)}, bf16[32,3072]{1,0:T(8,128)(2,1)S(1)}, u32[]{:S(2)}, u32[]{:S(2)}) collective-permute-start(bf16[32,3072]{1,0:T(8,128)(2,1)S(1)} %maximum_select_fusion.15), channel_id=1, source_target_pairs={{0,2},{2,0},{1,3},{3,1},{4,6},{6,4},{5,7},{7,5},{8,10},{10,8},{9,1... | collective-permute-start | bytes 589832 | tf_op jit(solution)/shard_map/ppermute | solution.py:28
  206.7 10.5 %collective-permute-start.27 = (bf16[64,3072]{1,0:T(8,128)(2,1)S(1)}, bf16[64,3072]{1,0:T(8,128)(2,1)}, u32[]{:S(2)}, u32[]{:S(2)}) collective-permute-start(bf16[64,3072]{1,0:T(8,128)(2,1)S(1)} %maximum_select_fusion.9), channel_id=1, source_target_pairs={{0,4},{4,0},{1,5},{5,1},{2,6},{6,2},{3,7},{7,3},{8,12},{12,8},{9,1... | collective-permute-start | bytes 1179656 | tf_op jit(solution)/shard_map/ppermute | solution.py:28
  235.4 9.5 %collective-permute-start.28 = (bf16[64,3072]{1,0:T(8,128)(2,1)S(1)}, bf16[64,3072]{1,0:T(8,128)(2,1)S(1)}, u32[]{:S(2)}, u32[]{:S(2)}) collective-permute-start(bf16[64,3072]{1,0:T(8,128)(2,1)S(1)} %select_convert_fusion.2), channel_id=1, source_target_pairs={{0,4},{4,0},{1,5},{5,1},{2,6},{6,2},{3,7},{7,3},{8,12},{12,8},{9,1... | collective-permute-start | bytes 1179656 | tf_op jit(solution)/shard_map/ppermute | solution.py:28
  245.1 5.7 %collective-permute-start.29 = (bf16[32,3072]{1,0:T(8,128)(2,1)S(1)}, bf16[32,3072]{1,0:T(8,128)(2,1)S(1)}, u32[]{:S(2)}, u32[]{:S(2)}) collective-permute-start(bf16[32,3072]{1,0:T(8,128)(2,1)S(1)} %select_convert_fusion.8), channel_id=1, source_target_pairs={{0,2},{2,0},{1,3},{3,1},{4,6},{6,4},{5,7},{7,5},{8,10},{10,8},{9,1... | collective-permute-start | bytes 589832 | tf_op jit(solution)/shard_map/ppermute | solution.py:28
  251.0 1.4 collective-permute-start.30
  252.4 8.0 %collective-permute-start.31 = (bf16[16,3072]{1,0:T(8,128)(2,1)S(1)}, bf16[16,3072]{1,0:T(8,128)(2,1)S(1)}, u32[]{:S(2)}, u32[]{:S(2)}) collective-permute-start(bf16[16,3072]{1,0:T(8,128)(2,1)S(1)} %add_convert_fusion.2), channel_id=1, source_target_pairs={{0,8},{1,9},{2,10},{3,11},{4,12},{5,13},{6,14},{7,15},{8,0},{9,1},... | collective-permute-start | bytes 294920 | tf_op jit(solution)/shard_map/ppermute | solution.py:33
  252.8 8.0 %collective-permute-start.24 = (bf16[16,64]{1,0:T(8,128)(2,1)S(1)}, bf16[16,64]{1,0:T(8,128)(2,1)S(1)}, u32[]{:S(2)}, u32[]{:S(2)}) collective-permute-start(bf16[16,64]{1,0:T(8,128)(2,1)S(1)} %copy-done.67), channel_id=1, source_target_pairs={{0,8},{1,9},{2,10},{3,11},{4,12},{5,13},{6,14},{7,15},{8,0},{9,1},... | collective-permute-start | bytes 6152 | tf_op jit(solution)/shard_map/ppermute | solution.py:33
  261.9 1.4 collective-permute-start.33
  263.3 7.0 %collective-permute-start.34 = (bf16[32,3072]{1,0:T(8,128)(2,1)S(1)}, bf16[32,3072]{1,0:T(8,128)(2,1)S(1)}, u32[]{:S(2)}, u32[]{:S(2)}) collective-permute-start(bf16[32,3072]{1,0:T(8,128)(2,1)S(1)} %maximum_select_fusion.16), channel_id=1, source_target_pairs={{0,2},{2,0},{1,3},{3,1},{4,6},{6,4},{5,7},{7,5},{8,10},{10,8},{9,1... | collective-permute-start | bytes 589832 | tf_op jit(solution)/shard_map/ppermute | solution.py:28
  270.4 10.5 %collective-permute-start.35 = (bf16[64,3072]{1,0:T(8,128)(2,1)S(1)}, bf16[64,3072]{1,0:T(8,128)(2,1)}, u32[]{:S(2)}, u32[]{:S(2)}) collective-permute-start(bf16[64,3072]{1,0:T(8,128)(2,1)S(1)} %maximum_select_fusion.10), channel_id=1, source_target_pairs={{0,4},{4,0},{1,5},{5,1},{2,6},{6,2},{3,7},{7,3},{8,12},{12,8},{9,1... | collective-permute-start | bytes 1179656 | tf_op jit(solution)/shard_map/ppermute | solution.py:28
  299.3 9.6 %collective-permute-start.36 = (bf16[64,3072]{1,0:T(8,128)(2,1)S(1)}, bf16[64,3072]{1,0:T(8,128)(2,1)S(1)}, u32[]{:S(2)}, u32[]{:S(2)}) collective-permute-start(bf16[64,3072]{1,0:T(8,128)(2,1)S(1)} %select_convert_fusion.1), channel_id=1, source_target_pairs={{0,4},{4,0},{1,5},{5,1},{2,6},{6,2},{3,7},{7,3},{8,12},{12,8},{9,1... | collective-permute-start | bytes 1179656 | tf_op jit(solution)/shard_map/ppermute | solution.py:28
  309.1 5.7 %collective-permute-start.37 = (bf16[32,3072]{1,0:T(8,128)(2,1)S(1)}, bf16[32,3072]{1,0:T(8,128)(2,1)S(1)}, u32[]{:S(2)}, u32[]{:S(2)}) collective-permute-start(bf16[32,3072]{1,0:T(8,128)(2,1)S(1)} %select_convert_fusion.7), channel_id=1, source_target_pairs={{0,2},{2,0},{1,3},{3,1},{4,6},{6,4},{5,7},{7,5},{8,10},{10,8},{9,1... | collective-permute-start | bytes 589832 | tf_op jit(solution)/shard_map/ppermute | solution.py:28
  314.9 1.4 collective-permute-start.38
  316.4 8.0 %collective-permute-start.39 = (bf16[16,3072]{1,0:T(8,128)(2,1)S(1)}, bf16[16,3072]{1,0:T(8,128)(2,1)S(1)}, u32[]{:S(2)}, u32[]{:S(2)}) collective-permute-start(bf16[16,3072]{1,0:T(8,128)(2,1)S(1)} %add_convert_fusion.1), channel_id=1, source_target_pairs={{0,8},{1,9},{2,10},{3,11},{4,12},{5,13},{6,14},{7,15},{8,0},{9,1},... | collective-permute-start | bytes 294920 | tf_op jit(solution)/shard_map/ppermute | solution.py:33
  316.8 8.0 %collective-permute-start.32 = (bf16[16,64]{1,0:T(8,128)(2,1)S(1)}, bf16[16,64]{1,0:T(8,128)(2,1)S(1)}, u32[]{:S(2)}, u32[]{:S(2)}) collective-permute-start(bf16[16,64]{1,0:T(8,128)(2,1)S(1)} %copy-done.68), channel_id=1, source_target_pairs={{0,8},{1,9},{2,10},{3,11},{4,12},{5,13},{6,14},{7,15},{8,0},{9,1},... | collective-permute-start | bytes 6152 | tf_op jit(solution)/shard_map/ppermute | solution.py:33
  325.9 1.4 collective-permute-start.41
  327.3 7.0 %collective-permute-start.42 = (bf16[32,3072]{1,0:T(8,128)(2,1)S(1)}, bf16[32,3072]{1,0:T(8,128)(2,1)S(1)}, u32[]{:S(2)}, u32[]{:S(2)}) collective-permute-start(bf16[32,3072]{1,0:T(8,128)(2,1)S(1)} %maximum_select_fusion.17), channel_id=1, source_target_pairs={{0,2},{2,0},{1,3},{3,1},{4,6},{6,4},{5,7},{7,5},{8,10},{10,8},{9,1... | collective-permute-start | bytes 589832 | tf_op jit(solution)/shard_map/ppermute | solution.py:28
  334.4 10.5 %collective-permute-start.43 = (bf16[64,3072]{1,0:T(8,128)(2,1)S(1)}, bf16[64,3072]{1,0:T(8,128)(2,1)}, u32[]{:S(2)}, u32[]{:S(2)}) collective-permute-start(bf16[64,3072]{1,0:T(8,128)(2,1)S(1)} %maximum_select_fusion.11), channel_id=1, source_target_pairs={{0,4},{4,0},{1,5},{5,1},{2,6},{6,2},{3,7},{7,3},{8,12},{12,8},{9,1... | collective-permute-start | bytes 1179656 | tf_op jit(solution)/shard_map/ppermute | solution.py:28
  363.1 9.5 %collective-permute-start.44 = (bf16[64,3072]{1,0:T(8,128)(2,1)S(1)}, bf16[64,3072]{1,0:T(8,128)(2,1)S(1)}, u32[]{:S(2)}, u32[]{:S(2)}) collective-permute-start(bf16[64,3072]{1,0:T(8,128)(2,1)S(1)} %select_convert_fusion), channel_id=1, source_target_pairs={{0,4},{4,0},{1,5},{5,1},{2,6},{6,2},{3,7},{7,3},{8,12},{12,8},{9,1... | collective-permute-start | bytes 1179656 | tf_op jit(solution)/shard_map/ppermute | solution.py:28
  372.8 5.7 %collective-permute-start.45 = (bf16[32,3072]{1,0:T(8,128)(2,1)S(1)}, bf16[32,3072]{1,0:T(8,128)(2,1)S(1)}, u32[]{:S(2)}, u32[]{:S(2)}) collective-permute-start(bf16[32,3072]{1,0:T(8,128)(2,1)S(1)} %select_convert_fusion.6), channel_id=1, source_target_pairs={{0,2},{2,0},{1,3},{3,1},{4,6},{6,4},{5,7},{7,5},{8,10},{10,8},{9,1... | collective-permute-start | bytes 589832 | tf_op jit(solution)/shard_map/ppermute | solution.py:28
  378.6 1.4 collective-permute-start.46
  380.0 8.0 %collective-permute-start.47 = (bf16[16,3072]{1,0:T(8,128)(2,1)S(1)}, bf16[16,3072]{1,0:T(8,128)(2,1)S(1)}, u32[]{:S(2)}, u32[]{:S(2)}) collective-permute-start(bf16[16,3072]{1,0:T(8,128)(2,1)S(1)} %add_convert_fusion), channel_id=1, source_target_pairs={{0,8},{1,9},{2,10},{3,11},{4,12},{5,13},{6,14},{7,15},{8,0},{9,1},... | collective-permute-start | bytes 294920 | tf_op jit(solution)/shard_map/ppermute | solution.py:33
  380.5 8.0 %collective-permute-start.40 = (bf16[16,64]{1,0:T(8,128)(2,1)S(1)}, bf16[16,64]{1,0:T(8,128)(2,1)S(1)}, u32[]{:S(2)}, u32[]{:S(2)}) collective-permute-start(bf16[16,64]{1,0:T(8,128)(2,1)S(1)} %copy-done.64), channel_id=1, source_target_pairs={{0,8},{1,9},{2,10},{3,11},{4,12},{5,13},{6,14},{7,15},{8,0},{9,1},... | collective-permute-start | bytes 6152 | tf_op jit(solution)/shard_map/ppermute | solution.py:33
  (70 other events, 844.7 us)
where the time goes:
time: 392 us; the launch traced here: 390 us
  waiting for transfers between devices  198 us (51%)
  matrix products  78.3 us (20%)
  starting transfers between devices  44.6 us (11%)
  other arithmetic  35.8 us (9%)
  local copies, waits for them, and re-layouts  20.6 us (5%)
  between operations  13.2 us (3%)
    ppermute x36, waiting for transfers between devices, partner(): return lax.ppermute(block, axis, route)  166 us
    ppermute x12, waiting for transfers between devices, from_behind(): lax.ppermute(value, axis, [(i, (i + by) % size) for i in range(size)])  31.7 us
    ppermute x36, starting transfers between devices, partner(): return lax.ppermute(block, axis, route)  25.7 us
    dot_general x6, matrix products, head_terms_of(): jnp.dot(normed, w_qkv[0], preferred_element_type=jnp.float32)  21.7 us
    ppermute x12, starting transfers between devices, from_behind(): lax.ppermute(value, axis, [(i, (i + by) % size) for i in range(size)])  18.9 us
    dot_general x6, matrix products, head_terms_of(): jnp.dot(normed, w_qkv[1], preferred_element_type=jnp.float32)  16.8 us
    dot_general x6, matrix products, head_terms_of(): fresh_values = jnp.dot(normed, w_qkv[2], preferred_element_type=jnp.float32)  15.2 us
    dot_general x2, local copies, waits for them, and re-layouts, head_terms_of(): jnp.dot(normed, w_qkv[0], preferred_element_type=jnp.float32)  9.4 us
  transfers between devices with their start and end apart: 48, of which 39 were waited for; matrix products, arithmetic and copies ran while one was open for 6% of the time, Pallas kernels for 0%

commit v1 on v0

v1 whole, which is shorter than its diff:
```python
import functools
import math

import jax
import jax.numpy as jnp
from jax import lax
from jax.experimental import pallas as pl
from jax.experimental.pallas import tpu as pltpu
from jax.sharding import PartitionSpec as P

HS = 128
GROUP = 8
VMEM = pltpu.VMEM
SMEM = pltpu.SMEM
EPS = 1e-6


def f32(value):
    return value.astype(jnp.float32)


def layer_norm(tokens, offset_row, scale_row):
    average = jnp.mean(tokens, axis=-1, keepdims=True)
    centred = tokens - average
    variance = jnp.mean(centred * centred, axis=-1, keepdims=True)
    return (centred * lax.rsqrt(variance + EPS) * (1.0 + scale_row) + offset_row).astype(
        jnp.bfloat16
    )


def dot(left, right):
    return jnp.dot(left, right, preferred_element_type=jnp.float32)


def block_kernel(with_latent, refs):
    if with_latent:
        (flags, own, other, latent, w_embed, mod, gains, w_qkv, w_out, k_in, v_in) = refs[:11]
        (kept, sent, k_cache, v_cache, normed, attended) = refs[11:]
    else:
        (flags, own, other, gains, w_qkv, w_out, k_in, v_in) = refs[:8]
        (kept, sent, k_cache, v_cache, normed, attended) = refs[8:]
    half = own.shape[0]
    rows = 2 * half
    heads = w_out.shape[0] // HS

    def take_rows():
        normed[:half, :] = own[...]
        normed[half:, :] = other[...]

    if with_latent:
        first = flags[0] == 0

        @pl.when(first)
        def _():
            hidden = f32(dot(latent[...], w_embed[...]).astype(jnp.bfloat16))
            normed[...] = layer_norm(hidden, mod[0:1, :], mod[1:2, :])

        pl.when(jnp.logical_not(first))(take_rows)
    else:
        take_rows()

    start = pl.multiple_of(flags[1] * rows, rows)
    k_cache[...] = k_in[...]
    v_cache[...] = v_in[...]

    def head_norm(values, gain_row):
        power = jnp.mean(values * values, axis=-1, keepdims=True)
        return (values * lax.rsqrt(power + EPS) * gain_row).astype(jnp.bfloat16)

    tokens = normed[...]
    keys = dot(tokens, w_qkv[1])
    for head in range(heads):
        part = slice(head * HS, (head + 1) * HS)
        k_cache[pl.ds(start, rows), part] = head_norm(keys[:, part], gains[1:2, :])
    v_cache[pl.ds(start, rows), :] = dot(tokens, w_qkv[2]).astype(jnp.bfloat16)
    queries = dot(tokens, w_qkv[0])
    for head in range(heads):
        part = slice(head * HS, (head + 1) * HS)
        query = head_norm(queries[:, part], gains[0:1, :])
        scores = lax.dot_general(
            query, k_cache[:, part], (((1,), (1,)), ((), ())), preferred_element_type=jnp.float32
        ) / math.sqrt(HS)
        weights = jnp.exp(scores)
        totals = jnp.sum(weights, axis=-1, keepdims=True)
        mixed = dot(weights.astype(jnp.bfloat16), v_cache[:, part])
        attended[:, part] = (mixed / totals).astype(jnp.bfloat16)
    width = w_out.shape[1]
    tile = width // 4
    heads_out = attended[...]
    for low in range(0, width, tile):
        projected = dot(heads_out, w_out[:, low : low + tile])
        kept[:, low : low + tile] = projected[:half, :]
        sent[:, low : low + tile] = projected[half:, :].astype(jnp.bfloat16)


def block(flags, own, other, latent, w_embed, mod, gains, w_qkv, w_out, k_cache, v_cache):
    half, width = own.shape
    columns = w_out.shape[0]
    with_latent = latent is not None
    args = [flags, own, other]
    if with_latent:
        args += [latent, w_embed, mod]
    args += [gains, w_qkv, w_out, k_cache, v_cache]
    count = len(args)
    flops = 2 * 2 * half * columns * width * 4
    whole = pl.BlockSpec(memory_space=VMEM)
    return pl.pallas_call(
        lambda *refs: block_kernel(with_latent, refs),
        out_shape=(
            jax.ShapeDtypeStruct((half, width), jnp.float32),
            jax.ShapeDtypeStruct((half, width), jnp.bfloat16),
            jax.ShapeDtypeStruct(k_cache.shape, jnp.bfloat16),
            jax.ShapeDtypeStruct(v_cache.shape, jnp.bfloat16),
        ),
        in_specs=[pl.BlockSpec(memory_space=SMEM)] + [whole] * (count - 1),
        out_specs=(whole,) * 4,
        scratch_shapes=[
            VMEM((2 * half, width), jnp.bfloat16),
            VMEM((2 * half, columns), jnp.bfloat16),
        ],
        input_output_aliases={count - 2: 2, count - 1: 3},
        compiler_params=pltpu.CompilerParams(vmem_limit_bytes=32 * 1024 * 1024),
        cost_estimate=pl.CostEstimate(
            flops=flops, bytes_accessed=4 * columns * width * 2, transcendentals=0
        ),
        name="block",
    )(*args)


def result_kernel(with_latent, refs):
    flags, kept, came, hidden, latent, gate, w_embed, out = refs

    def finish(base):
        out[...] = (base + gate[2:3, :] * (kept[...] + f32(came[...]))).astype(jnp.bfloat16)

    if with_latent:
        first = flags[0] == 0

        @pl.when(first)
        def _():
            finish(f32(dot(latent[...], w_embed[...]).astype(jnp.bfloat16)))

        @pl.when(jnp.logical_not(first))
        def _():
            finish(f32(hidden[...]))
    else:
        finish(f32(hidden[...]))


def result_rows(with_latent, flags, kept, came, hidden, latent, mod, w_embed):
    whole = pl.BlockSpec(memory_space=VMEM)
    return pl.pallas_call(
        lambda *refs: result_kernel(with_latent, refs),
        out_shape=jax.ShapeDtypeStruct(hidden.shape, jnp.bfloat16),
        in_specs=[pl.BlockSpec(memory_space=SMEM)] + [whole] * 6,
        out_specs=whole,
        compiler_params=pltpu.CompilerParams(vmem_limit_bytes=8 * 1024 * 1024),
        name="result",
    )(flags, kept, came, hidden, latent, mod, w_embed)


def renew_kernel(flags, kept, came, hidden, latent, mod, final_mod, w_final, out):
    last = flags[2] == 1

    @pl.when(last)
    def _():
        total = f32(hidden[...]) + mod[2:3, :] * (kept[...] + f32(came[...]))
        total = f32(total.astype(jnp.bfloat16))
        normed = layer_norm(total, final_mod[0:1, :], final_mod[1:2, :])
        velocity = dot(normed, w_final[...])
        out[...] = (f32(latent[...]) + velocity).astype(jnp.bfloat16)

    @pl.when(jnp.logical_not(last))
    def _():
        out[...] = latent[...]


def renew(flags, kept, came, hidden, latent, mod, final_mod, w_final):
    whole = pl.BlockSpec(memory_space=VMEM)
    return pl.pallas_call(
        renew_kernel,
        out_shape=jax.ShapeDtypeStruct(latent.shape, jnp.bfloat16),
        in_specs=[pl.BlockSpec(memory_space=SMEM)] + [whole] * 7,
        out_specs=whole,
        compiler_params=pltpu.CompilerParams(vmem_limit_bytes=8 * 1024 * 1024),
        name="renew",
    )(flags, kept, came, hidden, latent, mod, final_mod, w_final)


def norm_kernel(hidden, mod, out):
    out[...] = layer_norm(f32(hidden[...]), mod[0:1, :], mod[1:2, :])


def norm_rows(hidden, mod):
    whole = pl.BlockSpec(memory_space=VMEM)
    return pl.pallas_call(
        norm_kernel,
        out_shape=jax.ShapeDtypeStruct(hidden.shape, jnp.bfloat16),
        in_specs=[whole] * 2,
        out_specs=whole,
        compiler_params=pltpu.CompilerParams(vmem_limit_bytes=8 * 1024 * 1024),
        name="norm",
    )(hidden, mod)


def chip_partner(device, stage):
    return device ^ (4 if (device & 1) == stage else 2)


def routes(devices, partner_of):
    return [(device, partner_of(device)) for device in devices]


def send(value, route):
    return lax.ppermute(value, "section", route)


def stack(upper, lower):
    return jnp.concatenate([upper, lower], 0)


def gather_chips(rows, devices):
    rows = stack(rows, send(rows, routes(devices, lambda d: chip_partner(d, 1))))
    return stack(rows, send(rows, routes(devices, lambda d: chip_partner(d, 0))))


def reduce_rows(kept, sent, devices):
    kept = kept + f32(send(sent, routes(devices, lambda d: d ^ 1)))
    for stage in range(2):
        half = kept.shape[0] // 2
        came = send(
            kept[half:].astype(jnp.bfloat16), routes(devices, lambda d: chip_partner(d, stage))
        )
        if stage == 1:
            return (kept[:half], came)
        kept = kept[:half] + f32(came)


def body(
    hidden_in,
    latent_in,
    w_qkv,
    w_out,
    stale_kv,
    qk_gain,
    block_mod,
    final_mod,
    w_final,
    w_embed,
    patch_flow,
):
    size = lax.axis_size("section")
    ticks = patch_flow.shape[0]
    everyone = range(size)
    head, tail = range(GROUP), range(size - GROUP, size)
    front, rest = range(size - GROUP), range(GROUP, size)
    section = lax.axis_index("section") // GROUP
    is_last = (section == size // GROUP - 1).astype(jnp.int32)
    mod = lax.dynamic_index_in_dim(block_mod, section, 0, keepdims=False)
    gains = lax.dynamic_index_in_dim(qk_gain, section, 0, keepdims=False)
    patches = lax.dynamic_index_in_dim(patch_flow, section, 1, keepdims=False)
    k_cache, v_cache = stale_kv[0], stale_kv[1]

    hidden, latent = hidden_in, latent_in
    for tick in range(ticks):
        flags = jnp.stack([section.astype(jnp.int32), patches[tick], is_last])
        later = tick > 0
        own = gather_chips(norm_rows(hidden, mod), rest if later else everyone)
        other = send(own, routes(rest if later else everyone, lambda d: d ^ 1))
        latents = None
        if later:
            latents = gather_chips(latent, head)
            latents = stack(latents, send(latents, routes(head, lambda d: d ^ 1)))
        kept, sent, k_cache, v_cache = block(
            flags, own, other, latents, w_embed, mod, gains, w_qkv, w_out, k_cache, v_cache
        )
        total, came = reduce_rows(kept, sent, front)
        result = result_rows(later, flags, total, came, hidden, latent, mod, w_embed)
        moved = send(result, routes(front, lambda d: d + GROUP))
        kept, sent, result = lax.optimization_barrier((kept, sent, result))
        total, came = reduce_rows(kept, sent, tail)
        latent = renew(flags, total, came, hidden, latent, mod, final_mod, w_final)
        latent = send(latent, routes(everyone, lambda d: (d + GROUP) % size))
        hidden = moved
    embedded = dot(latent, w_embed).astype(jnp.bfloat16)
    return (jnp.where(section == 0, embedded, hidden), latent)


def solution(mesh):
    in_specs = (
        P(("groups", "section"), None),
        P(("groups", "section"), None),
        P(None, None, "section"),
        P("section", None),
        P("groups", None, "section"),
        P(),
        P("groups", None, None),
        P("groups", None),
        P(),
        P(),
        P(),
    )
    out_specs = (P(("groups", "section"), None), P(("groups", "section"), None))
    return jax.shard_map(body, mesh=mesh, in_specs=in_specs, out_specs=out_specs, check_vma=False)
```

time: 392 us -> 389 us (level)
  starting transfers between devices: 44.6 us -> 220 us
  waiting for transfers between devices: 198 us -> 103 us
  matrix products: 78.3 us -> 0.82 us
  Pallas kernels: 0 us -> 32.3 us
  other arithmetic: 35.8 us -> 8.46 us
  between operations: 13.2 us -> 2.22 us
    ppermute x48 -> x81, starting transfers between devices: 44.6 us -> 220 us  [send(): return lax.ppermute(value, 'section', route)]
    ppermute x48 -> x81, waiting for transfers between devices: 198 us -> 103 us  [send(): return lax.ppermute(value, 'section', route)]
    dot_general x48 -> x1, matrix products: 78.3 us -> 0.82 us  [dot(): return jnp.dot(left, right, preferred_element_type=jnp.float32)]
    pallas_call x0 -> x24, Pallas kernels: none -> 32.3 us  [the longest x6 22.9 us: block(): pl.pallas_call(lambda *refs: block_kernel(with_latent, refs), out_shape=(...]
    reduce_sum x24 -> x0, other arithmetic: 17.2 us -> none  [the longest x12 9.21 us: layer_norm(): variance = jnp.mean(centred * centred, axis=-1, keepdims=True)]
    dot_general x3 -> x0, local copies, waits for them, and re-layouts: 13.7 us -> none  [the longest x2 9.4 us: head_terms_of(): jnp.dot(normed, w_qkv[0], preferred_element_type=jnp.float32)]
    unnamed x142 -> x31, local copies, waits for them, and re-layouts: 1.29 us -> 13.4 us
    rsqrt x24 -> x0, other arithmetic: 6.66 us -> none  [the longest x12 6.56 us: head_norm(): lax.rsqrt(jnp.mean(values * values, axis=-1, keepdims=True) + 1e-06)]
  transfers between devices with their start and end apart: 48 -> 81, of which waited for: 39 -> 46; matrix products, arithmetic and copies ran while one was open for 6% -> 4% of each run, Pallas kernels for 0% -> 1%
where the time goes in v1:
time: 389 us; the launch traced here: 387 us
  starting transfers between devices  220 us (57%)
  waiting for transfers between devices  103 us (26%)
  Pallas kernels  32.3 us (8%)
  local copies, waits for them, and re-layouts  19.6 us (5%)
  other arithmetic  8.46 us (2%)
    ppermute x81, starting transfers between devices, send(): return lax.ppermute(value, 'section', route)  220 us
    ppermute x81, waiting for transfers between devices, send(): return lax.ppermute(value, 'section', route)  103 us
    pallas_call x6, Pallas kernels, block(): pl.pallas_call(lambda *refs: block_kernel(with_latent, refs), out_shape=(...  22.9 us
    unnamed x31, local copies, waits for them, and re-layouts  13.4 us
  transfers between devices with their start and end apart: 81, of which 46 were waited for; matrix products, arithmetic and copies ran while one was open for 4% of the time, Pallas kernels for 1%

profile of v1, /device:TPU:0, one launch (start us, length us, event | category | flops | bytes accessed | tf_op | source)
XLA Modules:
  0.0 387.2 jit_solution(15215524501575167312)
XLA Ops:
  2.7 3.1 collective-permute-start
  5.8 2.6 collective-permute-done
  16.8 3.0 copy-done.1
  21.5 3.0 block.6
  28.5 3.9 %collective-permute-start.4 = (bf16[32,3072]{1,0:T(8,128)(2,1)S(1)}, bf16[32,3072]{1,0:T(8,128)(2,1)S(1)}, u32[]{:S(2)}, u32[]{:S(2)}) collective-permute-start(bf16[32,3072]{1,0:T(8,128)(2,1)S(1)} %slice.369), channel_id=1, source_target_pairs={{0,4},{1,3},{2,6},{3,1},{4,0},{5,7},{6,2},{7,5},{16,20},{17,19},{1... | collective-permute-start | bytes 589832 | tf_op jit(solution)/shard_map/ppermute | solution.py:215
  32.4 3.6 collective-permute-done.4
  36.1 3.9 %collective-permute-start.5 = (bf16[16,3072]{1,0:T(8,128)(2,1)S(1)}, bf16[16,3072]{1,0:T(8,128)(2,1)S(1)}, u32[]{:S(2)}, u32[]{:S(2)}) collective-permute-start(bf16[16,3072]{1,0:T(8,128)(2,1)S(1)} %slice.381), channel_id=1, source_target_pairs={{0,2},{1,5},{2,0},{3,7},{4,6},{5,1},{6,4},{7,3},{16,18},{17,21},{1... | collective-permute-start | bytes 294920 | tf_op jit(solution)/shard_map/ppermute | solution.py:215
  40.0 2.6 collective-permute-done.5.refs_2_
  60.1 15.3 %collective-permute-start.13 = (bf16[16,64]{1,0:T(8,128)(2,1)S(1)}, bf16[16,64]{1,0:T(8,128)(2,1)S(1)}, u32[]{:S(2)}, u32[]{:S(2)}) collective-permute-start(bf16[16,64]{1,0:T(8,128)(2,1)S(1)} %renew.6), channel_id=1, source_target_pairs={{0,8},{1,9},{2,10},{3,11},{4,12},{5,13},{6,14},{7,15},{8,0},{9,1},... | collective-permute-start | bytes 6152 | tf_op jit(solution)/shard_map/ppermute | solution.py:215
  77.0 3.6 collective-permute-start.14
  82.5 3.3 collective-permute-start.15
  91.1 3.0 copy-done.2
  94.1 3.9 %block.7 = (f32[64,3072]{1,0:T(8,128)S(1)}, bf16[64,3072]{1,0:T(8,128)(2,1)S(1)}, bf16[256,384]{1,0:T(8,128)(2,1)S(1)}, bf16[256,384]{1,0:T(8,128)(2,1)S(1)}) custom-call(s32[3]{0:T(128)S(1)} %add_add_fusion.4.refs_0_.flags, bf16[64,3072]{1,0:T(8,128)(2,1)S(1)} %pad_maximum_fusion.1.refs_1_, ...), custom_call_target="tpu_custom_call", output_to_operand_aliasing={{2}: (9, {}), {3}: (10, {})} | custom-call | flops 1207959552 | bytes 9437184 | tf_op jit(solution)/shard_map/block/pallas_call | solution.py:107
  101.9 3.3 collective-permute-start.18
  105.3 4.2 %collective-permute-done.18 = bf16[32,3072]{1,0:T(8,128)(2,1)S(1)} collective-permute-done((bf16[32,3072]{1,0:T(8,128)(2,1)S(1)}, bf16[32,3072]{1,0:T(8,128)(2,1)S(1)}, u32[]{:S(2)}, u32[]{:S(2)}) %collective-permute-start.18) | collective-permute-done | bytes 196640 | tf_op jit(solution)/shard_map/ppermute | solution.py:215
  109.5 3.6 collective-permute-start.19
  113.2 2.9 collective-permute-done.19.refs_2_
  124.8 18.8 %collective-permute-start.27 = (bf16[16,64]{1,0:T(8,128)(2,1)S(1)}, bf16[16,64]{1,0:T(8,128)(2,1)S(1)}, u32[]{:S(2)}, u32[]{:S(2)}) collective-permute-start(bf16[16,64]{1,0:T(8,128)(2,1)S(1)} %renew.7), channel_id=1, source_target_pairs={{0,8},{1,9},{2,10},{3,11},{4,12},{5,13},{6,14},{7,15},{8,0},{9,1},... | collective-permute-start | bytes 6152 | tf_op jit(solution)/shard_map/ppermute | solution.py:215
  153.3 3.0 collective-permute-done.29
  159.3 4.1 %block.8 = (f32[64,3072]{1,0:T(8,128)S(1)}, bf16[64,3072]{1,0:T(8,128)(2,1)S(1)}, bf16[256,384]{1,0:T(8,128)(2,1)S(1)}, bf16[256,384]{1,0:T(8,128)(2,1)S(1)}) custom-call(s32[3]{0:T(128)S(1)} %add_add_fusion.3.refs_0_.flags, bf16[64,3072]{1,0:T(8,128)(2,1)S(1)} %pad_maximum_fusion.2.refs_1_, ...), custom_call_target="tpu_custom_call", output_to_operand_aliasing={{2}: (9, {}), {3}: (10, {})} | custom-call | flops 1207959552 | bytes 9437184 | tf_op jit(solution)/shard_map/block/pallas_call | solution.py:107
  169.7 5.0 %collective-permute-done.32 = bf16[32,3072]{1,0:T(8,128)(2,1)S(1)} collective-permute-done((bf16[32,3072]{1,0:T(8,128)(2,1)S(1)}, bf16[32,3072]{1,0:T(8,128)(2,1)S(1)}, u32[]{:S(2)}, u32[]{:S(2)}) %collective-permute-start.32) | collective-permute-done | bytes 196640 | tf_op jit(solution)/shard_map/ppermute | solution.py:215
  174.8 2.6 collective-permute-start.33
  177.4 3.9 %collective-permute-done.33.refs_2_ = bf16[16,3072]{1,0:T(8,128)(2,1)S(1)} collective-permute-done((bf16[16,3072]{1,0:T(8,128)(2,1)S(1)}, bf16[16,3072]{1,0:T(8,128)(2,1)S(1)}, u32[]{:S(2)}, u32[]{:S(2)}) %collective-permute-start.33) | collective-permute-done | bytes 98336 | tf_op jit(solution)/shard_map/ppermute | solution.py:215
  190.0 18.4 %collective-permute-start.41 = (bf16[16,64]{1,0:T(8,128)(2,1)S(1)}, bf16[16,64]{1,0:T(8,128)(2,1)S(1)}, u32[]{:S(2)}, u32[]{:S(2)}) collective-permute-start(bf16[16,64]{1,0:T(8,128)(2,1)S(1)} %renew.8), channel_id=1, source_target_pairs={{0,8},{1,9},{2,10},{3,11},{4,12},{5,13},{6,14},{7,15},{8,0},{9,1},... | collective-permute-start | bytes 6152 | tf_op jit(solution)/shard_map/ppermute | solution.py:215
  210.0 3.4 collective-permute-start.42
  215.4 3.7 collective-permute-start.43
  224.1 3.9 %block.9 = (f32[64,3072]{1,0:T(8,128)S(1)}, bf16[64,3072]{1,0:T(8,128)(2,1)S(1)}, bf16[256,384]{1,0:T(8,128)(2,1)S(1)}, bf16[256,384]{1,0:T(8,128)(2,1)S(1)}) custom-call(s32[3]{0:T(128)S(1)} %add_add_fusion.2.refs_0_.flags, bf16[64,3072]{1,0:T(8,128)(2,1)S(1)} %pad_maximum_fusion.3.refs_1_, ...), custom_call_target="tpu_custom_call", output_to_operand_aliasing={{2}: (9, {}), {3}: (10, {})} | custom-call | flops 1207959552 | bytes 9437184 | tf_op jit(solution)/shard_map/block/pallas_call | solution.py:107
  231.7 3.8 collective-permute-start.46
  235.5 3.8 collective-permute-done.46
  239.4 3.4 collective-permute-start.47
  242.8 3.1 collective-permute-done.47.refs_2_
  254.6 19.0 %collective-permute-start.55 = (bf16[16,64]{1,0:T(8,128)(2,1)S(1)}, bf16[16,64]{1,0:T(8,128)(2,1)S(1)}, u32[]{:S(2)}, u32[]{:S(2)}) collective-permute-start(bf16[16,64]{1,0:T(8,128)(2,1)S(1)} %renew.9), channel_id=1, source_target_pairs={{0,8},{1,9},{2,10},{3,11},{4,12},{5,13},{6,14},{7,15},{8,0},{9,1},... | collective-permute-start | bytes 6152 | tf_op jit(solution)/shard_map/ppermute | solution.py:215
  275.1 2.7 collective-permute-start.56
  280.6 3.4 collective-permute-start.57
  289.3 4.1 %block.10 = (f32[64,3072]{1,0:T(8,128)S(1)}, bf16[64,3072]{1,0:T(8,128)(2,1)S(1)}, bf16[256,384]{1,0:T(8,128)(2,1)S(1)}, bf16[256,384]{1,0:T(8,128)(2,1)S(1)}) custom-call(s32[3]{0:T(128)S(1)} %add_add_fusion.1.refs_0_.flags, bf16[64,3072]{1,0:T(8,128)(2,1)S(1)} %pad_maximum_fusion.4.refs_1_, ...), custom_call_target="tpu_custom_call", output_to_operand_aliasing={{2}: (9, {}), {3}: (10, {})} | custom-call | flops 1207959552 | bytes 9437184 | tf_op jit(solution)/shard_map/block/pallas_call | solution.py:107
  297.1 3.4 collective-permute-start.60
  300.6 4.1 %collective-permute-done.60 = bf16[32,3072]{1,0:T(8,128)(2,1)S(1)} collective-permute-done((bf16[32,3072]{1,0:T(8,128)(2,1)S(1)}, bf16[32,3072]{1,0:T(8,128)(2,1)S(1)}, u32[]{:S(2)}, u32[]{:S(2)}) %collective-permute-start.60) | collective-permute-done | bytes 196640 | tf_op jit(solution)/shard_map/ppermute | solution.py:215
  304.8 2.7 collective-permute-start.61
  307.5 3.7 collective-permute-done.61.refs_2_
  320.0 18.9 %collective-permute-start.69 = (bf16[16,64]{1,0:T(8,128)(2,1)S(1)}, bf16[16,64]{1,0:T(8,128)(2,1)S(1)}, u32[]{:S(2)}, u32[]{:S(2)}) collective-permute-start(bf16[16,64]{1,0:T(8,128)(2,1)S(1)} %renew.10), channel_id=1, source_target_pairs={{0,8},{1,9},{2,10},{3,11},{4,12},{5,13},{6,14},{7,15},{8,0},{9,1},... | collective-permute-start | bytes 6152 | tf_op jit(solution)/shard_map/ppermute | solution.py:215
  340.4 2.7 collective-permute-start.70
  345.9 3.4 collective-permute-start.71
  354.6 3.9 %block.11 = (f32[64,3072]{1,0:T(8,128)S(1)}, bf16[64,3072]{1,0:T(8,128)(2,1)S(1)}, bf16[256,384]{1,0:T(8,128)(2,1)S(1)}, bf16[256,384]{1,0:T(8,128)(2,1)S(1)}) custom-call(s32[3]{0:T(128)S(1)} %add_add_fusion.refs_0_.flags, bf16[64,3072]{1,0:T(8,128)(2,1)S(1)} %pad_maximum_fusion.5.refs_1_, ...), custom_call_target="tpu_custom_call", output_to_operand_aliasing={{2}: (9, {}), {3}: (10, {})} | custom-call | flops 1207959552 | bytes 9437184 | tf_op jit(solution)/shard_map/block/pallas_call | solution.py:107
  362.2 3.4 collective-permute-start.74
  365.6 4.2 %collective-permute-done.74 = bf16[32,3072]{1,0:T(8,128)(2,1)S(1)} collective-permute-done((bf16[32,3072]{1,0:T(8,128)(2,1)S(1)}, bf16[32,3072]{1,0:T(8,128)(2,1)S(1)}, u32[]{:S(2)}, u32[]{:S(2)}) %collective-permute-start.74) | collective-permute-done | bytes 196640 | tf_op jit(solution)/shard_map/ppermute | solution.py:215
  369.8 2.8 collective-permute-start.75
  372.6 3.7 collective-permute-done.75.refs_2_
  381.3 4.5 %collective-permute-done.79 = bf16[16,64]{1,0:T(8,128)(2,1)S(1)} collective-permute-done((bf16[16,64]{1,0:T(8,128)(2,1)S(1)}, bf16[16,64]{1,0:T(8,128)(2,1)S(1)}, u32[]{:S(2)}, u32[]{:S(2)}) %collective-permute-start.79) | collective-permute-done | bytes 2080 | tf_op jit(solution)/shard_map/ppermute | solution.py:215
  (268 shorter events, 144.8 us)
Async XLA Ops:
  2.7 5.7 %collective-permute-start = (bf16[16,3072]{1,0:T(8,128)(2,1)S(1)}, bf16[16,3072]{1,0:T(8,128)(2,1)S(1)}, u32[]{:S(2)}, u32[]{:S(2)}) collective-permute-start(bf16[16,3072]{1,0:T(8,128)(2,1)S(1)} %norm.6), channel_id=1, source_target_pairs={{0,2},{1,5},{2,0},{3,7},{4,6},{5,1},{6,4},{7,3},{8,10},{9,13},{10,... | collective-permute-start | bytes 294920 | tf_op jit(solution)/shard_map/ppermute | solution.py:215
  8.4 5.8 %collective-permute-start.1 = (bf16[32,3072]{1,0:T(8,128)(2,1)S(1)}, bf16[32,3072]{1,0:T(8,128)(2,1)S(1)}, u32[]{:S(2)}, u32[]{:S(2)}) collective-permute-start(bf16[32,3072]{1,0:T(8,128)(2,1)S(1)} %pad_maximum_fusion.6), channel_id=1, source_target_pairs={{0,4},{1,3},{2,6},{3,1},{4,0},{5,7},{6,2},{7,5},{8,12},{9,11},{10,... | collective-permute-start | bytes 589832 | tf_op jit(solution)/shard_map/ppermute | solution.py:215
  24.5 3.9 collective-permute-start.3
  28.5 7.6 %collective-permute-start.4 = (bf16[32,3072]{1,0:T(8,128)(2,1)S(1)}, bf16[32,3072]{1,0:T(8,128)(2,1)S(1)}, u32[]{:S(2)}, u32[]{:S(2)}) collective-permute-start(bf16[32,3072]{1,0:T(8,128)(2,1)S(1)} %slice.369), channel_id=1, source_target_pairs={{0,4},{1,3},{2,6},{3,1},{4,0},{5,7},{6,2},{7,5},{16,20},{17,19},{1... | collective-permute-start | bytes 589832 | tf_op jit(solution)/shard_map/ppermute | solution.py:215
  36.1 6.5 %collective-permute-start.5 = (bf16[16,3072]{1,0:T(8,128)(2,1)S(1)}, bf16[16,3072]{1,0:T(8,128)(2,1)S(1)}, u32[]{:S(2)}, u32[]{:S(2)}) collective-permute-start(bf16[16,3072]{1,0:T(8,128)(2,1)S(1)} %slice.381), channel_id=1, source_target_pairs={{0,2},{1,5},{2,0},{3,7},{4,6},{5,1},{6,4},{7,3},{16,18},{17,21},{1... | collective-permute-start | bytes 294920 | tf_op jit(solution)/shard_map/ppermute | solution.py:215
  43.2 5.1 %collective-permute-start.10 = (bf16[64,3072]{1,0:T(8,128)(2,1)S(1)}, bf16[64,3072]{1,0:T(8,128)(2,1)S(1)}, u32[]{:S(2)}, u32[]{:S(2)}) collective-permute-start(bf16[64,3072]{1,0:T(8,128)(2,1)S(1)} %get-tuple-element.39), channel_id=1, source_target_pairs={{8,9},{9,8},{10,11},{11,10},{12,13},{13,12},{14,15},{15,14},{24,25... | collective-permute-start | bytes 1179656 | tf_op jit(solution)/shard_map/ppermute | solution.py:215
  49.9 30.6 %collective-permute-start.8 = (bf16[32,3072]{1,0:T(8,128)(2,1)}, bf16[32,3072]{1,0:T(8,128)(2,1)}, u32[]{:S(2)}, u32[]{:S(2)}) collective-permute-start(bf16[32,3072]{1,0:T(8,128)(2,1)} %pad_maximum_fusion.7), channel_id=1, source_target_pairs={{8,12},{9,11},{10,14},{11,9},{12,8},{13,15},{14,10},{15,13},{24,28... | collective-permute-start | bytes 589832 | tf_op jit(solution)/shard_map/ppermute | solution.py:215
  53.6 4.4 %collective-permute-start.12 = (bf16[16,3072]{1,0:T(8,128)(2,1)}, bf16[16,3072]{1,0:T(8,128)(2,1)}, u32[]{:S(2)}, u32[]{:S(2)}) collective-permute-start(bf16[16,3072]{1,0:T(8,128)(2,1)} %slice.380), channel_id=1, source_target_pairs={{8,10},{9,13},{10,8},{11,15},{12,14},{13,9},{14,12},{15,11},{24,26... | collective-permute-start | bytes 294920 | tf_op jit(solution)/shard_map/ppermute | solution.py:215
  60.1 16.8 %collective-permute-start.13 = (bf16[16,64]{1,0:T(8,128)(2,1)S(1)}, bf16[16,64]{1,0:T(8,128)(2,1)S(1)}, u32[]{:S(2)}, u32[]{:S(2)}) collective-permute-start(bf16[16,64]{1,0:T(8,128)(2,1)S(1)} %renew.6), channel_id=1, source_target_pairs={{0,8},{1,9},{2,10},{3,11},{4,12},{5,13},{6,14},{7,15},{8,0},{9,1},... | collective-permute-start | bytes 6152 | tf_op jit(solution)/shard_map/ppermute | solution.py:215
  77.0 5.5 %collective-permute-start.14 = (bf16[16,64]{1,0:T(8,128)(2,1)S(1)}, bf16[16,64]{1,0:T(8,128)(2,1)S(1)}, u32[]{:S(2)}, u32[]{:S(2)}) collective-permute-start(bf16[16,64]{1,0:T(8,128)(2,1)S(1)} %collective-permute-done.13.refs_4_.latent), channel_id=1, source_target_pairs={{0,2},{1,5},{2,0},{3,7},{4,6},{5,1},{6,4},{7,3},{16,18},{17,21},{1... | collective-permute-start | bytes 6152 | tf_op jit(solution)/shard_map/ppermute | solution.py:215
  81.6 9.5 %collective-permute-start.9 = (bf16[64,3072]{1,0:T(8,128)(2,1)S(1)}, bf16[64,3072]{1,0:T(8,128)(2,1)S(1)}, u32[]{:S(2)}, u32[]{:S(2)}) collective-permute-start(bf16[64,3072]{1,0:T(8,128)(2,1)S(1)} %pad_maximum_fusion.1.refs_1_), channel_id=1, source_target_pairs={{8,9},{9,8},{10,11},{11,10},{12,13},{13,12},{14,15},{15,14},{24,25... | collective-permute-start | bytes 1179656 | tf_op jit(solution)/shard_map/ppermute | solution.py:215
  82.5 5.5 %collective-permute-start.15 = (bf16[32,64]{1,0:T(8,128)(2,1)S(1)}, bf16[32,64]{1,0:T(8,128)(2,1)S(1)}, u32[]{:S(2)}, u32[]{:S(2)}) collective-permute-start(bf16[32,64]{1,0:T(8,128)(2,1)S(1)} %pad_maximum_fusion.22), channel_id=1, source_target_pairs={{0,4},{1,3},{2,6},{3,1},{4,0},{5,7},{6,2},{7,5},{16,20},{17,19},{1... | collective-permute-start | bytes 12296 | tf_op jit(solution)/shard_map/ppermute | solution.py:215
  101.9 7.6 %collective-permute-start.18 = (bf16[32,3072]{1,0:T(8,128)(2,1)S(1)}, bf16[32,3072]{1,0:T(8,128)(2,1)S(1)}, u32[]{:S(2)}, u32[]{:S(2)}) collective-permute-start(bf16[32,3072]{1,0:T(8,128)(2,1)S(1)} %slice.367), channel_id=1, source_target_pairs={{0,4},{1,3},{2,6},{3,1},{4,0},{5,7},{6,2},{7,5},{16,20},{17,19},{1... | collective-permute-start | bytes 589832 | tf_op jit(solution)/shard_map/ppermute | solution.py:215
  109.5 6.5 %collective-permute-start.19 = (bf16[16,3072]{1,0:T(8,128)(2,1)S(1)}, bf16[16,3072]{1,0:T(8,128)(2,1)S(1)}, u32[]{:S(2)}, u32[]{:S(2)}) collective-permute-start(bf16[16,3072]{1,0:T(8,128)(2,1)S(1)} %slice.379), channel_id=1, source_target_pairs={{0,2},{1,5},{2,0},{3,7},{4,6},{5,1},{6,4},{7,3},{16,18},{17,21},{1... | collective-permute-start | bytes 294920 | tf_op jit(solution)/shard_map/ppermute | solution.py:215
  116.8 5.1 %collective-permute-start.24 = (bf16[64,3072]{1,0:T(8,128)(2,1)S(1)}, bf16[64,3072]{1,0:T(8,128)(2,1)S(1)}, u32[]{:S(2)}, u32[]{:S(2)}) collective-permute-start(bf16[64,3072]{1,0:T(8,128)(2,1)S(1)} %get-tuple-element.45), channel_id=1, source_target_pairs={{8,9},{9,8},{10,11},{11,10},{12,13},{13,12},{14,15},{15,14},{24,25... | collective-permute-start | bytes 1179656 | tf_op jit(solution)/shard_map/ppermute | solution.py:215
  122.7 25.0 %collective-permute-start.22 = (bf16[32,3072]{1,0:T(8,128)(2,1)S(1)}, bf16[32,3072]{1,0:T(8,128)(2,1)S(1)}, u32[]{:S(2)}, u32[]{:S(2)}) collective-permute-start(bf16[32,3072]{1,0:T(8,128)(2,1)S(1)} %pad_maximum_fusion.8), channel_id=1, source_target_pairs={{8,12},{9,11},{10,14},{11,9},{12,8},{13,15},{14,10},{15,13},{24,28... | collective-permute-start | bytes 589832 | tf_op jit(solution)/shard_map/ppermute | solution.py:215
  124.8 20.4 %collective-permute-start.27 = (bf16[16,64]{1,0:T(8,128)(2,1)S(1)}, bf16[16,64]{1,0:T(8,128)(2,1)S(1)}, u32[]{:S(2)}, u32[]{:S(2)}) collective-permute-start(bf16[16,64]{1,0:T(8,128)(2,1)S(1)} %renew.7), channel_id=1, source_target_pairs={{0,8},{1,9},{2,10},{3,11},{4,12},{5,13},{6,14},{7,15},{8,0},{9,1},... | collective-permute-start | bytes 6152 | tf_op jit(solution)/shard_map/ppermute | solution.py:215
  145.2 5.5 %collective-permute-start.28 = (bf16[16,64]{1,0:T(8,128)(2,1)S(1)}, bf16[16,64]{1,0:T(8,128)(2,1)S(1)}, u32[]{:S(2)}, u32[]{:S(2)}) collective-permute-start(bf16[16,64]{1,0:T(8,128)(2,1)S(1)} %collective-permute-done.27.refs_4_.latent), channel_id=1, source_target_pairs={{0,2},{1,5},{2,0},{3,7},{4,6},{5,1},{6,4},{7,3},{16,18},{17,21},{1... | collective-permute-start | bytes 6152 | tf_op jit(solution)/shard_map/ppermute | solution.py:215
  147.8 11.5 %collective-permute-start.23 = (bf16[64,3072]{1,0:T(8,128)(2,1)S(1)}, bf16[64,3072]{1,0:T(8,128)(2,1)S(1)}, u32[]{:S(2)}, u32[]{:S(2)}) collective-permute-start(bf16[64,3072]{1,0:T(8,128)(2,1)S(1)} %pad_maximum_fusion.2.refs_1_), channel_id=1, source_target_pairs={{8,9},{9,8},{10,11},{11,10},{12,13},{13,12},{14,15},{15,14},{24,25... | collective-permute-start | bytes 1179656 | tf_op jit(solution)/shard_map/ppermute | solution.py:215
  150.7 5.5 %collective-permute-start.29 = (bf16[32,64]{1,0:T(8,128)(2,1)S(1)}, bf16[32,64]{1,0:T(8,128)(2,1)S(1)}, u32[]{:S(2)}, u32[]{:S(2)}) collective-permute-start(bf16[32,64]{1,0:T(8,128)(2,1)S(1)} %pad_maximum_fusion.23), channel_id=1, source_target_pairs={{0,4},{1,3},{2,6},{3,1},{4,0},{5,7},{6,2},{7,5},{16,20},{17,19},{1... | collective-permute-start | bytes 12296 | tf_op jit(solution)/shard_map/ppermute | solution.py:215
  167.1 7.6 %collective-permute-start.32 = (bf16[32,3072]{1,0:T(8,128)(2,1)S(1)}, bf16[32,3072]{1,0:T(8,128)(2,1)S(1)}, u32[]{:S(2)}, u32[]{:S(2)}) collective-permute-start(bf16[32,3072]{1,0:T(8,128)(2,1)S(1)} %slice.365), channel_id=1, source_target_pairs={{0,4},{1,3},{2,6},{3,1},{4,0},{5,7},{6,2},{7,5},{16,20},{17,19},{1... | collective-permute-start | bytes 589832 | tf_op jit(solution)/shard_map/ppermute | solution.py:215
  174.8 6.5 %collective-permute-start.33 = (bf16[16,3072]{1,0:T(8,128)(2,1)S(1)}, bf16[16,3072]{1,0:T(8,128)(2,1)S(1)}, u32[]{:S(2)}, u32[]{:S(2)}) collective-permute-start(bf16[16,3072]{1,0:T(8,128)(2,1)S(1)} %slice.377), channel_id=1, source_target_pairs={{0,2},{1,5},{2,0},{3,7},{4,6},{5,1},{6,4},{7,3},{16,18},{17,21},{1... | collective-permute-start | bytes 294920 | tf_op jit(solution)/shard_map/ppermute | solution.py:215
  182.0 5.1 %collective-permute-start.38 = (bf16[64,3072]{1,0:T(8,128)(2,1)S(1)}, bf16[64,3072]{1,0:T(8,128)(2,1)S(1)}, u32[]{:S(2)}, u32[]{:S(2)}) collective-permute-start(bf16[64,3072]{1,0:T(8,128)(2,1)S(1)} %get-tuple-element.51), channel_id=1, source_target_pairs={{8,9},{9,8},{10,11},{11,10},{12,13},{13,12},{14,15},{15,14},{24,25... | collective-permute-start | bytes 1179656 | tf_op jit(solution)/shard_map/ppermute | solution.py:215
  188.0 25.4 %collective-permute-start.36 = (bf16[32,3072]{1,0:T(8,128)(2,1)S(1)}, bf16[32,3072]{1,0:T(8,128)(2,1)S(1)}, u32[]{:S(2)}, u32[]{:S(2)}) collective-permute-start(bf16[32,3072]{1,0:T(8,128)(2,1)S(1)} %pad_maximum_fusion.9), channel_id=1, source_target_pairs={{8,12},{9,11},{10,14},{11,9},{12,8},{13,15},{14,10},{15,13},{24,28... | collective-permute-start | bytes 589832 | tf_op jit(solution)/shard_map/ppermute | solution.py:215
  190.0 19.9 %collective-permute-start.41 = (bf16[16,64]{1,0:T(8,128)(2,1)S(1)}, bf16[16,64]{1,0:T(8,128)(2,1)S(1)}, u32[]{:S(2)}, u32[]{:S(2)}) collective-permute-start(bf16[16,64]{1,0:T(8,128)(2,1)S(1)} %renew.8), channel_id=1, source_target_pairs={{0,8},{1,9},{2,10},{3,11},{4,12},{5,13},{6,14},{7,15},{8,0},{9,1},... | collective-permute-start | bytes 6152 | tf_op jit(solution)/shard_map/ppermute | solution.py:215
  210.0 5.5 %collective-permute-start.42 = (bf16[16,64]{1,0:T(8,128)(2,1)S(1)}, bf16[16,64]{1,0:T(8,128)(2,1)S(1)}, u32[]{:S(2)}, u32[]{:S(2)}) collective-permute-start(bf16[16,64]{1,0:T(8,128)(2,1)S(1)} %collective-permute-done.41.refs_4_.latent), channel_id=1, source_target_pairs={{0,2},{1,5},{2,0},{3,7},{4,6},{5,1},{6,4},{7,3},{16,18},{17,21},{1... | collective-permute-start | bytes 6152 | tf_op jit(solution)/shard_map/ppermute | solution.py:215
  213.4 10.7 %collective-permute-start.37 = (bf16[64,3072]{1,0:T(8,128)(2,1)S(1)}, bf16[64,3072]{1,0:T(8,128)(2,1)S(1)}, u32[]{:S(2)}, u32[]{:S(2)}) collective-permute-start(bf16[64,3072]{1,0:T(8,128)(2,1)S(1)} %pad_maximum_fusion.3.refs_1_), channel_id=1, source_target_pairs={{8,9},{9,8},{10,11},{11,10},{12,13},{13,12},{14,15},{15,14},{24,25... | collective-permute-start | bytes 1179656 | tf_op jit(solution)/shard_map/ppermute | solution.py:215
  215.4 5.5 %collective-permute-start.43 = (bf16[32,64]{1,0:T(8,128)(2,1)S(1)}, bf16[32,64]{1,0:T(8,128)(2,1)S(1)}, u32[]{:S(2)}, u32[]{:S(2)}) collective-permute-start(bf16[32,64]{1,0:T(8,128)(2,1)S(1)} %pad_maximum_fusion.24), channel_id=1, source_target_pairs={{0,4},{1,3},{2,6},{3,1},{4,0},{5,7},{6,2},{7,5},{16,20},{17,19},{1... | collective-permute-start | bytes 12296 | tf_op jit(solution)/shard_map/ppermute | solution.py:215
  231.7 7.6 %collective-permute-start.46 = (bf16[32,3072]{1,0:T(8,128)(2,1)S(1)}, bf16[32,3072]{1,0:T(8,128)(2,1)S(1)}, u32[]{:S(2)}, u32[]{:S(2)}) collective-permute-start(bf16[32,3072]{1,0:T(8,128)(2,1)S(1)} %slice.363), channel_id=1, source_target_pairs={{0,4},{1,3},{2,6},{3,1},{4,0},{5,7},{6,2},{7,5},{16,20},{17,19},{1... | collective-permute-start | bytes 589832 | tf_op jit(solution)/shard_map/ppermute | solution.py:215
  239.4 6.5 %collective-permute-start.47 = (bf16[16,3072]{1,0:T(8,128)(2,1)S(1)}, bf16[16,3072]{1,0:T(8,128)(2,1)S(1)}, u32[]{:S(2)}, u32[]{:S(2)}) collective-permute-start(bf16[16,3072]{1,0:T(8,128)(2,1)S(1)} %slice.375), channel_id=1, source_target_pairs={{0,2},{1,5},{2,0},{3,7},{4,6},{5,1},{6,4},{7,3},{16,18},{17,21},{1... | collective-permute-start | bytes 294920 | tf_op jit(solution)/shard_map/ppermute | solution.py:215
  246.6 5.1 %collective-permute-start.52 = (bf16[64,3072]{1,0:T(8,128)(2,1)S(1)}, bf16[64,3072]{1,0:T(8,128)(2,1)S(1)}, u32[]{:S(2)}, u32[]{:S(2)}) collective-permute-start(bf16[64,3072]{1,0:T(8,128)(2,1)S(1)} %get-tuple-element.57), channel_id=1, source_target_pairs={{8,9},{9,8},{10,11},{11,10},{12,13},{13,12},{14,15},{15,14},{24,25... | collective-permute-start | bytes 1179656 | tf_op jit(solution)/shard_map/ppermute | solution.py:215
  252.6 25.3 %collective-permute-start.50 = (bf16[32,3072]{1,0:T(8,128)(2,1)S(1)}, bf16[32,3072]{1,0:T(8,128)(2,1)S(1)}, u32[]{:S(2)}, u32[]{:S(2)}) collective-permute-start(bf16[32,3072]{1,0:T(8,128)(2,1)S(1)} %pad_maximum_fusion.10), channel_id=1, source_target_pairs={{8,12},{9,11},{10,14},{11,9},{12,8},{13,15},{14,10},{15,13},{24,28... | collective-permute-start | bytes 589832 | tf_op jit(solution)/shard_map/ppermute | solution.py:215
  254.6 20.6 %collective-permute-start.55 = (bf16[16,64]{1,0:T(8,128)(2,1)S(1)}, bf16[16,64]{1,0:T(8,128)(2,1)S(1)}, u32[]{:S(2)}, u32[]{:S(2)}) collective-permute-start(bf16[16,64]{1,0:T(8,128)(2,1)S(1)} %renew.9), channel_id=1, source_target_pairs={{0,8},{1,9},{2,10},{3,11},{4,12},{5,13},{6,14},{7,15},{8,0},{9,1},... | collective-permute-start | bytes 6152 | tf_op jit(solution)/shard_map/ppermute | solution.py:215
  275.1 5.5 %collective-permute-start.56 = (bf16[16,64]{1,0:T(8,128)(2,1)S(1)}, bf16[16,64]{1,0:T(8,128)(2,1)S(1)}, u32[]{:S(2)}, u32[]{:S(2)}) collective-permute-start(bf16[16,64]{1,0:T(8,128)(2,1)S(1)} %collective-permute-done.55.refs_4_.latent), channel_id=1, source_target_pairs={{0,2},{1,5},{2,0},{3,7},{4,6},{5,1},{6,4},{7,3},{16,18},{17,21},{1... | collective-permute-start | bytes 6152 | tf_op jit(solution)/shard_map/ppermute | solution.py:215
  277.9 11.3 %collective-permute-start.51 = (bf16[64,3072]{1,0:T(8,128)(2,1)S(1)}, bf16[64,3072]{1,0:T(8,128)(2,1)S(1)}, u32[]{:S(2)}, u32[]{:S(2)}) collective-permute-start(bf16[64,3072]{1,0:T(8,128)(2,1)S(1)} %pad_maximum_fusion.4.refs_1_), channel_id=1, source_target_pairs={{8,9},{9,8},{10,11},{11,10},{12,13},{13,12},{14,15},{15,14},{24,25... | collective-permute-start | bytes 1179656 | tf_op jit(solution)/shard_map/ppermute | solution.py:215
  280.6 5.5 %collective-permute-start.57 = (bf16[32,64]{1,0:T(8,128)(2,1)S(1)}, bf16[32,64]{1,0:T(8,128)(2,1)S(1)}, u32[]{:S(2)}, u32[]{:S(2)}) collective-permute-start(bf16[32,64]{1,0:T(8,128)(2,1)S(1)} %pad_maximum_fusion.25), channel_id=1, source_target_pairs={{0,4},{1,3},{2,6},{3,1},{4,0},{5,7},{6,2},{7,5},{16,20},{17,19},{1... | collective-permute-start | bytes 12296 | tf_op jit(solution)/shard_map/ppermute | solution.py:215
  297.1 7.6 %collective-permute-start.60 = (bf16[32,3072]{1,0:T(8,128)(2,1)S(1)}, bf16[32,3072]{1,0:T(8,128)(2,1)S(1)}, u32[]{:S(2)}, u32[]{:S(2)}) collective-permute-start(bf16[32,3072]{1,0:T(8,128)(2,1)S(1)} %slice.361), channel_id=1, source_target_pairs={{0,4},{1,3},{2,6},{3,1},{4,0},{5,7},{6,2},{7,5},{16,20},{17,19},{1... | collective-permute-start | bytes 589832 | tf_op jit(solution)/shard_map/ppermute | solution.py:215
  304.8 6.5 %collective-permute-start.61 = (bf16[16,3072]{1,0:T(8,128)(2,1)S(1)}, bf16[16,3072]{1,0:T(8,128)(2,1)S(1)}, u32[]{:S(2)}, u32[]{:S(2)}) collective-permute-start(bf16[16,3072]{1,0:T(8,128)(2,1)S(1)} %slice.373), channel_id=1, source_target_pairs={{0,2},{1,5},{2,0},{3,7},{4,6},{5,1},{6,4},{7,3},{16,18},{17,21},{1... | collective-permute-start | bytes 294920 | tf_op jit(solution)/shard_map/ppermute | solution.py:215
  312.0 5.1 %collective-permute-start.66 = (bf16[64,3072]{1,0:T(8,128)(2,1)S(1)}, bf16[64,3072]{1,0:T(8,128)(2,1)S(1)}, u32[]{:S(2)}, u32[]{:S(2)}) collective-permute-start(bf16[64,3072]{1,0:T(8,128)(2,1)S(1)} %get-tuple-element.63), channel_id=1, source_target_pairs={{8,9},{9,8},{10,11},{11,10},{12,13},{13,12},{14,15},{15,14},{24,25... | collective-permute-start | bytes 1179656 | tf_op jit(solution)/shard_map/ppermute | solution.py:215
  318.0 25.2 %collective-permute-start.64 = (bf16[32,3072]{1,0:T(8,128)(2,1)S(1)}, bf16[32,3072]{1,0:T(8,128)(2,1)S(1)}, u32[]{:S(2)}, u32[]{:S(2)}) collective-permute-start(bf16[32,3072]{1,0:T(8,128)(2,1)S(1)} %pad_maximum_fusion.11), channel_id=1, source_target_pairs={{8,12},{9,11},{10,14},{11,9},{12,8},{13,15},{14,10},{15,13},{24,28... | collective-permute-start | bytes 589832 | tf_op jit(solution)/shard_map/ppermute | solution.py:215
  320.0 20.4 %collective-permute-start.69 = (bf16[16,64]{1,0:T(8,128)(2,1)S(1)}, bf16[16,64]{1,0:T(8,128)(2,1)S(1)}, u32[]{:S(2)}, u32[]{:S(2)}) collective-permute-start(bf16[16,64]{1,0:T(8,128)(2,1)S(1)} %renew.10), channel_id=1, source_target_pairs={{0,8},{1,9},{2,10},{3,11},{4,12},{5,13},{6,14},{7,15},{8,0},{9,1},... | collective-permute-start | bytes 6152 | tf_op jit(solution)/shard_map/ppermute | solution.py:215
  340.4 5.5 %collective-permute-start.70 = (bf16[16,64]{1,0:T(8,128)(2,1)S(1)}, bf16[16,64]{1,0:T(8,128)(2,1)S(1)}, u32[]{:S(2)}, u32[]{:S(2)}) collective-permute-start(bf16[16,64]{1,0:T(8,128)(2,1)S(1)} %collective-permute-done.69.refs_4_.latent), channel_id=1, source_target_pairs={{0,2},{1,5},{2,0},{3,7},{4,6},{5,1},{6,4},{7,3},{16,18},{17,21},{1... | collective-permute-start | bytes 6152 | tf_op jit(solution)/shard_map/ppermute | solution.py:215
  343.2 11.3 %collective-permute-start.65 = (bf16[64,3072]{1,0:T(8,128)(2,1)S(1)}, bf16[64,3072]{1,0:T(8,128)(2,1)S(1)}, u32[]{:S(2)}, u32[]{:S(2)}) collective-permute-start(bf16[64,3072]{1,0:T(8,128)(2,1)S(1)} %pad_maximum_fusion.5.refs_1_), channel_id=1, source_target_pairs={{8,9},{9,8},{10,11},{11,10},{12,13},{13,12},{14,15},{15,14},{24,25... | collective-permute-start | bytes 1179656 | tf_op jit(solution)/shard_map/ppermute | solution.py:215
  345.9 5.5 %collective-permute-start.71 = (bf16[32,64]{1,0:T(8,128)(2,1)S(1)}, bf16[32,64]{1,0:T(8,128)(2,1)S(1)}, u32[]{:S(2)}, u32[]{:S(2)}) collective-permute-start(bf16[32,64]{1,0:T(8,128)(2,1)S(1)} %pad_maximum_fusion.26), channel_id=1, source_target_pairs={{0,4},{1,3},{2,6},{3,1},{4,0},{5,7},{6,2},{7,5},{16,20},{17,19},{1... | collective-permute-start | bytes 12296 | tf_op jit(solution)/shard_map/ppermute | solution.py:215
  362.2 7.6 %collective-permute-start.74 = (bf16[32,3072]{1,0:T(8,128)(2,1)S(1)}, bf16[32,3072]{1,0:T(8,128)(2,1)S(1)}, u32[]{:S(2)}, u32[]{:S(2)}) collective-permute-start(bf16[32,3072]{1,0:T(8,128)(2,1)S(1)} %slice.359), channel_id=1, source_target_pairs={{0,4},{1,3},{2,6},{3,1},{4,0},{5,7},{6,2},{7,5},{16,20},{17,19},{1... | collective-permute-start | bytes 589832 | tf_op jit(solution)/shard_map/ppermute | solution.py:215
  369.8 6.5 %collective-permute-start.75 = (bf16[16,3072]{1,0:T(8,128)(2,1)S(1)}, bf16[16,3072]{1,0:T(8,128)(2,1)S(1)}, u32[]{:S(2)}, u32[]{:S(2)}) collective-permute-start(bf16[16,3072]{1,0:T(8,128)(2,1)S(1)} %slice.371), channel_id=1, source_target_pairs={{0,2},{1,5},{2,0},{3,7},{4,6},{5,1},{6,4},{7,3},{16,18},{17,21},{1... | collective-permute-start | bytes 294920 | tf_op jit(solution)/shard_map/ppermute | solution.py:215
  379.3 6.5 %collective-permute-start.80 = (bf16[16,3072]{1,0:T(8,128)(2,1)S(1)}, bf16[16,3072]{1,0:T(8,128)(2,1)S(1)}, u32[]{:S(2)}, u32[]{:S(2)}) collective-permute-start(bf16[16,3072]{1,0:T(8,128)(2,1)S(1)} %result.11), channel_id=1, source_target_pairs={{0,8},{1,9},{2,10},{3,11},{4,12},{5,13},{6,14},{7,15},{16,24},{17,... | collective-permute-start | bytes 294920 | tf_op jit(solution)/shard_map/ppermute | solution.py:215
  381.2 4.6 %collective-permute-start.79 = (bf16[16,64]{1,0:T(8,128)(2,1)S(1)}, bf16[16,64]{1,0:T(8,128)(2,1)S(1)}, u32[]{:S(2)}, u32[]{:S(2)}) collective-permute-start(bf16[16,64]{1,0:T(8,128)(2,1)S(1)} %renew.11), channel_id=1, source_target_pairs={{0,8},{1,9},{2,10},{3,11},{4,12},{5,13},{6,14},{7,15},{8,0},{9,1},... | collective-permute-start | bytes 6152 | tf_op jit(solution)/shard_map/ppermute | solution.py:215
  (47 other events, 280.5 us)

commit v2 on v1

v2 whole, which is shorter than its diff:
```python
import functools
import math

import jax
import jax.numpy as jnp
from jax import lax
from jax.experimental import pallas as pl
from jax.experimental.pallas import tpu as pltpu
from jax.sharding import PartitionSpec as P

HS = 128
GROUP = 8
VMEM = pltpu.VMEM
SMEM = pltpu.SMEM
EPS = 1e-6
CHIPS = 4
CHIP_STEPS = (6, 4, 2)
BLOCK_MIB = 8


def f32(value):
    return value.astype(jnp.float32)


def layer_norm(tokens, offset_row, scale_row):
    average = jnp.mean(tokens, axis=-1, keepdims=True)
    centred = tokens - average
    variance = jnp.mean(centred * centred, axis=-1, keepdims=True)
    return (centred * lax.rsqrt(variance + EPS) * (1.0 + scale_row) + offset_row).astype(
        jnp.bfloat16
    )


def dot(left, right):
    return jnp.dot(left, right, preferred_element_type=jnp.float32)


WHOLE = pl.BlockSpec(memory_space=VMEM)
SCALARS = pl.BlockSpec(memory_space=SMEM)
LANES = 128


def params(mebibytes):
    return pltpu.CompilerParams(vmem_limit_bytes=mebibytes * 1024 * 1024)


def block_kernel(
    flags, own, other, gains, w_qkv, w_out, k_in, v_in, kept, sent, k_cache, v_cache, normed, attended
):
    half = own.shape[0]
    rows = 2 * half
    heads = w_out.shape[0] // HS
    normed[:half, :] = own[...]
    normed[half:, :] = other[...]
    start = pl.multiple_of(flags[1] * rows, rows)
    k_cache[...] = k_in[...]
    v_cache[...] = v_in[...]

    def head_norm(values, gain_row):
        power = jnp.mean(values * values, axis=-1, keepdims=True)
        return (values * lax.rsqrt(power + EPS) * gain_row).astype(jnp.bfloat16)

    tokens = normed[...]
    keys = dot(tokens, w_qkv[1])
    for head in range(heads):
        part = slice(head * HS, (head + 1) * HS)
        k_cache[pl.ds(start, rows), part] = head_norm(keys[:, part], gains[1:2, :])
    v_cache[pl.ds(start, rows), :] = dot(tokens, w_qkv[2]).astype(jnp.bfloat16)
    queries = dot(tokens, w_qkv[0])
    for head in range(heads):
        part = slice(head * HS, (head + 1) * HS)
        query = head_norm(queries[:, part], gains[0:1, :])
        scores = lax.dot_general(
            query, k_cache[:, part], (((1,), (1,)), ((), ())), preferred_element_type=jnp.float32
        ) / math.sqrt(HS)
        weights = jnp.exp(scores)
        totals = jnp.sum(weights, axis=-1, keepdims=True)
        mixed = dot(weights.astype(jnp.bfloat16), v_cache[:, part])
        attended[:, part] = (mixed / totals).astype(jnp.bfloat16)
    width = w_out.shape[1]
    tile = width // 4
    heads_out = attended[...]
    for low in range(0, width, tile):
        projected = dot(heads_out, w_out[:, low : low + tile])
        kept[:, low : low + tile] = projected[:half, :]
        sent[:, low : low + tile] = projected[half:, :].astype(jnp.bfloat16)


def block(flags, own, other, gains, w_qkv, w_out, k_cache, v_cache):
    half, width = own.shape
    columns = w_out.shape[0]
    return pl.pallas_call(
        block_kernel,
        out_shape=(
            jax.ShapeDtypeStruct((half, width), jnp.float32),
            jax.ShapeDtypeStruct((half, width), jnp.bfloat16),
            jax.ShapeDtypeStruct(k_cache.shape, jnp.bfloat16),
            jax.ShapeDtypeStruct(v_cache.shape, jnp.bfloat16),
        ),
        in_specs=[SCALARS] + [WHOLE] * 7,
        out_specs=(WHOLE,) * 4,
        scratch_shapes=[
            VMEM((2 * half, width), jnp.bfloat16),
            VMEM((2 * half, columns), jnp.bfloat16),
        ],
        input_output_aliases={6: 2, 7: 3},
        compiler_params=params(BLOCK_MIB),
        cost_estimate=pl.CostEstimate(
            flops=16 * half * columns * width,
            bytes_accessed=8 * columns * width,
            transcendentals=0,
        ),
        name="block",
    )(flags, own, other, gains, w_qkv, w_out, k_cache, v_cache)


def split_kernel(kept, came, mine, *others):
    rows = mine.shape[0]
    mine[...] = kept[:rows, :] + f32(came[:rows, :])
    for place, out in enumerate(others):
        part = slice((place + 1) * rows, (place + 2) * rows)
        out[...] = (kept[part, :] + f32(came[part, :])).astype(jnp.bfloat16)


def split(kept, came):
    rows, width = kept.shape[0] // CHIPS, kept.shape[1]
    return pl.pallas_call(
        split_kernel,
        out_shape=(jax.ShapeDtypeStruct((rows, width), jnp.float32),)
        + (jax.ShapeDtypeStruct((rows, width), jnp.bfloat16),) * (CHIPS - 1),
        in_specs=[WHOLE] * 2,
        out_specs=(WHOLE,) * CHIPS,
        compiler_params=params(4),
        name="split",
    )(kept, came)


def finish_kernel(
    flags, mine, one, two, three, hidden, latent, mod, final_mod, w_final, w_embed, packet
):
    rows, width = mine.shape
    channels = latent.shape[1]
    total = mine[...] + f32(one[...]) + f32(two[...]) + f32(three[...])
    result = (f32(hidden[...]) + mod[2:3, :] * total).astype(jnp.bfloat16)
    last = flags[2] == 1

    @pl.when(last)
    def _():
        normed = layer_norm(f32(result), final_mod[0:1, :], final_mod[1:2, :])
        velocity = dot(normed, w_final[...])
        renewed = (f32(latent[...]) + velocity).astype(jnp.bfloat16)
        packet[:, :width] = dot(renewed, w_embed[...]).astype(jnp.bfloat16)
        packet[:, width : width + channels] = renewed

    @pl.when(jnp.logical_not(last))
    def _():
        packet[:, :width] = result
        packet[:, width : width + channels] = latent[...]


def finish(flags, parts, hidden, latent, mod, final_mod, w_final, w_embed):
    rows, width = hidden.shape
    return pl.pallas_call(
        finish_kernel,
        out_shape=jax.ShapeDtypeStruct((rows, width + LANES), jnp.bfloat16),
        in_specs=[SCALARS] + [WHOLE] * 10,
        out_specs=WHOLE,
        compiler_params=params(4),
        name="finish",
    )(flags, *parts, hidden, latent, mod, final_mod, w_final, w_embed)


def norm_kernel(packet, mod, hidden, latent, normed):
    width = hidden.shape[1]
    values = packet[:, :width]
    hidden[...] = values
    latent[...] = packet[:, width : width + latent.shape[1]]
    normed[...] = layer_norm(f32(values), mod[0:1, :], mod[1:2, :])


def open_packet(packet, mod, channels):
    rows, width = packet.shape[0], packet.shape[1] - LANES
    return pl.pallas_call(
        norm_kernel,
        out_shape=(
            jax.ShapeDtypeStruct((rows, width), jnp.bfloat16),
            jax.ShapeDtypeStruct((rows, channels), jnp.bfloat16),
            jax.ShapeDtypeStruct((rows, width), jnp.bfloat16),
        ),
        in_specs=[WHOLE] * 2,
        out_specs=(WHOLE,) * 3,
        compiler_params=params(4),
        name="norm",
    )(packet, mod)


def exchange(value, apart):
    route = [(device, device ^ apart) for device in range(lax.axis_size("section"))]
    return lax.ppermute(value, "section", route)


def gather_chips(rows):
    return jnp.concatenate([rows] + [exchange(rows, apart) for apart in CHIP_STEPS], 0)


def body(
    hidden_in,
    latent_in,
    w_qkv,
    w_out,
    stale_kv,
    qk_gain,
    block_mod,
    final_mod,
    w_final,
    w_embed,
    patch_flow,
):
    size = lax.axis_size("section")
    ticks = patch_flow.shape[0]
    channels = latent_in.shape[1]
    section = lax.axis_index("section") // GROUP
    is_last = (section == size // GROUP - 1).astype(jnp.int32)
    mod = lax.dynamic_index_in_dim(block_mod, section, 0, keepdims=False)
    gains = lax.dynamic_index_in_dim(qk_gain, section, 0, keepdims=False)
    patches = lax.dynamic_index_in_dim(patch_flow, section, 1, keepdims=False)
    k_cache, v_cache = stale_kv[0], stale_kv[1]
    onward = [(device, (device + GROUP) % size) for device in range(size)]

    packet = jnp.pad(
        jnp.concatenate([hidden_in, latent_in], 1), ((0, 0), (0, LANES - channels))
    )
    for tick in range(ticks):
        flags = jnp.stack([section.astype(jnp.int32), patches[tick], is_last])
        hidden, latent, normed = open_packet(packet, mod, channels)
        own = gather_chips(normed)
        other = exchange(own, 1)
        kept, sent, k_cache, v_cache = block(
            flags, own, other, gains, w_qkv, w_out, k_cache, v_cache
        )
        mine, *blocks = split(kept, exchange(sent, 1))
        parts = [mine] + [exchange(rows, apart) for rows, apart in zip(blocks, CHIP_STEPS)]
        packet = finish(flags, parts, hidden, latent, mod, final_mod, w_final, w_embed)
        packet = lax.ppermute(packet, "section", onward)
    width = hidden_in.shape[1]
    return (packet[:, :width], packet[:, width : width + channels])


def solution(mesh):
    in_specs = (
        P(("groups", "section"), None),
        P(("groups", "section"), None),
        P(None, None, "section"),
        P("section", None),
        P("groups", None, "section"),
        P(),
        P("groups", None, None),
        P("groups", None),
        P(),
        P(),
        P(),
    )
    out_specs = (P(("groups", "section"), None), P(("groups", "section"), None))
    return jax.shard_map(body, mesh=mesh, in_specs=in_specs, out_specs=out_specs, check_vma=False)
```

time: 389 us -> 215 us (0.55)
  starting transfers between devices: 220 us -> 63.5 us
  waiting for transfers between devices: 103 us -> 95 us
  Pallas kernels: 32.3 us -> 25.2 us
  local copies, waits for them, and re-layouts: 19.6 us -> 23.7 us
    ppermute x81 -> x54, starting transfers between devices: 220 us -> 63.5 us  [the longest x48 45.5 us: exchange(): return lax.ppermute(value, 'section', route)]
    ppermute x81 -> x54, waiting for transfers between devices: 103 us -> 95 us  [the longest x48 66 us: exchange(): return lax.ppermute(value, 'section', route)]
    pallas_call x24, Pallas kernels: 32.3 us -> 25.2 us  [the longest x6 18.2 us: block(): pl.pallas_call(block_kernel, out_shape=(jax.ShapeDtypeStruct((half, width...]
    unnamed x31 -> x58, local copies, waits for them, and re-layouts: 13.4 us -> 19.2 us
  transfers between devices with their start and end apart: 81 -> 54, of which waited for: 46 -> 41; matrix products, arithmetic and copies ran while one was open for 4% -> 4% of each run, Pallas kernels for 1% -> 0%
where the time goes in v2:
time: 215 us; the launch traced here: 214 us
  waiting for transfers between devices  95 us (44%)
  starting transfers between devices  63.5 us (30%)
  Pallas kernels  25.2 us (12%)
  local copies, waits for them, and re-layouts  23.7 us (11%)
  other arithmetic  5.16 us (2%)
    ppermute x48, waiting for transfers between devices, exchange(): return lax.ppermute(value, 'section', route)  66 us
    ppermute x48, starting transfers between devices, exchange(): return lax.ppermute(value, 'section', route)  45.5 us
    ppermute x6, waiting for transfers between devices, body(): packet = lax.ppermute(packet, 'section', onward)  29.1 us
    unnamed x58, local copies, waits for them, and re-layouts  19.2 us
    pallas_call x6, Pallas kernels, block(): pl.pallas_call(block_kernel, out_shape=(jax.ShapeDtypeStruct((half, width...  18.2 us
    ppermute x6, starting transfers between devices, body(): packet = lax.ppermute(packet, 'section', onward)  18 us
    pallas_call x6, Pallas kernels, finish(): pl.pallas_call(finish_kernel, out_shape=jax.ShapeDtypeStruct((rows, width...  4.48 us
  transfers between devices with their start and end apart: 54, of which 41 were waited for; matrix products, arithmetic and copies ran while one was open for 4% of the time, Pallas kernels for 0%

profile of v2, /device:TPU:0, one launch (start us, length us, event | category | flops | bytes accessed | tf_op | source)
XLA Modules:
  0.0 213.8 jit_solution(12166795347426805195)
XLA Ops:
  3.4 3.0 %collective-permute-start.2 = (bf16[16,3072]{1,0:T(8,128)(2,1)S(1)}, bf16[16,3072]{1,0:T(8,128)(2,1)S(1)}, u32[]{:S(2)}, u32[]{:S(2)}) collective-permute-start(bf16[16,3072]{1,0:T(8,128)(2,1)S(1)} %get-tuple-element.66), channel_id=1, source_target_pairs={{0,2},{1,3},{2,0},{3,1},{4,6},{5,7},{6,4},{7,5},{8,10},{9,11},{10,... | collective-permute-start | bytes 294920 | tf_op jit(solution)/shard_map/ppermute | solution.py:199
  9.3 4.1 %collective-permute-done = bf16[16,3072]{1,0:T(8,128)(2,1)S(1)} collective-permute-done((bf16[16,3072]{1,0:T(8,128)(2,1)S(1)}, bf16[16,3072]{1,0:T(8,128)(2,1)S(1)}, u32[]{:S(2)}, u32[]{:S(2)}) %collective-permute-start) | collective-permute-done | bytes 98336 | tf_op jit(solution)/shard_map/ppermute | solution.py:199
  16.2 3.0 %copy-done.1 = bf16[3,3072,384]{2,1,0:T(8,128)(2,1)S(1)} copy-done((bf16[3,3072,384]{2,1,0:T(8,128)(2,1)S(1)}, bf16[3,3072,384]{2,1,0:T(8,128)(2,1)}, u32[]{:S(2)}) %copy-start.1) | copy-done | bytes 7077912
  19.2 1.7 copy-done.4
  21.9 3.0 %block.6 = (f32[64,3072]{1,0:T(8,128)S(1)}, bf16[64,3072]{1,0:T(8,128)(2,1)S(1)}, bf16[256,384]{1,0:T(8,128)(2,1)S(1)}, bf16[256,384]{1,0:T(8,128)(2,1)S(1)}) custom-call(s32[3]{0:T(128)S(1)} %add_add_fusion.5.flags, bf16[64,3072]{1,0:T(8,128)(2,1)S(1)} %copy-done.12, ...), custom_call_target="tpu_custom_call", output_to_operand_aliasing={{2}: (6, {}), {3}: (7, {})} | custom-call | flops 1207959552 | bytes 9437184 | tf_op jit(solution)/shard_map/block/pallas_call | solution.py:92
  28.2 1.7 collective-permute-start.5
  33.1 2.0 collective-permute-done.5.one
  40.6 3.2 %collective-permute-start.8 = (bf16[16,3200]{1,0:T(8,128)(2,1)S(1)}, bf16[16,3200]{1,0:T(8,128)(2,1)S(1)}, u32[]{:S(2)}, u32[]{:S(2)}) collective-permute-start(bf16[16,3200]{1,0:T(8,128)(2,1)S(1)} %finish.6), channel_id=1, source_target_pairs={{0,8},{1,9},{2,10},{3,11},{4,12},{5,13},{6,14},{7,15},{8,0},{9,1},... | collective-permute-start | bytes 307208 | tf_op jit(solution)/shard_map/ppermute | solution.py:244
  43.8 5.1 %collective-permute-done.8.packet = bf16[16,3200]{1,0:T(8,128)(2,1)S(1)} collective-permute-done((bf16[16,3200]{1,0:T(8,128)(2,1)S(1)}, bf16[16,3200]{1,0:T(8,128)(2,1)S(1)}, u32[]{:S(2)}, u32[]{:S(2)}) %collective-permute-start.8) | collective-permute-done | bytes 102432 | tf_op jit(solution)/shard_map/ppermute | solution.py:244
  50.7 1.9 collective-permute-start.9
  52.7 4.5 %collective-permute-done.9 = bf16[16,3072]{1,0:T(8,128)(2,1)S(1)} collective-permute-done((bf16[16,3072]{1,0:T(8,128)(2,1)S(1)}, bf16[16,3072]{1,0:T(8,128)(2,1)S(1)}, u32[]{:S(2)}, u32[]{:S(2)}) %collective-permute-start.9) | collective-permute-done | bytes 98336 | tf_op jit(solution)/shard_map/ppermute | solution.py:199
  59.0 3.0 %copy-done.2 = bf16[3,3072,384]{2,1,0:T(8,128)(2,1)S(1)} copy-done((bf16[3,3072,384]{2,1,0:T(8,128)(2,1)S(1)}, bf16[3,3072,384]{2,1,0:T(8,128)(2,1)}, u32[]{:S(2)}) %copy-start.2) | copy-done | bytes 7077912
  63.0 3.0 %block.7 = (f32[64,3072]{1,0:T(8,128)S(1)}, bf16[64,3072]{1,0:T(8,128)(2,1)S(1)}, bf16[256,384]{1,0:T(8,128)(2,1)S(1)}, bf16[256,384]{1,0:T(8,128)(2,1)S(1)}) custom-call(s32[3]{0:T(128)S(1)} %add_add_fusion.4.flags, bf16[64,3072]{1,0:T(8,128)(2,1)S(1)} %constant_dynamic-update-slice_fusion.4.own, ...), custom_call_target="tpu_custom_call", output_to_operand_aliasing={{2}: (6, {}), {3}: (7, {})} | custom-call | flops 1207959552 | bytes 9437184 | tf_op jit(solution)/shard_map/block/pallas_call | solution.py:92
  69.8 1.6 collective-permute-start.16
  71.4 3.1 %collective-permute-done.14.one = bf16[16,3072]{1,0:T(8,128)(2,1)S(1)} collective-permute-done((bf16[16,3072]{1,0:T(8,128)(2,1)S(1)}, bf16[16,3072]{1,0:T(8,128)(2,1)S(1)}, u32[]{:S(2)}, u32[]{:S(2)}) %collective-permute-start.14) | collective-permute-done | bytes 98336 | tf_op jit(solution)/shard_map/ppermute | solution.py:199
  76.4 3.1 %collective-permute-start.17 = (bf16[16,3200]{1,0:T(8,128)(2,1)S(1)}, bf16[16,3200]{1,0:T(8,128)(2,1)S(1)}, u32[]{:S(2)}, u32[]{:S(2)}) collective-permute-start(bf16[16,3200]{1,0:T(8,128)(2,1)S(1)} %finish.7), channel_id=1, source_target_pairs={{0,8},{1,9},{2,10},{3,11},{4,12},{5,13},{6,14},{7,15},{8,0},{9,1},... | collective-permute-start | bytes 307208 | tf_op jit(solution)/shard_map/ppermute | solution.py:244
  79.5 4.9 %collective-permute-done.17.packet = bf16[16,3200]{1,0:T(8,128)(2,1)S(1)} collective-permute-done((bf16[16,3200]{1,0:T(8,128)(2,1)S(1)}, bf16[16,3200]{1,0:T(8,128)(2,1)S(1)}, u32[]{:S(2)}, u32[]{:S(2)}) %collective-permute-start.17) | collective-permute-done | bytes 102432 | tf_op jit(solution)/shard_map/ppermute | solution.py:244
  86.1 2.2 %collective-permute-start.18 = (bf16[16,3072]{1,0:T(8,128)(2,1)S(1)}, bf16[16,3072]{1,0:T(8,128)(2,1)S(1)}, u32[]{:S(2)}, u32[]{:S(2)}) collective-permute-start(bf16[16,3072]{1,0:T(8,128)(2,1)S(1)} %get-tuple-element.86), channel_id=1, source_target_pairs={{0,6},{1,7},{2,4},{3,5},{4,2},{5,3},{6,0},{7,1},{8,14},{9,15},{10,... | collective-permute-start | bytes 294920 | tf_op jit(solution)/shard_map/ppermute | solution.py:199
  88.2 4.3 %collective-permute-done.18 = bf16[16,3072]{1,0:T(8,128)(2,1)S(1)} collective-permute-done((bf16[16,3072]{1,0:T(8,128)(2,1)S(1)}, bf16[16,3072]{1,0:T(8,128)(2,1)S(1)}, u32[]{:S(2)}, u32[]{:S(2)}) %collective-permute-start.18) | collective-permute-done | bytes 98336 | tf_op jit(solution)/shard_map/ppermute | solution.py:199
  94.4 3.0 %copy-done.3 = bf16[3,3072,384]{2,1,0:T(8,128)(2,1)S(1)} copy-done((bf16[3,3072,384]{2,1,0:T(8,128)(2,1)S(1)}, bf16[3,3072,384]{2,1,0:T(8,128)(2,1)}, u32[]{:S(2)}) %copy-start.3) | copy-done | bytes 7077912
  97.4 3.0 %block.8 = (f32[64,3072]{1,0:T(8,128)S(1)}, bf16[64,3072]{1,0:T(8,128)(2,1)S(1)}, bf16[256,384]{1,0:T(8,128)(2,1)S(1)}, bf16[256,384]{1,0:T(8,128)(2,1)S(1)}) custom-call(s32[3]{0:T(128)S(1)} %add_add_fusion.3.flags, bf16[64,3072]{1,0:T(8,128)(2,1)S(1)} %constant_dynamic-update-slice_fusion.8.own, ...), custom_call_target="tpu_custom_call", output_to_operand_aliasing={{2}: (6, {}), {3}: (7, {})} | custom-call | flops 1207959552 | bytes 9437184 | tf_op jit(solution)/shard_map/block/pallas_call | solution.py:92
  100.7 1.6 collective-permute-done.22.came
  104.3 1.6 collective-permute-start.25
  105.9 3.1 %collective-permute-done.23.one = bf16[16,3072]{1,0:T(8,128)(2,1)S(1)} collective-permute-done((bf16[16,3072]{1,0:T(8,128)(2,1)S(1)}, bf16[16,3072]{1,0:T(8,128)(2,1)S(1)}, u32[]{:S(2)}, u32[]{:S(2)}) %collective-permute-start.23) | collective-permute-done | bytes 98336 | tf_op jit(solution)/shard_map/ppermute | solution.py:199
  111.1 3.0 %collective-permute-start.26 = (bf16[16,3200]{1,0:T(8,128)(2,1)S(1)}, bf16[16,3200]{1,0:T(8,128)(2,1)S(1)}, u32[]{:S(2)}, u32[]{:S(2)}) collective-permute-start(bf16[16,3200]{1,0:T(8,128)(2,1)S(1)} %finish.8), channel_id=1, source_target_pairs={{0,8},{1,9},{2,10},{3,11},{4,12},{5,13},{6,14},{7,15},{8,0},{9,1},... | collective-permute-start | bytes 307208 | tf_op jit(solution)/shard_map/ppermute | solution.py:244
  114.1 4.8 %collective-permute-done.26.packet = bf16[16,3200]{1,0:T(8,128)(2,1)S(1)} collective-permute-done((bf16[16,3200]{1,0:T(8,128)(2,1)S(1)}, bf16[16,3200]{1,0:T(8,128)(2,1)S(1)}, u32[]{:S(2)}, u32[]{:S(2)}) %collective-permute-start.26) | collective-permute-done | bytes 102432 | tf_op jit(solution)/shard_map/ppermute | solution.py:244
  120.5 2.2 %collective-permute-start.27 = (bf16[16,3072]{1,0:T(8,128)(2,1)S(1)}, bf16[16,3072]{1,0:T(8,128)(2,1)S(1)}, u32[]{:S(2)}, u32[]{:S(2)}) collective-permute-start(bf16[16,3072]{1,0:T(8,128)(2,1)S(1)} %get-tuple-element.97), channel_id=1, source_target_pairs={{0,6},{1,7},{2,4},{3,5},{4,2},{5,3},{6,0},{7,1},{8,14},{9,15},{10,... | collective-permute-start | bytes 294920 | tf_op jit(solution)/shard_map/ppermute | solution.py:199
  122.8 4.5 %collective-permute-done.27 = bf16[16,3072]{1,0:T(8,128)(2,1)S(1)} collective-permute-done((bf16[16,3072]{1,0:T(8,128)(2,1)S(1)}, bf16[16,3072]{1,0:T(8,128)(2,1)S(1)}, u32[]{:S(2)}, u32[]{:S(2)}) %collective-permute-start.27) | collective-permute-done | bytes 98336 | tf_op jit(solution)/shard_map/ppermute | solution.py:199
  129.1 3.0 %block.9 = (f32[64,3072]{1,0:T(8,128)S(1)}, bf16[64,3072]{1,0:T(8,128)(2,1)S(1)}, bf16[256,384]{1,0:T(8,128)(2,1)S(1)}, bf16[256,384]{1,0:T(8,128)(2,1)S(1)}) custom-call(s32[3]{0:T(128)S(1)} %add_add_fusion.2.flags, bf16[64,3072]{1,0:T(8,128)(2,1)S(1)} %constant_dynamic-update-slice_fusion.12.own, ...), custom_call_target="tpu_custom_call", output_to_operand_aliasing={{2}: (6, {}), {3}: (7, {})} | custom-call | flops 1207959552 | bytes 9437184 | tf_op jit(solution)/shard_map/block/pallas_call | solution.py:92
  136.0 1.6 collective-permute-start.34
  137.6 3.1 %collective-permute-done.32.one = bf16[16,3072]{1,0:T(8,128)(2,1)S(1)} collective-permute-done((bf16[16,3072]{1,0:T(8,128)(2,1)S(1)}, bf16[16,3072]{1,0:T(8,128)(2,1)S(1)}, u32[]{:S(2)}, u32[]{:S(2)}) %collective-permute-start.32) | collective-permute-done | bytes 98336 | tf_op jit(solution)/shard_map/ppermute | solution.py:199
  142.6 2.8 %collective-permute-start.35 = (bf16[16,3200]{1,0:T(8,128)(2,1)S(1)}, bf16[16,3200]{1,0:T(8,128)(2,1)S(1)}, u32[]{:S(2)}, u32[]{:S(2)}) collective-permute-start(bf16[16,3200]{1,0:T(8,128)(2,1)S(1)} %finish.9), channel_id=1, source_target_pairs={{0,8},{1,9},{2,10},{3,11},{4,12},{5,13},{6,14},{7,15},{8,0},{9,1},... | collective-permute-start | bytes 307208 | tf_op jit(solution)/shard_map/ppermute | solution.py:244
  145.4 4.7 %collective-permute-done.35.packet = bf16[16,3200]{1,0:T(8,128)(2,1)S(1)} collective-permute-done((bf16[16,3200]{1,0:T(8,128)(2,1)S(1)}, bf16[16,3200]{1,0:T(8,128)(2,1)S(1)}, u32[]{:S(2)}, u32[]{:S(2)}) %collective-permute-start.35) | collective-permute-done | bytes 102432 | tf_op jit(solution)/shard_map/ppermute | solution.py:244
  151.7 2.2 %collective-permute-start.36 = (bf16[16,3072]{1,0:T(8,128)(2,1)S(1)}, bf16[16,3072]{1,0:T(8,128)(2,1)S(1)}, u32[]{:S(2)}, u32[]{:S(2)}) collective-permute-start(bf16[16,3072]{1,0:T(8,128)(2,1)S(1)} %get-tuple-element.108), channel_id=1, source_target_pairs={{0,6},{1,7},{2,4},{3,5},{4,2},{5,3},{6,0},{7,1},{8,14},{9,15},{10,... | collective-permute-start | bytes 294920 | tf_op jit(solution)/shard_map/ppermute | solution.py:199
  153.9 4.4 %collective-permute-done.36 = bf16[16,3072]{1,0:T(8,128)(2,1)S(1)} collective-permute-done((bf16[16,3072]{1,0:T(8,128)(2,1)S(1)}, bf16[16,3072]{1,0:T(8,128)(2,1)S(1)}, u32[]{:S(2)}, u32[]{:S(2)}) %collective-permute-start.36) | collective-permute-done | bytes 98336 | tf_op jit(solution)/shard_map/ppermute | solution.py:199
  160.2 3.0 %block.10 = (f32[64,3072]{1,0:T(8,128)S(1)}, bf16[64,3072]{1,0:T(8,128)(2,1)S(1)}, bf16[256,384]{1,0:T(8,128)(2,1)S(1)}, bf16[256,384]{1,0:T(8,128)(2,1)S(1)}) custom-call(s32[3]{0:T(128)S(1)} %add_add_fusion.1.flags, bf16[64,3072]{1,0:T(8,128)(2,1)S(1)} %constant_dynamic-update-slice_fusion.16.own, ...), custom_call_target="tpu_custom_call", output_to_operand_aliasing={{2}: (6, {}), {3}: (7, {})} | custom-call | flops 1207959552 | bytes 9437184 | tf_op jit(solution)/shard_map/block/pallas_call | solution.py:92
  163.4 1.6 collective-permute-done.40.came
  167.0 1.6 collective-permute-start.43
  168.6 3.1 %collective-permute-done.41.one = bf16[16,3072]{1,0:T(8,128)(2,1)S(1)} collective-permute-done((bf16[16,3072]{1,0:T(8,128)(2,1)S(1)}, bf16[16,3072]{1,0:T(8,128)(2,1)S(1)}, u32[]{:S(2)}, u32[]{:S(2)}) %collective-permute-start.41) | collective-permute-done | bytes 98336 | tf_op jit(solution)/shard_map/ppermute | solution.py:199
  173.6 3.0 %collective-permute-start.44 = (bf16[16,3200]{1,0:T(8,128)(2,1)S(1)}, bf16[16,3200]{1,0:T(8,128)(2,1)S(1)}, u32[]{:S(2)}, u32[]{:S(2)}) collective-permute-start(bf16[16,3200]{1,0:T(8,128)(2,1)S(1)} %finish.10), channel_id=1, source_target_pairs={{0,8},{1,9},{2,10},{3,11},{4,12},{5,13},{6,14},{7,15},{8,0},{9,1},... | collective-permute-start | bytes 307208 | tf_op jit(solution)/shard_map/ppermute | solution.py:244
  176.6 4.7 %collective-permute-done.44.packet = bf16[16,3200]{1,0:T(8,128)(2,1)S(1)} collective-permute-done((bf16[16,3200]{1,0:T(8,128)(2,1)S(1)}, bf16[16,3200]{1,0:T(8,128)(2,1)S(1)}, u32[]{:S(2)}, u32[]{:S(2)}) %collective-permute-start.44) | collective-permute-done | bytes 102432 | tf_op jit(solution)/shard_map/ppermute | solution.py:244
  183.0 2.2 %collective-permute-start.45 = (bf16[16,3072]{1,0:T(8,128)(2,1)S(1)}, bf16[16,3072]{1,0:T(8,128)(2,1)S(1)}, u32[]{:S(2)}, u32[]{:S(2)}) collective-permute-start(bf16[16,3072]{1,0:T(8,128)(2,1)S(1)} %get-tuple-element.119), channel_id=1, source_target_pairs={{0,6},{1,7},{2,4},{3,5},{4,2},{5,3},{6,0},{7,1},{8,14},{9,15},{10,... | collective-permute-start | bytes 294920 | tf_op jit(solution)/shard_map/ppermute | solution.py:199
  185.1 4.5 %collective-permute-done.45 = bf16[16,3072]{1,0:T(8,128)(2,1)S(1)} collective-permute-done((bf16[16,3072]{1,0:T(8,128)(2,1)S(1)}, bf16[16,3072]{1,0:T(8,128)(2,1)S(1)}, u32[]{:S(2)}, u32[]{:S(2)}) %collective-permute-start.45) | collective-permute-done | bytes 98336 | tf_op jit(solution)/shard_map/ppermute | solution.py:199
  191.5 3.0 %block.11 = (f32[64,3072]{1,0:T(8,128)S(1)}, bf16[64,3072]{1,0:T(8,128)(2,1)S(1)}, bf16[256,384]{1,0:T(8,128)(2,1)S(1)}, bf16[256,384]{1,0:T(8,128)(2,1)S(1)}) custom-call(s32[3]{0:T(128)S(1)} %add_add_fusion.flags, bf16[64,3072]{1,0:T(8,128)(2,1)S(1)} %constant_dynamic-update-slice_fusion.20.own, ...), custom_call_target="tpu_custom_call", output_to_operand_aliasing={{2}: (6, {}), {3}: (7, {})} | custom-call | flops 1207959552 | bytes 9437184 | tf_op jit(solution)/shard_map/block/pallas_call | solution.py:92
  198.3 1.6 collective-permute-start.52
  200.0 3.1 %collective-permute-done.50.one = bf16[16,3072]{1,0:T(8,128)(2,1)S(1)} collective-permute-done((bf16[16,3072]{1,0:T(8,128)(2,1)S(1)}, bf16[16,3072]{1,0:T(8,128)(2,1)S(1)}, u32[]{:S(2)}, u32[]{:S(2)}) %collective-permute-start.50) | collective-permute-done | bytes 98336 | tf_op jit(solution)/shard_map/ppermute | solution.py:199
  205.0 2.9 %collective-permute-start.53 = (bf16[16,3200]{1,0:T(8,128)(2,1)S(1)}, bf16[16,3200]{1,0:T(8,128)(2,1)S(1)}, u32[]{:S(2)}, u32[]{:S(2)}) collective-permute-start(bf16[16,3200]{1,0:T(8,128)(2,1)S(1)} %finish.11), channel_id=1, source_target_pairs={{0,8},{1,9},{2,10},{3,11},{4,12},{5,13},{6,14},{7,15},{8,0},{9,1},... | collective-permute-start | bytes 307208 | tf_op jit(solution)/shard_map/ppermute | solution.py:244
  207.8 4.7 %collective-permute-done.53 = bf16[16,3200]{1,0:T(8,128)(2,1)S(1)} collective-permute-done((bf16[16,3200]{1,0:T(8,128)(2,1)S(1)}, bf16[16,3200]{1,0:T(8,128)(2,1)S(1)}, u32[]{:S(2)}, u32[]{:S(2)}) %collective-permute-start.53) | collective-permute-done | bytes 102432 | tf_op jit(solution)/shard_map/ppermute | solution.py:244
  (163 shorter events, 66.3 us)
Async XLA Ops:
  3.4 10.1 %collective-permute-start.2 = (bf16[16,3072]{1,0:T(8,128)(2,1)S(1)}, bf16[16,3072]{1,0:T(8,128)(2,1)S(1)}, u32[]{:S(2)}, u32[]{:S(2)}) collective-permute-start(bf16[16,3072]{1,0:T(8,128)(2,1)S(1)} %get-tuple-element.66), channel_id=1, source_target_pairs={{0,2},{1,3},{2,0},{3,1},{4,6},{5,7},{6,4},{7,5},{8,10},{9,11},{10,... | collective-permute-start | bytes 294920 | tf_op jit(solution)/shard_map/ppermute | solution.py:199
  6.4 7.1 %collective-permute-start.1 = (bf16[16,3072]{1,0:T(8,128)(2,1)S(1)}, bf16[16,3072]{1,0:T(8,128)(2,1)S(1)}, u32[]{:S(2)}, u32[]{:S(2)}) collective-permute-start(bf16[16,3072]{1,0:T(8,128)(2,1)S(1)} %get-tuple-element.66), channel_id=1, source_target_pairs={{0,4},{1,5},{2,6},{3,7},{4,0},{5,1},{6,2},{7,3},{8,12},{9,13},{10,... | collective-permute-start | bytes 294920 | tf_op jit(solution)/shard_map/ppermute | solution.py:199
  8.0 5.5 %collective-permute-start = (bf16[16,3072]{1,0:T(8,128)(2,1)S(1)}, bf16[16,3072]{1,0:T(8,128)(2,1)S(1)}, u32[]{:S(2)}, u32[]{:S(2)}) collective-permute-start(bf16[16,3072]{1,0:T(8,128)(2,1)S(1)} %get-tuple-element.66), channel_id=1, source_target_pairs={{0,6},{1,7},{2,4},{3,5},{4,2},{5,3},{6,0},{7,1},{8,14},{9,15},{10,... | collective-permute-start | bytes 294920 | tf_op jit(solution)/shard_map/ppermute | solution.py:199
  13.6 2.6 %collective-permute-start.3 = (bf16[64,3072]{1,0:T(8,128)(2,1)S(1)}, bf16[64,3072]{1,0:T(8,128)(2,1)S(1)}, u32[]{:S(2)}, u32[]{:S(2)}) collective-permute-start(bf16[64,3072]{1,0:T(8,128)(2,1)S(1)} %constant_dynamic-update-slice_fusion.own), channel_id=1, source_target_pairs={{0,1},{1,0},{2,3},{3,2},{4,5},{5,4},{6,7},{7,6},{8,9},{9,8},{10,11... | collective-permute-start | bytes 1179656 | tf_op jit(solution)/shard_map/ppermute | solution.py:199
  24.9 1.9 collective-permute-start.4
  28.2 6.9 %collective-permute-start.5 = (bf16[16,3072]{1,0:T(8,128)(2,1)}, bf16[16,3072]{1,0:T(8,128)(2,1)}, u32[]{:S(2)}, u32[]{:S(2)}) collective-permute-start(bf16[16,3072]{1,0:T(8,128)(2,1)} %get-tuple-element.70), channel_id=1, source_target_pairs={{0,6},{1,7},{2,4},{3,5},{4,2},{5,3},{6,0},{7,1},{8,14},{9,15},{10,... | collective-permute-start | bytes 294920 | tf_op jit(solution)/shard_map/ppermute | solution.py:199
  30.0 6.1 %collective-permute-start.6 = (bf16[16,3072]{1,0:T(8,128)(2,1)}, bf16[16,3072]{1,0:T(8,128)(2,1)}, u32[]{:S(2)}, u32[]{:S(2)}) collective-permute-start(bf16[16,3072]{1,0:T(8,128)(2,1)} %get-tuple-element.71), channel_id=1, source_target_pairs={{0,4},{1,5},{2,6},{3,7},{4,0},{5,1},{6,2},{7,3},{8,12},{9,13},{10,... | collective-permute-start | bytes 294920 | tf_op jit(solution)/shard_map/ppermute | solution.py:199
  30.6 6.0 %collective-permute-start.7 = (bf16[16,3072]{1,0:T(8,128)(2,1)}, bf16[16,3072]{1,0:T(8,128)(2,1)}, u32[]{:S(2)}, u32[]{:S(2)}) collective-permute-start(bf16[16,3072]{1,0:T(8,128)(2,1)} %get-tuple-element.72), channel_id=1, source_target_pairs={{0,2},{1,3},{2,0},{3,1},{4,6},{5,7},{6,4},{7,5},{8,10},{9,11},{10,... | collective-permute-start | bytes 294920 | tf_op jit(solution)/shard_map/ppermute | solution.py:199
  40.6 8.3 %collective-permute-start.8 = (bf16[16,3200]{1,0:T(8,128)(2,1)S(1)}, bf16[16,3200]{1,0:T(8,128)(2,1)S(1)}, u32[]{:S(2)}, u32[]{:S(2)}) collective-permute-start(bf16[16,3200]{1,0:T(8,128)(2,1)S(1)} %finish.6), channel_id=1, source_target_pairs={{0,8},{1,9},{2,10},{3,11},{4,12},{5,13},{6,14},{7,15},{8,0},{9,1},... | collective-permute-start | bytes 307208 | tf_op jit(solution)/shard_map/ppermute | solution.py:244
  49.1 8.1 %collective-permute-start.11 = (bf16[16,3072]{1,0:T(8,128)(2,1)S(1)}, bf16[16,3072]{1,0:T(8,128)(2,1)S(1)}, u32[]{:S(2)}, u32[]{:S(2)}) collective-permute-start(bf16[16,3072]{1,0:T(8,128)(2,1)S(1)} %get-tuple-element.75), channel_id=1, source_target_pairs={{0,2},{1,3},{2,0},{3,1},{4,6},{5,7},{6,4},{7,5},{8,10},{9,11},{10,... | collective-permute-start | bytes 294920 | tf_op jit(solution)/shard_map/ppermute | solution.py:199
  50.0 7.2 %collective-permute-start.10 = (bf16[16,3072]{1,0:T(8,128)(2,1)S(1)}, bf16[16,3072]{1,0:T(8,128)(2,1)S(1)}, u32[]{:S(2)}, u32[]{:S(2)}) collective-permute-start(bf16[16,3072]{1,0:T(8,128)(2,1)S(1)} %get-tuple-element.75), channel_id=1, source_target_pairs={{0,4},{1,5},{2,6},{3,7},{4,0},{5,1},{6,2},{7,3},{8,12},{9,13},{10,... | collective-permute-start | bytes 294920 | tf_op jit(solution)/shard_map/ppermute | solution.py:199
  50.7 6.4 %collective-permute-start.9 = (bf16[16,3072]{1,0:T(8,128)(2,1)S(1)}, bf16[16,3072]{1,0:T(8,128)(2,1)S(1)}, u32[]{:S(2)}, u32[]{:S(2)}) collective-permute-start(bf16[16,3072]{1,0:T(8,128)(2,1)S(1)} %get-tuple-element.75), channel_id=1, source_target_pairs={{0,6},{1,7},{2,4},{3,5},{4,2},{5,3},{6,0},{7,1},{8,14},{9,15},{10,... | collective-permute-start | bytes 294920 | tf_op jit(solution)/shard_map/ppermute | solution.py:199
  57.2 1.8 collective-permute-start.12
  66.0 1.8 collective-permute-start.13
  67.9 6.6 %collective-permute-start.14 = (bf16[16,3072]{1,0:T(8,128)(2,1)S(1)}, bf16[16,3072]{1,0:T(8,128)(2,1)S(1)}, u32[]{:S(2)}, u32[]{:S(2)}) collective-permute-start(bf16[16,3072]{1,0:T(8,128)(2,1)S(1)} %get-tuple-element.81), channel_id=1, source_target_pairs={{0,6},{1,7},{2,4},{3,5},{4,2},{5,3},{6,0},{7,1},{8,14},{9,15},{10,... | collective-permute-start | bytes 294920 | tf_op jit(solution)/shard_map/ppermute | solution.py:199
  69.1 5.6 %collective-permute-start.15 = (bf16[16,3072]{1,0:T(8,128)(2,1)S(1)}, bf16[16,3072]{1,0:T(8,128)(2,1)S(1)}, u32[]{:S(2)}, u32[]{:S(2)}) collective-permute-start(bf16[16,3072]{1,0:T(8,128)(2,1)S(1)} %get-tuple-element.82), channel_id=1, source_target_pairs={{0,4},{1,5},{2,6},{3,7},{4,0},{5,1},{6,2},{7,3},{8,12},{9,13},{10,... | collective-permute-start | bytes 294920 | tf_op jit(solution)/shard_map/ppermute | solution.py:199
  69.8 6.0 %collective-permute-start.16 = (bf16[16,3072]{1,0:T(8,128)(2,1)S(1)}, bf16[16,3072]{1,0:T(8,128)(2,1)S(1)}, u32[]{:S(2)}, u32[]{:S(2)}) collective-permute-start(bf16[16,3072]{1,0:T(8,128)(2,1)S(1)} %get-tuple-element.83), channel_id=1, source_target_pairs={{0,2},{1,3},{2,0},{3,1},{4,6},{5,7},{6,4},{7,5},{8,10},{9,11},{10,... | collective-permute-start | bytes 294920 | tf_op jit(solution)/shard_map/ppermute | solution.py:199
  76.4 8.0 %collective-permute-start.17 = (bf16[16,3200]{1,0:T(8,128)(2,1)S(1)}, bf16[16,3200]{1,0:T(8,128)(2,1)S(1)}, u32[]{:S(2)}, u32[]{:S(2)}) collective-permute-start(bf16[16,3200]{1,0:T(8,128)(2,1)S(1)} %finish.7), channel_id=1, source_target_pairs={{0,8},{1,9},{2,10},{3,11},{4,12},{5,13},{6,14},{7,15},{8,0},{9,1},... | collective-permute-start | bytes 307208 | tf_op jit(solution)/shard_map/ppermute | solution.py:244
  84.7 7.9 %collective-permute-start.20 = (bf16[16,3072]{1,0:T(8,128)(2,1)S(1)}, bf16[16,3072]{1,0:T(8,128)(2,1)S(1)}, u32[]{:S(2)}, u32[]{:S(2)}) collective-permute-start(bf16[16,3072]{1,0:T(8,128)(2,1)S(1)} %get-tuple-element.86), channel_id=1, source_target_pairs={{0,2},{1,3},{2,0},{3,1},{4,6},{5,7},{6,4},{7,5},{8,10},{9,11},{10,... | collective-permute-start | bytes 294920 | tf_op jit(solution)/shard_map/ppermute | solution.py:199
  85.4 7.1 %collective-permute-start.19 = (bf16[16,3072]{1,0:T(8,128)(2,1)S(1)}, bf16[16,3072]{1,0:T(8,128)(2,1)S(1)}, u32[]{:S(2)}, u32[]{:S(2)}) collective-permute-start(bf16[16,3072]{1,0:T(8,128)(2,1)S(1)} %get-tuple-element.86), channel_id=1, source_target_pairs={{0,4},{1,5},{2,6},{3,7},{4,0},{5,1},{6,2},{7,3},{8,12},{9,13},{10,... | collective-permute-start | bytes 294920 | tf_op jit(solution)/shard_map/ppermute | solution.py:199
  86.1 6.5 %collective-permute-start.18 = (bf16[16,3072]{1,0:T(8,128)(2,1)S(1)}, bf16[16,3072]{1,0:T(8,128)(2,1)S(1)}, u32[]{:S(2)}, u32[]{:S(2)}) collective-permute-start(bf16[16,3072]{1,0:T(8,128)(2,1)S(1)} %get-tuple-element.86), channel_id=1, source_target_pairs={{0,6},{1,7},{2,4},{3,5},{4,2},{5,3},{6,0},{7,1},{8,14},{9,15},{10,... | collective-permute-start | bytes 294920 | tf_op jit(solution)/shard_map/ppermute | solution.py:199
  92.6 1.8 collective-permute-start.21
  100.5 1.8 collective-permute-start.22
  102.3 6.6 %collective-permute-start.23 = (bf16[16,3072]{1,0:T(8,128)(2,1)S(1)}, bf16[16,3072]{1,0:T(8,128)(2,1)S(1)}, u32[]{:S(2)}, u32[]{:S(2)}) collective-permute-start(bf16[16,3072]{1,0:T(8,128)(2,1)S(1)} %get-tuple-element.92), channel_id=1, source_target_pairs={{0,6},{1,7},{2,4},{3,5},{4,2},{5,3},{6,0},{7,1},{8,14},{9,15},{10,... | collective-permute-start | bytes 294920 | tf_op jit(solution)/shard_map/ppermute | solution.py:199
  103.6 5.6 %collective-permute-start.24 = (bf16[16,3072]{1,0:T(8,128)(2,1)S(1)}, bf16[16,3072]{1,0:T(8,128)(2,1)S(1)}, u32[]{:S(2)}, u32[]{:S(2)}) collective-permute-start(bf16[16,3072]{1,0:T(8,128)(2,1)S(1)} %get-tuple-element.93), channel_id=1, source_target_pairs={{0,4},{1,5},{2,6},{3,7},{4,0},{5,1},{6,2},{7,3},{8,12},{9,13},{10,... | collective-permute-start | bytes 294920 | tf_op jit(solution)/shard_map/ppermute | solution.py:199
  104.3 6.0 %collective-permute-start.25 = (bf16[16,3072]{1,0:T(8,128)(2,1)S(1)}, bf16[16,3072]{1,0:T(8,128)(2,1)S(1)}, u32[]{:S(2)}, u32[]{:S(2)}) collective-permute-start(bf16[16,3072]{1,0:T(8,128)(2,1)S(1)} %get-tuple-element.94), channel_id=1, source_target_pairs={{0,2},{1,3},{2,0},{3,1},{4,6},{5,7},{6,4},{7,5},{8,10},{9,11},{10,... | collective-permute-start | bytes 294920 | tf_op jit(solution)/shard_map/ppermute | solution.py:199
  111.1 7.9 %collective-permute-start.26 = (bf16[16,3200]{1,0:T(8,128)(2,1)S(1)}, bf16[16,3200]{1,0:T(8,128)(2,1)S(1)}, u32[]{:S(2)}, u32[]{:S(2)}) collective-permute-start(bf16[16,3200]{1,0:T(8,128)(2,1)S(1)} %finish.8), channel_id=1, source_target_pairs={{0,8},{1,9},{2,10},{3,11},{4,12},{5,13},{6,14},{7,15},{8,0},{9,1},... | collective-permute-start | bytes 307208 | tf_op jit(solution)/shard_map/ppermute | solution.py:244
  119.2 8.1 %collective-permute-start.29 = (bf16[16,3072]{1,0:T(8,128)(2,1)S(1)}, bf16[16,3072]{1,0:T(8,128)(2,1)S(1)}, u32[]{:S(2)}, u32[]{:S(2)}) collective-permute-start(bf16[16,3072]{1,0:T(8,128)(2,1)S(1)} %get-tuple-element.97), channel_id=1, source_target_pairs={{0,2},{1,3},{2,0},{3,1},{4,6},{5,7},{6,4},{7,5},{8,10},{9,11},{10,... | collective-permute-start | bytes 294920 | tf_op jit(solution)/shard_map/ppermute | solution.py:199
  120.0 7.3 %collective-permute-start.28 = (bf16[16,3072]{1,0:T(8,128)(2,1)S(1)}, bf16[16,3072]{1,0:T(8,128)(2,1)S(1)}, u32[]{:S(2)}, u32[]{:S(2)}) collective-permute-start(bf16[16,3072]{1,0:T(8,128)(2,1)S(1)} %get-tuple-element.97), channel_id=1, source_target_pairs={{0,4},{1,5},{2,6},{3,7},{4,0},{5,1},{6,2},{7,3},{8,12},{9,13},{10,... | collective-permute-start | bytes 294920 | tf_op jit(solution)/shard_map/ppermute | solution.py:199
  120.5 6.7 %collective-permute-start.27 = (bf16[16,3072]{1,0:T(8,128)(2,1)S(1)}, bf16[16,3072]{1,0:T(8,128)(2,1)S(1)}, u32[]{:S(2)}, u32[]{:S(2)}) collective-permute-start(bf16[16,3072]{1,0:T(8,128)(2,1)S(1)} %get-tuple-element.97), channel_id=1, source_target_pairs={{0,6},{1,7},{2,4},{3,5},{4,2},{5,3},{6,0},{7,1},{8,14},{9,15},{10,... | collective-permute-start | bytes 294920 | tf_op jit(solution)/shard_map/ppermute | solution.py:199
  134.0 6.6 %collective-permute-start.32 = (bf16[16,3072]{1,0:T(8,128)(2,1)S(1)}, bf16[16,3072]{1,0:T(8,128)(2,1)S(1)}, u32[]{:S(2)}, u32[]{:S(2)}) collective-permute-start(bf16[16,3072]{1,0:T(8,128)(2,1)S(1)} %get-tuple-element.103), channel_id=1, source_target_pairs={{0,6},{1,7},{2,4},{3,5},{4,2},{5,3},{6,0},{7,1},{8,14},{9,15},{10,... | collective-permute-start | bytes 294920 | tf_op jit(solution)/shard_map/ppermute | solution.py:199
  135.1 5.8 %collective-permute-start.33 = (bf16[16,3072]{1,0:T(8,128)(2,1)S(1)}, bf16[16,3072]{1,0:T(8,128)(2,1)S(1)}, u32[]{:S(2)}, u32[]{:S(2)}) collective-permute-start(bf16[16,3072]{1,0:T(8,128)(2,1)S(1)} %get-tuple-element.104), channel_id=1, source_target_pairs={{0,4},{1,5},{2,6},{3,7},{4,0},{5,1},{6,2},{7,3},{8,12},{9,13},{10,... | collective-permute-start | bytes 294920 | tf_op jit(solution)/shard_map/ppermute | solution.py:199
  136.0 6.0 %collective-permute-start.34 = (bf16[16,3072]{1,0:T(8,128)(2,1)S(1)}, bf16[16,3072]{1,0:T(8,128)(2,1)S(1)}, u32[]{:S(2)}, u32[]{:S(2)}) collective-permute-start(bf16[16,3072]{1,0:T(8,128)(2,1)S(1)} %get-tuple-element.105), channel_id=1, source_target_pairs={{0,2},{1,3},{2,0},{3,1},{4,6},{5,7},{6,4},{7,5},{8,10},{9,11},{10,... | collective-permute-start | bytes 294920 | tf_op jit(solution)/shard_map/ppermute | solution.py:199
  142.6 7.6 %collective-permute-start.35 = (bf16[16,3200]{1,0:T(8,128)(2,1)S(1)}, bf16[16,3200]{1,0:T(8,128)(2,1)S(1)}, u32[]{:S(2)}, u32[]{:S(2)}) collective-permute-start(bf16[16,3200]{1,0:T(8,128)(2,1)S(1)} %finish.9), channel_id=1, source_target_pairs={{0,8},{1,9},{2,10},{3,11},{4,12},{5,13},{6,14},{7,15},{8,0},{9,1},... | collective-permute-start | bytes 307208 | tf_op jit(solution)/shard_map/ppermute | solution.py:244
  150.4 8.0 %collective-permute-start.38 = (bf16[16,3072]{1,0:T(8,128)(2,1)S(1)}, bf16[16,3072]{1,0:T(8,128)(2,1)S(1)}, u32[]{:S(2)}, u32[]{:S(2)}) collective-permute-start(bf16[16,3072]{1,0:T(8,128)(2,1)S(1)} %get-tuple-element.108), channel_id=1, source_target_pairs={{0,2},{1,3},{2,0},{3,1},{4,6},{5,7},{6,4},{7,5},{8,10},{9,11},{10,... | collective-permute-start | bytes 294920 | tf_op jit(solution)/shard_map/ppermute | solution.py:199
  151.3 7.1 %collective-permute-start.37 = (bf16[16,3072]{1,0:T(8,128)(2,1)S(1)}, bf16[16,3072]{1,0:T(8,128)(2,1)S(1)}, u32[]{:S(2)}, u32[]{:S(2)}) collective-permute-start(bf16[16,3072]{1,0:T(8,128)(2,1)S(1)} %get-tuple-element.108), channel_id=1, source_target_pairs={{0,4},{1,5},{2,6},{3,7},{4,0},{5,1},{6,2},{7,3},{8,12},{9,13},{10,... | collective-permute-start | bytes 294920 | tf_op jit(solution)/shard_map/ppermute | solution.py:199
  151.7 6.6 %collective-permute-start.36 = (bf16[16,3072]{1,0:T(8,128)(2,1)S(1)}, bf16[16,3072]{1,0:T(8,128)(2,1)S(1)}, u32[]{:S(2)}, u32[]{:S(2)}) collective-permute-start(bf16[16,3072]{1,0:T(8,128)(2,1)S(1)} %get-tuple-element.108), channel_id=1, source_target_pairs={{0,6},{1,7},{2,4},{3,5},{4,2},{5,3},{6,0},{7,1},{8,14},{9,15},{10,... | collective-permute-start | bytes 294920 | tf_op jit(solution)/shard_map/ppermute | solution.py:199
  165.1 6.6 %collective-permute-start.41 = (bf16[16,3072]{1,0:T(8,128)(2,1)S(1)}, bf16[16,3072]{1,0:T(8,128)(2,1)S(1)}, u32[]{:S(2)}, u32[]{:S(2)}) collective-permute-start(bf16[16,3072]{1,0:T(8,128)(2,1)S(1)} %get-tuple-element.114), channel_id=1, source_target_pairs={{0,6},{1,7},{2,4},{3,5},{4,2},{5,3},{6,0},{7,1},{8,14},{9,15},{10,... | collective-permute-start | bytes 294920 | tf_op jit(solution)/shard_map/ppermute | solution.py:199
  166.3 5.7 %collective-permute-start.42 = (bf16[16,3072]{1,0:T(8,128)(2,1)S(1)}, bf16[16,3072]{1,0:T(8,128)(2,1)S(1)}, u32[]{:S(2)}, u32[]{:S(2)}) collective-permute-start(bf16[16,3072]{1,0:T(8,128)(2,1)S(1)} %get-tuple-element.115), channel_id=1, source_target_pairs={{0,4},{1,5},{2,6},{3,7},{4,0},{5,1},{6,2},{7,3},{8,12},{9,13},{10,... | collective-permute-start | bytes 294920 | tf_op jit(solution)/shard_map/ppermute | solution.py:199
  167.0 6.0 %collective-permute-start.43 = (bf16[16,3072]{1,0:T(8,128)(2,1)S(1)}, bf16[16,3072]{1,0:T(8,128)(2,1)S(1)}, u32[]{:S(2)}, u32[]{:S(2)}) collective-permute-start(bf16[16,3072]{1,0:T(8,128)(2,1)S(1)} %get-tuple-element.116), channel_id=1, source_target_pairs={{0,2},{1,3},{2,0},{3,1},{4,6},{5,7},{6,4},{7,5},{8,10},{9,11},{10,... | collective-permute-start | bytes 294920 | tf_op jit(solution)/shard_map/ppermute | solution.py:199
  173.6 7.7 %collective-permute-start.44 = (bf16[16,3200]{1,0:T(8,128)(2,1)S(1)}, bf16[16,3200]{1,0:T(8,128)(2,1)S(1)}, u32[]{:S(2)}, u32[]{:S(2)}) collective-permute-start(bf16[16,3200]{1,0:T(8,128)(2,1)S(1)} %finish.10), channel_id=1, source_target_pairs={{0,8},{1,9},{2,10},{3,11},{4,12},{5,13},{6,14},{7,15},{8,0},{9,1},... | collective-permute-start | bytes 307208 | tf_op jit(solution)/shard_map/ppermute | solution.py:244
  181.6 8.1 %collective-permute-start.47 = (bf16[16,3072]{1,0:T(8,128)(2,1)S(1)}, bf16[16,3072]{1,0:T(8,128)(2,1)S(1)}, u32[]{:S(2)}, u32[]{:S(2)}) collective-permute-start(bf16[16,3072]{1,0:T(8,128)(2,1)S(1)} %get-tuple-element.119), channel_id=1, source_target_pairs={{0,2},{1,3},{2,0},{3,1},{4,6},{5,7},{6,4},{7,5},{8,10},{9,11},{10,... | collective-permute-start | bytes 294920 | tf_op jit(solution)/shard_map/ppermute | solution.py:199
  182.4 7.2 %collective-permute-start.46 = (bf16[16,3072]{1,0:T(8,128)(2,1)S(1)}, bf16[16,3072]{1,0:T(8,128)(2,1)S(1)}, u32[]{:S(2)}, u32[]{:S(2)}) collective-permute-start(bf16[16,3072]{1,0:T(8,128)(2,1)S(1)} %get-tuple-element.119), channel_id=1, source_target_pairs={{0,4},{1,5},{2,6},{3,7},{4,0},{5,1},{6,2},{7,3},{8,12},{9,13},{10,... | collective-permute-start | bytes 294920 | tf_op jit(solution)/shard_map/ppermute | solution.py:199
  183.0 6.7 %collective-permute-start.45 = (bf16[16,3072]{1,0:T(8,128)(2,1)S(1)}, bf16[16,3072]{1,0:T(8,128)(2,1)S(1)}, u32[]{:S(2)}, u32[]{:S(2)}) collective-permute-start(bf16[16,3072]{1,0:T(8,128)(2,1)S(1)} %get-tuple-element.119), channel_id=1, source_target_pairs={{0,6},{1,7},{2,4},{3,5},{4,2},{5,3},{6,0},{7,1},{8,14},{9,15},{10,... | collective-permute-start | bytes 294920 | tf_op jit(solution)/shard_map/ppermute | solution.py:199
  196.4 6.6 %collective-permute-start.50 = (bf16[16,3072]{1,0:T(8,128)(2,1)S(1)}, bf16[16,3072]{1,0:T(8,128)(2,1)S(1)}, u32[]{:S(2)}, u32[]{:S(2)}) collective-permute-start(bf16[16,3072]{1,0:T(8,128)(2,1)S(1)} %get-tuple-element.125), channel_id=1, source_target_pairs={{0,6},{1,7},{2,4},{3,5},{4,2},{5,3},{6,0},{7,1},{8,14},{9,15},{10,... | collective-permute-start | bytes 294920 | tf_op jit(solution)/shard_map/ppermute | solution.py:199
  197.5 5.8 %collective-permute-start.51 = (bf16[16,3072]{1,0:T(8,128)(2,1)S(1)}, bf16[16,3072]{1,0:T(8,128)(2,1)S(1)}, u32[]{:S(2)}, u32[]{:S(2)}) collective-permute-start(bf16[16,3072]{1,0:T(8,128)(2,1)S(1)} %get-tuple-element.126), channel_id=1, source_target_pairs={{0,4},{1,5},{2,6},{3,7},{4,0},{5,1},{6,2},{7,3},{8,12},{9,13},{10,... | collective-permute-start | bytes 294920 | tf_op jit(solution)/shard_map/ppermute | solution.py:199
  198.3 6.0 %collective-permute-start.52 = (bf16[16,3072]{1,0:T(8,128)(2,1)S(1)}, bf16[16,3072]{1,0:T(8,128)(2,1)S(1)}, u32[]{:S(2)}, u32[]{:S(2)}) collective-permute-start(bf16[16,3072]{1,0:T(8,128)(2,1)S(1)} %get-tuple-element.127), channel_id=1, source_target_pairs={{0,2},{1,3},{2,0},{3,1},{4,6},{5,7},{6,4},{7,5},{8,10},{9,11},{10,... | collective-permute-start | bytes 294920 | tf_op jit(solution)/shard_map/ppermute | solution.py:199
  205.0 7.6 %collective-permute-start.53 = (bf16[16,3200]{1,0:T(8,128)(2,1)S(1)}, bf16[16,3200]{1,0:T(8,128)(2,1)S(1)}, u32[]{:S(2)}, u32[]{:S(2)}) collective-permute-start(bf16[16,3200]{1,0:T(8,128)(2,1)S(1)} %finish.11), channel_id=1, source_target_pairs={{0,8},{1,9},{2,10},{3,11},{4,12},{5,13},{6,14},{7,15},{8,0},{9,1},... | collective-permute-start | bytes 307208 | tf_op jit(solution)/shard_map/ppermute | solution.py:244
  (25 other events, 231.2 us)

commit v3 on v2

v3 whole, which is shorter than its diff:
```python
import functools
import math

import jax
import jax.numpy as jnp
from jax import lax
from jax.experimental import pallas as pl
from jax.experimental.pallas import tpu as pltpu
from jax.sharding import PartitionSpec as P

HS = 128
GROUP = 8
CHIPS = 4
CHIP_STEPS = (6, 4, 2)
LANES = 128
EPS = 1e-6
VMEM = pltpu.VMEM
WHOLE = pl.BlockSpec(memory_space=pltpu.VMEM)
SCALARS = pl.BlockSpec(memory_space=pltpu.SMEM)


def f32(value):
    return value.astype(jnp.float32)


def dot(left, right):
    return jnp.dot(left, right, preferred_element_type=jnp.float32)


def dot_rows(left, right):
    return lax.dot_general(
        left, right, (((1,), (1,)), ((), ())), preferred_element_type=jnp.float32
    )


def params(mebibytes):
    return pltpu.CompilerParams(vmem_limit_bytes=mebibytes * 1024 * 1024)


def like(*shapes):
    return tuple(jax.ShapeDtypeStruct(shape, dtype) for shape, dtype in shapes)


def layer_norm(tokens, offset_row, scale_row):
    average = jnp.mean(tokens, axis=-1, keepdims=True)
    centred = tokens - average
    variance = jnp.mean(centred * centred, axis=-1, keepdims=True)
    return (centred * lax.rsqrt(variance + EPS) * (1.0 + scale_row) + offset_row).astype(
        jnp.bfloat16
    )


def head_norm(values, gain_row):
    power = jnp.mean(values * values, axis=-1, keepdims=True)
    return (values * lax.rsqrt(power + EPS) * gain_row).astype(jnp.bfloat16)


def block_kernel(
    tick, section, patch_flow, own, other, gains, w_qkv, w_out, kv_in, kept, sent, kv, normed, mixed
):
    half, width = own.shape
    rows = 2 * half
    heads = w_out.shape[0] // HS
    here = section[0]
    normed[:half, :] = own[...]
    normed[half:, :] = other[...]
    start = pl.multiple_of(patch_flow[here, tick] * rows, rows)
    kv[...] = kv_in[...]
    gain = gains[here]
    tokens = normed[...]
    keys = dot(tokens, w_qkv[1])
    for head in range(heads):
        part = slice(head * HS, (head + 1) * HS)
        kv[0, pl.ds(start, rows), part] = head_norm(keys[:, part], gain[1:2, :])
    kv[1, pl.ds(start, rows), :] = dot(tokens, w_qkv[2]).astype(jnp.bfloat16)
    queries = dot(tokens, w_qkv[0])
    for head in range(heads):
        part = slice(head * HS, (head + 1) * HS)
        query = head_norm(queries[:, part], gain[0:1, :])
        weights = jnp.exp(dot_rows(query, kv[0, :, part]) / math.sqrt(HS))
        totals = jnp.sum(weights, axis=-1, keepdims=True)
        attended = dot(weights.astype(jnp.bfloat16), kv[1, :, part])
        mixed[:, part] = (attended / totals).astype(jnp.bfloat16)
    tile = width // 4
    heads_out = mixed[...]
    for low in range(0, width, tile):
        projected = dot(heads_out, w_out[:, low : low + tile])
        kept[:, low : low + tile] = projected[:half, :]
        sent[:, low : low + tile] = projected[half:, :].astype(jnp.bfloat16)


def block(tick, section, patch_flow, own, other, gains, w_qkv, w_out, kv):
    half, width = own.shape
    columns = w_out.shape[0]
    return pl.pallas_call(
        functools.partial(block_kernel, tick),
        out_shape=like(
            ((half, width), jnp.float32), ((half, width), jnp.bfloat16), (kv.shape, jnp.bfloat16)
        ),
        in_specs=[SCALARS] * 2 + [WHOLE] * 6,
        out_specs=(WHOLE,) * 3,
        scratch_shapes=[
            VMEM((2 * half, width), jnp.bfloat16),
            VMEM((2 * half, columns), jnp.bfloat16),
        ],
        input_output_aliases={7: 2},
        compiler_params=params(8),
        cost_estimate=pl.CostEstimate(
            flops=16 * half * columns * width,
            bytes_accessed=8 * columns * width,
            transcendentals=0,
        ),
        name="block",
    )(section, patch_flow, own, other, gains, w_qkv, w_out, kv)


def split_kernel(kept, came, mine, *others):
    rows = mine.shape[0]
    mine[...] = kept[:rows, :] + f32(came[:rows, :])
    for place, out in enumerate(others):
        part = slice((place + 1) * rows, (place + 2) * rows)
        out[...] = (kept[part, :] + f32(came[part, :])).astype(jnp.bfloat16)


def split(kept, came):
    shape = (kept.shape[0] // CHIPS, kept.shape[1])
    return pl.pallas_call(
        split_kernel,
        out_shape=like((shape, jnp.float32), *[(shape, jnp.bfloat16)] * (CHIPS - 1)),
        in_specs=[WHOLE] * 2,
        out_specs=(WHOLE,) * CHIPS,
        compiler_params=params(4),
        name="split",
    )(kept, came)


def finish_kernel(
    section, mine, one, two, three, hidden, latent, mod, final_mod, w_final, w_embed, out, renewed
):
    last = mod.shape[1] - 1
    here = section[0]
    total = mine[...] + f32(one[...]) + f32(two[...]) + f32(three[...])
    gate = mod[2, pl.ds(here, 1), :]
    result = (f32(hidden[...]) + gate * total).astype(jnp.bfloat16)

    @pl.when(here == last)
    def _():
        normed = layer_norm(f32(result), final_mod[0:1, :], final_mod[1:2, :])
        velocity = dot_rows(normed, w_final[...])
        fresh = (f32(latent[...]) + velocity).astype(jnp.bfloat16)
        out[...] = dot(fresh, w_embed[...]).astype(jnp.bfloat16)
        renewed[...] = fresh

    @pl.when(here != last)
    def _():
        out[...] = result
        renewed[...] = latent[...]


def finish_packet_kernel(
    section, mine, one, two, three, packet, mod, final_mod, w_final, w_embed, *outs
):
    width, channels = w_embed.shape[1], w_embed.shape[0]
    views = [packet.at[:, :width], packet.at[:, width : width + channels]]
    if len(outs) == 1:
        outs = [outs[0].at[:, :width], outs[0].at[:, width : width + channels]]
    finish_kernel(
        section, mine, one, two, three, *views, mod, final_mod, w_final, w_embed, *outs
    )


def finish_first_kernel(
    section, mine, one, two, three, hidden, latent, mod, final_mod, w_final, w_embed, packet
):
    width, channels = w_embed.shape[1], w_embed.shape[0]
    outs = [packet.at[:, :width], packet.at[:, width : width + channels]]
    finish_kernel(
        section, mine, one, two, three, hidden, latent, mod, final_mod, w_final, w_embed, *outs
    )


def finish(section, parts, state, mod, final_mod, w_final, w_embed, packed):
    rows, width = parts[0].shape
    channels = w_embed.shape[0]
    shapes = [(rows, width + LANES)] if packed else [(rows, width), (rows, channels)]
    args = [*parts, *state, mod, final_mod, w_final, w_embed]
    return pl.pallas_call(
        finish_packet_kernel if len(state) == 1 else finish_first_kernel,
        out_shape=like(*[(shape, jnp.bfloat16) for shape in shapes]),
        in_specs=[SCALARS] + [WHOLE] * len(args),
        out_specs=(WHOLE,) * len(shapes),
        compiler_params=params(4),
        name="finish",
    )(section, *args)


def norm_kernel(section, values, mod, normed):
    here = section[0]
    tokens = f32(values[:, : normed.shape[1]])
    normed[...] = layer_norm(
        tokens, mod[0, pl.ds(here, 1), :], mod[1, pl.ds(here, 1), :]
    )


def norm(section, values, mod):
    return pl.pallas_call(
        norm_kernel,
        out_shape=jax.ShapeDtypeStruct((values.shape[0], mod.shape[2]), jnp.bfloat16),
        in_specs=[SCALARS] + [WHOLE] * 2,
        out_specs=WHOLE,
        compiler_params=params(4),
        name="norm",
    )(section, values, mod)


def exchange(value, apart):
    route = [(device, device ^ apart) for device in range(lax.axis_size("section"))]
    return lax.ppermute(value, "section", route)


def gather_chips(rows):
    return jnp.concatenate([rows] + [exchange(rows, apart) for apart in CHIP_STEPS], 0)


def body(
    hidden_in,
    latent_in,
    w_qkv,
    w_out,
    stale_kv,
    qk_gain,
    block_mod,
    final_mod,
    w_final,
    w_embed,
    patch_flow,
):
    size = lax.axis_size("section")
    ticks = patch_flow.shape[0]
    patch_flow = jnp.transpose(patch_flow)
    section = (lax.axis_index("section") // GROUP).astype(jnp.int32).reshape(1)
    mod = jnp.transpose(block_mod, (1, 0, 2))
    w_final = jnp.transpose(w_final)
    kv = stale_kv
    onward = [(device, (device + GROUP) % size) for device in range(size)]

    state = (hidden_in, latent_in)
    for tick in range(ticks):
        own = gather_chips(norm(section, state[0], mod))
        other = exchange(own, 1)
        kept, sent, kv = block(
            tick, section, patch_flow, own, other, qk_gain, w_qkv, w_out, kv
        )
        mine, *blocks = split(kept, exchange(sent, 1))
        parts = [mine] + [exchange(rows, apart) for rows, apart in zip(blocks, CHIP_STEPS)]
        packed = tick < ticks - 1
        state = finish(section, parts, state, mod, final_mod, w_final, w_embed, packed)
        state = tuple(lax.ppermute(value, "section", onward) for value in state)
    return state


def solution(mesh):
    in_specs = (
        P(("groups", "section"), None),
        P(("groups", "section"), None),
        P(None, None, "section"),
        P("section", None),
        P("groups", None, "section"),
        P(),
        P("groups", None, None),
        P("groups", None),
        P(),
        P(),
        P(),
    )
    out_specs = (P(("groups", "section"), None), P(("groups", "section"), None))
    return jax.shard_map(body, mesh=mesh, in_specs=in_specs, out_specs=out_specs, check_vma=False)
```

time: 215 us -> 198 us (0.921)
  local copies, waits for them, and re-layouts: 23.7 us -> 10.2 us
  waiting for transfers between devices: 95 us -> 102 us
  other arithmetic: 5.16 us -> 0.16 us
  Pallas kernels: 25.2 us -> 20.9 us
    unnamed x58 -> x35, local copies, waits for them, and re-layouts: 19.2 us -> 10.2 us
    ppermute x48, waiting for transfers between devices: 66 us -> 73.6 us  [exchange(): return lax.ppermute(value, 'section', route)]
    pallas_call x24, Pallas kernels: 25.2 us -> 20.9 us  [the longest x6 18.3 us: block(): pl.pallas_call(functools.partial(block_kernel, tick), out_shape=like(((ha...]
    another operation x6 -> x0, other arithmetic: 4.24 us -> none  [body(): flags = jnp.stack([section.astype(jnp.int32), patches[tick], is_last])]
    ppermute x6 -> x7, waiting for transfers between devices: 29.1 us -> 28.7 us  [body(): state = tuple((lax.ppermute(value, 'section', onward) for value in state))]
    ppermute x6 -> x7, starting transfers between devices: 18 us -> 18 us  [body(): state = tuple((lax.ppermute(value, 'section', onward) for value in state))]
  transfers between devices with their start and end apart: 54 -> 55, of which waited for: 41 -> 54; matrix products, arithmetic and copies ran while one was open for 4% -> 0% of each run, Pallas kernels for 0% -> 0%
where the time goes in v3:
time: 198 us
  waiting for transfers between devices  102 us (52%)
  starting transfers between devices  63.3 us (32%)
  Pallas kernels  20.9 us (11%)
  local copies, waits for them, and re-layouts  10.2 us (5%)
    ppermute x48, waiting for transfers between devices, exchange(): return lax.ppermute(value, 'section', route)  73.6 us
    ppermute x48, starting transfers between devices, exchange(): return lax.ppermute(value, 'section', route)  45.4 us
    ppermute x7, waiting for transfers between devices, body(): state = tuple((lax.ppermute(value, 'section', onward) for value in state))  28.7 us
    pallas_call x6, Pallas kernels, block(): pl.pallas_call(functools.partial(block_kernel, tick), out_shape=like(((ha...  18.3 us
    ppermute x7, starting transfers between devices, body(): state = tuple((lax.ppermute(value, 'section', onward) for value in state))  18 us
    unnamed x35, local copies, waits for them, and re-layouts  10.2 us
  transfers between devices with their start and end apart: 55, of which 54 were waited for; matrix products, arithmetic and copies ran while one was open for 0% of the time, Pallas kernels for 0%

profile of v3, /device:TPU:0, one launch (start us, length us, event | category | flops | bytes accessed | tf_op | source)
XLA Modules:
  0.0 197.8 jit_solution(1605639214539770204)
XLA Ops:
  3.8 3.1 %collective-permute-start.2 = (bf16[16,3072]{1,0:T(8,128)(2,1)S(1)}, bf16[16,3072]{1,0:T(8,128)(2,1)S(1)}, u32[]{:S(2)}, u32[]{:S(2)}) collective-permute-start(bf16[16,3072]{1,0:T(8,128)(2,1)S(1)} %norm.6), channel_id=1, source_target_pairs={{0,2},{1,3},{2,0},{3,1},{4,6},{5,7},{6,4},{7,5},{8,10},{9,11},{10,... | collective-permute-start | bytes 294920 | tf_op jit(solution)/shard_map/ppermute | solution.py:218
  9.6 2.7 %collective-permute-done.1 = bf16[16,3072]{1,0:T(8,128)(2,1)S(1)} collective-permute-done((bf16[16,3072]{1,0:T(8,128)(2,1)S(1)}, bf16[16,3072]{1,0:T(8,128)(2,1)S(1)}, u32[]{:S(2)}, u32[]{:S(2)}) %collective-permute-start.1) | collective-permute-done | bytes 98336 | tf_op jit(solution)/shard_map/ppermute | solution.py:218
  14.0 1.7 collective-permute-done.3.other
  15.7 3.0 %copy-done = bf16[3,3072,384]{2,1,0:T(8,128)(2,1)S(1)} copy-done((bf16[3,3072,384]{2,1,0:T(8,128)(2,1)S(1)}, bf16[3,3072,384]{2,1,0:T(8,128)(2,1)}, u32[]{:S(2)}) %copy-start) | copy-done | bytes 7077912
  18.8 1.7 copy-done.2
  21.8 3.0 %block.6 = (f32[64,3072]{1,0:T(8,128)S(1)}, bf16[64,3072]{1,0:T(8,128)(2,1)S(1)}, bf16[2,256,384]{2,1,0:T(8,128)(2,1)S(1)}) custom-call(s32[1]{0:T(128)} %bitcast.section, s32[2,6]{1,0:T(2,128)S(1)} %bitcast.22, bf16[64,3072]{1,0:T(8,128)(2,1)S(1)} %pad_maximum_fusion.own, ...), custom_call_target="tpu_custom_call", output_to_operand_aliasing={{2}: (7, {})} | custom-call | flops 1207959552 | bytes 9437184 | tf_op jit(solution)/shard_map/block/pallas_call | solution.py:95
  26.7 1.8 collective-permute-start.5
  30.3 3.1 %collective-permute-done.5.one = bf16[16,3072]{1,0:T(8,128)(2,1)S(1)} collective-permute-done((bf16[16,3072]{1,0:T(8,128)(2,1)S(1)}, bf16[16,3072]{1,0:T(8,128)(2,1)S(1)}, u32[]{:S(2)}, u32[]{:S(2)}) %collective-permute-start.5) | collective-permute-done | bytes 98336 | tf_op jit(solution)/shard_map/ppermute | solution.py:218
  34.8 3.2 %collective-permute-start.8 = (bf16[16,3200]{1,0:T(8,128)(2,1)S(1)}, bf16[16,3200]{1,0:T(8,128)(2,1)S(1)}, u32[]{:S(2)}, u32[]{:S(2)}) collective-permute-start(bf16[16,3200]{1,0:T(8,128)(2,1)S(1)} %finish.6), channel_id=1, source_target_pairs={{0,8},{1,9},{2,10},{3,11},{4,12},{5,13},{6,14},{7,15},{8,0},{9,1},... | collective-permute-start | bytes 307208 | tf_op jit(solution)/shard_map/ppermute | solution.py:258
  38.0 4.8 %collective-permute-done.8.values.packet = bf16[16,3200]{1,0:T(8,128)(2,1)S(1)} collective-permute-done((bf16[16,3200]{1,0:T(8,128)(2,1)S(1)}, bf16[16,3200]{1,0:T(8,128)(2,1)S(1)}, u32[]{:S(2)}, u32[]{:S(2)}) %collective-permute-start.8) | collective-permute-done | bytes 102432 | tf_op jit(solution)/shard_map/ppermute | solution.py:258
  44.7 2.0 collective-permute-start.9
  48.9 2.1 %collective-permute-done.9 = bf16[16,3072]{1,0:T(8,128)(2,1)S(1)} collective-permute-done((bf16[16,3072]{1,0:T(8,128)(2,1)S(1)}, bf16[16,3072]{1,0:T(8,128)(2,1)S(1)}, u32[]{:S(2)}, u32[]{:S(2)}) %collective-permute-start.9) | collective-permute-done | bytes 98336 | tf_op jit(solution)/shard_map/ppermute | solution.py:218
  51.1 1.7 collective-permute-done.12.other
  52.8 3.0 %block.7 = (f32[64,3072]{1,0:T(8,128)S(1)}, bf16[64,3072]{1,0:T(8,128)(2,1)S(1)}, bf16[2,256,384]{2,1,0:T(8,128)(2,1)S(1)}) custom-call(s32[1]{0:T(128)} %bitcast.section, s32[2,6]{1,0:T(2,128)S(1)} %bitcast.23, bf16[64,3072]{1,0:T(8,128)(2,1)S(1)} %pad_maximum_fusion.1.own, ...), custom_call_target="tpu_custom_call", output_to_operand_aliasing={{2}: (7, {})} | custom-call | flops 1207959552 | bytes 9437184 | tf_op jit(solution)/shard_map/block/pallas_call | solution.py:95
  61.3 3.1 %collective-permute-done.14.one = bf16[16,3072]{1,0:T(8,128)(2,1)S(1)} collective-permute-done((bf16[16,3072]{1,0:T(8,128)(2,1)S(1)}, bf16[16,3072]{1,0:T(8,128)(2,1)S(1)}, u32[]{:S(2)}, u32[]{:S(2)}) %collective-permute-start.14) | collective-permute-done | bytes 98336 | tf_op jit(solution)/shard_map/ppermute | solution.py:218
  65.7 3.2 %collective-permute-start.17 = (bf16[16,3200]{1,0:T(8,128)(2,1)S(1)}, bf16[16,3200]{1,0:T(8,128)(2,1)S(1)}, u32[]{:S(2)}, u32[]{:S(2)}) collective-permute-start(bf16[16,3200]{1,0:T(8,128)(2,1)S(1)} %finish.7), channel_id=1, source_target_pairs={{0,8},{1,9},{2,10},{3,11},{4,12},{5,13},{6,14},{7,15},{8,0},{9,1},... | collective-permute-start | bytes 307208 | tf_op jit(solution)/shard_map/ppermute | solution.py:258
  69.0 4.9 %collective-permute-done.17.values.packet = bf16[16,3200]{1,0:T(8,128)(2,1)S(1)} collective-permute-done((bf16[16,3200]{1,0:T(8,128)(2,1)S(1)}, bf16[16,3200]{1,0:T(8,128)(2,1)S(1)}, u32[]{:S(2)}, u32[]{:S(2)}) %collective-permute-start.17) | collective-permute-done | bytes 102432 | tf_op jit(solution)/shard_map/ppermute | solution.py:258
  75.3 2.4 %collective-permute-start.18 = (bf16[16,3072]{1,0:T(8,128)(2,1)S(1)}, bf16[16,3072]{1,0:T(8,128)(2,1)S(1)}, u32[]{:S(2)}, u32[]{:S(2)}) collective-permute-start(bf16[16,3072]{1,0:T(8,128)(2,1)S(1)} %norm.8), channel_id=1, source_target_pairs={{0,6},{1,7},{2,4},{3,5},{4,2},{5,3},{6,0},{7,1},{8,14},{9,15},{10,... | collective-permute-start | bytes 294920 | tf_op jit(solution)/shard_map/ppermute | solution.py:218
  80.1 2.1 %collective-permute-done.18 = bf16[16,3072]{1,0:T(8,128)(2,1)S(1)} collective-permute-done((bf16[16,3072]{1,0:T(8,128)(2,1)S(1)}, bf16[16,3072]{1,0:T(8,128)(2,1)S(1)}, u32[]{:S(2)}, u32[]{:S(2)}) %collective-permute-start.18) | collective-permute-done | bytes 98336 | tf_op jit(solution)/shard_map/ppermute | solution.py:218
  82.3 1.7 collective-permute-done.21.other
  84.0 3.0 %block.8 = (f32[64,3072]{1,0:T(8,128)S(1)}, bf16[64,3072]{1,0:T(8,128)(2,1)S(1)}, bf16[2,256,384]{2,1,0:T(8,128)(2,1)S(1)}) custom-call(s32[1]{0:T(128)} %bitcast.section, s32[2,6]{1,0:T(2,128)S(1)} %bitcast.24, bf16[64,3072]{1,0:T(8,128)(2,1)S(1)} %pad_maximum_fusion.2.own, ...), custom_call_target="tpu_custom_call", output_to_operand_aliasing={{2}: (7, {})} | custom-call | flops 1207959552 | bytes 9437184 | tf_op jit(solution)/shard_map/block/pallas_call | solution.py:95
  90.9 1.6 collective-permute-start.25
  92.5 3.1 %collective-permute-done.23.one = bf16[16,3072]{1,0:T(8,128)(2,1)S(1)} collective-permute-done((bf16[16,3072]{1,0:T(8,128)(2,1)S(1)}, bf16[16,3072]{1,0:T(8,128)(2,1)S(1)}, u32[]{:S(2)}, u32[]{:S(2)}) %collective-permute-start.23) | collective-permute-done | bytes 98336 | tf_op jit(solution)/shard_map/ppermute | solution.py:218
  97.1 2.7 %collective-permute-start.26 = (bf16[16,3200]{1,0:T(8,128)(2,1)S(1)}, bf16[16,3200]{1,0:T(8,128)(2,1)S(1)}, u32[]{:S(2)}, u32[]{:S(2)}) collective-permute-start(bf16[16,3200]{1,0:T(8,128)(2,1)S(1)} %finish.8), channel_id=1, source_target_pairs={{0,8},{1,9},{2,10},{3,11},{4,12},{5,13},{6,14},{7,15},{8,0},{9,1},... | collective-permute-start | bytes 307208 | tf_op jit(solution)/shard_map/ppermute | solution.py:258
  99.8 4.7 %collective-permute-done.26.values.packet = bf16[16,3200]{1,0:T(8,128)(2,1)S(1)} collective-permute-done((bf16[16,3200]{1,0:T(8,128)(2,1)S(1)}, bf16[16,3200]{1,0:T(8,128)(2,1)S(1)}, u32[]{:S(2)}, u32[]{:S(2)}) %collective-permute-start.26) | collective-permute-done | bytes 102432 | tf_op jit(solution)/shard_map/ppermute | solution.py:258
  106.2 2.1 %collective-permute-start.27 = (bf16[16,3072]{1,0:T(8,128)(2,1)S(1)}, bf16[16,3072]{1,0:T(8,128)(2,1)S(1)}, u32[]{:S(2)}, u32[]{:S(2)}) collective-permute-start(bf16[16,3072]{1,0:T(8,128)(2,1)S(1)} %norm.9), channel_id=1, source_target_pairs={{0,6},{1,7},{2,4},{3,5},{4,2},{5,3},{6,0},{7,1},{8,14},{9,15},{10,... | collective-permute-start | bytes 294920 | tf_op jit(solution)/shard_map/ppermute | solution.py:218
  110.6 2.1 %collective-permute-done.27 = bf16[16,3072]{1,0:T(8,128)(2,1)S(1)} collective-permute-done((bf16[16,3072]{1,0:T(8,128)(2,1)S(1)}, bf16[16,3072]{1,0:T(8,128)(2,1)S(1)}, u32[]{:S(2)}, u32[]{:S(2)}) %collective-permute-start.27) | collective-permute-done | bytes 98336 | tf_op jit(solution)/shard_map/ppermute | solution.py:218
  112.8 1.7 collective-permute-done.30.other
  114.6 3.0 %block.9 = (f32[64,3072]{1,0:T(8,128)S(1)}, bf16[64,3072]{1,0:T(8,128)(2,1)S(1)}, bf16[2,256,384]{2,1,0:T(8,128)(2,1)S(1)}) custom-call(s32[1]{0:T(128)} %bitcast.section, s32[2,6]{1,0:T(2,128)S(1)} %bitcast.25, bf16[64,3072]{1,0:T(8,128)(2,1)S(1)} %pad_maximum_fusion.3.own, ...), custom_call_target="tpu_custom_call", output_to_operand_aliasing={{2}: (7, {})} | custom-call | flops 1207959552 | bytes 9437184 | tf_op jit(solution)/shard_map/block/pallas_call | solution.py:95
  123.0 3.1 %collective-permute-done.32.one = bf16[16,3072]{1,0:T(8,128)(2,1)S(1)} collective-permute-done((bf16[16,3072]{1,0:T(8,128)(2,1)S(1)}, bf16[16,3072]{1,0:T(8,128)(2,1)S(1)}, u32[]{:S(2)}, u32[]{:S(2)}) %collective-permute-start.32) | collective-permute-done | bytes 98336 | tf_op jit(solution)/shard_map/ppermute | solution.py:218
  127.5 3.0 %collective-permute-start.35 = (bf16[16,3200]{1,0:T(8,128)(2,1)S(1)}, bf16[16,3200]{1,0:T(8,128)(2,1)S(1)}, u32[]{:S(2)}, u32[]{:S(2)}) collective-permute-start(bf16[16,3200]{1,0:T(8,128)(2,1)S(1)} %finish.9), channel_id=1, source_target_pairs={{0,8},{1,9},{2,10},{3,11},{4,12},{5,13},{6,14},{7,15},{8,0},{9,1},... | collective-permute-start | bytes 307208 | tf_op jit(solution)/shard_map/ppermute | solution.py:258
  130.5 4.8 %collective-permute-done.35.values.packet = bf16[16,3200]{1,0:T(8,128)(2,1)S(1)} collective-permute-done((bf16[16,3200]{1,0:T(8,128)(2,1)S(1)}, bf16[16,3200]{1,0:T(8,128)(2,1)S(1)}, u32[]{:S(2)}, u32[]{:S(2)}) %collective-permute-start.35) | collective-permute-done | bytes 102432 | tf_op jit(solution)/shard_map/ppermute | solution.py:258
  136.9 2.2 %collective-permute-start.36 = (bf16[16,3072]{1,0:T(8,128)(2,1)S(1)}, bf16[16,3072]{1,0:T(8,128)(2,1)S(1)}, u32[]{:S(2)}, u32[]{:S(2)}) collective-permute-start(bf16[16,3072]{1,0:T(8,128)(2,1)S(1)} %norm.10), channel_id=1, source_target_pairs={{0,6},{1,7},{2,4},{3,5},{4,2},{5,3},{6,0},{7,1},{8,14},{9,15},{10,... | collective-permute-start | bytes 294920 | tf_op jit(solution)/shard_map/ppermute | solution.py:218
  141.5 2.1 %collective-permute-done.36 = bf16[16,3072]{1,0:T(8,128)(2,1)S(1)} collective-permute-done((bf16[16,3072]{1,0:T(8,128)(2,1)S(1)}, bf16[16,3072]{1,0:T(8,128)(2,1)S(1)}, u32[]{:S(2)}, u32[]{:S(2)}) %collective-permute-start.36) | collective-permute-done | bytes 98336 | tf_op jit(solution)/shard_map/ppermute | solution.py:218
  143.7 1.7 collective-permute-done.39.other
  145.4 3.1 %block.10 = (f32[64,3072]{1,0:T(8,128)S(1)}, bf16[64,3072]{1,0:T(8,128)(2,1)S(1)}, bf16[2,256,384]{2,1,0:T(8,128)(2,1)S(1)}) custom-call(s32[1]{0:T(128)} %bitcast.section, s32[2,6]{1,0:T(2,128)S(1)} %bitcast.26, bf16[64,3072]{1,0:T(8,128)(2,1)S(1)} %pad_maximum_fusion.4.own, ...), custom_call_target="tpu_custom_call", output_to_operand_aliasing={{2}: (7, {})} | custom-call | flops 1207959552 | bytes 9437184 | tf_op jit(solution)/shard_map/block/pallas_call | solution.py:95
  152.3 1.6 collective-permute-start.43
  153.9 3.1 %collective-permute-done.41.one = bf16[16,3072]{1,0:T(8,128)(2,1)S(1)} collective-permute-done((bf16[16,3072]{1,0:T(8,128)(2,1)S(1)}, bf16[16,3072]{1,0:T(8,128)(2,1)S(1)}, u32[]{:S(2)}, u32[]{:S(2)}) %collective-permute-start.41) | collective-permute-done | bytes 98336 | tf_op jit(solution)/shard_map/ppermute | solution.py:218
  158.4 2.8 %collective-permute-start.44 = (bf16[16,3200]{1,0:T(8,128)(2,1)S(1)}, bf16[16,3200]{1,0:T(8,128)(2,1)S(1)}, u32[]{:S(2)}, u32[]{:S(2)}) collective-permute-start(bf16[16,3200]{1,0:T(8,128)(2,1)S(1)} %finish.10), channel_id=1, source_target_pairs={{0,8},{1,9},{2,10},{3,11},{4,12},{5,13},{6,14},{7,15},{8,0},{9,1},... | collective-permute-start | bytes 307208 | tf_op jit(solution)/shard_map/ppermute | solution.py:258
  161.1 4.7 %collective-permute-done.44.values.packet = bf16[16,3200]{1,0:T(8,128)(2,1)S(1)} collective-permute-done((bf16[16,3200]{1,0:T(8,128)(2,1)S(1)}, bf16[16,3200]{1,0:T(8,128)(2,1)S(1)}, u32[]{:S(2)}, u32[]{:S(2)}) %collective-permute-start.44) | collective-permute-done | bytes 102432 | tf_op jit(solution)/shard_map/ppermute | solution.py:258
  167.5 2.2 %collective-permute-start.45 = (bf16[16,3072]{1,0:T(8,128)(2,1)S(1)}, bf16[16,3072]{1,0:T(8,128)(2,1)S(1)}, u32[]{:S(2)}, u32[]{:S(2)}) collective-permute-start(bf16[16,3072]{1,0:T(8,128)(2,1)S(1)} %norm.11), channel_id=1, source_target_pairs={{0,6},{1,7},{2,4},{3,5},{4,2},{5,3},{6,0},{7,1},{8,14},{9,15},{10,... | collective-permute-start | bytes 294920 | tf_op jit(solution)/shard_map/ppermute | solution.py:218
  172.0 2.1 %collective-permute-done.45 = bf16[16,3072]{1,0:T(8,128)(2,1)S(1)} collective-permute-done((bf16[16,3072]{1,0:T(8,128)(2,1)S(1)}, bf16[16,3072]{1,0:T(8,128)(2,1)S(1)}, u32[]{:S(2)}, u32[]{:S(2)}) %collective-permute-start.45) | collective-permute-done | bytes 98336 | tf_op jit(solution)/shard_map/ppermute | solution.py:218
  174.2 1.7 collective-permute-done.48.other
  175.9 3.0 %block.11 = (f32[64,3072]{1,0:T(8,128)S(1)}, bf16[64,3072]{1,0:T(8,128)(2,1)S(1)}, bf16[2,256,384]{2,1,0:T(8,128)(2,1)S(1)}) custom-call(s32[1]{0:T(128)} %bitcast.section, s32[2,6]{1,0:T(2,128)S(1)} %bitcast.27, bf16[64,3072]{1,0:T(8,128)(2,1)S(1)} %pad_maximum_fusion.5.own, ...), custom_call_target="tpu_custom_call", output_to_operand_aliasing={{2}: (7, {})} | custom-call | flops 1207959552 | bytes 9437184 | tf_op jit(solution)/shard_map/block/pallas_call | solution.py:95
  182.8 1.6 collective-permute-start.52
  184.4 3.1 %collective-permute-done.50.one = bf16[16,3072]{1,0:T(8,128)(2,1)S(1)} collective-permute-done((bf16[16,3072]{1,0:T(8,128)(2,1)S(1)}, bf16[16,3072]{1,0:T(8,128)(2,1)S(1)}, u32[]{:S(2)}, u32[]{:S(2)}) %collective-permute-start.50) | collective-permute-done | bytes 98336 | tf_op jit(solution)/shard_map/ppermute | solution.py:218
  188.8 3.0 %collective-permute-start.53 = (bf16[16,3072]{1,0:T(8,128)(2,1)S(1)}, bf16[16,3072]{1,0:T(8,128)(2,1)S(1)}, u32[]{:S(2)}, u32[]{:S(2)}) collective-permute-start(bf16[16,3072]{1,0:T(8,128)(2,1)S(1)} %get-tuple-element.86), channel_id=1, source_target_pairs={{0,8},{1,9},{2,10},{3,11},{4,12},{5,13},{6,14},{7,15},{8,0},{9,1},... | collective-permute-start | bytes 294920 | tf_op jit(solution)/shard_map/ppermute | solution.py:258
  191.9 4.7 %collective-permute-done.54 = bf16[16,64]{1,0:T(8,128)(2,1)S(1)} collective-permute-done((bf16[16,64]{1,0:T(8,128)(2,1)S(1)}, bf16[16,64]{1,0:T(8,128)(2,1)S(1)}, u32[]{:S(2)}, u32[]{:S(2)}) %collective-permute-start.54) | collective-permute-done | bytes 2080 | tf_op jit(solution)/shard_map/ppermute | solution.py:258
  (127 shorter events, 64.8 us)
Async XLA Ops:
  3.8 5.9 %collective-permute-start.2 = (bf16[16,3072]{1,0:T(8,128)(2,1)S(1)}, bf16[16,3072]{1,0:T(8,128)(2,1)S(1)}, u32[]{:S(2)}, u32[]{:S(2)}) collective-permute-start(bf16[16,3072]{1,0:T(8,128)(2,1)S(1)} %norm.6), channel_id=1, source_target_pairs={{0,2},{1,3},{2,0},{3,1},{4,6},{5,7},{6,4},{7,5},{8,10},{9,11},{10,... | collective-permute-start | bytes 294920 | tf_op jit(solution)/shard_map/ppermute | solution.py:218
  6.8 5.5 %collective-permute-start.1 = (bf16[16,3072]{1,0:T(8,128)(2,1)S(1)}, bf16[16,3072]{1,0:T(8,128)(2,1)S(1)}, u32[]{:S(2)}, u32[]{:S(2)}) collective-permute-start(bf16[16,3072]{1,0:T(8,128)(2,1)S(1)} %norm.6), channel_id=1, source_target_pairs={{0,4},{1,5},{2,6},{3,7},{4,0},{5,1},{6,2},{7,3},{8,12},{9,13},{10,... | collective-permute-start | bytes 294920 | tf_op jit(solution)/shard_map/ppermute | solution.py:218
  8.4 5.5 %collective-permute-start = (bf16[16,3072]{1,0:T(8,128)(2,1)S(1)}, bf16[16,3072]{1,0:T(8,128)(2,1)S(1)}, u32[]{:S(2)}, u32[]{:S(2)}) collective-permute-start(bf16[16,3072]{1,0:T(8,128)(2,1)S(1)} %norm.6), channel_id=1, source_target_pairs={{0,6},{1,7},{2,4},{3,5},{4,2},{5,3},{6,0},{7,1},{8,14},{9,15},{10,... | collective-permute-start | bytes 294920 | tf_op jit(solution)/shard_map/ppermute | solution.py:218
  14.0 1.8 collective-permute-start.3
  24.9 1.8 collective-permute-start.4
  26.7 6.6 %collective-permute-start.5 = (bf16[16,3072]{1,0:T(8,128)(2,1)S(1)}, bf16[16,3072]{1,0:T(8,128)(2,1)S(1)}, u32[]{:S(2)}, u32[]{:S(2)}) collective-permute-start(bf16[16,3072]{1,0:T(8,128)(2,1)S(1)} %get-tuple-element.48), channel_id=1, source_target_pairs={{0,6},{1,7},{2,4},{3,5},{4,2},{5,3},{6,0},{7,1},{8,14},{9,15},{10,... | collective-permute-start | bytes 294920 | tf_op jit(solution)/shard_map/ppermute | solution.py:218
  28.5 5.6 %collective-permute-start.6 = (bf16[16,3072]{1,0:T(8,128)(2,1)S(1)}, bf16[16,3072]{1,0:T(8,128)(2,1)S(1)}, u32[]{:S(2)}, u32[]{:S(2)}) collective-permute-start(bf16[16,3072]{1,0:T(8,128)(2,1)S(1)} %get-tuple-element.49), channel_id=1, source_target_pairs={{0,4},{1,5},{2,6},{3,7},{4,0},{5,1},{6,2},{7,3},{8,12},{9,13},{10,... | collective-permute-start | bytes 294920 | tf_op jit(solution)/shard_map/ppermute | solution.py:218
  29.2 5.5 %collective-permute-start.7 = (bf16[16,3072]{1,0:T(8,128)(2,1)S(1)}, bf16[16,3072]{1,0:T(8,128)(2,1)S(1)}, u32[]{:S(2)}, u32[]{:S(2)}) collective-permute-start(bf16[16,3072]{1,0:T(8,128)(2,1)S(1)} %get-tuple-element.50), channel_id=1, source_target_pairs={{0,2},{1,3},{2,0},{3,1},{4,6},{5,7},{6,4},{7,5},{8,10},{9,11},{10,... | collective-permute-start | bytes 294920 | tf_op jit(solution)/shard_map/ppermute | solution.py:218
  34.8 8.1 %collective-permute-start.8 = (bf16[16,3200]{1,0:T(8,128)(2,1)S(1)}, bf16[16,3200]{1,0:T(8,128)(2,1)S(1)}, u32[]{:S(2)}, u32[]{:S(2)}) collective-permute-start(bf16[16,3200]{1,0:T(8,128)(2,1)S(1)} %finish.6), channel_id=1, source_target_pairs={{0,8},{1,9},{2,10},{3,11},{4,12},{5,13},{6,14},{7,15},{8,0},{9,1},... | collective-permute-start | bytes 307208 | tf_op jit(solution)/shard_map/ppermute | solution.py:258
  43.1 4.7 %collective-permute-start.11 = (bf16[16,3072]{1,0:T(8,128)(2,1)S(1)}, bf16[16,3072]{1,0:T(8,128)(2,1)S(1)}, u32[]{:S(2)}, u32[]{:S(2)}) collective-permute-start(bf16[16,3072]{1,0:T(8,128)(2,1)S(1)} %norm.7), channel_id=1, source_target_pairs={{0,2},{1,3},{2,0},{3,1},{4,6},{5,7},{6,4},{7,5},{8,10},{9,11},{10,... | collective-permute-start | bytes 294920 | tf_op jit(solution)/shard_map/ppermute | solution.py:218
  44.0 4.9 %collective-permute-start.10 = (bf16[16,3072]{1,0:T(8,128)(2,1)S(1)}, bf16[16,3072]{1,0:T(8,128)(2,1)S(1)}, u32[]{:S(2)}, u32[]{:S(2)}) collective-permute-start(bf16[16,3072]{1,0:T(8,128)(2,1)S(1)} %norm.7), channel_id=1, source_target_pairs={{0,4},{1,5},{2,6},{3,7},{4,0},{5,1},{6,2},{7,3},{8,12},{9,13},{10,... | collective-permute-start | bytes 294920 | tf_op jit(solution)/shard_map/ppermute | solution.py:218
  44.7 6.3 %collective-permute-start.9 = (bf16[16,3072]{1,0:T(8,128)(2,1)S(1)}, bf16[16,3072]{1,0:T(8,128)(2,1)S(1)}, u32[]{:S(2)}, u32[]{:S(2)}) collective-permute-start(bf16[16,3072]{1,0:T(8,128)(2,1)S(1)} %norm.7), channel_id=1, source_target_pairs={{0,6},{1,7},{2,4},{3,5},{4,2},{5,3},{6,0},{7,1},{8,14},{9,15},{10,... | collective-permute-start | bytes 294920 | tf_op jit(solution)/shard_map/ppermute | solution.py:218
  51.0 1.8 collective-permute-start.12
  55.9 1.8 collective-permute-start.13
  57.7 6.6 %collective-permute-start.14 = (bf16[16,3072]{1,0:T(8,128)(2,1)S(1)}, bf16[16,3072]{1,0:T(8,128)(2,1)S(1)}, u32[]{:S(2)}, u32[]{:S(2)}) collective-permute-start(bf16[16,3072]{1,0:T(8,128)(2,1)S(1)} %get-tuple-element.55), channel_id=1, source_target_pairs={{0,6},{1,7},{2,4},{3,5},{4,2},{5,3},{6,0},{7,1},{8,14},{9,15},{10,... | collective-permute-start | bytes 294920 | tf_op jit(solution)/shard_map/ppermute | solution.py:218
  59.1 5.5 %collective-permute-start.15 = (bf16[16,3072]{1,0:T(8,128)(2,1)S(1)}, bf16[16,3072]{1,0:T(8,128)(2,1)S(1)}, u32[]{:S(2)}, u32[]{:S(2)}) collective-permute-start(bf16[16,3072]{1,0:T(8,128)(2,1)S(1)} %get-tuple-element.56), channel_id=1, source_target_pairs={{0,4},{1,5},{2,6},{3,7},{4,0},{5,1},{6,2},{7,3},{8,12},{9,13},{10,... | collective-permute-start | bytes 294920 | tf_op jit(solution)/shard_map/ppermute | solution.py:218
  59.7 6.0 %collective-permute-start.16 = (bf16[16,3072]{1,0:T(8,128)(2,1)S(1)}, bf16[16,3072]{1,0:T(8,128)(2,1)S(1)}, u32[]{:S(2)}, u32[]{:S(2)}) collective-permute-start(bf16[16,3072]{1,0:T(8,128)(2,1)S(1)} %get-tuple-element.57), channel_id=1, source_target_pairs={{0,2},{1,3},{2,0},{3,1},{4,6},{5,7},{6,4},{7,5},{8,10},{9,11},{10,... | collective-permute-start | bytes 294920 | tf_op jit(solution)/shard_map/ppermute | solution.py:218
  65.7 8.1 %collective-permute-start.17 = (bf16[16,3200]{1,0:T(8,128)(2,1)S(1)}, bf16[16,3200]{1,0:T(8,128)(2,1)S(1)}, u32[]{:S(2)}, u32[]{:S(2)}) collective-permute-start(bf16[16,3200]{1,0:T(8,128)(2,1)S(1)} %finish.7), channel_id=1, source_target_pairs={{0,8},{1,9},{2,10},{3,11},{4,12},{5,13},{6,14},{7,15},{8,0},{9,1},... | collective-permute-start | bytes 307208 | tf_op jit(solution)/shard_map/ppermute | solution.py:258
  74.1 4.8 %collective-permute-start.20 = (bf16[16,3072]{1,0:T(8,128)(2,1)S(1)}, bf16[16,3072]{1,0:T(8,128)(2,1)S(1)}, u32[]{:S(2)}, u32[]{:S(2)}) collective-permute-start(bf16[16,3072]{1,0:T(8,128)(2,1)S(1)} %norm.8), channel_id=1, source_target_pairs={{0,2},{1,3},{2,0},{3,1},{4,6},{5,7},{6,4},{7,5},{8,10},{9,11},{10,... | collective-permute-start | bytes 294920 | tf_op jit(solution)/shard_map/ppermute | solution.py:218
  74.8 5.3 %collective-permute-start.19 = (bf16[16,3072]{1,0:T(8,128)(2,1)S(1)}, bf16[16,3072]{1,0:T(8,128)(2,1)S(1)}, u32[]{:S(2)}, u32[]{:S(2)}) collective-permute-start(bf16[16,3072]{1,0:T(8,128)(2,1)S(1)} %norm.8), channel_id=1, source_target_pairs={{0,4},{1,5},{2,6},{3,7},{4,0},{5,1},{6,2},{7,3},{8,12},{9,13},{10,... | collective-permute-start | bytes 294920 | tf_op jit(solution)/shard_map/ppermute | solution.py:218
  75.3 6.9 %collective-permute-start.18 = (bf16[16,3072]{1,0:T(8,128)(2,1)S(1)}, bf16[16,3072]{1,0:T(8,128)(2,1)S(1)}, u32[]{:S(2)}, u32[]{:S(2)}) collective-permute-start(bf16[16,3072]{1,0:T(8,128)(2,1)S(1)} %norm.8), channel_id=1, source_target_pairs={{0,6},{1,7},{2,4},{3,5},{4,2},{5,3},{6,0},{7,1},{8,14},{9,15},{10,... | collective-permute-start | bytes 294920 | tf_op jit(solution)/shard_map/ppermute | solution.py:218
  82.2 1.8 collective-permute-start.21
  88.9 6.6 %collective-permute-start.23 = (bf16[16,3072]{1,0:T(8,128)(2,1)S(1)}, bf16[16,3072]{1,0:T(8,128)(2,1)S(1)}, u32[]{:S(2)}, u32[]{:S(2)}) collective-permute-start(bf16[16,3072]{1,0:T(8,128)(2,1)S(1)} %get-tuple-element.62), channel_id=1, source_target_pairs={{0,6},{1,7},{2,4},{3,5},{4,2},{5,3},{6,0},{7,1},{8,14},{9,15},{10,... | collective-permute-start | bytes 294920 | tf_op jit(solution)/shard_map/ppermute | solution.py:218
  90.0 5.8 %collective-permute-start.24 = (bf16[16,3072]{1,0:T(8,128)(2,1)S(1)}, bf16[16,3072]{1,0:T(8,128)(2,1)S(1)}, u32[]{:S(2)}, u32[]{:S(2)}) collective-permute-start(bf16[16,3072]{1,0:T(8,128)(2,1)S(1)} %get-tuple-element.63), channel_id=1, source_target_pairs={{0,4},{1,5},{2,6},{3,7},{4,0},{5,1},{6,2},{7,3},{8,12},{9,13},{10,... | collective-permute-start | bytes 294920 | tf_op jit(solution)/shard_map/ppermute | solution.py:218
  90.9 6.0 %collective-permute-start.25 = (bf16[16,3072]{1,0:T(8,128)(2,1)S(1)}, bf16[16,3072]{1,0:T(8,128)(2,1)S(1)}, u32[]{:S(2)}, u32[]{:S(2)}) collective-permute-start(bf16[16,3072]{1,0:T(8,128)(2,1)S(1)} %get-tuple-element.64), channel_id=1, source_target_pairs={{0,2},{1,3},{2,0},{3,1},{4,6},{5,7},{6,4},{7,5},{8,10},{9,11},{10,... | collective-permute-start | bytes 294920 | tf_op jit(solution)/shard_map/ppermute | solution.py:218
  97.1 7.4 %collective-permute-start.26 = (bf16[16,3200]{1,0:T(8,128)(2,1)S(1)}, bf16[16,3200]{1,0:T(8,128)(2,1)S(1)}, u32[]{:S(2)}, u32[]{:S(2)}) collective-permute-start(bf16[16,3200]{1,0:T(8,128)(2,1)S(1)} %finish.8), channel_id=1, source_target_pairs={{0,8},{1,9},{2,10},{3,11},{4,12},{5,13},{6,14},{7,15},{8,0},{9,1},... | collective-permute-start | bytes 307208 | tf_op jit(solution)/shard_map/ppermute | solution.py:258
  104.8 4.7 %collective-permute-start.29 = (bf16[16,3072]{1,0:T(8,128)(2,1)S(1)}, bf16[16,3072]{1,0:T(8,128)(2,1)S(1)}, u32[]{:S(2)}, u32[]{:S(2)}) collective-permute-start(bf16[16,3072]{1,0:T(8,128)(2,1)S(1)} %norm.9), channel_id=1, source_target_pairs={{0,2},{1,3},{2,0},{3,1},{4,6},{5,7},{6,4},{7,5},{8,10},{9,11},{10,... | collective-permute-start | bytes 294920 | tf_op jit(solution)/shard_map/ppermute | solution.py:218
  105.6 5.0 %collective-permute-start.28 = (bf16[16,3072]{1,0:T(8,128)(2,1)S(1)}, bf16[16,3072]{1,0:T(8,128)(2,1)S(1)}, u32[]{:S(2)}, u32[]{:S(2)}) collective-permute-start(bf16[16,3072]{1,0:T(8,128)(2,1)S(1)} %norm.9), channel_id=1, source_target_pairs={{0,4},{1,5},{2,6},{3,7},{4,0},{5,1},{6,2},{7,3},{8,12},{9,13},{10,... | collective-permute-start | bytes 294920 | tf_op jit(solution)/shard_map/ppermute | solution.py:218
  106.2 6.5 %collective-permute-start.27 = (bf16[16,3072]{1,0:T(8,128)(2,1)S(1)}, bf16[16,3072]{1,0:T(8,128)(2,1)S(1)}, u32[]{:S(2)}, u32[]{:S(2)}) collective-permute-start(bf16[16,3072]{1,0:T(8,128)(2,1)S(1)} %norm.9), channel_id=1, source_target_pairs={{0,6},{1,7},{2,4},{3,5},{4,2},{5,3},{6,0},{7,1},{8,14},{9,15},{10,... | collective-permute-start | bytes 294920 | tf_op jit(solution)/shard_map/ppermute | solution.py:218
  119.5 6.6 %collective-permute-start.32 = (bf16[16,3072]{1,0:T(8,128)(2,1)S(1)}, bf16[16,3072]{1,0:T(8,128)(2,1)S(1)}, u32[]{:S(2)}, u32[]{:S(2)}) collective-permute-start(bf16[16,3072]{1,0:T(8,128)(2,1)S(1)} %get-tuple-element.69), channel_id=1, source_target_pairs={{0,6},{1,7},{2,4},{3,5},{4,2},{5,3},{6,0},{7,1},{8,14},{9,15},{10,... | collective-permute-start | bytes 294920 | tf_op jit(solution)/shard_map/ppermute | solution.py:218
  120.6 5.7 %collective-permute-start.33 = (bf16[16,3072]{1,0:T(8,128)(2,1)S(1)}, bf16[16,3072]{1,0:T(8,128)(2,1)S(1)}, u32[]{:S(2)}, u32[]{:S(2)}) collective-permute-start(bf16[16,3072]{1,0:T(8,128)(2,1)S(1)} %get-tuple-element.70), channel_id=1, source_target_pairs={{0,4},{1,5},{2,6},{3,7},{4,0},{5,1},{6,2},{7,3},{8,12},{9,13},{10,... | collective-permute-start | bytes 294920 | tf_op jit(solution)/shard_map/ppermute | solution.py:218
  121.4 6.0 %collective-permute-start.34 = (bf16[16,3072]{1,0:T(8,128)(2,1)S(1)}, bf16[16,3072]{1,0:T(8,128)(2,1)S(1)}, u32[]{:S(2)}, u32[]{:S(2)}) collective-permute-start(bf16[16,3072]{1,0:T(8,128)(2,1)S(1)} %get-tuple-element.71), channel_id=1, source_target_pairs={{0,2},{1,3},{2,0},{3,1},{4,6},{5,7},{6,4},{7,5},{8,10},{9,11},{10,... | collective-permute-start | bytes 294920 | tf_op jit(solution)/shard_map/ppermute | solution.py:218
  127.5 7.8 %collective-permute-start.35 = (bf16[16,3200]{1,0:T(8,128)(2,1)S(1)}, bf16[16,3200]{1,0:T(8,128)(2,1)S(1)}, u32[]{:S(2)}, u32[]{:S(2)}) collective-permute-start(bf16[16,3200]{1,0:T(8,128)(2,1)S(1)} %finish.9), channel_id=1, source_target_pairs={{0,8},{1,9},{2,10},{3,11},{4,12},{5,13},{6,14},{7,15},{8,0},{9,1},... | collective-permute-start | bytes 307208 | tf_op jit(solution)/shard_map/ppermute | solution.py:258
  135.5 4.8 %collective-permute-start.38 = (bf16[16,3072]{1,0:T(8,128)(2,1)S(1)}, bf16[16,3072]{1,0:T(8,128)(2,1)S(1)}, u32[]{:S(2)}, u32[]{:S(2)}) collective-permute-start(bf16[16,3072]{1,0:T(8,128)(2,1)S(1)} %norm.10), channel_id=1, source_target_pairs={{0,2},{1,3},{2,0},{3,1},{4,6},{5,7},{6,4},{7,5},{8,10},{9,11},{10,... | collective-permute-start | bytes 294920 | tf_op jit(solution)/shard_map/ppermute | solution.py:218
  136.3 5.2 %collective-permute-start.37 = (bf16[16,3072]{1,0:T(8,128)(2,1)S(1)}, bf16[16,3072]{1,0:T(8,128)(2,1)S(1)}, u32[]{:S(2)}, u32[]{:S(2)}) collective-permute-start(bf16[16,3072]{1,0:T(8,128)(2,1)S(1)} %norm.10), channel_id=1, source_target_pairs={{0,4},{1,5},{2,6},{3,7},{4,0},{5,1},{6,2},{7,3},{8,12},{9,13},{10,... | collective-permute-start | bytes 294920 | tf_op jit(solution)/shard_map/ppermute | solution.py:218
  136.9 6.8 %collective-permute-start.36 = (bf16[16,3072]{1,0:T(8,128)(2,1)S(1)}, bf16[16,3072]{1,0:T(8,128)(2,1)S(1)}, u32[]{:S(2)}, u32[]{:S(2)}) collective-permute-start(bf16[16,3072]{1,0:T(8,128)(2,1)S(1)} %norm.10), channel_id=1, source_target_pairs={{0,6},{1,7},{2,4},{3,5},{4,2},{5,3},{6,0},{7,1},{8,14},{9,15},{10,... | collective-permute-start | bytes 294920 | tf_op jit(solution)/shard_map/ppermute | solution.py:218
  150.4 6.6 %collective-permute-start.41 = (bf16[16,3072]{1,0:T(8,128)(2,1)S(1)}, bf16[16,3072]{1,0:T(8,128)(2,1)S(1)}, u32[]{:S(2)}, u32[]{:S(2)}) collective-permute-start(bf16[16,3072]{1,0:T(8,128)(2,1)S(1)} %get-tuple-element.76), channel_id=1, source_target_pairs={{0,6},{1,7},{2,4},{3,5},{4,2},{5,3},{6,0},{7,1},{8,14},{9,15},{10,... | collective-permute-start | bytes 294920 | tf_op jit(solution)/shard_map/ppermute | solution.py:218
  151.4 5.8 %collective-permute-start.42 = (bf16[16,3072]{1,0:T(8,128)(2,1)S(1)}, bf16[16,3072]{1,0:T(8,128)(2,1)S(1)}, u32[]{:S(2)}, u32[]{:S(2)}) collective-permute-start(bf16[16,3072]{1,0:T(8,128)(2,1)S(1)} %get-tuple-element.77), channel_id=1, source_target_pairs={{0,4},{1,5},{2,6},{3,7},{4,0},{5,1},{6,2},{7,3},{8,12},{9,13},{10,... | collective-permute-start | bytes 294920 | tf_op jit(solution)/shard_map/ppermute | solution.py:218
  152.3 6.0 %collective-permute-start.43 = (bf16[16,3072]{1,0:T(8,128)(2,1)S(1)}, bf16[16,3072]{1,0:T(8,128)(2,1)S(1)}, u32[]{:S(2)}, u32[]{:S(2)}) collective-permute-start(bf16[16,3072]{1,0:T(8,128)(2,1)S(1)} %get-tuple-element.78), channel_id=1, source_target_pairs={{0,2},{1,3},{2,0},{3,1},{4,6},{5,7},{6,4},{7,5},{8,10},{9,11},{10,... | collective-permute-start | bytes 294920 | tf_op jit(solution)/shard_map/ppermute | solution.py:218
  158.4 7.5 %collective-permute-start.44 = (bf16[16,3200]{1,0:T(8,128)(2,1)S(1)}, bf16[16,3200]{1,0:T(8,128)(2,1)S(1)}, u32[]{:S(2)}, u32[]{:S(2)}) collective-permute-start(bf16[16,3200]{1,0:T(8,128)(2,1)S(1)} %finish.10), channel_id=1, source_target_pairs={{0,8},{1,9},{2,10},{3,11},{4,12},{5,13},{6,14},{7,15},{8,0},{9,1},... | collective-permute-start | bytes 307208 | tf_op jit(solution)/shard_map/ppermute | solution.py:258
  166.1 4.7 %collective-permute-start.47 = (bf16[16,3072]{1,0:T(8,128)(2,1)S(1)}, bf16[16,3072]{1,0:T(8,128)(2,1)S(1)}, u32[]{:S(2)}, u32[]{:S(2)}) collective-permute-start(bf16[16,3072]{1,0:T(8,128)(2,1)S(1)} %norm.11), channel_id=1, source_target_pairs={{0,2},{1,3},{2,0},{3,1},{4,6},{5,7},{6,4},{7,5},{8,10},{9,11},{10,... | collective-permute-start | bytes 294920 | tf_op jit(solution)/shard_map/ppermute | solution.py:218
  167.0 5.0 %collective-permute-start.46 = (bf16[16,3072]{1,0:T(8,128)(2,1)S(1)}, bf16[16,3072]{1,0:T(8,128)(2,1)S(1)}, u32[]{:S(2)}, u32[]{:S(2)}) collective-permute-start(bf16[16,3072]{1,0:T(8,128)(2,1)S(1)} %norm.11), channel_id=1, source_target_pairs={{0,4},{1,5},{2,6},{3,7},{4,0},{5,1},{6,2},{7,3},{8,12},{9,13},{10,... | collective-permute-start | bytes 294920 | tf_op jit(solution)/shard_map/ppermute | solution.py:218
  167.5 6.6 %collective-permute-start.45 = (bf16[16,3072]{1,0:T(8,128)(2,1)S(1)}, bf16[16,3072]{1,0:T(8,128)(2,1)S(1)}, u32[]{:S(2)}, u32[]{:S(2)}) collective-permute-start(bf16[16,3072]{1,0:T(8,128)(2,1)S(1)} %norm.11), channel_id=1, source_target_pairs={{0,6},{1,7},{2,4},{3,5},{4,2},{5,3},{6,0},{7,1},{8,14},{9,15},{10,... | collective-permute-start | bytes 294920 | tf_op jit(solution)/shard_map/ppermute | solution.py:218
  180.8 6.6 %collective-permute-start.50 = (bf16[16,3072]{1,0:T(8,128)(2,1)S(1)}, bf16[16,3072]{1,0:T(8,128)(2,1)S(1)}, u32[]{:S(2)}, u32[]{:S(2)}) collective-permute-start(bf16[16,3072]{1,0:T(8,128)(2,1)S(1)} %get-tuple-element.83), channel_id=1, source_target_pairs={{0,6},{1,7},{2,4},{3,5},{4,2},{5,3},{6,0},{7,1},{8,14},{9,15},{10,... | collective-permute-start | bytes 294920 | tf_op jit(solution)/shard_map/ppermute | solution.py:218
  182.0 5.7 %collective-permute-start.51 = (bf16[16,3072]{1,0:T(8,128)(2,1)S(1)}, bf16[16,3072]{1,0:T(8,128)(2,1)S(1)}, u32[]{:S(2)}, u32[]{:S(2)}) collective-permute-start(bf16[16,3072]{1,0:T(8,128)(2,1)S(1)} %get-tuple-element.84), channel_id=1, source_target_pairs={{0,4},{1,5},{2,6},{3,7},{4,0},{5,1},{6,2},{7,3},{8,12},{9,13},{10,... | collective-permute-start | bytes 294920 | tf_op jit(solution)/shard_map/ppermute | solution.py:218
  182.8 6.0 %collective-permute-start.52 = (bf16[16,3072]{1,0:T(8,128)(2,1)S(1)}, bf16[16,3072]{1,0:T(8,128)(2,1)S(1)}, u32[]{:S(2)}, u32[]{:S(2)}) collective-permute-start(bf16[16,3072]{1,0:T(8,128)(2,1)S(1)} %get-tuple-element.85), channel_id=1, source_target_pairs={{0,2},{1,3},{2,0},{3,1},{4,6},{5,7},{6,4},{7,5},{8,10},{9,11},{10,... | collective-permute-start | bytes 294920 | tf_op jit(solution)/shard_map/ppermute | solution.py:218
  188.8 7.7 %collective-permute-start.53 = (bf16[16,3072]{1,0:T(8,128)(2,1)S(1)}, bf16[16,3072]{1,0:T(8,128)(2,1)S(1)}, u32[]{:S(2)}, u32[]{:S(2)}) collective-permute-start(bf16[16,3072]{1,0:T(8,128)(2,1)S(1)} %get-tuple-element.86), channel_id=1, source_target_pairs={{0,8},{1,9},{2,10},{3,11},{4,12},{5,13},{6,14},{7,15},{8,0},{9,1},... | collective-permute-start | bytes 294920 | tf_op jit(solution)/shard_map/ppermute | solution.py:258
  191.8 4.8 %collective-permute-start.54 = (bf16[16,64]{1,0:T(8,128)(2,1)S(1)}, bf16[16,64]{1,0:T(8,128)(2,1)S(1)}, u32[]{:S(2)}, u32[]{:S(2)}) collective-permute-start(bf16[16,64]{1,0:T(8,128)(2,1)S(1)} %get-tuple-element.87), channel_id=1, source_target_pairs={{0,8},{1,9},{2,10},{3,11},{4,12},{5,13},{6,14},{7,15},{8,0},{9,1},... | collective-permute-start | bytes 6152 | tf_op jit(solution)/shard_map/ppermute | solution.py:258
  (23 other events, 342.5 us)

commit v4 on v3

--- a/solution.py
+++ b/solution.py
@@ -11,7 +11,7 @@
 HS = 128
 GROUP = 8
 CHIPS = 4
-CHIP_STEPS = (6, 4, 2)
+CHIP_STEPS = (2, 4, 6)
 LANES = 128
 EPS = 1e-6
 VMEM = pltpu.VMEM
@@ -134,9 +134,14 @@
     )(kept, came)
 
 
-def finish_kernel(
-    section, mine, one, two, three, hidden, latent, mod, final_mod, w_final, w_embed, out, renewed
-):
+def finish_kernel(first_tick, *refs):
+    (section, mine, one, two, three), refs = refs[:5], refs[5:]
+    mod, final_mod, w_final, w_embed, packet = refs[-5:]
+    width, channels = w_embed.shape[1], w_embed.shape[0]
+    if first_tick:
+        hidden, latent = refs[:2]
+    else:
+        hidden, latent = refs[0].at[:, :width], refs[0].at[:, width : width + channels]
     last = mod.shape[1] - 1
     here = section[0]
     total = mine[...] + f32(one[...]) + f32(two[...]) + f32(three[...])
@@ -148,47 +153,23 @@
         normed = layer_norm(f32(result), final_mod[0:1, :], final_mod[1:2, :])
         velocity = dot_rows(normed, w_final[...])
         fresh = (f32(latent[...]) + velocity).astype(jnp.bfloat16)
-        out[...] = dot(fresh, w_embed[...]).astype(jnp.bfloat16)
-        renewed[...] = fresh
+        packet[:, :width] = dot(fresh, w_embed[...]).astype(jnp.bfloat16)
+        packet[:, width : width + channels] = fresh
 
     @pl.when(here != last)
     def _():
-        out[...] = result
-        renewed[...] = latent[...]
-
-
-def finish_packet_kernel(
-    section, mine, one, two, three, packet, mod, final_mod, w_final, w_embed, *outs
-):
-    width, channels = w_embed.shape[1], w_embed.shape[0]
-    views = [packet.at[:, :width], packet.at[:, width : width + channels]]
-    if len(outs) == 1:
-        outs = [outs[0].at[:, :width], outs[0].at[:, width : width + channels]]
-    finish_kernel(
-        section, mine, one, two, three, *views, mod, final_mod, w_final, w_embed, *outs
-    )
-
-
-def finish_first_kernel(
-    section, mine, one, two, three, hidden, latent, mod, final_mod, w_final, w_embed, packet
-):
-    width, channels = w_embed.shape[1], w_embed.shape[0]
-    outs = [packet.at[:, :width], packet.at[:, width : width + channels]]
-    finish_kernel(
-        section, mine, one, two, three, hidden, latent, mod, final_mod, w_final, w_embed, *outs
-    )
-
-
-def finish(section, parts, state, mod, final_mod, w_final, w_embed, packed):
+        packet[:, :width] = result
+        packet[:, width : width + channels] = latent[...]
+
+
+def finish(section, parts, state, mod, final_mod, w_final, w_embed):
     rows, width = parts[0].shape
-    channels = w_embed.shape[0]
-    shapes = [(rows, width + LANES)] if packed else [(rows, width), (rows, channels)]
     args = [*parts, *state, mod, final_mod, w_final, w_embed]
     return pl.pallas_call(
-        finish_packet_kernel if len(state) == 1 else finish_first_kernel,
-        out_shape=like(*[(shape, jnp.bfloat16) for shape in shapes]),
+        functools.partial(finish_kernel, len(state) == 2),
+        out_shape=jax.ShapeDtypeStruct((rows, width + LANES), jnp.bfloat16),
         in_specs=[SCALARS] + [WHOLE] * len(args),
-        out_specs=(WHOLE,) * len(shapes),
+        out_specs=WHOLE,
         compiler_params=params(4),
         name="finish",
     )(section, *args)
@@ -211,6 +192,78 @@
         compiler_params=params(4),
         name="norm",
     )(section, values, mod)
+
+
+def load_kernel(count, *refs):
+    sources, targets, semaphores = refs[:count], refs[count : 2 * count], refs[2 * count :]
+    copies = [pltpu.make_async_copy(*each) for each in zip(sources, targets, semaphores)]
+    for copy in copies:
+        copy.start()
+    for copy in copies:
+        copy.wait()
+
+
+def load(*arrays):
+    count = len(arrays)
+    size = sum(array.size * array.dtype.itemsize for array in arrays)
+    return pl.pallas_call(
+        functools.partial(load_kernel, count),
+        out_shape=tuple(pltpu.VMEM(array.shape, array.dtype) for array in arrays),
+        in_specs=[pl.BlockSpec(memory_space=pltpu.HBM)] * count,
+        out_specs=(WHOLE,) * count,
+        scratch_shapes=[pltpu.SemaphoreType.DMA(())] * count,
+        compiler_params=params(60 - -(-size >> 20)),
+        cost_estimate=pl.CostEstimate(flops=0, bytes_accessed=2 * size, transcendentals=0),
+        name="load",
+    )(*arrays)
+
+
+def first_kernel(section, hidden_in, mod_in, hidden, mod, normed, one, two):
+    copies = [
+        pltpu.make_async_copy(hidden_in, hidden, one),
+        pltpu.make_async_copy(mod_in, mod, two),
+    ]
+    for copy in copies:
+        copy.start()
+    for copy in copies:
+        copy.wait()
+    norm_kernel(section, hidden, mod, normed)
+
+
+def first(section, hidden, mod):
+    far = pl.BlockSpec(memory_space=pltpu.HBM)
+    return pl.pallas_call(
+        first_kernel,
+        out_shape=(
+            VMEM(hidden.shape, hidden.dtype),
+            VMEM(mod.shape, mod.dtype),
+            jax.ShapeDtypeStruct(hidden.shape, jnp.bfloat16),
+        ),
+        in_specs=[SCALARS, far, far],
+        out_specs=(WHOLE,) * 3,
+        scratch_shapes=[pltpu.SemaphoreType.DMA(())] * 2,
+        compiler_params=params(60),
+        name="first",
+    )(section, hidden, mod)
+
+
+def open_kernel(packet, hidden, latent):
+    width = hidden.shape[1]
+    hidden[...] = packet[:, :width]
+    latent[...] = packet[:, width : width + latent.shape[1]]
+
+
+def open_packet(packet, width, channels):
+    return pl.pallas_call(
+        open_kernel,
+        out_shape=like(
+            ((packet.shape[0], width), jnp.bfloat16), ((packet.shape[0], channels), jnp.bfloat16)
+        ),
+        in_specs=[WHOLE],
+        out_specs=(WHOLE,) * 2,
+        compiler_params=params(4),
+        name="open",
+    )(packet)
 
 
 def exchange(value, apart):
@@ -237,26 +290,30 @@
 ):
     size = lax.axis_size("section")
     ticks = patch_flow.shape[0]
-    patch_flow = jnp.transpose(patch_flow)
     section = (lax.axis_index("section") // GROUP).astype(jnp.int32).reshape(1)
-    mod = jnp.transpose(block_mod, (1, 0, 2))
+    width, channels = hidden_in.shape[1], latent_in.shape[1]
     w_final = jnp.transpose(w_final)
-    kv = stale_kv
     onward = [(device, (device + GROUP) % size) for device in range(size)]
 
-    state = (hidden_in, latent_in)
+    hidden, mod, normed = first(section, hidden_in, jnp.transpose(block_mod, (1, 0, 2)))
+    held = (w_qkv, w_out, qk_gain, jnp.transpose(patch_flow), stale_kv)
+    normed, *held = lax.optimization_barrier((normed, *held))
+    held = load(*held)
+    state = (hidden, latent_in)
     for tick in range(ticks):
-        own = gather_chips(norm(section, state[0], mod))
+        if tick > 0:
+            normed = norm(section, state[0], mod)
+        own = gather_chips(normed)
+        if tick == 0:
+            own, w_qkv, w_out, gains, patch_flow, kv = lax.optimization_barrier((own, *held))
         other = exchange(own, 1)
-        kept, sent, kv = block(
-            tick, section, patch_flow, own, other, qk_gain, w_qkv, w_out, kv
-        )
+        kept, sent, kv = block(tick, section, patch_flow, own, other, gains, w_qkv, w_out, kv)
         mine, *blocks = split(kept, exchange(sent, 1))
-        parts = [mine] + [exchange(rows, apart) for rows, apart in zip(blocks, CHIP_STEPS)]
-        packed = tick < ticks - 1
-        state = finish(section, parts, state, mod, final_mod, w_final, w_embed, packed)
-        state = tuple(lax.ppermute(value, "section", onward) for value in state)
-    return state
+        came = [exchange(rows, apart) for rows, apart in zip(blocks, CHIP_STEPS)]
+        parts = [mine] + came[::-1]
+        packet = finish(section, parts, state, mod, final_mod, w_final, w_embed)
+        state = (lax.ppermute(packet, "section", onward),)
+    return open_packet(state[0], width, channels)
 
 
 def solution(mesh):

time: 198 us -> 187 us (0.944)
  local copies, waits for them, and re-layouts: 10.2 us -> 0.03 us
  waiting for transfers between devices: 102 us -> 94.3 us
  Pallas kernels: 20.9 us -> 26.9 us
    unnamed x35 -> x10, local copies, waits for them, and re-layouts: 10.2 us -> 0.03 us
    ppermute x48, waiting for transfers between devices: 73.6 us -> 65.2 us  [exchange(): return lax.ppermute(value, 'section', route)]
    pallas_call x6 -> x9, Pallas kernels: 0.75 us -> 7.12 us  [the longest x1 3.9 us: load(): pl.pallas_call(functools.partial(load_kernel, count), out_shape=tuple((pl...]
    ppermute x7 -> x6, starting transfers between devices: 18 us -> 18.7 us  [body(): state = (lax.ppermute(packet, 'section', onward),)]
    ppermute x7 -> x6, waiting for transfers between devices: 28.7 us -> 29.1 us  [body(): state = (lax.ppermute(packet, 'section', onward),)]
  transfers between devices with their start and end apart: 55 -> 54, of which waited for: 54 -> 52; matrix products, arithmetic and copies ran while one was open for 0% -> 0% of each run, Pallas kernels for 0% -> 2%
where the time goes in v4:
time: 187 us
  waiting for transfers between devices  94.3 us (50%)
  starting transfers between devices  64.1 us (34%)
  Pallas kernels  26.9 us (14%)
    ppermute x48, waiting for transfers between devices, exchange(): return lax.ppermute(value, 'section', route)  65.2 us
    ppermute x48, starting transfers between devices, exchange(): return lax.ppermute(value, 'section', route)  45.4 us
    ppermute x6, waiting for transfers between devices, body(): state = (lax.ppermute(packet, 'section', onward),)  29.1 us
    ppermute x6, starting transfers between devices, body(): state = (lax.ppermute(packet, 'section', onward),)  18.7 us
    pallas_call x6, Pallas kernels, block(): pl.pallas_call(functools.partial(block_kernel, tick), out_shape=like(((ha...  18.1 us
    pallas_call x1, Pallas kernels, load(): pl.pallas_call(functools.partial(load_kernel, count), out_shape=tuple((pl...  3.9 us
  transfers between devices with their start and end apart: 54, of which 52 were waited for; matrix products, arithmetic and copies ran while one was open for 0% of the time, Pallas kernels for 2%

profile of v4, /device:TPU:0, one launch (start us, length us, event | category | flops | bytes accessed | tf_op | source)
XLA Modules:
  0.0 186.5 jit_solution(10158389600878086018)
XLA Ops:
  0.6 1.8 first.1
  2.5 4.1 %collective-permute-start.2 = (bf16[16,3072]{1,0:T(8,128)(2,1)}, bf16[16,3072]{1,0:T(8,128)(2,1)S(1)}, u32[]{:S(2)}, u32[]{:S(2)}) collective-permute-start(bf16[16,3072]{1,0:T(8,128)(2,1)} %get-tuple-element.64), channel_id=1, source_target_pairs={{0,6},{1,7},{2,4},{3,5},{4,2},{5,3},{6,0},{7,1},{8,14},{9,15},{10,... | collective-permute-start | bytes 294920 | tf_op jit(solution)/shard_map/ppermute | solution.py:271
  7.2 3.9 %load.1 = (bf16[3,3072,384]{2,1,0:T(8,128)(2,1)S(1)}, bf16[384,3072]{1,0:T(8,128)(2,1)S(1)}, f32[2,2,128]{2,1,0:T(2,128)S(1)}, s32[2,6]{1,0:T(2,128)S(1)}, bf16[2,256,384]{2,1,0:T(8,128)(2,1)S(1)}) custom-call(bf16[3,3072,384]{2,1,0:T(8,128)(2,1)} %refs_0_, bf16[384,3072]{1,0:T(8,128)(2,1)} %refs_1_, f32[2,2,128]{2,1,0:T(2,128)} %refs_2_, s32[2,6]{1,0:T(2,128)} %bitcast.11, ...), custom_call_target="tpu_custom_call" | custom-call | bytes 19664992 | tf_op jit(solution)/shard_map/load/pallas_call | solution.py:209
  12.0 1.7 collective-permute-done.3.other
  13.8 3.0 %block.6 = (f32[64,3072]{1,0:T(8,128)S(1)}, bf16[64,3072]{1,0:T(8,128)(2,1)S(1)}, bf16[2,256,384]{2,1,0:T(8,128)(2,1)S(1)}) custom-call(s32[1]{0:T(128)} %bitcast.section.refs_0_, s32[2,6]{1,0:T(2,128)S(1)} %get-tuple-element.75.patch_flow, bf16[64,3072]{1,0:T(8,128)(2,1)S(1)} %pad_maximum_fusion.own, ...), custom_call_target="tpu_custom_call", output_to_operand_aliasing={{2}: (7, {})} | custom-call | flops 1207959552 | bytes 9437184 | tf_op jit(solution)/shard_map/block/pallas_call | solution.py:95
  17.0 1.6 collective-permute-done.4.came
  18.7 2.4 %collective-permute-start.5 = (bf16[16,3072]{1,0:T(8,128)(2,1)S(1)}, bf16[16,3072]{1,0:T(8,128)(2,1)S(1)}, u32[]{:S(2)}, u32[]{:S(2)}) collective-permute-start(bf16[16,3072]{1,0:T(8,128)(2,1)S(1)} %get-tuple-element.84), channel_id=1, source_target_pairs={{0,6},{1,7},{2,4},{3,5},{4,2},{5,3},{6,0},{7,1},{8,14},{9,15},{10,... | collective-permute-start | bytes 294920 | tf_op jit(solution)/shard_map/ppermute | solution.py:271
  22.2 2.9 %collective-permute-done.5.refs_2_ = bf16[16,3072]{1,0:T(8,128)(2,1)S(1)} collective-permute-done((bf16[16,3072]{1,0:T(8,128)(2,1)S(1)}, bf16[16,3072]{1,0:T(8,128)(2,1)S(1)}, u32[]{:S(2)}, u32[]{:S(2)}) %collective-permute-start.5) | collective-permute-done | bytes 98336 | tf_op jit(solution)/shard_map/ppermute | solution.py:271
  26.7 3.3 %collective-permute-start.8 = (bf16[16,3200]{1,0:T(8,128)(2,1)S(1)}, bf16[16,3200]{1,0:T(8,128)(2,1)S(1)}, u32[]{:S(2)}, u32[]{:S(2)}) collective-permute-start(bf16[16,3200]{1,0:T(8,128)(2,1)S(1)} %finish.6), channel_id=1, source_target_pairs={{0,8},{1,9},{2,10},{3,11},{4,12},{5,13},{6,14},{7,15},{8,0},{9,1},... | collective-permute-start | bytes 307208 | tf_op jit(solution)/shard_map/ppermute | solution.py:315
  30.0 4.7 %collective-permute-done.8.values.refs_5_ = bf16[16,3200]{1,0:T(8,128)(2,1)S(1)} collective-permute-done((bf16[16,3200]{1,0:T(8,128)(2,1)S(1)}, bf16[16,3200]{1,0:T(8,128)(2,1)S(1)}, u32[]{:S(2)}, u32[]{:S(2)}) %collective-permute-start.8) | collective-permute-done | bytes 102432 | tf_op jit(solution)/shard_map/ppermute | solution.py:315
  34.9 1.8 collective-permute-start.11
  38.4 2.4 %collective-permute-done.11 = bf16[16,3072]{1,0:T(8,128)(2,1)S(1)} collective-permute-done((bf16[16,3072]{1,0:T(8,128)(2,1)S(1)}, bf16[16,3072]{1,0:T(8,128)(2,1)S(1)}, u32[]{:S(2)}, u32[]{:S(2)}) %collective-permute-start.11) | collective-permute-done | bytes 98336 | tf_op jit(solution)/shard_map/ppermute | solution.py:271
  42.7 1.7 collective-permute-done.12.other
  44.5 3.0 %block.7 = (f32[64,3072]{1,0:T(8,128)S(1)}, bf16[64,3072]{1,0:T(8,128)(2,1)S(1)}, bf16[2,256,384]{2,1,0:T(8,128)(2,1)S(1)}) custom-call(s32[1]{0:T(128)} %bitcast.section.refs_0_, s32[2,6]{1,0:T(2,128)S(1)} %get-tuple-element.75.patch_flow, bf16[64,3072]{1,0:T(8,128)(2,1)S(1)} %pad_maximum_fusion.1.own, ...), custom_call_target="tpu_custom_call", output_to_operand_aliasing={{2}: (7, {})} | custom-call | flops 1207959552 | bytes 9437184 | tf_op jit(solution)/shard_map/block/pallas_call | solution.py:95
  49.3 1.8 collective-permute-start.14
  52.9 3.1 %collective-permute-done.14.refs_2_ = bf16[16,3072]{1,0:T(8,128)(2,1)S(1)} collective-permute-done((bf16[16,3072]{1,0:T(8,128)(2,1)S(1)}, bf16[16,3072]{1,0:T(8,128)(2,1)S(1)}, u32[]{:S(2)}, u32[]{:S(2)}) %collective-permute-start.14) | collective-permute-done | bytes 98336 | tf_op jit(solution)/shard_map/ppermute | solution.py:271
  57.4 3.2 %collective-permute-start.17 = (bf16[16,3200]{1,0:T(8,128)(2,1)S(1)}, bf16[16,3200]{1,0:T(8,128)(2,1)S(1)}, u32[]{:S(2)}, u32[]{:S(2)}) collective-permute-start(bf16[16,3200]{1,0:T(8,128)(2,1)S(1)} %finish.7), channel_id=1, source_target_pairs={{0,8},{1,9},{2,10},{3,11},{4,12},{5,13},{6,14},{7,15},{8,0},{9,1},... | collective-permute-start | bytes 307208 | tf_op jit(solution)/shard_map/ppermute | solution.py:315
  60.5 4.9 %collective-permute-done.17.values.refs_5_ = bf16[16,3200]{1,0:T(8,128)(2,1)S(1)} collective-permute-done((bf16[16,3200]{1,0:T(8,128)(2,1)S(1)}, bf16[16,3200]{1,0:T(8,128)(2,1)S(1)}, u32[]{:S(2)}, u32[]{:S(2)}) %collective-permute-start.17) | collective-permute-done | bytes 102432 | tf_op jit(solution)/shard_map/ppermute | solution.py:315
  69.2 2.4 %collective-permute-done.20 = bf16[16,3072]{1,0:T(8,128)(2,1)S(1)} collective-permute-done((bf16[16,3072]{1,0:T(8,128)(2,1)S(1)}, bf16[16,3072]{1,0:T(8,128)(2,1)S(1)}, u32[]{:S(2)}, u32[]{:S(2)}) %collective-permute-start.20) | collective-permute-done | bytes 98336 | tf_op jit(solution)/shard_map/ppermute | solution.py:271
  72.8 1.7 collective-permute-done.21.other
  74.5 3.0 %block.8 = (f32[64,3072]{1,0:T(8,128)S(1)}, bf16[64,3072]{1,0:T(8,128)(2,1)S(1)}, bf16[2,256,384]{2,1,0:T(8,128)(2,1)S(1)}) custom-call(s32[1]{0:T(128)} %bitcast.section.refs_0_, s32[2,6]{1,0:T(2,128)S(1)} %get-tuple-element.75.patch_flow, bf16[64,3072]{1,0:T(8,128)(2,1)S(1)} %pad_maximum_fusion.2.own, ...), custom_call_target="tpu_custom_call", output_to_operand_aliasing={{2}: (7, {})} | custom-call | flops 1207959552 | bytes 9437184 | tf_op jit(solution)/shard_map/block/pallas_call | solution.py:95
  77.7 1.6 collective-permute-done.22.came
  79.3 1.7 collective-permute-start.23
  82.9 3.1 %collective-permute-done.23.refs_2_ = bf16[16,3072]{1,0:T(8,128)(2,1)S(1)} collective-permute-done((bf16[16,3072]{1,0:T(8,128)(2,1)S(1)}, bf16[16,3072]{1,0:T(8,128)(2,1)S(1)}, u32[]{:S(2)}, u32[]{:S(2)}) %collective-permute-start.23) | collective-permute-done | bytes 98336 | tf_op jit(solution)/shard_map/ppermute | solution.py:271
  87.5 3.0 %collective-permute-start.26 = (bf16[16,3200]{1,0:T(8,128)(2,1)S(1)}, bf16[16,3200]{1,0:T(8,128)(2,1)S(1)}, u32[]{:S(2)}, u32[]{:S(2)}) collective-permute-start(bf16[16,3200]{1,0:T(8,128)(2,1)S(1)} %finish.8), channel_id=1, source_target_pairs={{0,8},{1,9},{2,10},{3,11},{4,12},{5,13},{6,14},{7,15},{8,0},{9,1},... | collective-permute-start | bytes 307208 | tf_op jit(solution)/shard_map/ppermute | solution.py:315
  90.6 4.9 %collective-permute-done.26.values.refs_5_ = bf16[16,3200]{1,0:T(8,128)(2,1)S(1)} collective-permute-done((bf16[16,3200]{1,0:T(8,128)(2,1)S(1)}, bf16[16,3200]{1,0:T(8,128)(2,1)S(1)}, u32[]{:S(2)}, u32[]{:S(2)}) %collective-permute-start.26) | collective-permute-done | bytes 102432 | tf_op jit(solution)/shard_map/ppermute | solution.py:315
  99.3 2.4 %collective-permute-done.29 = bf16[16,3072]{1,0:T(8,128)(2,1)S(1)} collective-permute-done((bf16[16,3072]{1,0:T(8,128)(2,1)S(1)}, bf16[16,3072]{1,0:T(8,128)(2,1)S(1)}, u32[]{:S(2)}, u32[]{:S(2)}) %collective-permute-start.29) | collective-permute-done | bytes 98336 | tf_op jit(solution)/shard_map/ppermute | solution.py:271
  103.1 1.7 collective-permute-done.30.other
  104.8 3.0 %block.9 = (f32[64,3072]{1,0:T(8,128)S(1)}, bf16[64,3072]{1,0:T(8,128)(2,1)S(1)}, bf16[2,256,384]{2,1,0:T(8,128)(2,1)S(1)}) custom-call(s32[1]{0:T(128)} %bitcast.section.refs_0_, s32[2,6]{1,0:T(2,128)S(1)} %get-tuple-element.75.patch_flow, bf16[64,3072]{1,0:T(8,128)(2,1)S(1)} %pad_maximum_fusion.3.own, ...), custom_call_target="tpu_custom_call", output_to_operand_aliasing={{2}: (7, {})} | custom-call | flops 1207959552 | bytes 9437184 | tf_op jit(solution)/shard_map/block/pallas_call | solution.py:95
  109.7 1.8 collective-permute-start.32
  113.3 3.1 %collective-permute-done.32.refs_2_ = bf16[16,3072]{1,0:T(8,128)(2,1)S(1)} collective-permute-done((bf16[16,3072]{1,0:T(8,128)(2,1)S(1)}, bf16[16,3072]{1,0:T(8,128)(2,1)S(1)}, u32[]{:S(2)}, u32[]{:S(2)}) %collective-permute-start.32) | collective-permute-done | bytes 98336 | tf_op jit(solution)/shard_map/ppermute | solution.py:271
  117.7 3.1 %collective-permute-start.35 = (bf16[16,3200]{1,0:T(8,128)(2,1)S(1)}, bf16[16,3200]{1,0:T(8,128)(2,1)S(1)}, u32[]{:S(2)}, u32[]{:S(2)}) collective-permute-start(bf16[16,3200]{1,0:T(8,128)(2,1)S(1)} %finish.9), channel_id=1, source_target_pairs={{0,8},{1,9},{2,10},{3,11},{4,12},{5,13},{6,14},{7,15},{8,0},{9,1},... | collective-permute-start | bytes 307208 | tf_op jit(solution)/shard_map/ppermute | solution.py:315
  120.8 4.9 %collective-permute-done.35.values.refs_5_ = bf16[16,3200]{1,0:T(8,128)(2,1)S(1)} collective-permute-done((bf16[16,3200]{1,0:T(8,128)(2,1)S(1)}, bf16[16,3200]{1,0:T(8,128)(2,1)S(1)}, u32[]{:S(2)}, u32[]{:S(2)}) %collective-permute-start.35) | collective-permute-done | bytes 102432 | tf_op jit(solution)/shard_map/ppermute | solution.py:315
  129.5 2.4 %collective-permute-done.38 = bf16[16,3072]{1,0:T(8,128)(2,1)S(1)} collective-permute-done((bf16[16,3072]{1,0:T(8,128)(2,1)S(1)}, bf16[16,3072]{1,0:T(8,128)(2,1)S(1)}, u32[]{:S(2)}, u32[]{:S(2)}) %collective-permute-start.38) | collective-permute-done | bytes 98336 | tf_op jit(solution)/shard_map/ppermute | solution.py:271
  133.1 1.7 collective-permute-done.39.other
  134.8 3.0 %block.10 = (f32[64,3072]{1,0:T(8,128)S(1)}, bf16[64,3072]{1,0:T(8,128)(2,1)S(1)}, bf16[2,256,384]{2,1,0:T(8,128)(2,1)S(1)}) custom-call(s32[1]{0:T(128)} %bitcast.section.refs_0_, s32[2,6]{1,0:T(2,128)S(1)} %get-tuple-element.75.patch_flow, bf16[64,3072]{1,0:T(8,128)(2,1)S(1)} %pad_maximum_fusion.4.own, ...), custom_call_target="tpu_custom_call", output_to_operand_aliasing={{2}: (7, {})} | custom-call | flops 1207959552 | bytes 9437184 | tf_op jit(solution)/shard_map/block/pallas_call | solution.py:95
  138.0 1.6 collective-permute-done.40.came
  139.7 1.8 collective-permute-start.41
  143.3 3.1 %collective-permute-done.41.refs_2_ = bf16[16,3072]{1,0:T(8,128)(2,1)S(1)} collective-permute-done((bf16[16,3072]{1,0:T(8,128)(2,1)S(1)}, bf16[16,3072]{1,0:T(8,128)(2,1)S(1)}, u32[]{:S(2)}, u32[]{:S(2)}) %collective-permute-start.41) | collective-permute-done | bytes 98336 | tf_op jit(solution)/shard_map/ppermute | solution.py:271
  147.7 3.1 %collective-permute-start.44 = (bf16[16,3200]{1,0:T(8,128)(2,1)S(1)}, bf16[16,3200]{1,0:T(8,128)(2,1)S(1)}, u32[]{:S(2)}, u32[]{:S(2)}) collective-permute-start(bf16[16,3200]{1,0:T(8,128)(2,1)S(1)} %finish.10), channel_id=1, source_target_pairs={{0,8},{1,9},{2,10},{3,11},{4,12},{5,13},{6,14},{7,15},{8,0},{9,1},... | collective-permute-start | bytes 307208 | tf_op jit(solution)/shard_map/ppermute | solution.py:315
  150.8 4.9 %collective-permute-done.44.values.refs_5_ = bf16[16,3200]{1,0:T(8,128)(2,1)S(1)} collective-permute-done((bf16[16,3200]{1,0:T(8,128)(2,1)S(1)}, bf16[16,3200]{1,0:T(8,128)(2,1)S(1)}, u32[]{:S(2)}, u32[]{:S(2)}) %collective-permute-start.44) | collective-permute-done | bytes 102432 | tf_op jit(solution)/shard_map/ppermute | solution.py:315
  159.5 2.4 %collective-permute-done.47 = bf16[16,3072]{1,0:T(8,128)(2,1)S(1)} collective-permute-done((bf16[16,3072]{1,0:T(8,128)(2,1)S(1)}, bf16[16,3072]{1,0:T(8,128)(2,1)S(1)}, u32[]{:S(2)}, u32[]{:S(2)}) %collective-permute-start.47) | collective-permute-done | bytes 98336 | tf_op jit(solution)/shard_map/ppermute | solution.py:271
  163.3 1.7 collective-permute-done.48.other
  165.0 3.0 %block.11 = (f32[64,3072]{1,0:T(8,128)S(1)}, bf16[64,3072]{1,0:T(8,128)(2,1)S(1)}, bf16[2,256,384]{2,1,0:T(8,128)(2,1)S(1)}) custom-call(s32[1]{0:T(128)} %bitcast.section.refs_0_, s32[2,6]{1,0:T(2,128)S(1)} %get-tuple-element.75.patch_flow, bf16[64,3072]{1,0:T(8,128)(2,1)S(1)} %pad_maximum_fusion.5.own, ...), custom_call_target="tpu_custom_call", output_to_operand_aliasing={{2}: (7, {})} | custom-call | flops 1207959552 | bytes 9437184 | tf_op jit(solution)/shard_map/block/pallas_call | solution.py:95
  169.9 1.7 collective-permute-start.50
  173.4 3.1 %collective-permute-done.50.refs_2_ = bf16[16,3072]{1,0:T(8,128)(2,1)S(1)} collective-permute-done((bf16[16,3072]{1,0:T(8,128)(2,1)S(1)}, bf16[16,3072]{1,0:T(8,128)(2,1)S(1)}, u32[]{:S(2)}, u32[]{:S(2)}) %collective-permute-start.50) | collective-permute-done | bytes 98336 | tf_op jit(solution)/shard_map/ppermute | solution.py:271
  177.9 3.1 %collective-permute-start.53 = (bf16[16,3200]{1,0:T(8,128)(2,1)S(1)}, bf16[16,3200]{1,0:T(8,128)(2,1)S(1)}, u32[]{:S(2)}, u32[]{:S(2)}) collective-permute-start(bf16[16,3200]{1,0:T(8,128)(2,1)S(1)} %finish.11), channel_id=1, source_target_pairs={{0,8},{1,9},{2,10},{3,11},{4,12},{5,13},{6,14},{7,15},{8,0},{9,1},... | collective-permute-start | bytes 307208 | tf_op jit(solution)/shard_map/ppermute | solution.py:315
  181.0 4.9 %collective-permute-done.53.packet = bf16[16,3200]{1,0:T(8,128)(2,1)S(1)} collective-permute-done((bf16[16,3200]{1,0:T(8,128)(2,1)S(1)}, bf16[16,3200]{1,0:T(8,128)(2,1)S(1)}, u32[]{:S(2)}, u32[]{:S(2)}) %collective-permute-start.53) | collective-permute-done | bytes 102432 | tf_op jit(solution)/shard_map/ppermute | solution.py:315
  (102 shorter events, 51.4 us)
Async XLA Ops:
  2.5 8.7 %collective-permute-start.2 = (bf16[16,3072]{1,0:T(8,128)(2,1)}, bf16[16,3072]{1,0:T(8,128)(2,1)S(1)}, u32[]{:S(2)}, u32[]{:S(2)}) collective-permute-start(bf16[16,3072]{1,0:T(8,128)(2,1)} %get-tuple-element.64), channel_id=1, source_target_pairs={{0,6},{1,7},{2,4},{3,5},{4,2},{5,3},{6,0},{7,1},{8,14},{9,15},{10,... | collective-permute-start | bytes 294920 | tf_op jit(solution)/shard_map/ppermute | solution.py:271
  6.6 5.4 %collective-permute-start.1 = (bf16[16,3072]{1,0:T(8,128)(2,1)}, bf16[16,3072]{1,0:T(8,128)(2,1)S(1)}, u32[]{:S(2)}, u32[]{:S(2)}) collective-permute-start(bf16[16,3072]{1,0:T(8,128)(2,1)} %get-tuple-element.64), channel_id=1, source_target_pairs={{0,4},{1,5},{2,6},{3,7},{4,0},{5,1},{6,2},{7,3},{8,12},{9,13},{10,... | collective-permute-start | bytes 294920 | tf_op jit(solution)/shard_map/ppermute | solution.py:271
  7.0 4.9 %collective-permute-start = (bf16[16,3072]{1,0:T(8,128)(2,1)}, bf16[16,3072]{1,0:T(8,128)(2,1)S(1)}, u32[]{:S(2)}, u32[]{:S(2)}) collective-permute-start(bf16[16,3072]{1,0:T(8,128)(2,1)} %get-tuple-element.64), channel_id=1, source_target_pairs={{0,2},{1,3},{2,0},{3,1},{4,6},{5,7},{6,4},{7,5},{8,10},{9,11},{10,... | collective-permute-start | bytes 294920 | tf_op jit(solution)/shard_map/ppermute | solution.py:271
  12.0 1.8 collective-permute-start.3
  16.8 1.8 collective-permute-start.4
  18.7 6.5 %collective-permute-start.5 = (bf16[16,3072]{1,0:T(8,128)(2,1)S(1)}, bf16[16,3072]{1,0:T(8,128)(2,1)S(1)}, u32[]{:S(2)}, u32[]{:S(2)}) collective-permute-start(bf16[16,3072]{1,0:T(8,128)(2,1)S(1)} %get-tuple-element.84), channel_id=1, source_target_pairs={{0,6},{1,7},{2,4},{3,5},{4,2},{5,3},{6,0},{7,1},{8,14},{9,15},{10,... | collective-permute-start | bytes 294920 | tf_op jit(solution)/shard_map/ppermute | solution.py:271
  21.1 5.4 %collective-permute-start.6 = (bf16[16,3072]{1,0:T(8,128)(2,1)S(1)}, bf16[16,3072]{1,0:T(8,128)(2,1)S(1)}, u32[]{:S(2)}, u32[]{:S(2)}) collective-permute-start(bf16[16,3072]{1,0:T(8,128)(2,1)S(1)} %get-tuple-element.85), channel_id=1, source_target_pairs={{0,4},{1,5},{2,6},{3,7},{4,0},{5,1},{6,2},{7,3},{8,12},{9,13},{10,... | collective-permute-start | bytes 294920 | tf_op jit(solution)/shard_map/ppermute | solution.py:271
  21.5 5.0 %collective-permute-start.7 = (bf16[16,3072]{1,0:T(8,128)(2,1)S(1)}, bf16[16,3072]{1,0:T(8,128)(2,1)S(1)}, u32[]{:S(2)}, u32[]{:S(2)}) collective-permute-start(bf16[16,3072]{1,0:T(8,128)(2,1)S(1)} %get-tuple-element.86), channel_id=1, source_target_pairs={{0,2},{1,3},{2,0},{3,1},{4,6},{5,7},{6,4},{7,5},{8,10},{9,11},{10,... | collective-permute-start | bytes 294920 | tf_op jit(solution)/shard_map/ppermute | solution.py:271
  26.7 7.9 %collective-permute-start.8 = (bf16[16,3200]{1,0:T(8,128)(2,1)S(1)}, bf16[16,3200]{1,0:T(8,128)(2,1)S(1)}, u32[]{:S(2)}, u32[]{:S(2)}) collective-permute-start(bf16[16,3200]{1,0:T(8,128)(2,1)S(1)} %finish.6), channel_id=1, source_target_pairs={{0,8},{1,9},{2,10},{3,11},{4,12},{5,13},{6,14},{7,15},{8,0},{9,1},... | collective-permute-start | bytes 307208 | tf_op jit(solution)/shard_map/ppermute | solution.py:315
  34.9 5.9 %collective-permute-start.11 = (bf16[16,3072]{1,0:T(8,128)(2,1)S(1)}, bf16[16,3072]{1,0:T(8,128)(2,1)S(1)}, u32[]{:S(2)}, u32[]{:S(2)}) collective-permute-start(bf16[16,3072]{1,0:T(8,128)(2,1)S(1)} %norm.5), channel_id=1, source_target_pairs={{0,6},{1,7},{2,4},{3,5},{4,2},{5,3},{6,0},{7,1},{8,14},{9,15},{10,... | collective-permute-start | bytes 294920 | tf_op jit(solution)/shard_map/ppermute | solution.py:271
  36.7 5.4 %collective-permute-start.10 = (bf16[16,3072]{1,0:T(8,128)(2,1)S(1)}, bf16[16,3072]{1,0:T(8,128)(2,1)S(1)}, u32[]{:S(2)}, u32[]{:S(2)}) collective-permute-start(bf16[16,3072]{1,0:T(8,128)(2,1)S(1)} %norm.5), channel_id=1, source_target_pairs={{0,4},{1,5},{2,6},{3,7},{4,0},{5,1},{6,2},{7,3},{8,12},{9,13},{10,... | collective-permute-start | bytes 294920 | tf_op jit(solution)/shard_map/ppermute | solution.py:271
  38.0 4.6 %collective-permute-start.9 = (bf16[16,3072]{1,0:T(8,128)(2,1)S(1)}, bf16[16,3072]{1,0:T(8,128)(2,1)S(1)}, u32[]{:S(2)}, u32[]{:S(2)}) collective-permute-start(bf16[16,3072]{1,0:T(8,128)(2,1)S(1)} %norm.5), channel_id=1, source_target_pairs={{0,2},{1,3},{2,0},{3,1},{4,6},{5,7},{6,4},{7,5},{8,10},{9,11},{10,... | collective-permute-start | bytes 294920 | tf_op jit(solution)/shard_map/ppermute | solution.py:271
  42.7 1.8 collective-permute-start.12
  47.5 1.8 collective-permute-start.13
  49.3 6.6 %collective-permute-start.14 = (bf16[16,3072]{1,0:T(8,128)(2,1)S(1)}, bf16[16,3072]{1,0:T(8,128)(2,1)S(1)}, u32[]{:S(2)}, u32[]{:S(2)}) collective-permute-start(bf16[16,3072]{1,0:T(8,128)(2,1)S(1)} %get-tuple-element.93), channel_id=1, source_target_pairs={{0,6},{1,7},{2,4},{3,5},{4,2},{5,3},{6,0},{7,1},{8,14},{9,15},{10,... | collective-permute-start | bytes 294920 | tf_op jit(solution)/shard_map/ppermute | solution.py:271
  51.2 5.6 %collective-permute-start.15 = (bf16[16,3072]{1,0:T(8,128)(2,1)S(1)}, bf16[16,3072]{1,0:T(8,128)(2,1)S(1)}, u32[]{:S(2)}, u32[]{:S(2)}) collective-permute-start(bf16[16,3072]{1,0:T(8,128)(2,1)S(1)} %get-tuple-element.94), channel_id=1, source_target_pairs={{0,4},{1,5},{2,6},{3,7},{4,0},{5,1},{6,2},{7,3},{8,12},{9,13},{10,... | collective-permute-start | bytes 294920 | tf_op jit(solution)/shard_map/ppermute | solution.py:271
  51.8 5.4 %collective-permute-start.16 = (bf16[16,3072]{1,0:T(8,128)(2,1)S(1)}, bf16[16,3072]{1,0:T(8,128)(2,1)S(1)}, u32[]{:S(2)}, u32[]{:S(2)}) collective-permute-start(bf16[16,3072]{1,0:T(8,128)(2,1)S(1)} %get-tuple-element.95), channel_id=1, source_target_pairs={{0,2},{1,3},{2,0},{3,1},{4,6},{5,7},{6,4},{7,5},{8,10},{9,11},{10,... | collective-permute-start | bytes 294920 | tf_op jit(solution)/shard_map/ppermute | solution.py:271
  57.4 8.0 %collective-permute-start.17 = (bf16[16,3200]{1,0:T(8,128)(2,1)S(1)}, bf16[16,3200]{1,0:T(8,128)(2,1)S(1)}, u32[]{:S(2)}, u32[]{:S(2)}) collective-permute-start(bf16[16,3200]{1,0:T(8,128)(2,1)S(1)} %finish.7), channel_id=1, source_target_pairs={{0,8},{1,9},{2,10},{3,11},{4,12},{5,13},{6,14},{7,15},{8,0},{9,1},... | collective-permute-start | bytes 307208 | tf_op jit(solution)/shard_map/ppermute | solution.py:315
  65.6 6.0 %collective-permute-start.20 = (bf16[16,3072]{1,0:T(8,128)(2,1)S(1)}, bf16[16,3072]{1,0:T(8,128)(2,1)S(1)}, u32[]{:S(2)}, u32[]{:S(2)}) collective-permute-start(bf16[16,3072]{1,0:T(8,128)(2,1)S(1)} %norm.6), channel_id=1, source_target_pairs={{0,6},{1,7},{2,4},{3,5},{4,2},{5,3},{6,0},{7,1},{8,14},{9,15},{10,... | collective-permute-start | bytes 294920 | tf_op jit(solution)/shard_map/ppermute | solution.py:271
  66.6 5.3 %collective-permute-start.19 = (bf16[16,3072]{1,0:T(8,128)(2,1)S(1)}, bf16[16,3072]{1,0:T(8,128)(2,1)S(1)}, u32[]{:S(2)}, u32[]{:S(2)}) collective-permute-start(bf16[16,3072]{1,0:T(8,128)(2,1)S(1)} %norm.6), channel_id=1, source_target_pairs={{0,4},{1,5},{2,6},{3,7},{4,0},{5,1},{6,2},{7,3},{8,12},{9,13},{10,... | collective-permute-start | bytes 294920 | tf_op jit(solution)/shard_map/ppermute | solution.py:271
  67.9 4.7 %collective-permute-start.18 = (bf16[16,3072]{1,0:T(8,128)(2,1)S(1)}, bf16[16,3072]{1,0:T(8,128)(2,1)S(1)}, u32[]{:S(2)}, u32[]{:S(2)}) collective-permute-start(bf16[16,3072]{1,0:T(8,128)(2,1)S(1)} %norm.6), channel_id=1, source_target_pairs={{0,2},{1,3},{2,0},{3,1},{4,6},{5,7},{6,4},{7,5},{8,10},{9,11},{10,... | collective-permute-start | bytes 294920 | tf_op jit(solution)/shard_map/ppermute | solution.py:271
  72.7 1.8 collective-permute-start.21
  77.5 1.8 collective-permute-start.22
  79.3 6.6 %collective-permute-start.23 = (bf16[16,3072]{1,0:T(8,128)(2,1)S(1)}, bf16[16,3072]{1,0:T(8,128)(2,1)S(1)}, u32[]{:S(2)}, u32[]{:S(2)}) collective-permute-start(bf16[16,3072]{1,0:T(8,128)(2,1)S(1)} %get-tuple-element.100), channel_id=1, source_target_pairs={{0,6},{1,7},{2,4},{3,5},{4,2},{5,3},{6,0},{7,1},{8,14},{9,15},{10,... | collective-permute-start | bytes 294920 | tf_op jit(solution)/shard_map/ppermute | solution.py:271
  81.1 5.9 %collective-permute-start.24 = (bf16[16,3072]{1,0:T(8,128)(2,1)S(1)}, bf16[16,3072]{1,0:T(8,128)(2,1)S(1)}, u32[]{:S(2)}, u32[]{:S(2)}) collective-permute-start(bf16[16,3072]{1,0:T(8,128)(2,1)S(1)} %get-tuple-element.101), channel_id=1, source_target_pairs={{0,4},{1,5},{2,6},{3,7},{4,0},{5,1},{6,2},{7,3},{8,12},{9,13},{10,... | collective-permute-start | bytes 294920 | tf_op jit(solution)/shard_map/ppermute | solution.py:271
  82.0 5.2 %collective-permute-start.25 = (bf16[16,3072]{1,0:T(8,128)(2,1)S(1)}, bf16[16,3072]{1,0:T(8,128)(2,1)S(1)}, u32[]{:S(2)}, u32[]{:S(2)}) collective-permute-start(bf16[16,3072]{1,0:T(8,128)(2,1)S(1)} %get-tuple-element.102), channel_id=1, source_target_pairs={{0,2},{1,3},{2,0},{3,1},{4,6},{5,7},{6,4},{7,5},{8,10},{9,11},{10,... | collective-permute-start | bytes 294920 | tf_op jit(solution)/shard_map/ppermute | solution.py:271
  87.5 7.9 %collective-permute-start.26 = (bf16[16,3200]{1,0:T(8,128)(2,1)S(1)}, bf16[16,3200]{1,0:T(8,128)(2,1)S(1)}, u32[]{:S(2)}, u32[]{:S(2)}) collective-permute-start(bf16[16,3200]{1,0:T(8,128)(2,1)S(1)} %finish.8), channel_id=1, source_target_pairs={{0,8},{1,9},{2,10},{3,11},{4,12},{5,13},{6,14},{7,15},{8,0},{9,1},... | collective-permute-start | bytes 307208 | tf_op jit(solution)/shard_map/ppermute | solution.py:315
  95.7 6.0 %collective-permute-start.29 = (bf16[16,3072]{1,0:T(8,128)(2,1)S(1)}, bf16[16,3072]{1,0:T(8,128)(2,1)S(1)}, u32[]{:S(2)}, u32[]{:S(2)}) collective-permute-start(bf16[16,3072]{1,0:T(8,128)(2,1)S(1)} %norm.7), channel_id=1, source_target_pairs={{0,6},{1,7},{2,4},{3,5},{4,2},{5,3},{6,0},{7,1},{8,14},{9,15},{10,... | collective-permute-start | bytes 294920 | tf_op jit(solution)/shard_map/ppermute | solution.py:271
  97.1 5.4 %collective-permute-start.28 = (bf16[16,3072]{1,0:T(8,128)(2,1)S(1)}, bf16[16,3072]{1,0:T(8,128)(2,1)S(1)}, u32[]{:S(2)}, u32[]{:S(2)}) collective-permute-start(bf16[16,3072]{1,0:T(8,128)(2,1)S(1)} %norm.7), channel_id=1, source_target_pairs={{0,4},{1,5},{2,6},{3,7},{4,0},{5,1},{6,2},{7,3},{8,12},{9,13},{10,... | collective-permute-start | bytes 294920 | tf_op jit(solution)/shard_map/ppermute | solution.py:271
  98.4 4.6 %collective-permute-start.27 = (bf16[16,3072]{1,0:T(8,128)(2,1)S(1)}, bf16[16,3072]{1,0:T(8,128)(2,1)S(1)}, u32[]{:S(2)}, u32[]{:S(2)}) collective-permute-start(bf16[16,3072]{1,0:T(8,128)(2,1)S(1)} %norm.7), channel_id=1, source_target_pairs={{0,2},{1,3},{2,0},{3,1},{4,6},{5,7},{6,4},{7,5},{8,10},{9,11},{10,... | collective-permute-start | bytes 294920 | tf_op jit(solution)/shard_map/ppermute | solution.py:271
  109.7 6.6 %collective-permute-start.32 = (bf16[16,3072]{1,0:T(8,128)(2,1)S(1)}, bf16[16,3072]{1,0:T(8,128)(2,1)S(1)}, u32[]{:S(2)}, u32[]{:S(2)}) collective-permute-start(bf16[16,3072]{1,0:T(8,128)(2,1)S(1)} %get-tuple-element.107), channel_id=1, source_target_pairs={{0,6},{1,7},{2,4},{3,5},{4,2},{5,3},{6,0},{7,1},{8,14},{9,15},{10,... | collective-permute-start | bytes 294920 | tf_op jit(solution)/shard_map/ppermute | solution.py:271
  111.5 5.6 %collective-permute-start.33 = (bf16[16,3072]{1,0:T(8,128)(2,1)S(1)}, bf16[16,3072]{1,0:T(8,128)(2,1)S(1)}, u32[]{:S(2)}, u32[]{:S(2)}) collective-permute-start(bf16[16,3072]{1,0:T(8,128)(2,1)S(1)} %get-tuple-element.108), channel_id=1, source_target_pairs={{0,4},{1,5},{2,6},{3,7},{4,0},{5,1},{6,2},{7,3},{8,12},{9,13},{10,... | collective-permute-start | bytes 294920 | tf_op jit(solution)/shard_map/ppermute | solution.py:271
  112.2 5.5 %collective-permute-start.34 = (bf16[16,3072]{1,0:T(8,128)(2,1)S(1)}, bf16[16,3072]{1,0:T(8,128)(2,1)S(1)}, u32[]{:S(2)}, u32[]{:S(2)}) collective-permute-start(bf16[16,3072]{1,0:T(8,128)(2,1)S(1)} %get-tuple-element.109), channel_id=1, source_target_pairs={{0,2},{1,3},{2,0},{3,1},{4,6},{5,7},{6,4},{7,5},{8,10},{9,11},{10,... | collective-permute-start | bytes 294920 | tf_op jit(solution)/shard_map/ppermute | solution.py:271
  117.7 8.0 %collective-permute-start.35 = (bf16[16,3200]{1,0:T(8,128)(2,1)S(1)}, bf16[16,3200]{1,0:T(8,128)(2,1)S(1)}, u32[]{:S(2)}, u32[]{:S(2)}) collective-permute-start(bf16[16,3200]{1,0:T(8,128)(2,1)S(1)} %finish.9), channel_id=1, source_target_pairs={{0,8},{1,9},{2,10},{3,11},{4,12},{5,13},{6,14},{7,15},{8,0},{9,1},... | collective-permute-start | bytes 307208 | tf_op jit(solution)/shard_map/ppermute | solution.py:315
  125.9 6.0 %collective-permute-start.38 = (bf16[16,3072]{1,0:T(8,128)(2,1)S(1)}, bf16[16,3072]{1,0:T(8,128)(2,1)S(1)}, u32[]{:S(2)}, u32[]{:S(2)}) collective-permute-start(bf16[16,3072]{1,0:T(8,128)(2,1)S(1)} %norm.8), channel_id=1, source_target_pairs={{0,6},{1,7},{2,4},{3,5},{4,2},{5,3},{6,0},{7,1},{8,14},{9,15},{10,... | collective-permute-start | bytes 294920 | tf_op jit(solution)/shard_map/ppermute | solution.py:271
  127.1 5.4 %collective-permute-start.37 = (bf16[16,3072]{1,0:T(8,128)(2,1)S(1)}, bf16[16,3072]{1,0:T(8,128)(2,1)S(1)}, u32[]{:S(2)}, u32[]{:S(2)}) collective-permute-start(bf16[16,3072]{1,0:T(8,128)(2,1)S(1)} %norm.8), channel_id=1, source_target_pairs={{0,4},{1,5},{2,6},{3,7},{4,0},{5,1},{6,2},{7,3},{8,12},{9,13},{10,... | collective-permute-start | bytes 294920 | tf_op jit(solution)/shard_map/ppermute | solution.py:271
  128.4 4.6 %collective-permute-start.36 = (bf16[16,3072]{1,0:T(8,128)(2,1)S(1)}, bf16[16,3072]{1,0:T(8,128)(2,1)S(1)}, u32[]{:S(2)}, u32[]{:S(2)}) collective-permute-start(bf16[16,3072]{1,0:T(8,128)(2,1)S(1)} %norm.8), channel_id=1, source_target_pairs={{0,2},{1,3},{2,0},{3,1},{4,6},{5,7},{6,4},{7,5},{8,10},{9,11},{10,... | collective-permute-start | bytes 294920 | tf_op jit(solution)/shard_map/ppermute | solution.py:271
  139.7 6.6 %collective-permute-start.41 = (bf16[16,3072]{1,0:T(8,128)(2,1)S(1)}, bf16[16,3072]{1,0:T(8,128)(2,1)S(1)}, u32[]{:S(2)}, u32[]{:S(2)}) collective-permute-start(bf16[16,3072]{1,0:T(8,128)(2,1)S(1)} %get-tuple-element.114), channel_id=1, source_target_pairs={{0,6},{1,7},{2,4},{3,5},{4,2},{5,3},{6,0},{7,1},{8,14},{9,15},{10,... | collective-permute-start | bytes 294920 | tf_op jit(solution)/shard_map/ppermute | solution.py:271
  141.5 5.8 %collective-permute-start.42 = (bf16[16,3072]{1,0:T(8,128)(2,1)S(1)}, bf16[16,3072]{1,0:T(8,128)(2,1)S(1)}, u32[]{:S(2)}, u32[]{:S(2)}) collective-permute-start(bf16[16,3072]{1,0:T(8,128)(2,1)S(1)} %get-tuple-element.115), channel_id=1, source_target_pairs={{0,4},{1,5},{2,6},{3,7},{4,0},{5,1},{6,2},{7,3},{8,12},{9,13},{10,... | collective-permute-start | bytes 294920 | tf_op jit(solution)/shard_map/ppermute | solution.py:271
  142.3 5.3 %collective-permute-start.43 = (bf16[16,3072]{1,0:T(8,128)(2,1)S(1)}, bf16[16,3072]{1,0:T(8,128)(2,1)S(1)}, u32[]{:S(2)}, u32[]{:S(2)}) collective-permute-start(bf16[16,3072]{1,0:T(8,128)(2,1)S(1)} %get-tuple-element.116), channel_id=1, source_target_pairs={{0,2},{1,3},{2,0},{3,1},{4,6},{5,7},{6,4},{7,5},{8,10},{9,11},{10,... | collective-permute-start | bytes 294920 | tf_op jit(solution)/shard_map/ppermute | solution.py:271
  147.7 8.0 %collective-permute-start.44 = (bf16[16,3200]{1,0:T(8,128)(2,1)S(1)}, bf16[16,3200]{1,0:T(8,128)(2,1)S(1)}, u32[]{:S(2)}, u32[]{:S(2)}) collective-permute-start(bf16[16,3200]{1,0:T(8,128)(2,1)S(1)} %finish.10), channel_id=1, source_target_pairs={{0,8},{1,9},{2,10},{3,11},{4,12},{5,13},{6,14},{7,15},{8,0},{9,1},... | collective-permute-start | bytes 307208 | tf_op jit(solution)/shard_map/ppermute | solution.py:315
  156.0 6.0 %collective-permute-start.47 = (bf16[16,3072]{1,0:T(8,128)(2,1)S(1)}, bf16[16,3072]{1,0:T(8,128)(2,1)S(1)}, u32[]{:S(2)}, u32[]{:S(2)}) collective-permute-start(bf16[16,3072]{1,0:T(8,128)(2,1)S(1)} %norm.9), channel_id=1, source_target_pairs={{0,6},{1,7},{2,4},{3,5},{4,2},{5,3},{6,0},{7,1},{8,14},{9,15},{10,... | collective-permute-start | bytes 294920 | tf_op jit(solution)/shard_map/ppermute | solution.py:271
  157.3 5.4 %collective-permute-start.46 = (bf16[16,3072]{1,0:T(8,128)(2,1)S(1)}, bf16[16,3072]{1,0:T(8,128)(2,1)S(1)}, u32[]{:S(2)}, u32[]{:S(2)}) collective-permute-start(bf16[16,3072]{1,0:T(8,128)(2,1)S(1)} %norm.9), channel_id=1, source_target_pairs={{0,4},{1,5},{2,6},{3,7},{4,0},{5,1},{6,2},{7,3},{8,12},{9,13},{10,... | collective-permute-start | bytes 294920 | tf_op jit(solution)/shard_map/ppermute | solution.py:271
  158.6 4.6 %collective-permute-start.45 = (bf16[16,3072]{1,0:T(8,128)(2,1)S(1)}, bf16[16,3072]{1,0:T(8,128)(2,1)S(1)}, u32[]{:S(2)}, u32[]{:S(2)}) collective-permute-start(bf16[16,3072]{1,0:T(8,128)(2,1)S(1)} %norm.9), channel_id=1, source_target_pairs={{0,2},{1,3},{2,0},{3,1},{4,6},{5,7},{6,4},{7,5},{8,10},{9,11},{10,... | collective-permute-start | bytes 294920 | tf_op jit(solution)/shard_map/ppermute | solution.py:271
  169.9 6.6 %collective-permute-start.50 = (bf16[16,3072]{1,0:T(8,128)(2,1)S(1)}, bf16[16,3072]{1,0:T(8,128)(2,1)S(1)}, u32[]{:S(2)}, u32[]{:S(2)}) collective-permute-start(bf16[16,3072]{1,0:T(8,128)(2,1)S(1)} %get-tuple-element.121), channel_id=1, source_target_pairs={{0,6},{1,7},{2,4},{3,5},{4,2},{5,3},{6,0},{7,1},{8,14},{9,15},{10,... | collective-permute-start | bytes 294920 | tf_op jit(solution)/shard_map/ppermute | solution.py:271
  171.6 5.7 %collective-permute-start.51 = (bf16[16,3072]{1,0:T(8,128)(2,1)S(1)}, bf16[16,3072]{1,0:T(8,128)(2,1)S(1)}, u32[]{:S(2)}, u32[]{:S(2)}) collective-permute-start(bf16[16,3072]{1,0:T(8,128)(2,1)S(1)} %get-tuple-element.122), channel_id=1, source_target_pairs={{0,4},{1,5},{2,6},{3,7},{4,0},{5,1},{6,2},{7,3},{8,12},{9,13},{10,... | collective-permute-start | bytes 294920 | tf_op jit(solution)/shard_map/ppermute | solution.py:271
  172.4 5.4 %collective-permute-start.52 = (bf16[16,3072]{1,0:T(8,128)(2,1)S(1)}, bf16[16,3072]{1,0:T(8,128)(2,1)S(1)}, u32[]{:S(2)}, u32[]{:S(2)}) collective-permute-start(bf16[16,3072]{1,0:T(8,128)(2,1)S(1)} %get-tuple-element.123), channel_id=1, source_target_pairs={{0,2},{1,3},{2,0},{3,1},{4,6},{5,7},{6,4},{7,5},{8,10},{9,11},{10,... | collective-permute-start | bytes 294920 | tf_op jit(solution)/shard_map/ppermute | solution.py:271
  177.9 8.0 %collective-permute-start.53 = (bf16[16,3200]{1,0:T(8,128)(2,1)S(1)}, bf16[16,3200]{1,0:T(8,128)(2,1)S(1)}, u32[]{:S(2)}, u32[]{:S(2)}) collective-permute-start(bf16[16,3200]{1,0:T(8,128)(2,1)S(1)} %finish.11), channel_id=1, source_target_pairs={{0,8},{1,9},{2,10},{3,11},{4,12},{5,13},{6,14},{7,15},{8,0},{9,1},... | collective-permute-start | bytes 307208 | tf_op jit(solution)/shard_map/ppermute | solution.py:315
  (11 other events, 81.9 us)

commit v5 on v4

--- a/solution.py
+++ b/solution.py
@@ -56,24 +56,28 @@
 
 
 def block_kernel(
-    tick, section, patch_flow, own, other, gains, w_qkv, w_out, kv_in, kept, sent, kv, normed, mixed
+    tick, section, patch_flow, *refs
 ):
-    half, width = own.shape
+    pieces, refs = refs[: 2 * CHIPS], refs[2 * CHIPS :]
+    gains, w_qkv, w_out, kv_in, kept, sent, ahead, kv, normed, mixed = refs
+    part_rows, width = pieces[0].shape
+    half = CHIPS * part_rows
     rows = 2 * half
     heads = w_out.shape[0] // HS
     here = section[0]
-    normed[:half, :] = own[...]
-    normed[half:, :] = other[...]
+    for place, piece in enumerate(pieces):
+        normed[place * part_rows : (place + 1) * part_rows, :] = piece[...]
     start = pl.multiple_of(patch_flow[here, tick] * rows, rows)
     kv[...] = kv_in[...]
     gain = gains[here]
     tokens = normed[...]
-    keys = dot(tokens, w_qkv[1])
+    columns = w_out.shape[0]
+    products = dot(tokens, w_qkv[...])
+    queries, keys = products[:, :columns], products[:, columns : 2 * columns]
     for head in range(heads):
         part = slice(head * HS, (head + 1) * HS)
         kv[0, pl.ds(start, rows), part] = head_norm(keys[:, part], gain[1:2, :])
-    kv[1, pl.ds(start, rows), :] = dot(tokens, w_qkv[2]).astype(jnp.bfloat16)
-    queries = dot(tokens, w_qkv[0])
+    kv[1, pl.ds(start, rows), :] = products[:, 2 * columns :].astype(jnp.bfloat16)
     for head in range(heads):
         part = slice(head * HS, (head + 1) * HS)
         query = head_norm(queries[:, part], gain[0:1, :])
@@ -83,27 +87,32 @@
         mixed[:, part] = (attended / totals).astype(jnp.bfloat16)
     tile = width // 4
     heads_out = mixed[...]
+    edge = rows - half // CHIPS
     for low in range(0, width, tile):
         projected = dot(heads_out, w_out[:, low : low + tile])
         kept[:, low : low + tile] = projected[:half, :]
-        sent[:, low : low + tile] = projected[half:, :].astype(jnp.bfloat16)
-
-
-def block(tick, section, patch_flow, own, other, gains, w_qkv, w_out, kv):
-    half, width = own.shape
+        sent[:, low : low + tile] = projected[half:edge, :].astype(jnp.bfloat16)
+        ahead[:, low : low + tile] = projected[edge:, :].astype(jnp.bfloat16)
+
+
+def block(tick, section, patch_flow, pieces, gains, w_qkv, w_out, kv):
+    half, width = CHIPS * pieces[0].shape[0], pieces[0].shape[1]
     columns = w_out.shape[0]
     return pl.pallas_call(
         functools.partial(block_kernel, tick),
         out_shape=like(
-            ((half, width), jnp.float32), ((half, width), jnp.bfloat16), (kv.shape, jnp.bfloat16)
+            ((half, width), jnp.float32),
+            ((half - half // CHIPS, width), jnp.bfloat16),
+            ((half // CHIPS, width), jnp.bfloat16),
+            (kv.shape, jnp.bfloat16),
         ),
-        in_specs=[SCALARS] * 2 + [WHOLE] * 6,
-        out_specs=(WHOLE,) * 3,
+        in_specs=[SCALARS] * 2 + [WHOLE] * (4 + 2 * CHIPS),
+        out_specs=(WHOLE,) * 4,
         scratch_shapes=[
             VMEM((2 * half, width), jnp.bfloat16),
             VMEM((2 * half, columns), jnp.bfloat16),
         ],
-        input_output_aliases={7: 2},
+        input_output_aliases={5 + 2 * CHIPS: 3},
         compiler_params=params(8),
         cost_estimate=pl.CostEstimate(
             flops=16 * half * columns * width,
@@ -111,7 +120,23 @@
             transcendentals=0,
         ),
         name="block",
-    )(section, patch_flow, own, other, gains, w_qkv, w_out, kv)
+    )(section, patch_flow, *pieces, gains, w_qkv, w_out, kv)
+
+
+def split_last_kernel(kept, came, out):
+    rows = out.shape[0]
+    out[...] = (kept[-rows:, :] + f32(came[...])).astype(jnp.bfloat16)
+
+
+def split_last(kept, came):
+    return pl.pallas_call(
+        split_last_kernel,
+        out_shape=jax.ShapeDtypeStruct(came.shape, jnp.bfloat16),
+        in_specs=[WHOLE] * 2,
+        out_specs=WHOLE,
+        compiler_params=params(4),
+        name="split_last",
+    )(kept, came)
 
 
 def split_kernel(kept, came, mine, *others):
@@ -126,9 +151,9 @@
     shape = (kept.shape[0] // CHIPS, kept.shape[1])
     return pl.pallas_call(
         split_kernel,
-        out_shape=like((shape, jnp.float32), *[(shape, jnp.bfloat16)] * (CHIPS - 1)),
+        out_shape=like((shape, jnp.float32), *[(shape, jnp.bfloat16)] * (CHIPS - 2)),
         in_specs=[WHOLE] * 2,
-        out_specs=(WHOLE,) * CHIPS,
+        out_specs=(WHOLE,) * (CHIPS - 1),
         compiler_params=params(4),
         name="split",
     )(kept, came)
@@ -138,10 +163,9 @@
     (section, mine, one, two, three), refs = refs[:5], refs[5:]
     mod, final_mod, w_final, w_embed, packet = refs[-5:]
     width, channels = w_embed.shape[1], w_embed.shape[0]
-    if first_tick:
-        hidden, latent = refs[:2]
-    else:
-        hidden, latent = refs[0].at[:, :width], refs[0].at[:, width : width + channels]
+    hidden, latent = refs[:2]
+    if not first_tick:
+        latent = latent.at[:, width : width + channels]
     last = mod.shape[1] - 1
     here = section[0]
     total = mine[...] + f32(one[...]) + f32(two[...]) + f32(three[...])
@@ -153,7 +177,6 @@
         normed = layer_norm(f32(result), final_mod[0:1, :], final_mod[1:2, :])
         velocity = dot_rows(normed, w_final[...])
         fresh = (f32(latent[...]) + velocity).astype(jnp.bfloat16)
-        packet[:, :width] = dot(fresh, w_embed[...]).astype(jnp.bfloat16)
         packet[:, width : width + channels] = fresh
 
     @pl.when(here != last)
@@ -166,7 +189,7 @@
     rows, width = parts[0].shape
     args = [*parts, *state, mod, final_mod, w_final, w_embed]
     return pl.pallas_call(
-        functools.partial(finish_kernel, len(state) == 2),
+        functools.partial(finish_kernel, state[1].shape[1] == w_embed.shape[0]),
         out_shape=jax.ShapeDtypeStruct((rows, width + LANES), jnp.bfloat16),
         in_specs=[SCALARS] + [WHOLE] * len(args),
         out_specs=WHOLE,
@@ -175,28 +198,54 @@
     )(section, *args)
 
 
-def norm_kernel(section, values, mod, normed):
+def norm_here(section, tokens, mod):
     here = section[0]
-    tokens = f32(values[:, : normed.shape[1]])
-    normed[...] = layer_norm(
-        tokens, mod[0, pl.ds(here, 1), :], mod[1, pl.ds(here, 1), :]
-    )
-
-
-def norm(section, values, mod):
+    return layer_norm(tokens, mod[0, pl.ds(here, 1), :], mod[1, pl.ds(here, 1), :])
+
+
+def arrive(section, packet, w_embed, hidden):
+    width, channels = w_embed.shape[1], w_embed.shape[0]
+
+    @pl.when(section[0] == 0)
+    def _():
+        latent = packet[:, width : width + channels]
+        hidden[...] = dot(latent, w_embed[...]).astype(jnp.bfloat16)
+
+    @pl.when(section[0] != 0)
+    def _():
+        hidden[...] = packet[:, :width]
+
+
+def norm_kernel(section, packet, mod, w_embed, hidden, normed):
+    arrive(section, packet, w_embed, hidden)
+    normed[...] = norm_here(section, f32(hidden[...]), mod)
+
+
+def norm(section, packet, mod, w_embed):
+    shape = ((packet.shape[0], mod.shape[2]), jnp.bfloat16)
     return pl.pallas_call(
         norm_kernel,
-        out_shape=jax.ShapeDtypeStruct((values.shape[0], mod.shape[2]), jnp.bfloat16),
-        in_specs=[SCALARS] + [WHOLE] * 2,
-        out_specs=WHOLE,
+        out_shape=like(shape, shape),
+        in_specs=[SCALARS] + [WHOLE] * 3,
+        out_specs=(WHOLE,) * 2,
         compiler_params=params(4),
         name="norm",
-    )(section, values, mod)
+    )(section, packet, mod, w_embed)
 
 
 def load_kernel(count, *refs):
     sources, targets, semaphores = refs[:count], refs[count : 2 * count], refs[2 * count :]
-    copies = [pltpu.make_async_copy(*each) for each in zip(sources, targets, semaphores)]
+    parts, _, columns = sources[0].shape
+    copies = [
+        pltpu.make_async_copy(
+            sources[0].at[part],
+            targets[0].at[:, part * columns : (part + 1) * columns],
+            semaphores[count + part],
+        )
+        for part in range(parts)
+    ]
+    rest = zip(sources[1:], targets[1:], semaphores[1:count])
+    copies += [pltpu.make_async_copy(*each) for each in rest]
     for copy in copies:
         copy.start()
     for copy in copies:
@@ -205,13 +254,15 @@
 
 def load(*arrays):
     count = len(arrays)
+    parts, depth, columns = arrays[0].shape
+    shapes = [(depth, parts * columns)] + [array.shape for array in arrays[1:]]
     size = sum(array.size * array.dtype.itemsize for array in arrays)
     return pl.pallas_call(
         functools.partial(load_kernel, count),
-        out_shape=tuple(pltpu.VMEM(array.shape, array.dtype) for array in arrays),
+        out_shape=tuple(VMEM(shape, array.dtype) for shape, array in zip(shapes, arrays)),
         in_specs=[pl.BlockSpec(memory_space=pltpu.HBM)] * count,
         out_specs=(WHOLE,) * count,
-        scratch_shapes=[pltpu.SemaphoreType.DMA(())] * count,
+        scratch_shapes=[pltpu.SemaphoreType.DMA(())] * (count + parts),
         compiler_params=params(60 - -(-size >> 20)),
         cost_estimate=pl.CostEstimate(flops=0, bytes_accessed=2 * size, transcendentals=0),
         name="load",
@@ -227,7 +278,7 @@
         copy.start()
     for copy in copies:
         copy.wait()
-    norm_kernel(section, hidden, mod, normed)
+    normed[...] = norm_here(section, f32(hidden[...]), mod)
 
 
 def first(section, hidden, mod):
@@ -247,23 +298,24 @@
     )(section, hidden, mod)
 
 
-def open_kernel(packet, hidden, latent):
+def open_kernel(section, packet, w_embed, hidden, latent):
     width = hidden.shape[1]
-    hidden[...] = packet[:, :width]
+    arrive(section, packet, w_embed, hidden)
     latent[...] = packet[:, width : width + latent.shape[1]]
 
 
-def open_packet(packet, width, channels):
+def open_packet(section, packet, w_embed):
+    channels, width = w_embed.shape
     return pl.pallas_call(
         open_kernel,
         out_shape=like(
             ((packet.shape[0], width), jnp.bfloat16), ((packet.shape[0], channels), jnp.bfloat16)
         ),
-        in_specs=[WHOLE],
+        in_specs=[SCALARS] + [WHOLE] * 2,
         out_specs=(WHOLE,) * 2,
         compiler_params=params(4),
         name="open",
-    )(packet)
+    )(section, packet, w_embed)
 
 
 def exchange(value, apart):
@@ -272,7 +324,7 @@
 
 
 def gather_chips(rows):
-    return jnp.concatenate([rows] + [exchange(rows, apart) for apart in CHIP_STEPS], 0)
+    return [rows] + [exchange(rows, apart) for apart in CHIP_STEPS]
 
 
 def body(
@@ -291,7 +343,6 @@
     size = lax.axis_size("section")
     ticks = patch_flow.shape[0]
     section = (lax.axis_index("section") // GROUP).astype(jnp.int32).reshape(1)
-    width, channels = hidden_in.shape[1], latent_in.shape[1]
     w_final = jnp.transpose(w_final)
     onward = [(device, (device + GROUP) % size) for device in range(size)]
 
@@ -302,18 +353,20 @@
     state = (hidden, latent_in)
     for tick in range(ticks):
         if tick > 0:
-            normed = norm(section, state[0], mod)
+            hidden, normed = norm(section, packet, mod, w_embed)
+            state = (hidden, packet)
         own = gather_chips(normed)
         if tick == 0:
             own, w_qkv, w_out, gains, patch_flow, kv = lax.optimization_barrier((own, *held))
-        other = exchange(own, 1)
-        kept, sent, kv = block(tick, section, patch_flow, own, other, gains, w_qkv, w_out, kv)
+        pieces = own + [exchange(piece, 1) for piece in own]
+        kept, sent, ahead, kv = block(tick, section, patch_flow, pieces, gains, w_qkv, w_out, kv)
+        ahead = split_last(kept, exchange(ahead, 1))
         mine, *blocks = split(kept, exchange(sent, 1))
-        came = [exchange(rows, apart) for rows, apart in zip(blocks, CHIP_STEPS)]
+        came = [exchange(rows, apart) for rows, apart in zip([*blocks, ahead], CHIP_STEPS)]
         parts = [mine] + came[::-1]
         packet = finish(section, parts, state, mod, final_mod, w_final, w_embed)
-        state = (lax.ppermute(packet, "section", onward),)
-    return open_packet(state[0], width, channels)
+        packet = lax.ppermute(packet, "section", onward)
+    return open_packet(section, packet, w_embed)
 
 
 def solution(mesh):

time: 187 us -> 182 us (0.973)
  waiting for transfers between devices: 94.3 us -> 90 us
    ppermute x48 -> x72, waiting for transfers between devices: 65.2 us -> 59.3 us  [exchange(): return lax.ppermute(value, 'section', route)]
    ppermute x6, starting transfers between devices: 18.7 us -> 15.1 us  [body(): packet = lax.ppermute(packet, 'section', onward)]
    ppermute x48 -> x72, starting transfers between devices: 45.4 us -> 49.1 us  [exchange(): return lax.ppermute(value, 'section', route)]
    pallas_call x12 -> x18, Pallas kernels: 5.84 us -> 6.85 us  [the longest x1 3.92 us: load(): pl.pallas_call(functools.partial(load_kernel, count), out_shape=tuple((VM...]
  transfers between devices with their start and end apart: 54 -> 78, of which waited for: 52 -> 61; matrix products, arithmetic and copies ran while one was open for 0% -> 0% of each run, Pallas kernels for 2% -> 2%
where the time goes in v5:
time: 182 us
  waiting for transfers between devices  90 us (49%)
  starting transfers between devices  64.1 us (35%)
  Pallas kernels  26.6 us (15%)
    ppermute x72, waiting for transfers between devices, exchange(): return lax.ppermute(value, 'section', route)  59.3 us
    ppermute x72, starting transfers between devices, exchange(): return lax.ppermute(value, 'section', route)  49.1 us
    ppermute x6, waiting for transfers between devices, body(): packet = lax.ppermute(packet, 'section', onward)  30.8 us
    pallas_call x6, Pallas kernels, block(): pl.pallas_call(functools.partial(block_kernel, tick), out_shape=like(((ha...  16.7 us
    ppermute x6, starting transfers between devices, body(): packet = lax.ppermute(packet, 'section', onward)  15.1 us
    pallas_call x1, Pallas kernels, load(): pl.pallas_call(functools.partial(load_kernel, count), out_shape=tuple((VM...  3.92 us
  transfers between devices with their start and end apart: 78, of which 61 were waited for; matrix products, arithmetic and copies ran while one was open for 0% of the time, Pallas kernels for 2%

profile of v5, /device:TPU:0, one launch (start us, length us, event | category | flops | bytes accessed | tf_op | source)
XLA Modules:
  0.0 181.7 jit_solution(14296929243016564340)
XLA Ops:
  0.6 1.8 %first.1 = (bf16[16,3072]{1,0:T(8,128)(2,1)S(1)}, f32[3,2,3072]{2,1,0:T(2,128)S(1)}, bf16[16,3072]{1,0:T(8,128)(2,1)}) custom-call(s32[1]{0:T(128)} %bitcast.section.refs_0_, bf16[16,3072]{1,0:T(8,128)(2,1)} %hidden_in.1, f32[3,2,3072]{2,1,0:T(2,128)} %bitcast.10), custom_call_target="tpu_custom_call" | custom-call | tf_op jit(solution)/shard_map/first/pallas_call | solution.py:286
  2.5 4.1 %collective-permute-start.2 = (bf16[16,3072]{1,0:T(8,128)(2,1)}, bf16[16,3072]{1,0:T(8,128)(2,1)S(1)}, u32[]{:S(2)}, u32[]{:S(2)}) collective-permute-start(bf16[16,3072]{1,0:T(8,128)(2,1)} %get-tuple-element.89.refs_0_), channel_id=1, source_target_pairs={{0,6},{1,7},{2,4},{3,5},{4,2},{5,3},{6,0},{7,1},{8,14},{9,15},{10,... | collective-permute-start | bytes 294920 | tf_op jit(solution)/shard_map/ppermute | solution.py:323
  7.2 3.9 %load.1 = (bf16[3072,1152]{1,0:T(8,128)(2,1)S(1)}, bf16[384,3072]{1,0:T(8,128)(2,1)S(1)}, f32[2,2,128]{2,1,0:T(2,128)S(1)}, s32[2,6]{1,0:T(2,128)S(1)}, bf16[2,256,384]{2,1,0:T(8,128)(2,1)S(1)}) custom-call(bf16[3,3072,384]{2,1,0:T(8,128)(2,1)} %refs_0_, bf16[384,3072]{1,0:T(8,128)(2,1)} %refs_1_, f32[2,2,128]{2,1,0:T(2,128)} %refs_2_, s32[2,6]{1,0:T(2,128)} %bitcast.11, ...), custom_call_target="tpu_custom_call" | custom-call | bytes 19664992 | tf_op jit(solution)/shard_map/load/pallas_call | solution.py:260
  13.9 2.8 %block.6 = (f32[64,3072]{1,0:T(8,128)S(1)}, bf16[48,3072]{1,0:T(8,128)(2,1)S(1)}, bf16[16,3072]{1,0:T(8,128)(2,1)S(1)}, bf16[2,256,384]{2,1,0:T(8,128)(2,1)S(1)}) custom-call(s32[1]{0:T(128)} %bitcast.section.refs_0_, s32[2,6]{1,0:T(2,128)S(1)} %get-tuple-element.88.patch_flow, bf16[16,3072]{1,0:T(8,128)(2,1)S(1)} %copy-done.3, ...), custom_call_target="tpu_custom_call", output_to_operand_aliasing={{3}: (13, {})} | custom-call | flops 1207959552 | bytes 9437184 | tf_op jit(solution)/shard_map/block/pallas_call | solution.py:101
  17.3 1.2 collective-permute-done.8.came
  18.5 2.4 %collective-permute-start.9 = (bf16[16,3072]{1,0:T(8,128)(2,1)S(1)}, bf16[16,3072]{1,0:T(8,128)(2,1)S(1)}, u32[]{:S(2)}, u32[]{:S(2)}) collective-permute-start(bf16[16,3072]{1,0:T(8,128)(2,1)S(1)} %split_last.6), channel_id=1, source_target_pairs={{0,6},{1,7},{2,4},{3,5},{4,2},{5,3},{6,0},{7,1},{8,14},{9,15},{10,... | collective-permute-start | bytes 294920 | tf_op jit(solution)/shard_map/ppermute | solution.py:323
  22.2 2.9 %collective-permute-done.9.refs_2_ = bf16[16,3072]{1,0:T(8,128)(2,1)S(1)} collective-permute-done((bf16[16,3072]{1,0:T(8,128)(2,1)S(1)}, bf16[16,3072]{1,0:T(8,128)(2,1)S(1)}, u32[]{:S(2)}, u32[]{:S(2)}) %collective-permute-start.9) | collective-permute-done | bytes 98336 | tf_op jit(solution)/shard_map/ppermute | solution.py:323
  25.1 1.5 collective-permute-done.10.refs_3_
  26.8 3.1 %collective-permute-start.12 = (bf16[16,3200]{1,0:T(8,128)(2,1)S(1)}, bf16[16,3200]{1,0:T(8,128)(2,1)S(1)}, u32[]{:S(2)}, u32[]{:S(2)}) collective-permute-start(bf16[16,3200]{1,0:T(8,128)(2,1)S(1)} %finish.6), channel_id=1, source_target_pairs={{0,8},{1,9},{2,10},{3,11},{4,12},{5,13},{6,14},{7,15},{8,0},{9,1},... | collective-permute-start | bytes 307208 | tf_op jit(solution)/shard_map/ppermute | solution.py:368
  29.8 4.8 %collective-permute-done.12.packet.refs_6_ = bf16[16,3200]{1,0:T(8,128)(2,1)S(1)} collective-permute-done((bf16[16,3200]{1,0:T(8,128)(2,1)S(1)}, bf16[16,3200]{1,0:T(8,128)(2,1)S(1)}, u32[]{:S(2)}, u32[]{:S(2)}) %collective-permute-start.12) | collective-permute-done | bytes 102432 | tf_op jit(solution)/shard_map/ppermute | solution.py:368
  35.1 1.8 collective-permute-start.15
  36.9 1.3 collective-permute-start.14
  38.7 2.4 %collective-permute-done.15.refs_3_ = bf16[16,3072]{1,0:T(8,128)(2,1)S(1)} collective-permute-done((bf16[16,3072]{1,0:T(8,128)(2,1)S(1)}, bf16[16,3072]{1,0:T(8,128)(2,1)S(1)}, u32[]{:S(2)}, u32[]{:S(2)}) %collective-permute-start.15) | collective-permute-done | bytes 98336 | tf_op jit(solution)/shard_map/ppermute | solution.py:323
  41.1 1.3 collective-permute-done.14.refs_2_
  44.1 2.8 %block.7 = (f32[64,3072]{1,0:T(8,128)S(1)}, bf16[48,3072]{1,0:T(8,128)(2,1)S(1)}, bf16[16,3072]{1,0:T(8,128)(2,1)S(1)}, bf16[2,256,384]{2,1,0:T(8,128)(2,1)S(1)}) custom-call(s32[1]{0:T(128)} %bitcast.section.refs_0_, s32[2,6]{1,0:T(2,128)S(1)} %get-tuple-element.88.patch_flow, ...), custom_call_target="tpu_custom_call", output_to_operand_aliasing={{3}: (13, {})} | custom-call | flops 1207959552 | bytes 9437184 | tf_op jit(solution)/shard_map/block/pallas_call | solution.py:101
  48.7 1.9 %collective-permute-start.22 = (bf16[16,3072]{1,0:T(8,128)(2,1)S(1)}, bf16[16,3072]{1,0:T(8,128)(2,1)S(1)}, u32[]{:S(2)}, u32[]{:S(2)}) collective-permute-start(bf16[16,3072]{1,0:T(8,128)(2,1)S(1)} %split_last.7), channel_id=1, source_target_pairs={{0,6},{1,7},{2,4},{3,5},{4,2},{5,3},{6,0},{7,1},{8,14},{9,15},{10,... | collective-permute-start | bytes 294920 | tf_op jit(solution)/shard_map/ppermute | solution.py:323
  52.4 2.9 %collective-permute-done.22.refs_2_ = bf16[16,3072]{1,0:T(8,128)(2,1)S(1)} collective-permute-done((bf16[16,3072]{1,0:T(8,128)(2,1)S(1)}, bf16[16,3072]{1,0:T(8,128)(2,1)S(1)}, u32[]{:S(2)}, u32[]{:S(2)}) %collective-permute-start.22) | collective-permute-done | bytes 98336 | tf_op jit(solution)/shard_map/ppermute | solution.py:323
  56.8 2.8 %collective-permute-start.25 = (bf16[16,3200]{1,0:T(8,128)(2,1)S(1)}, bf16[16,3200]{1,0:T(8,128)(2,1)S(1)}, u32[]{:S(2)}, u32[]{:S(2)}) collective-permute-start(bf16[16,3200]{1,0:T(8,128)(2,1)S(1)} %finish.7), channel_id=1, source_target_pairs={{0,8},{1,9},{2,10},{3,11},{4,12},{5,13},{6,14},{7,15},{8,0},{9,1},... | collective-permute-start | bytes 307208 | tf_op jit(solution)/shard_map/ppermute | solution.py:368
  59.6 5.0 %collective-permute-done.25.packet.refs_6_ = bf16[16,3200]{1,0:T(8,128)(2,1)S(1)} collective-permute-done((bf16[16,3200]{1,0:T(8,128)(2,1)S(1)}, bf16[16,3200]{1,0:T(8,128)(2,1)S(1)}, u32[]{:S(2)}, u32[]{:S(2)}) %collective-permute-start.25) | collective-permute-done | bytes 102432 | tf_op jit(solution)/shard_map/ppermute | solution.py:368
  66.0 1.5 collective-permute-start.27
  68.6 2.0 %collective-permute-done.28.refs_3_ = bf16[16,3072]{1,0:T(8,128)(2,1)S(1)} collective-permute-done((bf16[16,3072]{1,0:T(8,128)(2,1)S(1)}, bf16[16,3072]{1,0:T(8,128)(2,1)S(1)}, u32[]{:S(2)}, u32[]{:S(2)}) %collective-permute-start.28) | collective-permute-done | bytes 98336 | tf_op jit(solution)/shard_map/ppermute | solution.py:323
  73.4 2.8 %block.8 = (f32[64,3072]{1,0:T(8,128)S(1)}, bf16[48,3072]{1,0:T(8,128)(2,1)S(1)}, bf16[16,3072]{1,0:T(8,128)(2,1)S(1)}, bf16[2,256,384]{2,1,0:T(8,128)(2,1)S(1)}) custom-call(s32[1]{0:T(128)} %bitcast.section.refs_0_, s32[2,6]{1,0:T(2,128)S(1)} %get-tuple-element.88.patch_flow, ...), custom_call_target="tpu_custom_call", output_to_operand_aliasing={{3}: (13, {})} | custom-call | flops 1207959552 | bytes 9437184 | tf_op jit(solution)/shard_map/block/pallas_call | solution.py:101
  78.0 1.4 collective-permute-start.35
  81.7 2.9 %collective-permute-done.35.refs_2_ = bf16[16,3072]{1,0:T(8,128)(2,1)S(1)} collective-permute-done((bf16[16,3072]{1,0:T(8,128)(2,1)S(1)}, bf16[16,3072]{1,0:T(8,128)(2,1)S(1)}, u32[]{:S(2)}, u32[]{:S(2)}) %collective-permute-start.35) | collective-permute-done | bytes 98336 | tf_op jit(solution)/shard_map/ppermute | solution.py:323
  86.1 2.5 %collective-permute-start.38 = (bf16[16,3200]{1,0:T(8,128)(2,1)S(1)}, bf16[16,3200]{1,0:T(8,128)(2,1)S(1)}, u32[]{:S(2)}, u32[]{:S(2)}) collective-permute-start(bf16[16,3200]{1,0:T(8,128)(2,1)S(1)} %finish.8), channel_id=1, source_target_pairs={{0,8},{1,9},{2,10},{3,11},{4,12},{5,13},{6,14},{7,15},{8,0},{9,1},... | collective-permute-start | bytes 307208 | tf_op jit(solution)/shard_map/ppermute | solution.py:368
  88.6 5.1 %collective-permute-done.38.packet.refs_6_ = bf16[16,3200]{1,0:T(8,128)(2,1)S(1)} collective-permute-done((bf16[16,3200]{1,0:T(8,128)(2,1)S(1)}, bf16[16,3200]{1,0:T(8,128)(2,1)S(1)}, u32[]{:S(2)}, u32[]{:S(2)}) %collective-permute-start.38) | collective-permute-done | bytes 102432 | tf_op jit(solution)/shard_map/ppermute | solution.py:368
  95.1 1.8 collective-permute-start.40
  97.8 2.0 %collective-permute-done.41.refs_3_ = bf16[16,3072]{1,0:T(8,128)(2,1)S(1)} collective-permute-done((bf16[16,3072]{1,0:T(8,128)(2,1)S(1)}, bf16[16,3072]{1,0:T(8,128)(2,1)S(1)}, u32[]{:S(2)}, u32[]{:S(2)}) %collective-permute-start.41) | collective-permute-done | bytes 98336 | tf_op jit(solution)/shard_map/ppermute | solution.py:323
  102.8 2.8 %block.9 = (f32[64,3072]{1,0:T(8,128)S(1)}, bf16[48,3072]{1,0:T(8,128)(2,1)S(1)}, bf16[16,3072]{1,0:T(8,128)(2,1)S(1)}, bf16[2,256,384]{2,1,0:T(8,128)(2,1)S(1)}) custom-call(s32[1]{0:T(128)} %bitcast.section.refs_0_, s32[2,6]{1,0:T(2,128)S(1)} %get-tuple-element.88.patch_flow, ...), custom_call_target="tpu_custom_call", output_to_operand_aliasing={{3}: (13, {})} | custom-call | flops 1207959552 | bytes 9437184 | tf_op jit(solution)/shard_map/block/pallas_call | solution.py:101
  108.6 1.4 collective-permute-start.49
  111.1 2.9 %collective-permute-done.48.refs_2_ = bf16[16,3072]{1,0:T(8,128)(2,1)S(1)} collective-permute-done((bf16[16,3072]{1,0:T(8,128)(2,1)S(1)}, bf16[16,3072]{1,0:T(8,128)(2,1)S(1)}, u32[]{:S(2)}, u32[]{:S(2)}) %collective-permute-start.48) | collective-permute-done | bytes 98336 | tf_op jit(solution)/shard_map/ppermute | solution.py:323
  115.4 2.1 %collective-permute-start.51 = (bf16[16,3200]{1,0:T(8,128)(2,1)S(1)}, bf16[16,3200]{1,0:T(8,128)(2,1)S(1)}, u32[]{:S(2)}, u32[]{:S(2)}) collective-permute-start(bf16[16,3200]{1,0:T(8,128)(2,1)S(1)} %finish.9), channel_id=1, source_target_pairs={{0,8},{1,9},{2,10},{3,11},{4,12},{5,13},{6,14},{7,15},{8,0},{9,1},... | collective-permute-start | bytes 307208 | tf_op jit(solution)/shard_map/ppermute | solution.py:368
  117.5 5.4 %collective-permute-done.51.packet.refs_6_ = bf16[16,3200]{1,0:T(8,128)(2,1)S(1)} collective-permute-done((bf16[16,3200]{1,0:T(8,128)(2,1)S(1)}, bf16[16,3200]{1,0:T(8,128)(2,1)S(1)}, u32[]{:S(2)}, u32[]{:S(2)}) %collective-permute-start.51) | collective-permute-done | bytes 102432 | tf_op jit(solution)/shard_map/ppermute | solution.py:368
  124.0 1.7 collective-permute-start.53
  126.9 2.3 %collective-permute-done.54.refs_3_ = bf16[16,3072]{1,0:T(8,128)(2,1)S(1)} collective-permute-done((bf16[16,3072]{1,0:T(8,128)(2,1)S(1)}, bf16[16,3072]{1,0:T(8,128)(2,1)S(1)}, u32[]{:S(2)}, u32[]{:S(2)}) %collective-permute-start.54) | collective-permute-done | bytes 98336 | tf_op jit(solution)/shard_map/ppermute | solution.py:323
  131.6 2.8 %block.10 = (f32[64,3072]{1,0:T(8,128)S(1)}, bf16[48,3072]{1,0:T(8,128)(2,1)S(1)}, bf16[16,3072]{1,0:T(8,128)(2,1)S(1)}, bf16[2,256,384]{2,1,0:T(8,128)(2,1)S(1)}) custom-call(s32[1]{0:T(128)} %bitcast.section.refs_0_, s32[2,6]{1,0:T(2,128)S(1)} %get-tuple-element.88.patch_flow, ...), custom_call_target="tpu_custom_call", output_to_operand_aliasing={{3}: (13, {})} | custom-call | flops 1207959552 | bytes 9437184 | tf_op jit(solution)/shard_map/block/pallas_call | solution.py:101
  136.2 1.3 collective-permute-start.61
  137.6 1.4 collective-permute-start.62
  139.9 2.9 %collective-permute-done.61.refs_2_ = bf16[16,3072]{1,0:T(8,128)(2,1)S(1)} collective-permute-done((bf16[16,3072]{1,0:T(8,128)(2,1)S(1)}, bf16[16,3072]{1,0:T(8,128)(2,1)S(1)}, u32[]{:S(2)}, u32[]{:S(2)}) %collective-permute-start.61) | collective-permute-done | bytes 98336 | tf_op jit(solution)/shard_map/ppermute | solution.py:323
  144.2 2.4 %collective-permute-start.64 = (bf16[16,3200]{1,0:T(8,128)(2,1)S(1)}, bf16[16,3200]{1,0:T(8,128)(2,1)S(1)}, u32[]{:S(2)}, u32[]{:S(2)}) collective-permute-start(bf16[16,3200]{1,0:T(8,128)(2,1)S(1)} %finish.10), channel_id=1, source_target_pairs={{0,8},{1,9},{2,10},{3,11},{4,12},{5,13},{6,14},{7,15},{8,0},{9,1},... | collective-permute-start | bytes 307208 | tf_op jit(solution)/shard_map/ppermute | solution.py:368
  146.6 5.1 %collective-permute-done.64.packet.refs_6_ = bf16[16,3200]{1,0:T(8,128)(2,1)S(1)} collective-permute-done((bf16[16,3200]{1,0:T(8,128)(2,1)S(1)}, bf16[16,3200]{1,0:T(8,128)(2,1)S(1)}, u32[]{:S(2)}, u32[]{:S(2)}) %collective-permute-start.64) | collective-permute-done | bytes 102432 | tf_op jit(solution)/shard_map/ppermute | solution.py:368
  153.0 1.9 %collective-permute-start.66 = (bf16[16,3072]{1,0:T(8,128)(2,1)S(1)}, bf16[16,3072]{1,0:T(8,128)(2,1)S(1)}, u32[]{:S(2)}, u32[]{:S(2)}) collective-permute-start(bf16[16,3072]{1,0:T(8,128)(2,1)S(1)} %get-tuple-element.141.refs_0_), channel_id=1, source_target_pairs={{0,4},{1,5},{2,6},{3,7},{4,0},{5,1},{6,2},{7,3},{8,12},{9,13},{10,... | collective-permute-start | bytes 294920 | tf_op jit(solution)/shard_map/ppermute | solution.py:323
  155.7 2.1 %collective-permute-done.67.refs_3_ = bf16[16,3072]{1,0:T(8,128)(2,1)S(1)} collective-permute-done((bf16[16,3072]{1,0:T(8,128)(2,1)S(1)}, bf16[16,3072]{1,0:T(8,128)(2,1)S(1)}, u32[]{:S(2)}, u32[]{:S(2)}) %collective-permute-start.67) | collective-permute-done | bytes 98336 | tf_op jit(solution)/shard_map/ppermute | solution.py:323
  160.8 2.8 %block.11 = (f32[64,3072]{1,0:T(8,128)S(1)}, bf16[48,3072]{1,0:T(8,128)(2,1)S(1)}, bf16[16,3072]{1,0:T(8,128)(2,1)S(1)}, bf16[2,256,384]{2,1,0:T(8,128)(2,1)S(1)}) custom-call(s32[1]{0:T(128)} %bitcast.section.refs_0_, s32[2,6]{1,0:T(2,128)S(1)} %get-tuple-element.88.patch_flow, ...), custom_call_target="tpu_custom_call", output_to_operand_aliasing={{3}: (13, {})} | custom-call | flops 1207959552 | bytes 9437184 | tf_op jit(solution)/shard_map/block/pallas_call | solution.py:101
  166.5 1.4 collective-permute-start.75
  169.1 2.9 %collective-permute-done.74.refs_2_ = bf16[16,3072]{1,0:T(8,128)(2,1)S(1)} collective-permute-done((bf16[16,3072]{1,0:T(8,128)(2,1)S(1)}, bf16[16,3072]{1,0:T(8,128)(2,1)S(1)}, u32[]{:S(2)}, u32[]{:S(2)}) %collective-permute-start.74) | collective-permute-done | bytes 98336 | tf_op jit(solution)/shard_map/ppermute | solution.py:323
  173.4 2.2 %collective-permute-start.77 = (bf16[16,3200]{1,0:T(8,128)(2,1)S(1)}, bf16[16,3200]{1,0:T(8,128)(2,1)S(1)}, u32[]{:S(2)}, u32[]{:S(2)}) collective-permute-start(bf16[16,3200]{1,0:T(8,128)(2,1)S(1)} %finish.11), channel_id=1, source_target_pairs={{0,8},{1,9},{2,10},{3,11},{4,12},{5,13},{6,14},{7,15},{8,0},{9,1},... | collective-permute-start | bytes 307208 | tf_op jit(solution)/shard_map/ppermute | solution.py:368
  175.6 5.4 %collective-permute-done.77.packet = bf16[16,3200]{1,0:T(8,128)(2,1)S(1)} collective-permute-done((bf16[16,3200]{1,0:T(8,128)(2,1)S(1)}, bf16[16,3200]{1,0:T(8,128)(2,1)S(1)}, u32[]{:S(2)}, u32[]{:S(2)}) %collective-permute-start.77) | collective-permute-done | bytes 102432 | tf_op jit(solution)/shard_map/ppermute | solution.py:368
  (150 shorter events, 54.9 us)
Async XLA Ops:
  2.5 8.7 %collective-permute-start.2 = (bf16[16,3072]{1,0:T(8,128)(2,1)}, bf16[16,3072]{1,0:T(8,128)(2,1)S(1)}, u32[]{:S(2)}, u32[]{:S(2)}) collective-permute-start(bf16[16,3072]{1,0:T(8,128)(2,1)} %get-tuple-element.89.refs_0_), channel_id=1, source_target_pairs={{0,6},{1,7},{2,4},{3,5},{4,2},{5,3},{6,0},{7,1},{8,14},{9,15},{10,... | collective-permute-start | bytes 294920 | tf_op jit(solution)/shard_map/ppermute | solution.py:323
  6.6 5.4 %collective-permute-start.1 = (bf16[16,3072]{1,0:T(8,128)(2,1)}, bf16[16,3072]{1,0:T(8,128)(2,1)S(1)}, u32[]{:S(2)}, u32[]{:S(2)}) collective-permute-start(bf16[16,3072]{1,0:T(8,128)(2,1)} %get-tuple-element.89.refs_0_), channel_id=1, source_target_pairs={{0,4},{1,5},{2,6},{3,7},{4,0},{5,1},{6,2},{7,3},{8,12},{9,13},{10,... | collective-permute-start | bytes 294920 | tf_op jit(solution)/shard_map/ppermute | solution.py:323
  7.0 4.9 %collective-permute-start = (bf16[16,3072]{1,0:T(8,128)(2,1)}, bf16[16,3072]{1,0:T(8,128)(2,1)S(1)}, u32[]{:S(2)}, u32[]{:S(2)}) collective-permute-start(bf16[16,3072]{1,0:T(8,128)(2,1)} %get-tuple-element.89.refs_0_), channel_id=1, source_target_pairs={{0,2},{1,3},{2,0},{3,1},{4,6},{5,7},{6,4},{7,5},{8,10},{9,11},{10,... | collective-permute-start | bytes 294920 | tf_op jit(solution)/shard_map/ppermute | solution.py:323
  16.7 4.3 %collective-permute-start.7 = (bf16[48,3072]{1,0:T(8,128)(2,1)S(1)}, bf16[48,3072]{1,0:T(8,128)(2,1)S(1)}, u32[]{:S(2)}, u32[]{:S(2)}) collective-permute-start(bf16[48,3072]{1,0:T(8,128)(2,1)S(1)} %get-tuple-element.98), channel_id=1, source_target_pairs={{0,1},{1,0},{2,3},{3,2},{4,5},{5,4},{6,7},{7,6},{8,9},{9,8},{10,11... | collective-permute-start | bytes 884744 | tf_op jit(solution)/shard_map/ppermute | solution.py:323
  18.5 6.6 %collective-permute-start.9 = (bf16[16,3072]{1,0:T(8,128)(2,1)S(1)}, bf16[16,3072]{1,0:T(8,128)(2,1)S(1)}, u32[]{:S(2)}, u32[]{:S(2)}) collective-permute-start(bf16[16,3072]{1,0:T(8,128)(2,1)S(1)} %split_last.6), channel_id=1, source_target_pairs={{0,6},{1,7},{2,4},{3,5},{4,2},{5,3},{6,0},{7,1},{8,14},{9,15},{10,... | collective-permute-start | bytes 294920 | tf_op jit(solution)/shard_map/ppermute | solution.py:323
  21.0 5.5 %collective-permute-start.10 = (bf16[16,3072]{1,0:T(8,128)(2,1)S(1)}, bf16[16,3072]{1,0:T(8,128)(2,1)S(1)}, u32[]{:S(2)}, u32[]{:S(2)}) collective-permute-start(bf16[16,3072]{1,0:T(8,128)(2,1)S(1)} %get-tuple-element.101), channel_id=1, source_target_pairs={{0,4},{1,5},{2,6},{3,7},{4,0},{5,1},{6,2},{7,3},{8,12},{9,13},{10,... | collective-permute-start | bytes 294920 | tf_op jit(solution)/shard_map/ppermute | solution.py:323
  21.5 5.1 %collective-permute-start.11 = (bf16[16,3072]{1,0:T(8,128)(2,1)S(1)}, bf16[16,3072]{1,0:T(8,128)(2,1)S(1)}, u32[]{:S(2)}, u32[]{:S(2)}) collective-permute-start(bf16[16,3072]{1,0:T(8,128)(2,1)S(1)} %get-tuple-element.102), channel_id=1, source_target_pairs={{0,2},{1,3},{2,0},{3,1},{4,6},{5,7},{6,4},{7,5},{8,10},{9,11},{10,... | collective-permute-start | bytes 294920 | tf_op jit(solution)/shard_map/ppermute | solution.py:323
  26.8 7.9 %collective-permute-start.12 = (bf16[16,3200]{1,0:T(8,128)(2,1)S(1)}, bf16[16,3200]{1,0:T(8,128)(2,1)S(1)}, u32[]{:S(2)}, u32[]{:S(2)}) collective-permute-start(bf16[16,3200]{1,0:T(8,128)(2,1)S(1)} %finish.6), channel_id=1, source_target_pairs={{0,8},{1,9},{2,10},{3,11},{4,12},{5,13},{6,14},{7,15},{8,0},{9,1},... | collective-permute-start | bytes 307208 | tf_op jit(solution)/shard_map/ppermute | solution.py:368
  35.1 6.0 %collective-permute-start.15 = (bf16[16,3072]{1,0:T(8,128)(2,1)S(1)}, bf16[16,3072]{1,0:T(8,128)(2,1)S(1)}, u32[]{:S(2)}, u32[]{:S(2)}) collective-permute-start(bf16[16,3072]{1,0:T(8,128)(2,1)S(1)} %get-tuple-element.105.refs_0_), channel_id=1, source_target_pairs={{0,6},{1,7},{2,4},{3,5},{4,2},{5,3},{6,0},{7,1},{8,14},{9,15},{10,... | collective-permute-start | bytes 294920 | tf_op jit(solution)/shard_map/ppermute | solution.py:323
  36.9 5.5 %collective-permute-start.14 = (bf16[16,3072]{1,0:T(8,128)(2,1)S(1)}, bf16[16,3072]{1,0:T(8,128)(2,1)S(1)}, u32[]{:S(2)}, u32[]{:S(2)}) collective-permute-start(bf16[16,3072]{1,0:T(8,128)(2,1)S(1)} %get-tuple-element.105.refs_0_), channel_id=1, source_target_pairs={{0,4},{1,5},{2,6},{3,7},{4,0},{5,1},{6,2},{7,3},{8,12},{9,13},{10,... | collective-permute-start | bytes 294920 | tf_op jit(solution)/shard_map/ppermute | solution.py:323
  38.2 4.6 %collective-permute-start.13 = (bf16[16,3072]{1,0:T(8,128)(2,1)S(1)}, bf16[16,3072]{1,0:T(8,128)(2,1)S(1)}, u32[]{:S(2)}, u32[]{:S(2)}) collective-permute-start(bf16[16,3072]{1,0:T(8,128)(2,1)S(1)} %get-tuple-element.105.refs_0_), channel_id=1, source_target_pairs={{0,2},{1,3},{2,0},{3,1},{4,6},{5,7},{6,4},{7,5},{8,10},{9,11},{10,... | collective-permute-start | bytes 294920 | tf_op jit(solution)/shard_map/ppermute | solution.py:323
  38.6 4.3 %collective-permute-start.16 = (bf16[16,3072]{1,0:T(8,128)(2,1)S(1)}, bf16[16,3072]{1,0:T(8,128)(2,1)S(1)}, u32[]{:S(2)}, u32[]{:S(2)}) collective-permute-start(bf16[16,3072]{1,0:T(8,128)(2,1)S(1)} %get-tuple-element.105.refs_0_), channel_id=1, source_target_pairs={{0,1},{1,0},{2,3},{3,2},{4,5},{5,4},{6,7},{7,6},{8,9},{9,8},{10,11... | collective-permute-start | bytes 294920 | tf_op jit(solution)/shard_map/ppermute | solution.py:323
  46.9 3.7 %collective-permute-start.20 = (bf16[48,3072]{1,0:T(8,128)(2,1)S(1)}, bf16[48,3072]{1,0:T(8,128)(2,1)S(1)}, u32[]{:S(2)}, u32[]{:S(2)}) collective-permute-start(bf16[48,3072]{1,0:T(8,128)(2,1)S(1)} %get-tuple-element.108), channel_id=1, source_target_pairs={{0,1},{1,0},{2,3},{3,2},{4,5},{5,4},{6,7},{7,6},{8,9},{9,8},{10,11... | collective-permute-start | bytes 884744 | tf_op jit(solution)/shard_map/ppermute | solution.py:323
  48.7 6.6 %collective-permute-start.22 = (bf16[16,3072]{1,0:T(8,128)(2,1)S(1)}, bf16[16,3072]{1,0:T(8,128)(2,1)S(1)}, u32[]{:S(2)}, u32[]{:S(2)}) collective-permute-start(bf16[16,3072]{1,0:T(8,128)(2,1)S(1)} %split_last.7), channel_id=1, source_target_pairs={{0,6},{1,7},{2,4},{3,5},{4,2},{5,3},{6,0},{7,1},{8,14},{9,15},{10,... | collective-permute-start | bytes 294920 | tf_op jit(solution)/shard_map/ppermute | solution.py:323
  50.7 5.5 %collective-permute-start.23 = (bf16[16,3072]{1,0:T(8,128)(2,1)S(1)}, bf16[16,3072]{1,0:T(8,128)(2,1)S(1)}, u32[]{:S(2)}, u32[]{:S(2)}) collective-permute-start(bf16[16,3072]{1,0:T(8,128)(2,1)S(1)} %get-tuple-element.111), channel_id=1, source_target_pairs={{0,4},{1,5},{2,6},{3,7},{4,0},{5,1},{6,2},{7,3},{8,12},{9,13},{10,... | collective-permute-start | bytes 294920 | tf_op jit(solution)/shard_map/ppermute | solution.py:323
  51.4 5.3 %collective-permute-start.24 = (bf16[16,3072]{1,0:T(8,128)(2,1)S(1)}, bf16[16,3072]{1,0:T(8,128)(2,1)S(1)}, u32[]{:S(2)}, u32[]{:S(2)}) collective-permute-start(bf16[16,3072]{1,0:T(8,128)(2,1)S(1)} %get-tuple-element.112), channel_id=1, source_target_pairs={{0,2},{1,3},{2,0},{3,1},{4,6},{5,7},{6,4},{7,5},{8,10},{9,11},{10,... | collective-permute-start | bytes 294920 | tf_op jit(solution)/shard_map/ppermute | solution.py:323
  56.8 7.8 %collective-permute-start.25 = (bf16[16,3200]{1,0:T(8,128)(2,1)S(1)}, bf16[16,3200]{1,0:T(8,128)(2,1)S(1)}, u32[]{:S(2)}, u32[]{:S(2)}) collective-permute-start(bf16[16,3200]{1,0:T(8,128)(2,1)S(1)} %finish.7), channel_id=1, source_target_pairs={{0,8},{1,9},{2,10},{3,11},{4,12},{5,13},{6,14},{7,15},{8,0},{9,1},... | collective-permute-start | bytes 307208 | tf_op jit(solution)/shard_map/ppermute | solution.py:368
  65.0 5.6 %collective-permute-start.28 = (bf16[16,3072]{1,0:T(8,128)(2,1)S(1)}, bf16[16,3072]{1,0:T(8,128)(2,1)S(1)}, u32[]{:S(2)}, u32[]{:S(2)}) collective-permute-start(bf16[16,3072]{1,0:T(8,128)(2,1)S(1)} %get-tuple-element.114.refs_0_), channel_id=1, source_target_pairs={{0,6},{1,7},{2,4},{3,5},{4,2},{5,3},{6,0},{7,1},{8,14},{9,15},{10,... | collective-permute-start | bytes 294920 | tf_op jit(solution)/shard_map/ppermute | solution.py:323
  66.0 5.3 %collective-permute-start.27 = (bf16[16,3072]{1,0:T(8,128)(2,1)S(1)}, bf16[16,3072]{1,0:T(8,128)(2,1)S(1)}, u32[]{:S(2)}, u32[]{:S(2)}) collective-permute-start(bf16[16,3072]{1,0:T(8,128)(2,1)S(1)} %get-tuple-element.114.refs_0_), channel_id=1, source_target_pairs={{0,4},{1,5},{2,6},{3,7},{4,0},{5,1},{6,2},{7,3},{8,12},{9,13},{10,... | collective-permute-start | bytes 294920 | tf_op jit(solution)/shard_map/ppermute | solution.py:323
  67.5 4.6 %collective-permute-start.26 = (bf16[16,3072]{1,0:T(8,128)(2,1)S(1)}, bf16[16,3072]{1,0:T(8,128)(2,1)S(1)}, u32[]{:S(2)}, u32[]{:S(2)}) collective-permute-start(bf16[16,3072]{1,0:T(8,128)(2,1)S(1)} %get-tuple-element.114.refs_0_), channel_id=1, source_target_pairs={{0,2},{1,3},{2,0},{3,1},{4,6},{5,7},{6,4},{7,5},{8,10},{9,11},{10,... | collective-permute-start | bytes 294920 | tf_op jit(solution)/shard_map/ppermute | solution.py:323
  68.6 3.6 %collective-permute-start.29 = (bf16[16,3072]{1,0:T(8,128)(2,1)S(1)}, bf16[16,3072]{1,0:T(8,128)(2,1)S(1)}, u32[]{:S(2)}, u32[]{:S(2)}) collective-permute-start(bf16[16,3072]{1,0:T(8,128)(2,1)S(1)} %get-tuple-element.114.refs_0_), channel_id=1, source_target_pairs={{0,1},{1,0},{2,3},{3,2},{4,5},{5,4},{6,7},{7,6},{8,9},{9,8},{10,11... | collective-permute-start | bytes 294920 | tf_op jit(solution)/shard_map/ppermute | solution.py:323
  78.0 6.6 %collective-permute-start.35 = (bf16[16,3072]{1,0:T(8,128)(2,1)S(1)}, bf16[16,3072]{1,0:T(8,128)(2,1)S(1)}, u32[]{:S(2)}, u32[]{:S(2)}) collective-permute-start(bf16[16,3072]{1,0:T(8,128)(2,1)S(1)} %split_last.8), channel_id=1, source_target_pairs={{0,6},{1,7},{2,4},{3,5},{4,2},{5,3},{6,0},{7,1},{8,14},{9,15},{10,... | collective-permute-start | bytes 294920 | tf_op jit(solution)/shard_map/ppermute | solution.py:323
  79.6 6.0 %collective-permute-start.36 = (bf16[16,3072]{1,0:T(8,128)(2,1)S(1)}, bf16[16,3072]{1,0:T(8,128)(2,1)S(1)}, u32[]{:S(2)}, u32[]{:S(2)}) collective-permute-start(bf16[16,3072]{1,0:T(8,128)(2,1)S(1)} %get-tuple-element.120), channel_id=1, source_target_pairs={{0,4},{1,5},{2,6},{3,7},{4,0},{5,1},{6,2},{7,3},{8,12},{9,13},{10,... | collective-permute-start | bytes 294920 | tf_op jit(solution)/shard_map/ppermute | solution.py:323
  80.7 5.2 %collective-permute-start.37 = (bf16[16,3072]{1,0:T(8,128)(2,1)S(1)}, bf16[16,3072]{1,0:T(8,128)(2,1)S(1)}, u32[]{:S(2)}, u32[]{:S(2)}) collective-permute-start(bf16[16,3072]{1,0:T(8,128)(2,1)S(1)} %get-tuple-element.121), channel_id=1, source_target_pairs={{0,2},{1,3},{2,0},{3,1},{4,6},{5,7},{6,4},{7,5},{8,10},{9,11},{10,... | collective-permute-start | bytes 294920 | tf_op jit(solution)/shard_map/ppermute | solution.py:323
  86.1 7.6 %collective-permute-start.38 = (bf16[16,3200]{1,0:T(8,128)(2,1)S(1)}, bf16[16,3200]{1,0:T(8,128)(2,1)S(1)}, u32[]{:S(2)}, u32[]{:S(2)}) collective-permute-start(bf16[16,3200]{1,0:T(8,128)(2,1)S(1)} %finish.8), channel_id=1, source_target_pairs={{0,8},{1,9},{2,10},{3,11},{4,12},{5,13},{6,14},{7,15},{8,0},{9,1},... | collective-permute-start | bytes 307208 | tf_op jit(solution)/shard_map/ppermute | solution.py:368
  94.2 5.6 %collective-permute-start.41 = (bf16[16,3072]{1,0:T(8,128)(2,1)S(1)}, bf16[16,3072]{1,0:T(8,128)(2,1)S(1)}, u32[]{:S(2)}, u32[]{:S(2)}) collective-permute-start(bf16[16,3072]{1,0:T(8,128)(2,1)S(1)} %get-tuple-element.123.refs_0_), channel_id=1, source_target_pairs={{0,6},{1,7},{2,4},{3,5},{4,2},{5,3},{6,0},{7,1},{8,14},{9,15},{10,... | collective-permute-start | bytes 294920 | tf_op jit(solution)/shard_map/ppermute | solution.py:323
  95.1 5.4 %collective-permute-start.40 = (bf16[16,3072]{1,0:T(8,128)(2,1)S(1)}, bf16[16,3072]{1,0:T(8,128)(2,1)S(1)}, u32[]{:S(2)}, u32[]{:S(2)}) collective-permute-start(bf16[16,3072]{1,0:T(8,128)(2,1)S(1)} %get-tuple-element.123.refs_0_), channel_id=1, source_target_pairs={{0,4},{1,5},{2,6},{3,7},{4,0},{5,1},{6,2},{7,3},{8,12},{9,13},{10,... | collective-permute-start | bytes 294920 | tf_op jit(solution)/shard_map/ppermute | solution.py:323
  96.9 4.6 %collective-permute-start.39 = (bf16[16,3072]{1,0:T(8,128)(2,1)S(1)}, bf16[16,3072]{1,0:T(8,128)(2,1)S(1)}, u32[]{:S(2)}, u32[]{:S(2)}) collective-permute-start(bf16[16,3072]{1,0:T(8,128)(2,1)S(1)} %get-tuple-element.123.refs_0_), channel_id=1, source_target_pairs={{0,2},{1,3},{2,0},{3,1},{4,6},{5,7},{6,4},{7,5},{8,10},{9,11},{10,... | collective-permute-start | bytes 294920 | tf_op jit(solution)/shard_map/ppermute | solution.py:323
  97.8 3.7 %collective-permute-start.42 = (bf16[16,3072]{1,0:T(8,128)(2,1)S(1)}, bf16[16,3072]{1,0:T(8,128)(2,1)S(1)}, u32[]{:S(2)}, u32[]{:S(2)}) collective-permute-start(bf16[16,3072]{1,0:T(8,128)(2,1)S(1)} %get-tuple-element.123.refs_0_), channel_id=1, source_target_pairs={{0,1},{1,0},{2,3},{3,2},{4,5},{5,4},{6,7},{7,6},{8,9},{9,8},{10,11... | collective-permute-start | bytes 294920 | tf_op jit(solution)/shard_map/ppermute | solution.py:323
  107.4 6.6 %collective-permute-start.48 = (bf16[16,3072]{1,0:T(8,128)(2,1)S(1)}, bf16[16,3072]{1,0:T(8,128)(2,1)S(1)}, u32[]{:S(2)}, u32[]{:S(2)}) collective-permute-start(bf16[16,3072]{1,0:T(8,128)(2,1)S(1)} %split_last.9), channel_id=1, source_target_pairs={{0,6},{1,7},{2,4},{3,5},{4,2},{5,3},{6,0},{7,1},{8,14},{9,15},{10,... | collective-permute-start | bytes 294920 | tf_op jit(solution)/shard_map/ppermute | solution.py:323
  108.6 6.1 %collective-permute-start.49 = (bf16[16,3072]{1,0:T(8,128)(2,1)S(1)}, bf16[16,3072]{1,0:T(8,128)(2,1)S(1)}, u32[]{:S(2)}, u32[]{:S(2)}) collective-permute-start(bf16[16,3072]{1,0:T(8,128)(2,1)S(1)} %get-tuple-element.129), channel_id=1, source_target_pairs={{0,4},{1,5},{2,6},{3,7},{4,0},{5,1},{6,2},{7,3},{8,12},{9,13},{10,... | collective-permute-start | bytes 294920 | tf_op jit(solution)/shard_map/ppermute | solution.py:323
  110.0 5.3 %collective-permute-start.50 = (bf16[16,3072]{1,0:T(8,128)(2,1)S(1)}, bf16[16,3072]{1,0:T(8,128)(2,1)S(1)}, u32[]{:S(2)}, u32[]{:S(2)}) collective-permute-start(bf16[16,3072]{1,0:T(8,128)(2,1)S(1)} %get-tuple-element.130), channel_id=1, source_target_pairs={{0,2},{1,3},{2,0},{3,1},{4,6},{5,7},{6,4},{7,5},{8,10},{9,11},{10,... | collective-permute-start | bytes 294920 | tf_op jit(solution)/shard_map/ppermute | solution.py:323
  115.4 7.5 %collective-permute-start.51 = (bf16[16,3200]{1,0:T(8,128)(2,1)S(1)}, bf16[16,3200]{1,0:T(8,128)(2,1)S(1)}, u32[]{:S(2)}, u32[]{:S(2)}) collective-permute-start(bf16[16,3200]{1,0:T(8,128)(2,1)S(1)} %finish.9), channel_id=1, source_target_pairs={{0,8},{1,9},{2,10},{3,11},{4,12},{5,13},{6,14},{7,15},{8,0},{9,1},... | collective-permute-start | bytes 307208 | tf_op jit(solution)/shard_map/ppermute | solution.py:368
  123.3 5.8 %collective-permute-start.54 = (bf16[16,3072]{1,0:T(8,128)(2,1)S(1)}, bf16[16,3072]{1,0:T(8,128)(2,1)S(1)}, u32[]{:S(2)}, u32[]{:S(2)}) collective-permute-start(bf16[16,3072]{1,0:T(8,128)(2,1)S(1)} %get-tuple-element.132.refs_0_), channel_id=1, source_target_pairs={{0,6},{1,7},{2,4},{3,5},{4,2},{5,3},{6,0},{7,1},{8,14},{9,15},{10,... | collective-permute-start | bytes 294920 | tf_op jit(solution)/shard_map/ppermute | solution.py:323
  124.0 5.3 %collective-permute-start.53 = (bf16[16,3072]{1,0:T(8,128)(2,1)S(1)}, bf16[16,3072]{1,0:T(8,128)(2,1)S(1)}, u32[]{:S(2)}, u32[]{:S(2)}) collective-permute-start(bf16[16,3072]{1,0:T(8,128)(2,1)S(1)} %get-tuple-element.132.refs_0_), channel_id=1, source_target_pairs={{0,4},{1,5},{2,6},{3,7},{4,0},{5,1},{6,2},{7,3},{8,12},{9,13},{10,... | collective-permute-start | bytes 294920 | tf_op jit(solution)/shard_map/ppermute | solution.py:323
  125.7 4.6 %collective-permute-start.52 = (bf16[16,3072]{1,0:T(8,128)(2,1)S(1)}, bf16[16,3072]{1,0:T(8,128)(2,1)S(1)}, u32[]{:S(2)}, u32[]{:S(2)}) collective-permute-start(bf16[16,3072]{1,0:T(8,128)(2,1)S(1)} %get-tuple-element.132.refs_0_), channel_id=1, source_target_pairs={{0,2},{1,3},{2,0},{3,1},{4,6},{5,7},{6,4},{7,5},{8,10},{9,11},{10,... | collective-permute-start | bytes 294920 | tf_op jit(solution)/shard_map/ppermute | solution.py:323
  136.2 6.6 %collective-permute-start.61 = (bf16[16,3072]{1,0:T(8,128)(2,1)S(1)}, bf16[16,3072]{1,0:T(8,128)(2,1)S(1)}, u32[]{:S(2)}, u32[]{:S(2)}) collective-permute-start(bf16[16,3072]{1,0:T(8,128)(2,1)S(1)} %split_last.10), channel_id=1, source_target_pairs={{0,6},{1,7},{2,4},{3,5},{4,2},{5,3},{6,0},{7,1},{8,14},{9,15},{10,... | collective-permute-start | bytes 294920 | tf_op jit(solution)/shard_map/ppermute | solution.py:323
  137.6 6.2 %collective-permute-start.62 = (bf16[16,3072]{1,0:T(8,128)(2,1)S(1)}, bf16[16,3072]{1,0:T(8,128)(2,1)S(1)}, u32[]{:S(2)}, u32[]{:S(2)}) collective-permute-start(bf16[16,3072]{1,0:T(8,128)(2,1)S(1)} %get-tuple-element.138), channel_id=1, source_target_pairs={{0,4},{1,5},{2,6},{3,7},{4,0},{5,1},{6,2},{7,3},{8,12},{9,13},{10,... | collective-permute-start | bytes 294920 | tf_op jit(solution)/shard_map/ppermute | solution.py:323
  139.0 5.1 %collective-permute-start.63 = (bf16[16,3072]{1,0:T(8,128)(2,1)S(1)}, bf16[16,3072]{1,0:T(8,128)(2,1)S(1)}, u32[]{:S(2)}, u32[]{:S(2)}) collective-permute-start(bf16[16,3072]{1,0:T(8,128)(2,1)S(1)} %get-tuple-element.139), channel_id=1, source_target_pairs={{0,2},{1,3},{2,0},{3,1},{4,6},{5,7},{6,4},{7,5},{8,10},{9,11},{10,... | collective-permute-start | bytes 294920 | tf_op jit(solution)/shard_map/ppermute | solution.py:323
  144.2 7.5 %collective-permute-start.64 = (bf16[16,3200]{1,0:T(8,128)(2,1)S(1)}, bf16[16,3200]{1,0:T(8,128)(2,1)S(1)}, u32[]{:S(2)}, u32[]{:S(2)}) collective-permute-start(bf16[16,3200]{1,0:T(8,128)(2,1)S(1)} %finish.10), channel_id=1, source_target_pairs={{0,8},{1,9},{2,10},{3,11},{4,12},{5,13},{6,14},{7,15},{8,0},{9,1},... | collective-permute-start | bytes 307208 | tf_op jit(solution)/shard_map/ppermute | solution.py:368
  152.1 5.7 %collective-permute-start.67 = (bf16[16,3072]{1,0:T(8,128)(2,1)S(1)}, bf16[16,3072]{1,0:T(8,128)(2,1)S(1)}, u32[]{:S(2)}, u32[]{:S(2)}) collective-permute-start(bf16[16,3072]{1,0:T(8,128)(2,1)S(1)} %get-tuple-element.141.refs_0_), channel_id=1, source_target_pairs={{0,6},{1,7},{2,4},{3,5},{4,2},{5,3},{6,0},{7,1},{8,14},{9,15},{10,... | collective-permute-start | bytes 294920 | tf_op jit(solution)/shard_map/ppermute | solution.py:323
  153.0 5.7 %collective-permute-start.66 = (bf16[16,3072]{1,0:T(8,128)(2,1)S(1)}, bf16[16,3072]{1,0:T(8,128)(2,1)S(1)}, u32[]{:S(2)}, u32[]{:S(2)}) collective-permute-start(bf16[16,3072]{1,0:T(8,128)(2,1)S(1)} %get-tuple-element.141.refs_0_), channel_id=1, source_target_pairs={{0,4},{1,5},{2,6},{3,7},{4,0},{5,1},{6,2},{7,3},{8,12},{9,13},{10,... | collective-permute-start | bytes 294920 | tf_op jit(solution)/shard_map/ppermute | solution.py:323
  154.9 4.6 %collective-permute-start.65 = (bf16[16,3072]{1,0:T(8,128)(2,1)S(1)}, bf16[16,3072]{1,0:T(8,128)(2,1)S(1)}, u32[]{:S(2)}, u32[]{:S(2)}) collective-permute-start(bf16[16,3072]{1,0:T(8,128)(2,1)S(1)} %get-tuple-element.141.refs_0_), channel_id=1, source_target_pairs={{0,2},{1,3},{2,0},{3,1},{4,6},{5,7},{6,4},{7,5},{8,10},{9,11},{10,... | collective-permute-start | bytes 294920 | tf_op jit(solution)/shard_map/ppermute | solution.py:323
  155.7 3.8 %collective-permute-start.68 = (bf16[16,3072]{1,0:T(8,128)(2,1)S(1)}, bf16[16,3072]{1,0:T(8,128)(2,1)S(1)}, u32[]{:S(2)}, u32[]{:S(2)}) collective-permute-start(bf16[16,3072]{1,0:T(8,128)(2,1)S(1)} %get-tuple-element.141.refs_0_), channel_id=1, source_target_pairs={{0,1},{1,0},{2,3},{3,2},{4,5},{5,4},{6,7},{7,6},{8,9},{9,8},{10,11... | collective-permute-start | bytes 294920 | tf_op jit(solution)/shard_map/ppermute | solution.py:323
  165.4 6.6 %collective-permute-start.74 = (bf16[16,3072]{1,0:T(8,128)(2,1)S(1)}, bf16[16,3072]{1,0:T(8,128)(2,1)S(1)}, u32[]{:S(2)}, u32[]{:S(2)}) collective-permute-start(bf16[16,3072]{1,0:T(8,128)(2,1)S(1)} %split_last.11), channel_id=1, source_target_pairs={{0,6},{1,7},{2,4},{3,5},{4,2},{5,3},{6,0},{7,1},{8,14},{9,15},{10,... | collective-permute-start | bytes 294920 | tf_op jit(solution)/shard_map/ppermute | solution.py:323
  166.5 6.2 %collective-permute-start.75 = (bf16[16,3072]{1,0:T(8,128)(2,1)S(1)}, bf16[16,3072]{1,0:T(8,128)(2,1)S(1)}, u32[]{:S(2)}, u32[]{:S(2)}) collective-permute-start(bf16[16,3072]{1,0:T(8,128)(2,1)S(1)} %get-tuple-element.147), channel_id=1, source_target_pairs={{0,4},{1,5},{2,6},{3,7},{4,0},{5,1},{6,2},{7,3},{8,12},{9,13},{10,... | collective-permute-start | bytes 294920 | tf_op jit(solution)/shard_map/ppermute | solution.py:323
  167.9 5.4 %collective-permute-start.76 = (bf16[16,3072]{1,0:T(8,128)(2,1)S(1)}, bf16[16,3072]{1,0:T(8,128)(2,1)S(1)}, u32[]{:S(2)}, u32[]{:S(2)}) collective-permute-start(bf16[16,3072]{1,0:T(8,128)(2,1)S(1)} %get-tuple-element.148), channel_id=1, source_target_pairs={{0,2},{1,3},{2,0},{3,1},{4,6},{5,7},{6,4},{7,5},{8,10},{9,11},{10,... | collective-permute-start | bytes 294920 | tf_op jit(solution)/shard_map/ppermute | solution.py:323
  173.4 7.5 %collective-permute-start.77 = (bf16[16,3200]{1,0:T(8,128)(2,1)S(1)}, bf16[16,3200]{1,0:T(8,128)(2,1)S(1)}, u32[]{:S(2)}, u32[]{:S(2)}) collective-permute-start(bf16[16,3200]{1,0:T(8,128)(2,1)S(1)} %finish.11), channel_id=1, source_target_pairs={{0,8},{1,9},{2,10},{3,11},{4,12},{5,13},{6,14},{7,15},{8,0},{9,1},... | collective-permute-start | bytes 307208 | tf_op jit(solution)/shard_map/ppermute | solution.py:368
  (35 other events, 122.8 us)

commit v6 on v5

--- a/solution.py
+++ b/solution.py
@@ -55,10 +55,15 @@
     return (values * lax.rsqrt(power + EPS) * gain_row).astype(jnp.bfloat16)
 
 
-def block_kernel(
-    tick, section, patch_flow, *refs
-):
+def norm_here(section, tokens, mod):
+    here = section[0]
+    return layer_norm(tokens, mod[0, pl.ds(here, 1), :], mod[1, pl.ds(here, 1), :])
+
+
+def block_kernel(tick, section, patch_flow, *refs):
     pieces, refs = refs[: 2 * CHIPS], refs[2 * CHIPS :]
+    if tick == 0:
+        mod, refs = refs[0], refs[1:]
     gains, w_qkv, w_out, kv_in, kept, sent, ahead, kv, normed, mixed = refs
     part_rows, width = pieces[0].shape
     half = CHIPS * part_rows
@@ -66,7 +71,10 @@
     heads = w_out.shape[0] // HS
     here = section[0]
     for place, piece in enumerate(pieces):
-        normed[place * part_rows : (place + 1) * part_rows, :] = piece[...]
+        values = piece[...]
+        if tick == 0:
+            values = norm_here(section, f32(values), mod)
+        normed[place * part_rows : (place + 1) * part_rows, :] = values
     start = pl.multiple_of(patch_flow[here, tick] * rows, rows)
     kv[...] = kv_in[...]
     gain = gains[here]
@@ -95,9 +103,10 @@
         ahead[:, low : low + tile] = projected[edge:, :].astype(jnp.bfloat16)
 
 
-def block(tick, section, patch_flow, pieces, gains, w_qkv, w_out, kv):
+def block(tick, section, patch_flow, pieces, mod, gains, w_qkv, w_out, kv):
     half, width = CHIPS * pieces[0].shape[0], pieces[0].shape[1]
     columns = w_out.shape[0]
+    args = [section, patch_flow, *pieces] + [mod] * (tick == 0) + [gains, w_qkv, w_out, kv]
     return pl.pallas_call(
         functools.partial(block_kernel, tick),
         out_shape=like(
@@ -106,13 +115,13 @@
             ((half // CHIPS, width), jnp.bfloat16),
             (kv.shape, jnp.bfloat16),
         ),
-        in_specs=[SCALARS] * 2 + [WHOLE] * (4 + 2 * CHIPS),
+        in_specs=[SCALARS] * 2 + [WHOLE] * (len(args) - 2),
         out_specs=(WHOLE,) * 4,
         scratch_shapes=[
             VMEM((2 * half, width), jnp.bfloat16),
             VMEM((2 * half, columns), jnp.bfloat16),
         ],
-        input_output_aliases={5 + 2 * CHIPS: 3},
+        input_output_aliases={len(args) - 1: 3},
         compiler_params=params(8),
         cost_estimate=pl.CostEstimate(
             flops=16 * half * columns * width,
@@ -120,7 +129,7 @@
             transcendentals=0,
         ),
         name="block",
-    )(section, patch_flow, *pieces, gains, w_qkv, w_out, kv)
+    )(*args)
 
 
 def split_last_kernel(kept, came, out):
@@ -196,11 +205,6 @@
         compiler_params=params(4),
         name="finish",
     )(section, *args)
-
-
-def norm_here(section, tokens, mod):
-    here = section[0]
-    return layer_norm(tokens, mod[0, pl.ds(here, 1), :], mod[1, pl.ds(here, 1), :])
 
 
 def arrive(section, packet, w_embed, hidden):
@@ -267,35 +271,6 @@
         cost_estimate=pl.CostEstimate(flops=0, bytes_accessed=2 * size, transcendentals=0),
         name="load",
     )(*arrays)
-
-
-def first_kernel(section, hidden_in, mod_in, hidden, mod, normed, one, two):
-    copies = [
-        pltpu.make_async_copy(hidden_in, hidden, one),
-        pltpu.make_async_copy(mod_in, mod, two),
-    ]
-    for copy in copies:
-        copy.start()
-    for copy in copies:
-        copy.wait()
-    normed[...] = norm_here(section, f32(hidden[...]), mod)
-
-
-def first(section, hidden, mod):
-    far = pl.BlockSpec(memory_space=pltpu.HBM)
-    return pl.pallas_call(
-        first_kernel,
-        out_shape=(
-            VMEM(hidden.shape, hidden.dtype),
-            VMEM(mod.shape, mod.dtype),
-            jax.ShapeDtypeStruct(hidden.shape, jnp.bfloat16),
-        ),
-        in_specs=[SCALARS, far, far],
-        out_specs=(WHOLE,) * 3,
-        scratch_shapes=[pltpu.SemaphoreType.DMA(())] * 2,
-        compiler_params=params(60),
-        name="first",
-    )(section, hidden, mod)
 
 
 def open_kernel(section, packet, w_embed, hidden, latent):
@@ -345,27 +320,28 @@
     section = (lax.axis_index("section") // GROUP).astype(jnp.int32).reshape(1)
     w_final = jnp.transpose(w_final)
     onward = [(device, (device + GROUP) % size) for device in range(size)]
-
-    hidden, mod, normed = first(section, hidden_in, jnp.transpose(block_mod, (1, 0, 2)))
-    held = (w_qkv, w_out, qk_gain, jnp.transpose(patch_flow), stale_kv)
-    normed, *held = lax.optimization_barrier((normed, *held))
-    held = load(*held)
-    state = (hidden, latent_in)
+    across = [(device, target ^ (GROUP // 2)) for device, target in onward]
+
+    mod = jnp.transpose(block_mod, (1, 0, 2))
+    held = load(w_qkv, w_out, qk_gain, jnp.transpose(patch_flow), stale_kv, mod)
+    section, normed = lax.optimization_barrier((section, hidden_in))
+    state = (hidden_in, latent_in)
     for tick in range(ticks):
         if tick > 0:
             hidden, normed = norm(section, packet, mod, w_embed)
             state = (hidden, packet)
         own = gather_chips(normed)
         if tick == 0:
-            own, w_qkv, w_out, gains, patch_flow, kv = lax.optimization_barrier((own, *held))
+            own, w_qkv, w_out, gains, patch_flow, kv, mod = lax.optimization_barrier((own, *held))
         pieces = own + [exchange(piece, 1) for piece in own]
-        kept, sent, ahead, kv = block(tick, section, patch_flow, pieces, gains, w_qkv, w_out, kv)
+        kept, sent, ahead, kv = block(tick, section, patch_flow, pieces, mod, gains, w_qkv, w_out, kv)
         ahead = split_last(kept, exchange(ahead, 1))
         mine, *blocks = split(kept, exchange(sent, 1))
         came = [exchange(rows, apart) for rows, apart in zip([*blocks, ahead], CHIP_STEPS)]
         parts = [mine] + came[::-1]
         packet = finish(section, parts, state, mod, final_mod, w_final, w_embed)
-        packet = lax.ppermute(packet, "section", onward)
+        swaps = tick < ticks - ticks % 2
+        packet = lax.ppermute(packet, "section", across if swaps else onward)
     return open_packet(section, packet, w_embed)
 
 

time: 182 us -> 176 us (0.967)
  waiting for transfers between devices: 90 us -> 78.7 us
  starting transfers between devices: 64.1 us -> 70.8 us
    ppermute x6, waiting for transfers between devices: 30.8 us -> 19 us  [body(): packet = lax.ppermute(packet, 'section', across if swaps else onward)]
    ppermute x6, starting transfers between devices: 15.1 us -> 20.6 us  [body(): packet = lax.ppermute(packet, 'section', across if swaps else onward)]
    pallas_call x1 -> x0, Pallas kernels: 1.83 us -> none  [first(): pl.pallas_call(first_kernel, out_shape=(VMEM(hidden.shape, hidden.dtype),...]
  transfers between devices with their start and end apart: 78 -> 78, of which waited for: 61 -> 62; matrix products, arithmetic and copies ran while one was open for 0% -> 0% of each run, Pallas kernels for 2% -> 3%
where the time goes in v6:
time: 176 us
  waiting for transfers between devices  78.7 us (45%)
  starting transfers between devices  70.8 us (40%)
  Pallas kernels  25.1 us (14%)
    ppermute x72, waiting for transfers between devices, exchange(): return lax.ppermute(value, 'section', route)  59.7 us
    ppermute x72, starting transfers between devices, exchange(): return lax.ppermute(value, 'section', route)  50.3 us
    ppermute x6, starting transfers between devices, body(): packet = lax.ppermute(packet, 'section', across if swaps else onward)  20.6 us
    ppermute x6, waiting for transfers between devices, body(): packet = lax.ppermute(packet, 'section', across if swaps else onward)  19 us
    pallas_call x6, Pallas kernels, block(): pl.pallas_call(functools.partial(block_kernel, tick), out_shape=like(((ha...  17 us
    pallas_call x1, Pallas kernels, load(): pl.pallas_call(functools.partial(load_kernel, count), out_shape=tuple((VM...  3.97 us
  transfers between devices with their start and end apart: 78, of which 62 were waited for; matrix products, arithmetic and copies ran while one was open for 0% of the time, Pallas kernels for 3%

profile of v6, /device:TPU:0, one launch (start us, length us, event | category | flops | bytes accessed | tf_op | source)
XLA Modules:
  0.0 175.7 jit_solution(6942986273870596647)
XLA Ops:
  0.7 4.1 %collective-permute-start.2 = (bf16[16,3072]{1,0:T(8,128)(2,1)}, bf16[16,3072]{1,0:T(8,128)(2,1)S(1)}, u32[]{:S(2)}, u32[]{:S(2)}) collective-permute-start(bf16[16,3072]{1,0:T(8,128)(2,1)} %refs_5_.1), channel_id=1, source_target_pairs={{0,6},{1,7},{2,4},{3,5},{4,2},{5,3},{6,0},{7,1},{8,14},{9,15},{10,... | collective-permute-start | bytes 294920 | tf_op jit(solution)/shard_map/ppermute | solution.py:298
  5.4 4.0 %load.1 = (bf16[3072,1152]{1,0:T(8,128)(2,1)S(1)}, bf16[384,3072]{1,0:T(8,128)(2,1)S(1)}, f32[2,2,128]{2,1,0:T(2,128)S(1)}, s32[2,6]{1,0:T(2,128)S(1)}, bf16[2,2...) custom-call(bf16[3,3072,384]{2,1,0:T(8,128)(2,1)} %refs_0_.1, bf16[384,3072]{1,0:T(8,128)(2,1)} %refs_1_.1, ...), custom_call_target="tpu_custom_call" | custom-call | bytes 19812448 | tf_op jit(solution)/shard_map/load/pallas_call | solution.py:264
  12.1 3.1 %block.6 = (f32[64,3072]{1,0:T(8,128)S(1)}, bf16[48,3072]{1,0:T(8,128)(2,1)S(1)}, bf16[16,3072]{1,0:T(8,128)(2,1)S(1)}, bf16[2,256,384]{2,1,0:T(8,128)(2,1)S(1)}) custom-call(s32[1]{0:T(128)} %bitcast.section.refs_0_, s32[2,6]{1,0:T(2,128)S(1)} %get-tuple-element.79.patch_flow, bf16[16,3072]{1,0:T(8,128)(2,1)S(1)} %copy-done.3, ...), custom_call_target="tpu_custom_call", output_to_operand_aliasing={{3}: (14, {})} | custom-call | flops 1207959552 | bytes 9437184 | tf_op jit(solution)/shard_map/block/pallas_call | solution.py:110
  17.0 2.5 %collective-permute-start.9 = (bf16[16,3072]{1,0:T(8,128)(2,1)S(1)}, bf16[16,3072]{1,0:T(8,128)(2,1)S(1)}, u32[]{:S(2)}, u32[]{:S(2)}) collective-permute-start(bf16[16,3072]{1,0:T(8,128)(2,1)S(1)} %split_last.6), channel_id=1, source_target_pairs={{0,6},{1,7},{2,4},{3,5},{4,2},{5,3},{6,0},{7,1},{8,14},{9,15},{10,... | collective-permute-start | bytes 294920 | tf_op jit(solution)/shard_map/ppermute | solution.py:298
  20.7 2.9 %collective-permute-done.9.refs_2_ = bf16[16,3072]{1,0:T(8,128)(2,1)S(1)} collective-permute-done((bf16[16,3072]{1,0:T(8,128)(2,1)S(1)}, bf16[16,3072]{1,0:T(8,128)(2,1)S(1)}, u32[]{:S(2)}, u32[]{:S(2)}) %collective-permute-start.9) | collective-permute-done | bytes 98336 | tf_op jit(solution)/shard_map/ppermute | solution.py:298
  23.6 1.5 collective-permute-done.10.refs_3_
  25.3 4.2 %collective-permute-start.12 = (bf16[16,3200]{1,0:T(8,128)(2,1)S(1)}, bf16[16,3200]{1,0:T(8,128)(2,1)S(1)}, u32[]{:S(2)}, u32[]{:S(2)}) collective-permute-start(bf16[16,3200]{1,0:T(8,128)(2,1)S(1)} %finish.6), channel_id=1, source_target_pairs={{0,12},{1,13},{2,14},{3,15},{4,8},{5,9},{6,10},{7,11},{8,4},{9,5},... | collective-permute-start | bytes 307208 | tf_op jit(solution)/shard_map/ppermute | solution.py:344
  29.5 2.7 %collective-permute-done.12.packet.refs_6_ = bf16[16,3200]{1,0:T(8,128)(2,1)S(1)} collective-permute-done((bf16[16,3200]{1,0:T(8,128)(2,1)S(1)}, bf16[16,3200]{1,0:T(8,128)(2,1)S(1)}, u32[]{:S(2)}, u32[]{:S(2)}) %collective-permute-start.12) | collective-permute-done | bytes 102432 | tf_op jit(solution)/shard_map/ppermute | solution.py:344
  32.6 2.7 %collective-permute-start.15 = (bf16[16,3072]{1,0:T(8,128)(2,1)S(1)}, bf16[16,3072]{1,0:T(8,128)(2,1)S(1)}, u32[]{:S(2)}, u32[]{:S(2)}) collective-permute-start(bf16[16,3072]{1,0:T(8,128)(2,1)S(1)} %get-tuple-element.95.refs_0_), channel_id=1, source_target_pairs={{0,6},{1,7},{2,4},{3,5},{4,2},{5,3},{6,0},{7,1},{8,14},{9,15},{10,... | collective-permute-start | bytes 294920 | tf_op jit(solution)/shard_map/ppermute | solution.py:298
  36.2 2.4 %collective-permute-done.15.refs_3_ = bf16[16,3072]{1,0:T(8,128)(2,1)S(1)} collective-permute-done((bf16[16,3072]{1,0:T(8,128)(2,1)S(1)}, bf16[16,3072]{1,0:T(8,128)(2,1)S(1)}, u32[]{:S(2)}, u32[]{:S(2)}) %collective-permute-start.15) | collective-permute-done | bytes 98336 | tf_op jit(solution)/shard_map/ppermute | solution.py:298
  38.6 1.4 collective-permute-done.14.refs_2_
  41.5 2.8 %block.7 = (f32[64,3072]{1,0:T(8,128)S(1)}, bf16[48,3072]{1,0:T(8,128)(2,1)S(1)}, bf16[16,3072]{1,0:T(8,128)(2,1)S(1)}, bf16[2,256,384]{2,1,0:T(8,128)(2,1)S(1)}) custom-call(s32[1]{0:T(128)} %bitcast.section.refs_0_, s32[2,6]{1,0:T(2,128)S(1)} %get-tuple-element.79.patch_flow, ...), custom_call_target="tpu_custom_call", output_to_operand_aliasing={{3}: (13, {})} | custom-call | flops 1207959552 | bytes 9437184 | tf_op jit(solution)/shard_map/block/pallas_call | solution.py:110
  44.9 1.2 collective-permute-done.21.came
  46.1 2.0 %collective-permute-start.22 = (bf16[16,3072]{1,0:T(8,128)(2,1)S(1)}, bf16[16,3072]{1,0:T(8,128)(2,1)S(1)}, u32[]{:S(2)}, u32[]{:S(2)}) collective-permute-start(bf16[16,3072]{1,0:T(8,128)(2,1)S(1)} %split_last.7), channel_id=1, source_target_pairs={{0,6},{1,7},{2,4},{3,5},{4,2},{5,3},{6,0},{7,1},{8,14},{9,15},{10,... | collective-permute-start | bytes 294920 | tf_op jit(solution)/shard_map/ppermute | solution.py:298
  49.8 2.8 %collective-permute-done.22.refs_2_ = bf16[16,3072]{1,0:T(8,128)(2,1)S(1)} collective-permute-done((bf16[16,3072]{1,0:T(8,128)(2,1)S(1)}, bf16[16,3072]{1,0:T(8,128)(2,1)S(1)}, u32[]{:S(2)}, u32[]{:S(2)}) %collective-permute-start.22) | collective-permute-done | bytes 98336 | tf_op jit(solution)/shard_map/ppermute | solution.py:298
  54.2 3.7 %collective-permute-start.25 = (bf16[16,3200]{1,0:T(8,128)(2,1)S(1)}, bf16[16,3200]{1,0:T(8,128)(2,1)S(1)}, u32[]{:S(2)}, u32[]{:S(2)}) collective-permute-start(bf16[16,3200]{1,0:T(8,128)(2,1)S(1)} %finish.7), channel_id=1, source_target_pairs={{0,12},{1,13},{2,14},{3,15},{4,8},{5,9},{6,10},{7,11},{8,4},{9,5},... | collective-permute-start | bytes 307208 | tf_op jit(solution)/shard_map/ppermute | solution.py:344
  58.0 2.8 %collective-permute-done.25.packet.refs_6_ = bf16[16,3200]{1,0:T(8,128)(2,1)S(1)} collective-permute-done((bf16[16,3200]{1,0:T(8,128)(2,1)S(1)}, bf16[16,3200]{1,0:T(8,128)(2,1)S(1)}, u32[]{:S(2)}, u32[]{:S(2)}) %collective-permute-start.25) | collective-permute-done | bytes 102432 | tf_op jit(solution)/shard_map/ppermute | solution.py:344
  61.2 2.1 %collective-permute-start.28 = (bf16[16,3072]{1,0:T(8,128)(2,1)S(1)}, bf16[16,3072]{1,0:T(8,128)(2,1)S(1)}, u32[]{:S(2)}, u32[]{:S(2)}) collective-permute-start(bf16[16,3072]{1,0:T(8,128)(2,1)S(1)} %get-tuple-element.104.refs_0_), channel_id=1, source_target_pairs={{0,6},{1,7},{2,4},{3,5},{4,2},{5,3},{6,0},{7,1},{8,14},{9,15},{10,... | collective-permute-start | bytes 294920 | tf_op jit(solution)/shard_map/ppermute | solution.py:298
  64.8 2.9 %collective-permute-done.28.refs_3_ = bf16[16,3072]{1,0:T(8,128)(2,1)S(1)} collective-permute-done((bf16[16,3072]{1,0:T(8,128)(2,1)S(1)}, bf16[16,3072]{1,0:T(8,128)(2,1)S(1)}, u32[]{:S(2)}, u32[]{:S(2)}) %collective-permute-start.28) | collective-permute-done | bytes 98336 | tf_op jit(solution)/shard_map/ppermute | solution.py:298
  69.8 2.8 %block.8 = (f32[64,3072]{1,0:T(8,128)S(1)}, bf16[48,3072]{1,0:T(8,128)(2,1)S(1)}, bf16[16,3072]{1,0:T(8,128)(2,1)S(1)}, bf16[2,256,384]{2,1,0:T(8,128)(2,1)S(1)}) custom-call(s32[1]{0:T(128)} %bitcast.section.refs_0_, s32[2,6]{1,0:T(2,128)S(1)} %get-tuple-element.79.patch_flow, ...), custom_call_target="tpu_custom_call", output_to_operand_aliasing={{3}: (13, {})} | custom-call | flops 1207959552 | bytes 9437184 | tf_op jit(solution)/shard_map/block/pallas_call | solution.py:110
  74.4 2.4 %collective-permute-start.35 = (bf16[16,3072]{1,0:T(8,128)(2,1)S(1)}, bf16[16,3072]{1,0:T(8,128)(2,1)S(1)}, u32[]{:S(2)}, u32[]{:S(2)}) collective-permute-start(bf16[16,3072]{1,0:T(8,128)(2,1)S(1)} %split_last.8), channel_id=1, source_target_pairs={{0,6},{1,7},{2,4},{3,5},{4,2},{5,3},{6,0},{7,1},{8,14},{9,15},{10,... | collective-permute-start | bytes 294920 | tf_op jit(solution)/shard_map/ppermute | solution.py:298
  78.1 2.5 %collective-permute-done.35.refs_2_ = bf16[16,3072]{1,0:T(8,128)(2,1)S(1)} collective-permute-done((bf16[16,3072]{1,0:T(8,128)(2,1)S(1)}, bf16[16,3072]{1,0:T(8,128)(2,1)S(1)}, u32[]{:S(2)}, u32[]{:S(2)}) %collective-permute-start.35) | collective-permute-done | bytes 98336 | tf_op jit(solution)/shard_map/ppermute | solution.py:298
  80.5 1.6 collective-permute-done.36.refs_3_
  82.4 3.7 %collective-permute-start.38 = (bf16[16,3200]{1,0:T(8,128)(2,1)S(1)}, bf16[16,3200]{1,0:T(8,128)(2,1)S(1)}, u32[]{:S(2)}, u32[]{:S(2)}) collective-permute-start(bf16[16,3200]{1,0:T(8,128)(2,1)S(1)} %finish.8), channel_id=1, source_target_pairs={{0,12},{1,13},{2,14},{3,15},{4,8},{5,9},{6,10},{7,11},{8,4},{9,5},... | collective-permute-start | bytes 307208 | tf_op jit(solution)/shard_map/ppermute | solution.py:344
  86.1 2.9 %collective-permute-done.38.packet.refs_6_ = bf16[16,3200]{1,0:T(8,128)(2,1)S(1)} collective-permute-done((bf16[16,3200]{1,0:T(8,128)(2,1)S(1)}, bf16[16,3200]{1,0:T(8,128)(2,1)S(1)}, u32[]{:S(2)}, u32[]{:S(2)}) %collective-permute-start.38) | collective-permute-done | bytes 102432 | tf_op jit(solution)/shard_map/ppermute | solution.py:344
  89.5 3.0 %collective-permute-start.41 = (bf16[16,3072]{1,0:T(8,128)(2,1)S(1)}, bf16[16,3072]{1,0:T(8,128)(2,1)S(1)}, u32[]{:S(2)}, u32[]{:S(2)}) collective-permute-start(bf16[16,3072]{1,0:T(8,128)(2,1)S(1)} %get-tuple-element.113.refs_0_), channel_id=1, source_target_pairs={{0,6},{1,7},{2,4},{3,5},{4,2},{5,3},{6,0},{7,1},{8,14},{9,15},{10,... | collective-permute-start | bytes 294920 | tf_op jit(solution)/shard_map/ppermute | solution.py:298
  93.1 2.5 %collective-permute-done.41.refs_3_ = bf16[16,3072]{1,0:T(8,128)(2,1)S(1)} collective-permute-done((bf16[16,3072]{1,0:T(8,128)(2,1)S(1)}, bf16[16,3072]{1,0:T(8,128)(2,1)S(1)}, u32[]{:S(2)}, u32[]{:S(2)}) %collective-permute-start.41) | collective-permute-done | bytes 98336 | tf_op jit(solution)/shard_map/ppermute | solution.py:298
  95.7 1.4 collective-permute-done.40.refs_2_
  98.6 2.8 %block.9 = (f32[64,3072]{1,0:T(8,128)S(1)}, bf16[48,3072]{1,0:T(8,128)(2,1)S(1)}, bf16[16,3072]{1,0:T(8,128)(2,1)S(1)}, bf16[2,256,384]{2,1,0:T(8,128)(2,1)S(1)}) custom-call(s32[1]{0:T(128)} %bitcast.section.refs_0_, s32[2,6]{1,0:T(2,128)S(1)} %get-tuple-element.79.patch_flow, ...), custom_call_target="tpu_custom_call", output_to_operand_aliasing={{3}: (13, {})} | custom-call | flops 1207959552 | bytes 9437184 | tf_op jit(solution)/shard_map/block/pallas_call | solution.py:110
  103.2 2.5 %collective-permute-start.48 = (bf16[16,3072]{1,0:T(8,128)(2,1)S(1)}, bf16[16,3072]{1,0:T(8,128)(2,1)S(1)}, u32[]{:S(2)}, u32[]{:S(2)}) collective-permute-start(bf16[16,3072]{1,0:T(8,128)(2,1)S(1)} %split_last.9), channel_id=1, source_target_pairs={{0,6},{1,7},{2,4},{3,5},{4,2},{5,3},{6,0},{7,1},{8,14},{9,15},{10,... | collective-permute-start | bytes 294920 | tf_op jit(solution)/shard_map/ppermute | solution.py:298
  106.9 2.7 %collective-permute-done.48.refs_2_ = bf16[16,3072]{1,0:T(8,128)(2,1)S(1)} collective-permute-done((bf16[16,3072]{1,0:T(8,128)(2,1)S(1)}, bf16[16,3072]{1,0:T(8,128)(2,1)S(1)}, u32[]{:S(2)}, u32[]{:S(2)}) %collective-permute-start.48) | collective-permute-done | bytes 98336 | tf_op jit(solution)/shard_map/ppermute | solution.py:298
  111.4 3.1 %collective-permute-start.51 = (bf16[16,3200]{1,0:T(8,128)(2,1)S(1)}, bf16[16,3200]{1,0:T(8,128)(2,1)S(1)}, u32[]{:S(2)}, u32[]{:S(2)}) collective-permute-start(bf16[16,3200]{1,0:T(8,128)(2,1)S(1)} %finish.9), channel_id=1, source_target_pairs={{0,12},{1,13},{2,14},{3,15},{4,8},{5,9},{6,10},{7,11},{8,4},{9,5},... | collective-permute-start | bytes 307208 | tf_op jit(solution)/shard_map/ppermute | solution.py:344
  114.5 3.4 %collective-permute-done.51.packet.refs_6_ = bf16[16,3200]{1,0:T(8,128)(2,1)S(1)} collective-permute-done((bf16[16,3200]{1,0:T(8,128)(2,1)S(1)}, bf16[16,3200]{1,0:T(8,128)(2,1)S(1)}, u32[]{:S(2)}, u32[]{:S(2)}) %collective-permute-start.51) | collective-permute-done | bytes 102432 | tf_op jit(solution)/shard_map/ppermute | solution.py:344
  118.3 2.4 %collective-permute-start.54 = (bf16[16,3072]{1,0:T(8,128)(2,1)S(1)}, bf16[16,3072]{1,0:T(8,128)(2,1)S(1)}, u32[]{:S(2)}, u32[]{:S(2)}) collective-permute-start(bf16[16,3072]{1,0:T(8,128)(2,1)S(1)} %get-tuple-element.122.refs_0_), channel_id=1, source_target_pairs={{0,6},{1,7},{2,4},{3,5},{4,2},{5,3},{6,0},{7,1},{8,14},{9,15},{10,... | collective-permute-start | bytes 294920 | tf_op jit(solution)/shard_map/ppermute | solution.py:298
  121.9 3.1 %collective-permute-done.54.refs_3_ = bf16[16,3072]{1,0:T(8,128)(2,1)S(1)} collective-permute-done((bf16[16,3072]{1,0:T(8,128)(2,1)S(1)}, bf16[16,3072]{1,0:T(8,128)(2,1)S(1)}, u32[]{:S(2)}, u32[]{:S(2)}) %collective-permute-start.54) | collective-permute-done | bytes 98336 | tf_op jit(solution)/shard_map/ppermute | solution.py:298
  127.0 2.8 %block.10 = (f32[64,3072]{1,0:T(8,128)S(1)}, bf16[48,3072]{1,0:T(8,128)(2,1)S(1)}, bf16[16,3072]{1,0:T(8,128)(2,1)S(1)}, bf16[2,256,384]{2,1,0:T(8,128)(2,1)S(1)}) custom-call(s32[1]{0:T(128)} %bitcast.section.refs_0_, s32[2,6]{1,0:T(2,128)S(1)} %get-tuple-element.79.patch_flow, ...), custom_call_target="tpu_custom_call", output_to_operand_aliasing={{3}: (13, {})} | custom-call | flops 1207959552 | bytes 9437184 | tf_op jit(solution)/shard_map/block/pallas_call | solution.py:110
  131.6 2.3 %collective-permute-start.61 = (bf16[16,3072]{1,0:T(8,128)(2,1)S(1)}, bf16[16,3072]{1,0:T(8,128)(2,1)S(1)}, u32[]{:S(2)}, u32[]{:S(2)}) collective-permute-start(bf16[16,3072]{1,0:T(8,128)(2,1)S(1)} %split_last.10), channel_id=1, source_target_pairs={{0,6},{1,7},{2,4},{3,5},{4,2},{5,3},{6,0},{7,1},{8,14},{9,15},{10,... | collective-permute-start | bytes 294920 | tf_op jit(solution)/shard_map/ppermute | solution.py:298
  135.3 2.7 %collective-permute-done.61.refs_2_ = bf16[16,3072]{1,0:T(8,128)(2,1)S(1)} collective-permute-done((bf16[16,3072]{1,0:T(8,128)(2,1)S(1)}, bf16[16,3072]{1,0:T(8,128)(2,1)S(1)}, u32[]{:S(2)}, u32[]{:S(2)}) %collective-permute-start.61) | collective-permute-done | bytes 98336 | tf_op jit(solution)/shard_map/ppermute | solution.py:298
  138.0 1.3 collective-permute-done.62.refs_3_
  139.7 2.9 %collective-permute-start.64 = (bf16[16,3200]{1,0:T(8,128)(2,1)S(1)}, bf16[16,3200]{1,0:T(8,128)(2,1)S(1)}, u32[]{:S(2)}, u32[]{:S(2)}) collective-permute-start(bf16[16,3200]{1,0:T(8,128)(2,1)S(1)} %finish.10), channel_id=1, source_target_pairs={{0,12},{1,13},{2,14},{3,15},{4,8},{5,9},{6,10},{7,11},{8,4},{9,5},... | collective-permute-start | bytes 307208 | tf_op jit(solution)/shard_map/ppermute | solution.py:344
  142.6 3.6 %collective-permute-done.64.packet.refs_6_ = bf16[16,3200]{1,0:T(8,128)(2,1)S(1)} collective-permute-done((bf16[16,3200]{1,0:T(8,128)(2,1)S(1)}, bf16[16,3200]{1,0:T(8,128)(2,1)S(1)}, u32[]{:S(2)}, u32[]{:S(2)}) %collective-permute-start.64) | collective-permute-done | bytes 102432 | tf_op jit(solution)/shard_map/ppermute | solution.py:344
  146.6 2.7 %collective-permute-start.67 = (bf16[16,3072]{1,0:T(8,128)(2,1)S(1)}, bf16[16,3072]{1,0:T(8,128)(2,1)S(1)}, u32[]{:S(2)}, u32[]{:S(2)}) collective-permute-start(bf16[16,3072]{1,0:T(8,128)(2,1)S(1)} %get-tuple-element.131.refs_0_), channel_id=1, source_target_pairs={{0,6},{1,7},{2,4},{3,5},{4,2},{5,3},{6,0},{7,1},{8,14},{9,15},{10,... | collective-permute-start | bytes 294920 | tf_op jit(solution)/shard_map/ppermute | solution.py:298
  150.2 2.8 %collective-permute-done.67.refs_3_ = bf16[16,3072]{1,0:T(8,128)(2,1)S(1)} collective-permute-done((bf16[16,3072]{1,0:T(8,128)(2,1)S(1)}, bf16[16,3072]{1,0:T(8,128)(2,1)S(1)}, u32[]{:S(2)}, u32[]{:S(2)}) %collective-permute-start.67) | collective-permute-done | bytes 98336 | tf_op jit(solution)/shard_map/ppermute | solution.py:298
  155.5 2.8 %block.11 = (f32[64,3072]{1,0:T(8,128)S(1)}, bf16[48,3072]{1,0:T(8,128)(2,1)S(1)}, bf16[16,3072]{1,0:T(8,128)(2,1)S(1)}, bf16[2,256,384]{2,1,0:T(8,128)(2,1)S(1)}) custom-call(s32[1]{0:T(128)} %bitcast.section.refs_0_, s32[2,6]{1,0:T(2,128)S(1)} %get-tuple-element.79.patch_flow, ...), custom_call_target="tpu_custom_call", output_to_operand_aliasing={{3}: (13, {})} | custom-call | flops 1207959552 | bytes 9437184 | tf_op jit(solution)/shard_map/block/pallas_call | solution.py:110
  160.1 2.2 %collective-permute-start.74 = (bf16[16,3072]{1,0:T(8,128)(2,1)S(1)}, bf16[16,3072]{1,0:T(8,128)(2,1)S(1)}, u32[]{:S(2)}, u32[]{:S(2)}) collective-permute-start(bf16[16,3072]{1,0:T(8,128)(2,1)S(1)} %split_last.11), channel_id=1, source_target_pairs={{0,6},{1,7},{2,4},{3,5},{4,2},{5,3},{6,0},{7,1},{8,14},{9,15},{10,... | collective-permute-start | bytes 294920 | tf_op jit(solution)/shard_map/ppermute | solution.py:298
  163.8 2.9 %collective-permute-done.74.refs_2_ = bf16[16,3072]{1,0:T(8,128)(2,1)S(1)} collective-permute-done((bf16[16,3072]{1,0:T(8,128)(2,1)S(1)}, bf16[16,3072]{1,0:T(8,128)(2,1)S(1)}, u32[]{:S(2)}, u32[]{:S(2)}) %collective-permute-start.74) | collective-permute-done | bytes 98336 | tf_op jit(solution)/shard_map/ppermute | solution.py:298
  168.3 2.9 %collective-permute-start.77 = (bf16[16,3200]{1,0:T(8,128)(2,1)S(1)}, bf16[16,3200]{1,0:T(8,128)(2,1)S(1)}, u32[]{:S(2)}, u32[]{:S(2)}) collective-permute-start(bf16[16,3200]{1,0:T(8,128)(2,1)S(1)} %finish.11), channel_id=1, source_target_pairs={{0,12},{1,13},{2,14},{3,15},{4,8},{5,9},{6,10},{7,11},{8,4},{9,5},... | collective-permute-start | bytes 307208 | tf_op jit(solution)/shard_map/ppermute | solution.py:344
  171.3 3.6 %collective-permute-done.77.packet = bf16[16,3200]{1,0:T(8,128)(2,1)S(1)} collective-permute-done((bf16[16,3200]{1,0:T(8,128)(2,1)S(1)}, bf16[16,3200]{1,0:T(8,128)(2,1)S(1)}, u32[]{:S(2)}, u32[]{:S(2)}) %collective-permute-start.77) | collective-permute-done | bytes 102432 | tf_op jit(solution)/shard_map/ppermute | solution.py:344
  (149 shorter events, 44.7 us)
Async XLA Ops:
  0.7 8.7 %collective-permute-start.2 = (bf16[16,3072]{1,0:T(8,128)(2,1)}, bf16[16,3072]{1,0:T(8,128)(2,1)S(1)}, u32[]{:S(2)}, u32[]{:S(2)}) collective-permute-start(bf16[16,3072]{1,0:T(8,128)(2,1)} %refs_5_.1), channel_id=1, source_target_pairs={{0,6},{1,7},{2,4},{3,5},{4,2},{5,3},{6,0},{7,1},{8,14},{9,15},{10,... | collective-permute-start | bytes 294920 | tf_op jit(solution)/shard_map/ppermute | solution.py:298
  4.7 5.4 %collective-permute-start.1 = (bf16[16,3072]{1,0:T(8,128)(2,1)}, bf16[16,3072]{1,0:T(8,128)(2,1)S(1)}, u32[]{:S(2)}, u32[]{:S(2)}) collective-permute-start(bf16[16,3072]{1,0:T(8,128)(2,1)} %refs_5_.1), channel_id=1, source_target_pairs={{0,4},{1,5},{2,6},{3,7},{4,0},{5,1},{6,2},{7,3},{8,12},{9,13},{10,... | collective-permute-start | bytes 294920 | tf_op jit(solution)/shard_map/ppermute | solution.py:298
  5.2 4.9 %collective-permute-start = (bf16[16,3072]{1,0:T(8,128)(2,1)}, bf16[16,3072]{1,0:T(8,128)(2,1)S(1)}, u32[]{:S(2)}, u32[]{:S(2)}) collective-permute-start(bf16[16,3072]{1,0:T(8,128)(2,1)} %refs_5_.1), channel_id=1, source_target_pairs={{0,2},{1,3},{2,0},{3,1},{4,6},{5,7},{6,4},{7,5},{8,10},{9,11},{10,... | collective-permute-start | bytes 294920 | tf_op jit(solution)/shard_map/ppermute | solution.py:298
  15.2 4.3 %collective-permute-start.7 = (bf16[48,3072]{1,0:T(8,128)(2,1)S(1)}, bf16[48,3072]{1,0:T(8,128)(2,1)S(1)}, u32[]{:S(2)}, u32[]{:S(2)}) collective-permute-start(bf16[48,3072]{1,0:T(8,128)(2,1)S(1)} %get-tuple-element.90), channel_id=1, source_target_pairs={{0,1},{1,0},{2,3},{3,2},{4,5},{5,4},{6,7},{7,6},{8,9},{9,8},{10,11... | collective-permute-start | bytes 884744 | tf_op jit(solution)/shard_map/ppermute | solution.py:298
  17.0 6.6 %collective-permute-start.9 = (bf16[16,3072]{1,0:T(8,128)(2,1)S(1)}, bf16[16,3072]{1,0:T(8,128)(2,1)S(1)}, u32[]{:S(2)}, u32[]{:S(2)}) collective-permute-start(bf16[16,3072]{1,0:T(8,128)(2,1)S(1)} %split_last.6), channel_id=1, source_target_pairs={{0,6},{1,7},{2,4},{3,5},{4,2},{5,3},{6,0},{7,1},{8,14},{9,15},{10,... | collective-permute-start | bytes 294920 | tf_op jit(solution)/shard_map/ppermute | solution.py:298
  19.6 5.5 %collective-permute-start.10 = (bf16[16,3072]{1,0:T(8,128)(2,1)S(1)}, bf16[16,3072]{1,0:T(8,128)(2,1)S(1)}, u32[]{:S(2)}, u32[]{:S(2)}) collective-permute-start(bf16[16,3072]{1,0:T(8,128)(2,1)S(1)} %get-tuple-element.93), channel_id=1, source_target_pairs={{0,4},{1,5},{2,6},{3,7},{4,0},{5,1},{6,2},{7,3},{8,12},{9,13},{10,... | collective-permute-start | bytes 294920 | tf_op jit(solution)/shard_map/ppermute | solution.py:298
  20.1 5.1 %collective-permute-start.11 = (bf16[16,3072]{1,0:T(8,128)(2,1)S(1)}, bf16[16,3072]{1,0:T(8,128)(2,1)S(1)}, u32[]{:S(2)}, u32[]{:S(2)}) collective-permute-start(bf16[16,3072]{1,0:T(8,128)(2,1)S(1)} %get-tuple-element.94), channel_id=1, source_target_pairs={{0,2},{1,3},{2,0},{3,1},{4,6},{5,7},{6,4},{7,5},{8,10},{9,11},{10,... | collective-permute-start | bytes 294920 | tf_op jit(solution)/shard_map/ppermute | solution.py:298
  25.3 6.9 %collective-permute-start.12 = (bf16[16,3200]{1,0:T(8,128)(2,1)S(1)}, bf16[16,3200]{1,0:T(8,128)(2,1)S(1)}, u32[]{:S(2)}, u32[]{:S(2)}) collective-permute-start(bf16[16,3200]{1,0:T(8,128)(2,1)S(1)} %finish.6), channel_id=1, source_target_pairs={{0,12},{1,13},{2,14},{3,15},{4,8},{5,9},{6,10},{7,11},{8,4},{9,5},... | collective-permute-start | bytes 307208 | tf_op jit(solution)/shard_map/ppermute | solution.py:344
  32.6 6.0 %collective-permute-start.15 = (bf16[16,3072]{1,0:T(8,128)(2,1)S(1)}, bf16[16,3072]{1,0:T(8,128)(2,1)S(1)}, u32[]{:S(2)}, u32[]{:S(2)}) collective-permute-start(bf16[16,3072]{1,0:T(8,128)(2,1)S(1)} %get-tuple-element.95.refs_0_), channel_id=1, source_target_pairs={{0,6},{1,7},{2,4},{3,5},{4,2},{5,3},{6,0},{7,1},{8,14},{9,15},{10,... | collective-permute-start | bytes 294920 | tf_op jit(solution)/shard_map/ppermute | solution.py:298
  35.3 4.7 %collective-permute-start.14 = (bf16[16,3072]{1,0:T(8,128)(2,1)S(1)}, bf16[16,3072]{1,0:T(8,128)(2,1)S(1)}, u32[]{:S(2)}, u32[]{:S(2)}) collective-permute-start(bf16[16,3072]{1,0:T(8,128)(2,1)S(1)} %get-tuple-element.95.refs_0_), channel_id=1, source_target_pairs={{0,4},{1,5},{2,6},{3,7},{4,0},{5,1},{6,2},{7,3},{8,12},{9,13},{10,... | collective-permute-start | bytes 294920 | tf_op jit(solution)/shard_map/ppermute | solution.py:298
  35.6 4.6 %collective-permute-start.13 = (bf16[16,3072]{1,0:T(8,128)(2,1)S(1)}, bf16[16,3072]{1,0:T(8,128)(2,1)S(1)}, u32[]{:S(2)}, u32[]{:S(2)}) collective-permute-start(bf16[16,3072]{1,0:T(8,128)(2,1)S(1)} %get-tuple-element.95.refs_0_), channel_id=1, source_target_pairs={{0,2},{1,3},{2,0},{3,1},{4,6},{5,7},{6,4},{7,5},{8,10},{9,11},{10,... | collective-permute-start | bytes 294920 | tf_op jit(solution)/shard_map/ppermute | solution.py:298
  36.2 4.3 %collective-permute-start.16 = (bf16[16,3072]{1,0:T(8,128)(2,1)S(1)}, bf16[16,3072]{1,0:T(8,128)(2,1)S(1)}, u32[]{:S(2)}, u32[]{:S(2)}) collective-permute-start(bf16[16,3072]{1,0:T(8,128)(2,1)S(1)} %get-tuple-element.95.refs_0_), channel_id=1, source_target_pairs={{0,1},{1,0},{2,3},{3,2},{4,5},{5,4},{6,7},{7,6},{8,9},{9,8},{10,11... | collective-permute-start | bytes 294920 | tf_op jit(solution)/shard_map/ppermute | solution.py:298
  46.1 6.5 %collective-permute-start.22 = (bf16[16,3072]{1,0:T(8,128)(2,1)S(1)}, bf16[16,3072]{1,0:T(8,128)(2,1)S(1)}, u32[]{:S(2)}, u32[]{:S(2)}) collective-permute-start(bf16[16,3072]{1,0:T(8,128)(2,1)S(1)} %split_last.7), channel_id=1, source_target_pairs={{0,6},{1,7},{2,4},{3,5},{4,2},{5,3},{6,0},{7,1},{8,14},{9,15},{10,... | collective-permute-start | bytes 294920 | tf_op jit(solution)/shard_map/ppermute | solution.py:298
  48.2 5.4 %collective-permute-start.23 = (bf16[16,3072]{1,0:T(8,128)(2,1)S(1)}, bf16[16,3072]{1,0:T(8,128)(2,1)S(1)}, u32[]{:S(2)}, u32[]{:S(2)}) collective-permute-start(bf16[16,3072]{1,0:T(8,128)(2,1)S(1)} %get-tuple-element.101), channel_id=1, source_target_pairs={{0,4},{1,5},{2,6},{3,7},{4,0},{5,1},{6,2},{7,3},{8,12},{9,13},{10,... | collective-permute-start | bytes 294920 | tf_op jit(solution)/shard_map/ppermute | solution.py:298
  48.8 5.3 %collective-permute-start.24 = (bf16[16,3072]{1,0:T(8,128)(2,1)S(1)}, bf16[16,3072]{1,0:T(8,128)(2,1)S(1)}, u32[]{:S(2)}, u32[]{:S(2)}) collective-permute-start(bf16[16,3072]{1,0:T(8,128)(2,1)S(1)} %get-tuple-element.102), channel_id=1, source_target_pairs={{0,2},{1,3},{2,0},{3,1},{4,6},{5,7},{6,4},{7,5},{8,10},{9,11},{10,... | collective-permute-start | bytes 294920 | tf_op jit(solution)/shard_map/ppermute | solution.py:298
  54.2 6.5 %collective-permute-start.25 = (bf16[16,3200]{1,0:T(8,128)(2,1)S(1)}, bf16[16,3200]{1,0:T(8,128)(2,1)S(1)}, u32[]{:S(2)}, u32[]{:S(2)}) collective-permute-start(bf16[16,3200]{1,0:T(8,128)(2,1)S(1)} %finish.7), channel_id=1, source_target_pairs={{0,12},{1,13},{2,14},{3,15},{4,8},{5,9},{6,10},{7,11},{8,4},{9,5},... | collective-permute-start | bytes 307208 | tf_op jit(solution)/shard_map/ppermute | solution.py:344
  61.2 6.4 %collective-permute-start.28 = (bf16[16,3072]{1,0:T(8,128)(2,1)S(1)}, bf16[16,3072]{1,0:T(8,128)(2,1)S(1)}, u32[]{:S(2)}, u32[]{:S(2)}) collective-permute-start(bf16[16,3072]{1,0:T(8,128)(2,1)S(1)} %get-tuple-element.104.refs_0_), channel_id=1, source_target_pairs={{0,6},{1,7},{2,4},{3,5},{4,2},{5,3},{6,0},{7,1},{8,14},{9,15},{10,... | collective-permute-start | bytes 294920 | tf_op jit(solution)/shard_map/ppermute | solution.py:298
  63.3 4.7 %collective-permute-start.27 = (bf16[16,3072]{1,0:T(8,128)(2,1)S(1)}, bf16[16,3072]{1,0:T(8,128)(2,1)S(1)}, u32[]{:S(2)}, u32[]{:S(2)}) collective-permute-start(bf16[16,3072]{1,0:T(8,128)(2,1)S(1)} %get-tuple-element.104.refs_0_), channel_id=1, source_target_pairs={{0,4},{1,5},{2,6},{3,7},{4,0},{5,1},{6,2},{7,3},{8,12},{9,13},{10,... | collective-permute-start | bytes 294920 | tf_op jit(solution)/shard_map/ppermute | solution.py:298
  63.7 4.8 %collective-permute-start.26 = (bf16[16,3072]{1,0:T(8,128)(2,1)S(1)}, bf16[16,3072]{1,0:T(8,128)(2,1)S(1)}, u32[]{:S(2)}, u32[]{:S(2)}) collective-permute-start(bf16[16,3072]{1,0:T(8,128)(2,1)S(1)} %get-tuple-element.104.refs_0_), channel_id=1, source_target_pairs={{0,2},{1,3},{2,0},{3,1},{4,6},{5,7},{6,4},{7,5},{8,10},{9,11},{10,... | collective-permute-start | bytes 294920 | tf_op jit(solution)/shard_map/ppermute | solution.py:298
  72.6 4.2 %collective-permute-start.33 = (bf16[48,3072]{1,0:T(8,128)(2,1)S(1)}, bf16[48,3072]{1,0:T(8,128)(2,1)S(1)}, u32[]{:S(2)}, u32[]{:S(2)}) collective-permute-start(bf16[48,3072]{1,0:T(8,128)(2,1)S(1)} %get-tuple-element.107), channel_id=1, source_target_pairs={{0,1},{1,0},{2,3},{3,2},{4,5},{5,4},{6,7},{7,6},{8,9},{9,8},{10,11... | collective-permute-start | bytes 884744 | tf_op jit(solution)/shard_map/ppermute | solution.py:298
  74.4 6.2 %collective-permute-start.35 = (bf16[16,3072]{1,0:T(8,128)(2,1)S(1)}, bf16[16,3072]{1,0:T(8,128)(2,1)S(1)}, u32[]{:S(2)}, u32[]{:S(2)}) collective-permute-start(bf16[16,3072]{1,0:T(8,128)(2,1)S(1)} %split_last.8), channel_id=1, source_target_pairs={{0,6},{1,7},{2,4},{3,5},{4,2},{5,3},{6,0},{7,1},{8,14},{9,15},{10,... | collective-permute-start | bytes 294920 | tf_op jit(solution)/shard_map/ppermute | solution.py:298
  76.9 5.3 %collective-permute-start.36 = (bf16[16,3072]{1,0:T(8,128)(2,1)S(1)}, bf16[16,3072]{1,0:T(8,128)(2,1)S(1)}, u32[]{:S(2)}, u32[]{:S(2)}) collective-permute-start(bf16[16,3072]{1,0:T(8,128)(2,1)S(1)} %get-tuple-element.110), channel_id=1, source_target_pairs={{0,4},{1,5},{2,6},{3,7},{4,0},{5,1},{6,2},{7,3},{8,12},{9,13},{10,... | collective-permute-start | bytes 294920 | tf_op jit(solution)/shard_map/ppermute | solution.py:298
  77.2 5.1 %collective-permute-start.37 = (bf16[16,3072]{1,0:T(8,128)(2,1)S(1)}, bf16[16,3072]{1,0:T(8,128)(2,1)S(1)}, u32[]{:S(2)}, u32[]{:S(2)}) collective-permute-start(bf16[16,3072]{1,0:T(8,128)(2,1)S(1)} %get-tuple-element.111), channel_id=1, source_target_pairs={{0,2},{1,3},{2,0},{3,1},{4,6},{5,7},{6,4},{7,5},{8,10},{9,11},{10,... | collective-permute-start | bytes 294920 | tf_op jit(solution)/shard_map/ppermute | solution.py:298
  82.4 6.5 %collective-permute-start.38 = (bf16[16,3200]{1,0:T(8,128)(2,1)S(1)}, bf16[16,3200]{1,0:T(8,128)(2,1)S(1)}, u32[]{:S(2)}, u32[]{:S(2)}) collective-permute-start(bf16[16,3200]{1,0:T(8,128)(2,1)S(1)} %finish.8), channel_id=1, source_target_pairs={{0,12},{1,13},{2,14},{3,15},{4,8},{5,9},{6,10},{7,11},{8,4},{9,5},... | collective-permute-start | bytes 307208 | tf_op jit(solution)/shard_map/ppermute | solution.py:344
  89.5 6.1 %collective-permute-start.41 = (bf16[16,3072]{1,0:T(8,128)(2,1)S(1)}, bf16[16,3072]{1,0:T(8,128)(2,1)S(1)}, u32[]{:S(2)}, u32[]{:S(2)}) collective-permute-start(bf16[16,3072]{1,0:T(8,128)(2,1)S(1)} %get-tuple-element.113.refs_0_), channel_id=1, source_target_pairs={{0,6},{1,7},{2,4},{3,5},{4,2},{5,3},{6,0},{7,1},{8,14},{9,15},{10,... | collective-permute-start | bytes 294920 | tf_op jit(solution)/shard_map/ppermute | solution.py:298
  92.5 4.6 %collective-permute-start.40 = (bf16[16,3072]{1,0:T(8,128)(2,1)S(1)}, bf16[16,3072]{1,0:T(8,128)(2,1)S(1)}, u32[]{:S(2)}, u32[]{:S(2)}) collective-permute-start(bf16[16,3072]{1,0:T(8,128)(2,1)S(1)} %get-tuple-element.113.refs_0_), channel_id=1, source_target_pairs={{0,4},{1,5},{2,6},{3,7},{4,0},{5,1},{6,2},{7,3},{8,12},{9,13},{10,... | collective-permute-start | bytes 294920 | tf_op jit(solution)/shard_map/ppermute | solution.py:298
  92.5 4.7 %collective-permute-start.39 = (bf16[16,3072]{1,0:T(8,128)(2,1)S(1)}, bf16[16,3072]{1,0:T(8,128)(2,1)S(1)}, u32[]{:S(2)}, u32[]{:S(2)}) collective-permute-start(bf16[16,3072]{1,0:T(8,128)(2,1)S(1)} %get-tuple-element.113.refs_0_), channel_id=1, source_target_pairs={{0,2},{1,3},{2,0},{3,1},{4,6},{5,7},{6,4},{7,5},{8,10},{9,11},{10,... | collective-permute-start | bytes 294920 | tf_op jit(solution)/shard_map/ppermute | solution.py:298
  93.1 4.5 %collective-permute-start.42 = (bf16[16,3072]{1,0:T(8,128)(2,1)S(1)}, bf16[16,3072]{1,0:T(8,128)(2,1)S(1)}, u32[]{:S(2)}, u32[]{:S(2)}) collective-permute-start(bf16[16,3072]{1,0:T(8,128)(2,1)S(1)} %get-tuple-element.113.refs_0_), channel_id=1, source_target_pairs={{0,1},{1,0},{2,3},{3,2},{4,5},{5,4},{6,7},{7,6},{8,9},{9,8},{10,11... | collective-permute-start | bytes 294920 | tf_op jit(solution)/shard_map/ppermute | solution.py:298
  101.3 4.4 %collective-permute-start.46 = (bf16[48,3072]{1,0:T(8,128)(2,1)S(1)}, bf16[48,3072]{1,0:T(8,128)(2,1)S(1)}, u32[]{:S(2)}, u32[]{:S(2)}) collective-permute-start(bf16[48,3072]{1,0:T(8,128)(2,1)S(1)} %get-tuple-element.116), channel_id=1, source_target_pairs={{0,1},{1,0},{2,3},{3,2},{4,5},{5,4},{6,7},{7,6},{8,9},{9,8},{10,11... | collective-permute-start | bytes 884744 | tf_op jit(solution)/shard_map/ppermute | solution.py:298
  103.2 6.5 %collective-permute-start.48 = (bf16[16,3072]{1,0:T(8,128)(2,1)S(1)}, bf16[16,3072]{1,0:T(8,128)(2,1)S(1)}, u32[]{:S(2)}, u32[]{:S(2)}) collective-permute-start(bf16[16,3072]{1,0:T(8,128)(2,1)S(1)} %split_last.9), channel_id=1, source_target_pairs={{0,6},{1,7},{2,4},{3,5},{4,2},{5,3},{6,0},{7,1},{8,14},{9,15},{10,... | collective-permute-start | bytes 294920 | tf_op jit(solution)/shard_map/ppermute | solution.py:298
  105.8 4.9 %collective-permute-start.49 = (bf16[16,3072]{1,0:T(8,128)(2,1)S(1)}, bf16[16,3072]{1,0:T(8,128)(2,1)S(1)}, u32[]{:S(2)}, u32[]{:S(2)}) collective-permute-start(bf16[16,3072]{1,0:T(8,128)(2,1)S(1)} %get-tuple-element.119), channel_id=1, source_target_pairs={{0,4},{1,5},{2,6},{3,7},{4,0},{5,1},{6,2},{7,3},{8,12},{9,13},{10,... | collective-permute-start | bytes 294920 | tf_op jit(solution)/shard_map/ppermute | solution.py:298
  105.8 5.4 %collective-permute-start.50 = (bf16[16,3072]{1,0:T(8,128)(2,1)S(1)}, bf16[16,3072]{1,0:T(8,128)(2,1)S(1)}, u32[]{:S(2)}, u32[]{:S(2)}) collective-permute-start(bf16[16,3072]{1,0:T(8,128)(2,1)S(1)} %get-tuple-element.120), channel_id=1, source_target_pairs={{0,2},{1,3},{2,0},{3,1},{4,6},{5,7},{6,4},{7,5},{8,10},{9,11},{10,... | collective-permute-start | bytes 294920 | tf_op jit(solution)/shard_map/ppermute | solution.py:298
  111.4 6.5 %collective-permute-start.51 = (bf16[16,3200]{1,0:T(8,128)(2,1)S(1)}, bf16[16,3200]{1,0:T(8,128)(2,1)S(1)}, u32[]{:S(2)}, u32[]{:S(2)}) collective-permute-start(bf16[16,3200]{1,0:T(8,128)(2,1)S(1)} %finish.9), channel_id=1, source_target_pairs={{0,12},{1,13},{2,14},{3,15},{4,8},{5,9},{6,10},{7,11},{8,4},{9,5},... | collective-permute-start | bytes 307208 | tf_op jit(solution)/shard_map/ppermute | solution.py:344
  118.3 6.6 %collective-permute-start.54 = (bf16[16,3072]{1,0:T(8,128)(2,1)S(1)}, bf16[16,3072]{1,0:T(8,128)(2,1)S(1)}, u32[]{:S(2)}, u32[]{:S(2)}) collective-permute-start(bf16[16,3072]{1,0:T(8,128)(2,1)S(1)} %get-tuple-element.122.refs_0_), channel_id=1, source_target_pairs={{0,6},{1,7},{2,4},{3,5},{4,2},{5,3},{6,0},{7,1},{8,14},{9,15},{10,... | collective-permute-start | bytes 294920 | tf_op jit(solution)/shard_map/ppermute | solution.py:298
  120.7 4.7 %collective-permute-start.53 = (bf16[16,3072]{1,0:T(8,128)(2,1)S(1)}, bf16[16,3072]{1,0:T(8,128)(2,1)S(1)}, u32[]{:S(2)}, u32[]{:S(2)}) collective-permute-start(bf16[16,3072]{1,0:T(8,128)(2,1)S(1)} %get-tuple-element.122.refs_0_), channel_id=1, source_target_pairs={{0,4},{1,5},{2,6},{3,7},{4,0},{5,1},{6,2},{7,3},{8,12},{9,13},{10,... | collective-permute-start | bytes 294920 | tf_op jit(solution)/shard_map/ppermute | solution.py:298
  120.7 5.0 %collective-permute-start.52 = (bf16[16,3072]{1,0:T(8,128)(2,1)S(1)}, bf16[16,3072]{1,0:T(8,128)(2,1)S(1)}, u32[]{:S(2)}, u32[]{:S(2)}) collective-permute-start(bf16[16,3072]{1,0:T(8,128)(2,1)S(1)} %get-tuple-element.122.refs_0_), channel_id=1, source_target_pairs={{0,2},{1,3},{2,0},{3,1},{4,6},{5,7},{6,4},{7,5},{8,10},{9,11},{10,... | collective-permute-start | bytes 294920 | tf_op jit(solution)/shard_map/ppermute | solution.py:298
  131.6 6.4 %collective-permute-start.61 = (bf16[16,3072]{1,0:T(8,128)(2,1)S(1)}, bf16[16,3072]{1,0:T(8,128)(2,1)S(1)}, u32[]{:S(2)}, u32[]{:S(2)}) collective-permute-start(bf16[16,3072]{1,0:T(8,128)(2,1)S(1)} %split_last.10), channel_id=1, source_target_pairs={{0,6},{1,7},{2,4},{3,5},{4,2},{5,3},{6,0},{7,1},{8,14},{9,15},{10,... | collective-permute-start | bytes 294920 | tf_op jit(solution)/shard_map/ppermute | solution.py:298
  134.0 5.3 %collective-permute-start.62 = (bf16[16,3072]{1,0:T(8,128)(2,1)S(1)}, bf16[16,3072]{1,0:T(8,128)(2,1)S(1)}, u32[]{:S(2)}, u32[]{:S(2)}) collective-permute-start(bf16[16,3072]{1,0:T(8,128)(2,1)S(1)} %get-tuple-element.128), channel_id=1, source_target_pairs={{0,4},{1,5},{2,6},{3,7},{4,0},{5,1},{6,2},{7,3},{8,12},{9,13},{10,... | collective-permute-start | bytes 294920 | tf_op jit(solution)/shard_map/ppermute | solution.py:298
  134.3 5.3 %collective-permute-start.63 = (bf16[16,3072]{1,0:T(8,128)(2,1)S(1)}, bf16[16,3072]{1,0:T(8,128)(2,1)S(1)}, u32[]{:S(2)}, u32[]{:S(2)}) collective-permute-start(bf16[16,3072]{1,0:T(8,128)(2,1)S(1)} %get-tuple-element.129), channel_id=1, source_target_pairs={{0,2},{1,3},{2,0},{3,1},{4,6},{5,7},{6,4},{7,5},{8,10},{9,11},{10,... | collective-permute-start | bytes 294920 | tf_op jit(solution)/shard_map/ppermute | solution.py:298
  139.7 6.5 %collective-permute-start.64 = (bf16[16,3200]{1,0:T(8,128)(2,1)S(1)}, bf16[16,3200]{1,0:T(8,128)(2,1)S(1)}, u32[]{:S(2)}, u32[]{:S(2)}) collective-permute-start(bf16[16,3200]{1,0:T(8,128)(2,1)S(1)} %finish.10), channel_id=1, source_target_pairs={{0,12},{1,13},{2,14},{3,15},{4,8},{5,9},{6,10},{7,11},{8,4},{9,5},... | collective-permute-start | bytes 307208 | tf_op jit(solution)/shard_map/ppermute | solution.py:344
  146.6 6.4 %collective-permute-start.67 = (bf16[16,3072]{1,0:T(8,128)(2,1)S(1)}, bf16[16,3072]{1,0:T(8,128)(2,1)S(1)}, u32[]{:S(2)}, u32[]{:S(2)}) collective-permute-start(bf16[16,3072]{1,0:T(8,128)(2,1)S(1)} %get-tuple-element.131.refs_0_), channel_id=1, source_target_pairs={{0,6},{1,7},{2,4},{3,5},{4,2},{5,3},{6,0},{7,1},{8,14},{9,15},{10,... | collective-permute-start | bytes 294920 | tf_op jit(solution)/shard_map/ppermute | solution.py:298
  149.3 4.8 %collective-permute-start.66 = (bf16[16,3072]{1,0:T(8,128)(2,1)S(1)}, bf16[16,3072]{1,0:T(8,128)(2,1)S(1)}, u32[]{:S(2)}, u32[]{:S(2)}) collective-permute-start(bf16[16,3072]{1,0:T(8,128)(2,1)S(1)} %get-tuple-element.131.refs_0_), channel_id=1, source_target_pairs={{0,4},{1,5},{2,6},{3,7},{4,0},{5,1},{6,2},{7,3},{8,12},{9,13},{10,... | collective-permute-start | bytes 294920 | tf_op jit(solution)/shard_map/ppermute | solution.py:298
  149.3 4.8 %collective-permute-start.65 = (bf16[16,3072]{1,0:T(8,128)(2,1)S(1)}, bf16[16,3072]{1,0:T(8,128)(2,1)S(1)}, u32[]{:S(2)}, u32[]{:S(2)}) collective-permute-start(bf16[16,3072]{1,0:T(8,128)(2,1)S(1)} %get-tuple-element.131.refs_0_), channel_id=1, source_target_pairs={{0,2},{1,3},{2,0},{3,1},{4,6},{5,7},{6,4},{7,5},{8,10},{9,11},{10,... | collective-permute-start | bytes 294920 | tf_op jit(solution)/shard_map/ppermute | solution.py:298
  150.2 4.4 %collective-permute-start.68 = (bf16[16,3072]{1,0:T(8,128)(2,1)S(1)}, bf16[16,3072]{1,0:T(8,128)(2,1)S(1)}, u32[]{:S(2)}, u32[]{:S(2)}) collective-permute-start(bf16[16,3072]{1,0:T(8,128)(2,1)S(1)} %get-tuple-element.131.refs_0_), channel_id=1, source_target_pairs={{0,1},{1,0},{2,3},{3,2},{4,5},{5,4},{6,7},{7,6},{8,9},{9,8},{10,11... | collective-permute-start | bytes 294920 | tf_op jit(solution)/shard_map/ppermute | solution.py:298
  160.1 6.6 %collective-permute-start.74 = (bf16[16,3072]{1,0:T(8,128)(2,1)S(1)}, bf16[16,3072]{1,0:T(8,128)(2,1)S(1)}, u32[]{:S(2)}, u32[]{:S(2)}) collective-permute-start(bf16[16,3072]{1,0:T(8,128)(2,1)S(1)} %split_last.11), channel_id=1, source_target_pairs={{0,6},{1,7},{2,4},{3,5},{4,2},{5,3},{6,0},{7,1},{8,14},{9,15},{10,... | collective-permute-start | bytes 294920 | tf_op jit(solution)/shard_map/ppermute | solution.py:298
  162.4 5.0 %collective-permute-start.75 = (bf16[16,3072]{1,0:T(8,128)(2,1)S(1)}, bf16[16,3072]{1,0:T(8,128)(2,1)S(1)}, u32[]{:S(2)}, u32[]{:S(2)}) collective-permute-start(bf16[16,3072]{1,0:T(8,128)(2,1)S(1)} %get-tuple-element.137), channel_id=1, source_target_pairs={{0,4},{1,5},{2,6},{3,7},{4,0},{5,1},{6,2},{7,3},{8,12},{9,13},{10,... | collective-permute-start | bytes 294920 | tf_op jit(solution)/shard_map/ppermute | solution.py:298
  162.6 5.6 %collective-permute-start.76 = (bf16[16,3072]{1,0:T(8,128)(2,1)S(1)}, bf16[16,3072]{1,0:T(8,128)(2,1)S(1)}, u32[]{:S(2)}, u32[]{:S(2)}) collective-permute-start(bf16[16,3072]{1,0:T(8,128)(2,1)S(1)} %get-tuple-element.138), channel_id=1, source_target_pairs={{0,2},{1,3},{2,0},{3,1},{4,6},{5,7},{6,4},{7,5},{8,10},{9,11},{10,... | collective-permute-start | bytes 294920 | tf_op jit(solution)/shard_map/ppermute | solution.py:298
  168.3 6.5 %collective-permute-start.77 = (bf16[16,3200]{1,0:T(8,128)(2,1)S(1)}, bf16[16,3200]{1,0:T(8,128)(2,1)S(1)}, u32[]{:S(2)}, u32[]{:S(2)}) collective-permute-start(bf16[16,3200]{1,0:T(8,128)(2,1)S(1)} %finish.11), channel_id=1, source_target_pairs={{0,12},{1,13},{2,14},{3,15},{4,8},{5,9},{6,10},{7,11},{8,4},{9,5},... | collective-permute-start | bytes 307208 | tf_op jit(solution)/shard_map/ppermute | solution.py:344
  (35 other events, 127.7 us)

commit v7 on v6

--- a/solution.py
+++ b/solution.py
@@ -7,6 +7,7 @@
 from jax.experimental import pallas as pl
 from jax.experimental.pallas import tpu as pltpu
 from jax.sharding import PartitionSpec as P
+
 
 HS = 128
 GROUP = 8
@@ -335,8 +336,10 @@
             own, w_qkv, w_out, gains, patch_flow, kv, mod = lax.optimization_barrier((own, *held))
         pieces = own + [exchange(piece, 1) for piece in own]
         kept, sent, ahead, kv = block(tick, section, patch_flow, pieces, mod, gains, w_qkv, w_out, kv)
-        ahead = split_last(kept, exchange(ahead, 1))
-        mine, *blocks = split(kept, exchange(sent, 1))
+        crossed = exchange(ahead, 1)
+        came = exchange(sent, 1)
+        ahead = split_last(kept, crossed)
+        mine, *blocks = split(kept, came)
         came = [exchange(rows, apart) for rows, apart in zip([*blocks, ahead], CHIP_STEPS)]
         parts = [mine] + came[::-1]
         packet = finish(section, parts, state, mod, final_mod, w_final, w_embed)

time: 176 us -> 176 us (level)
  no operation moved by 1% of the time
where the time goes in v7:
time: 176 us
  waiting for transfers between devices  78.7 us (45%)
  starting transfers between devices  70.8 us (40%)
  Pallas kernels  25.1 us (14%)
    ppermute x72, waiting for transfers between devices, exchange(): return lax.ppermute(value, 'section', route)  59.7 us
    ppermute x72, starting transfers between devices, exchange(): return lax.ppermute(value, 'section', route)  50.3 us
    ppermute x6, starting transfers between devices, body(): packet = lax.ppermute(packet, 'section', across if swaps else onward)  20.6 us
    ppermute x6, waiting for transfers between devices, body(): packet = lax.ppermute(packet, 'section', across if swaps else onward)  19 us
    pallas_call x6, Pallas kernels, block(): pl.pallas_call(functools.partial(block_kernel, tick), out_shape=like(((ha...  17 us
    pallas_call x1, Pallas kernels, load(): pl.pallas_call(functools.partial(load_kernel, count), out_shape=tuple((VM...  3.97 us
  transfers between devices with their start and end apart: 78, of which 62 were waited for; matrix products, arithmetic and copies ran while one was open for 0% of the time, Pallas kernels for 3%

profile of v7, /device:TPU:0, one launch (start us, length us, event | category | flops | bytes accessed | tf_op | source)
XLA Modules:
  0.0 175.7 jit_solution(6942986273870596647)
XLA Ops:
  0.7 4.1 %collective-permute-start.2 = (bf16[16,3072]{1,0:T(8,128)(2,1)}, bf16[16,3072]{1,0:T(8,128)(2,1)S(1)}, u32[]{:S(2)}, u32[]{:S(2)}) collective-permute-start(bf16[16,3072]{1,0:T(8,128)(2,1)} %refs_5_.1), channel_id=1, source_target_pairs={{0,6},{1,7},{2,4},{3,5},{4,2},{5,3},{6,0},{7,1},{8,14},{9,15},{10,... | collective-permute-start | bytes 294920 | tf_op jit(solution)/shard_map/ppermute | solution.py:299
  5.4 4.0 %load.1 = (bf16[3072,1152]{1,0:T(8,128)(2,1)S(1)}, bf16[384,3072]{1,0:T(8,128)(2,1)S(1)}, f32[2,2,128]{2,1,0:T(2,128)S(1)}, s32[2,6]{1,0:T(2,128)S(1)}, bf16[2,2...) custom-call(bf16[3,3072,384]{2,1,0:T(8,128)(2,1)} %refs_0_.1, bf16[384,3072]{1,0:T(8,128)(2,1)} %refs_1_.1, ...), custom_call_target="tpu_custom_call" | custom-call | bytes 19812448 | tf_op jit(solution)/shard_map/load/pallas_call | solution.py:265
  12.1 3.1 %block.6 = (f32[64,3072]{1,0:T(8,128)S(1)}, bf16[48,3072]{1,0:T(8,128)(2,1)S(1)}, bf16[16,3072]{1,0:T(8,128)(2,1)S(1)}, bf16[2,256,384]{2,1,0:T(8,128)(2,1)S(1)}) custom-call(s32[1]{0:T(128)} %bitcast.section.refs_0_, s32[2,6]{1,0:T(2,128)S(1)} %get-tuple-element.79.patch_flow, bf16[16,3072]{1,0:T(8,128)(2,1)S(1)} %copy-done.3, ...), custom_call_target="tpu_custom_call", output_to_operand_aliasing={{3}: (14, {})} | custom-call | flops 1207959552 | bytes 9437184 | tf_op jit(solution)/shard_map/block/pallas_call | solution.py:111
  15.8 1.2 collective-permute-done.8.came
  17.0 2.5 %collective-permute-start.9 = (bf16[16,3072]{1,0:T(8,128)(2,1)S(1)}, bf16[16,3072]{1,0:T(8,128)(2,1)S(1)}, u32[]{:S(2)}, u32[]{:S(2)}) collective-permute-start(bf16[16,3072]{1,0:T(8,128)(2,1)S(1)} %split_last.6), channel_id=1, source_target_pairs={{0,6},{1,7},{2,4},{3,5},{4,2},{5,3},{6,0},{7,1},{8,14},{9,15},{10,... | collective-permute-start | bytes 294920 | tf_op jit(solution)/shard_map/ppermute | solution.py:299
  20.7 2.9 %collective-permute-done.9.refs_2_ = bf16[16,3072]{1,0:T(8,128)(2,1)S(1)} collective-permute-done((bf16[16,3072]{1,0:T(8,128)(2,1)S(1)}, bf16[16,3072]{1,0:T(8,128)(2,1)S(1)}, u32[]{:S(2)}, u32[]{:S(2)}) %collective-permute-start.9) | collective-permute-done | bytes 98336 | tf_op jit(solution)/shard_map/ppermute | solution.py:299
  23.6 1.5 collective-permute-done.10.refs_3_
  25.3 4.2 %collective-permute-start.12 = (bf16[16,3200]{1,0:T(8,128)(2,1)S(1)}, bf16[16,3200]{1,0:T(8,128)(2,1)S(1)}, u32[]{:S(2)}, u32[]{:S(2)}) collective-permute-start(bf16[16,3200]{1,0:T(8,128)(2,1)S(1)} %finish.6), channel_id=1, source_target_pairs={{0,12},{1,13},{2,14},{3,15},{4,8},{5,9},{6,10},{7,11},{8,4},{9,5},... | collective-permute-start | bytes 307208 | tf_op jit(solution)/shard_map/ppermute | solution.py:347
  29.5 2.7 %collective-permute-done.12.packet.refs_6_ = bf16[16,3200]{1,0:T(8,128)(2,1)S(1)} collective-permute-done((bf16[16,3200]{1,0:T(8,128)(2,1)S(1)}, bf16[16,3200]{1,0:T(8,128)(2,1)S(1)}, u32[]{:S(2)}, u32[]{:S(2)}) %collective-permute-start.12) | collective-permute-done | bytes 102432 | tf_op jit(solution)/shard_map/ppermute | solution.py:347
  32.6 2.7 %collective-permute-start.15 = (bf16[16,3072]{1,0:T(8,128)(2,1)S(1)}, bf16[16,3072]{1,0:T(8,128)(2,1)S(1)}, u32[]{:S(2)}, u32[]{:S(2)}) collective-permute-start(bf16[16,3072]{1,0:T(8,128)(2,1)S(1)} %get-tuple-element.95.refs_0_), channel_id=1, source_target_pairs={{0,6},{1,7},{2,4},{3,5},{4,2},{5,3},{6,0},{7,1},{8,14},{9,15},{10,... | collective-permute-start | bytes 294920 | tf_op jit(solution)/shard_map/ppermute | solution.py:299
  36.2 2.4 %collective-permute-done.15.refs_3_ = bf16[16,3072]{1,0:T(8,128)(2,1)S(1)} collective-permute-done((bf16[16,3072]{1,0:T(8,128)(2,1)S(1)}, bf16[16,3072]{1,0:T(8,128)(2,1)S(1)}, u32[]{:S(2)}, u32[]{:S(2)}) %collective-permute-start.15) | collective-permute-done | bytes 98336 | tf_op jit(solution)/shard_map/ppermute | solution.py:299
  38.6 1.4 collective-permute-done.14.refs_2_
  41.5 2.8 %block.7 = (f32[64,3072]{1,0:T(8,128)S(1)}, bf16[48,3072]{1,0:T(8,128)(2,1)S(1)}, bf16[16,3072]{1,0:T(8,128)(2,1)S(1)}, bf16[2,256,384]{2,1,0:T(8,128)(2,1)S(1)}) custom-call(s32[1]{0:T(128)} %bitcast.section.refs_0_, s32[2,6]{1,0:T(2,128)S(1)} %get-tuple-element.79.patch_flow, ...), custom_call_target="tpu_custom_call", output_to_operand_aliasing={{3}: (13, {})} | custom-call | flops 1207959552 | bytes 9437184 | tf_op jit(solution)/shard_map/block/pallas_call | solution.py:111
  46.1 2.0 %collective-permute-start.22 = (bf16[16,3072]{1,0:T(8,128)(2,1)S(1)}, bf16[16,3072]{1,0:T(8,128)(2,1)S(1)}, u32[]{:S(2)}, u32[]{:S(2)}) collective-permute-start(bf16[16,3072]{1,0:T(8,128)(2,1)S(1)} %split_last.7), channel_id=1, source_target_pairs={{0,6},{1,7},{2,4},{3,5},{4,2},{5,3},{6,0},{7,1},{8,14},{9,15},{10,... | collective-permute-start | bytes 294920 | tf_op jit(solution)/shard_map/ppermute | solution.py:299
  49.8 2.8 %collective-permute-done.22.refs_2_ = bf16[16,3072]{1,0:T(8,128)(2,1)S(1)} collective-permute-done((bf16[16,3072]{1,0:T(8,128)(2,1)S(1)}, bf16[16,3072]{1,0:T(8,128)(2,1)S(1)}, u32[]{:S(2)}, u32[]{:S(2)}) %collective-permute-start.22) | collective-permute-done | bytes 98336 | tf_op jit(solution)/shard_map/ppermute | solution.py:299
  54.2 3.7 %collective-permute-start.25 = (bf16[16,3200]{1,0:T(8,128)(2,1)S(1)}, bf16[16,3200]{1,0:T(8,128)(2,1)S(1)}, u32[]{:S(2)}, u32[]{:S(2)}) collective-permute-start(bf16[16,3200]{1,0:T(8,128)(2,1)S(1)} %finish.7), channel_id=1, source_target_pairs={{0,12},{1,13},{2,14},{3,15},{4,8},{5,9},{6,10},{7,11},{8,4},{9,5},... | collective-permute-start | bytes 307208 | tf_op jit(solution)/shard_map/ppermute | solution.py:347
  58.0 2.8 %collective-permute-done.25.packet.refs_6_ = bf16[16,3200]{1,0:T(8,128)(2,1)S(1)} collective-permute-done((bf16[16,3200]{1,0:T(8,128)(2,1)S(1)}, bf16[16,3200]{1,0:T(8,128)(2,1)S(1)}, u32[]{:S(2)}, u32[]{:S(2)}) %collective-permute-start.25) | collective-permute-done | bytes 102432 | tf_op jit(solution)/shard_map/ppermute | solution.py:347
  61.2 2.1 %collective-permute-start.28 = (bf16[16,3072]{1,0:T(8,128)(2,1)S(1)}, bf16[16,3072]{1,0:T(8,128)(2,1)S(1)}, u32[]{:S(2)}, u32[]{:S(2)}) collective-permute-start(bf16[16,3072]{1,0:T(8,128)(2,1)S(1)} %get-tuple-element.104.refs_0_), channel_id=1, source_target_pairs={{0,6},{1,7},{2,4},{3,5},{4,2},{5,3},{6,0},{7,1},{8,14},{9,15},{10,... | collective-permute-start | bytes 294920 | tf_op jit(solution)/shard_map/ppermute | solution.py:299
  64.8 2.9 %collective-permute-done.28.refs_3_ = bf16[16,3072]{1,0:T(8,128)(2,1)S(1)} collective-permute-done((bf16[16,3072]{1,0:T(8,128)(2,1)S(1)}, bf16[16,3072]{1,0:T(8,128)(2,1)S(1)}, u32[]{:S(2)}, u32[]{:S(2)}) %collective-permute-start.28) | collective-permute-done | bytes 98336 | tf_op jit(solution)/shard_map/ppermute | solution.py:299
  69.8 2.8 %block.8 = (f32[64,3072]{1,0:T(8,128)S(1)}, bf16[48,3072]{1,0:T(8,128)(2,1)S(1)}, bf16[16,3072]{1,0:T(8,128)(2,1)S(1)}, bf16[2,256,384]{2,1,0:T(8,128)(2,1)S(1)}) custom-call(s32[1]{0:T(128)} %bitcast.section.refs_0_, s32[2,6]{1,0:T(2,128)S(1)} %get-tuple-element.79.patch_flow, ...), custom_call_target="tpu_custom_call", output_to_operand_aliasing={{3}: (13, {})} | custom-call | flops 1207959552 | bytes 9437184 | tf_op jit(solution)/shard_map/block/pallas_call | solution.py:111
  74.4 2.4 %collective-permute-start.35 = (bf16[16,3072]{1,0:T(8,128)(2,1)S(1)}, bf16[16,3072]{1,0:T(8,128)(2,1)S(1)}, u32[]{:S(2)}, u32[]{:S(2)}) collective-permute-start(bf16[16,3072]{1,0:T(8,128)(2,1)S(1)} %split_last.8), channel_id=1, source_target_pairs={{0,6},{1,7},{2,4},{3,5},{4,2},{5,3},{6,0},{7,1},{8,14},{9,15},{10,... | collective-permute-start | bytes 294920 | tf_op jit(solution)/shard_map/ppermute | solution.py:299
  78.1 2.5 %collective-permute-done.35.refs_2_ = bf16[16,3072]{1,0:T(8,128)(2,1)S(1)} collective-permute-done((bf16[16,3072]{1,0:T(8,128)(2,1)S(1)}, bf16[16,3072]{1,0:T(8,128)(2,1)S(1)}, u32[]{:S(2)}, u32[]{:S(2)}) %collective-permute-start.35) | collective-permute-done | bytes 98336 | tf_op jit(solution)/shard_map/ppermute | solution.py:299
  80.5 1.6 collective-permute-done.36.refs_3_
  82.4 3.7 %collective-permute-start.38 = (bf16[16,3200]{1,0:T(8,128)(2,1)S(1)}, bf16[16,3200]{1,0:T(8,128)(2,1)S(1)}, u32[]{:S(2)}, u32[]{:S(2)}) collective-permute-start(bf16[16,3200]{1,0:T(8,128)(2,1)S(1)} %finish.8), channel_id=1, source_target_pairs={{0,12},{1,13},{2,14},{3,15},{4,8},{5,9},{6,10},{7,11},{8,4},{9,5},... | collective-permute-start | bytes 307208 | tf_op jit(solution)/shard_map/ppermute | solution.py:347
  86.1 2.9 %collective-permute-done.38.packet.refs_6_ = bf16[16,3200]{1,0:T(8,128)(2,1)S(1)} collective-permute-done((bf16[16,3200]{1,0:T(8,128)(2,1)S(1)}, bf16[16,3200]{1,0:T(8,128)(2,1)S(1)}, u32[]{:S(2)}, u32[]{:S(2)}) %collective-permute-start.38) | collective-permute-done | bytes 102432 | tf_op jit(solution)/shard_map/ppermute | solution.py:347
  89.5 3.0 %collective-permute-start.41 = (bf16[16,3072]{1,0:T(8,128)(2,1)S(1)}, bf16[16,3072]{1,0:T(8,128)(2,1)S(1)}, u32[]{:S(2)}, u32[]{:S(2)}) collective-permute-start(bf16[16,3072]{1,0:T(8,128)(2,1)S(1)} %get-tuple-element.113.refs_0_), channel_id=1, source_target_pairs={{0,6},{1,7},{2,4},{3,5},{4,2},{5,3},{6,0},{7,1},{8,14},{9,15},{10,... | collective-permute-start | bytes 294920 | tf_op jit(solution)/shard_map/ppermute | solution.py:299
  93.1 2.5 %collective-permute-done.41.refs_3_ = bf16[16,3072]{1,0:T(8,128)(2,1)S(1)} collective-permute-done((bf16[16,3072]{1,0:T(8,128)(2,1)S(1)}, bf16[16,3072]{1,0:T(8,128)(2,1)S(1)}, u32[]{:S(2)}, u32[]{:S(2)}) %collective-permute-start.41) | collective-permute-done | bytes 98336 | tf_op jit(solution)/shard_map/ppermute | solution.py:299
  95.7 1.4 collective-permute-done.40.refs_2_
  98.6 2.8 %block.9 = (f32[64,3072]{1,0:T(8,128)S(1)}, bf16[48,3072]{1,0:T(8,128)(2,1)S(1)}, bf16[16,3072]{1,0:T(8,128)(2,1)S(1)}, bf16[2,256,384]{2,1,0:T(8,128)(2,1)S(1)}) custom-call(s32[1]{0:T(128)} %bitcast.section.refs_0_, s32[2,6]{1,0:T(2,128)S(1)} %get-tuple-element.79.patch_flow, ...), custom_call_target="tpu_custom_call", output_to_operand_aliasing={{3}: (13, {})} | custom-call | flops 1207959552 | bytes 9437184 | tf_op jit(solution)/shard_map/block/pallas_call | solution.py:111
  103.2 2.5 %collective-permute-start.48 = (bf16[16,3072]{1,0:T(8,128)(2,1)S(1)}, bf16[16,3072]{1,0:T(8,128)(2,1)S(1)}, u32[]{:S(2)}, u32[]{:S(2)}) collective-permute-start(bf16[16,3072]{1,0:T(8,128)(2,1)S(1)} %split_last.9), channel_id=1, source_target_pairs={{0,6},{1,7},{2,4},{3,5},{4,2},{5,3},{6,0},{7,1},{8,14},{9,15},{10,... | collective-permute-start | bytes 294920 | tf_op jit(solution)/shard_map/ppermute | solution.py:299
  106.9 2.7 %collective-permute-done.48.refs_2_ = bf16[16,3072]{1,0:T(8,128)(2,1)S(1)} collective-permute-done((bf16[16,3072]{1,0:T(8,128)(2,1)S(1)}, bf16[16,3072]{1,0:T(8,128)(2,1)S(1)}, u32[]{:S(2)}, u32[]{:S(2)}) %collective-permute-start.48) | collective-permute-done | bytes 98336 | tf_op jit(solution)/shard_map/ppermute | solution.py:299
  111.4 3.1 %collective-permute-start.51 = (bf16[16,3200]{1,0:T(8,128)(2,1)S(1)}, bf16[16,3200]{1,0:T(8,128)(2,1)S(1)}, u32[]{:S(2)}, u32[]{:S(2)}) collective-permute-start(bf16[16,3200]{1,0:T(8,128)(2,1)S(1)} %finish.9), channel_id=1, source_target_pairs={{0,12},{1,13},{2,14},{3,15},{4,8},{5,9},{6,10},{7,11},{8,4},{9,5},... | collective-permute-start | bytes 307208 | tf_op jit(solution)/shard_map/ppermute | solution.py:347
  114.5 3.4 %collective-permute-done.51.packet.refs_6_ = bf16[16,3200]{1,0:T(8,128)(2,1)S(1)} collective-permute-done((bf16[16,3200]{1,0:T(8,128)(2,1)S(1)}, bf16[16,3200]{1,0:T(8,128)(2,1)S(1)}, u32[]{:S(2)}, u32[]{:S(2)}) %collective-permute-start.51) | collective-permute-done | bytes 102432 | tf_op jit(solution)/shard_map/ppermute | solution.py:347
  118.3 2.4 %collective-permute-start.54 = (bf16[16,3072]{1,0:T(8,128)(2,1)S(1)}, bf16[16,3072]{1,0:T(8,128)(2,1)S(1)}, u32[]{:S(2)}, u32[]{:S(2)}) collective-permute-start(bf16[16,3072]{1,0:T(8,128)(2,1)S(1)} %get-tuple-element.122.refs_0_), channel_id=1, source_target_pairs={{0,6},{1,7},{2,4},{3,5},{4,2},{5,3},{6,0},{7,1},{8,14},{9,15},{10,... | collective-permute-start | bytes 294920 | tf_op jit(solution)/shard_map/ppermute | solution.py:299
  121.9 3.1 %collective-permute-done.54.refs_3_ = bf16[16,3072]{1,0:T(8,128)(2,1)S(1)} collective-permute-done((bf16[16,3072]{1,0:T(8,128)(2,1)S(1)}, bf16[16,3072]{1,0:T(8,128)(2,1)S(1)}, u32[]{:S(2)}, u32[]{:S(2)}) %collective-permute-start.54) | collective-permute-done | bytes 98336 | tf_op jit(solution)/shard_map/ppermute | solution.py:299
  127.0 2.8 %block.10 = (f32[64,3072]{1,0:T(8,128)S(1)}, bf16[48,3072]{1,0:T(8,128)(2,1)S(1)}, bf16[16,3072]{1,0:T(8,128)(2,1)S(1)}, bf16[2,256,384]{2,1,0:T(8,128)(2,1)S(1)}) custom-call(s32[1]{0:T(128)} %bitcast.section.refs_0_, s32[2,6]{1,0:T(2,128)S(1)} %get-tuple-element.79.patch_flow, ...), custom_call_target="tpu_custom_call", output_to_operand_aliasing={{3}: (13, {})} | custom-call | flops 1207959552 | bytes 9437184 | tf_op jit(solution)/shard_map/block/pallas_call | solution.py:111
  131.6 2.3 %collective-permute-start.61 = (bf16[16,3072]{1,0:T(8,128)(2,1)S(1)}, bf16[16,3072]{1,0:T(8,128)(2,1)S(1)}, u32[]{:S(2)}, u32[]{:S(2)}) collective-permute-start(bf16[16,3072]{1,0:T(8,128)(2,1)S(1)} %split_last.10), channel_id=1, source_target_pairs={{0,6},{1,7},{2,4},{3,5},{4,2},{5,3},{6,0},{7,1},{8,14},{9,15},{10,... | collective-permute-start | bytes 294920 | tf_op jit(solution)/shard_map/ppermute | solution.py:299
  135.3 2.7 %collective-permute-done.61.refs_2_ = bf16[16,3072]{1,0:T(8,128)(2,1)S(1)} collective-permute-done((bf16[16,3072]{1,0:T(8,128)(2,1)S(1)}, bf16[16,3072]{1,0:T(8,128)(2,1)S(1)}, u32[]{:S(2)}, u32[]{:S(2)}) %collective-permute-start.61) | collective-permute-done | bytes 98336 | tf_op jit(solution)/shard_map/ppermute | solution.py:299
  138.0 1.3 collective-permute-done.62.refs_3_
  139.7 2.9 %collective-permute-start.64 = (bf16[16,3200]{1,0:T(8,128)(2,1)S(1)}, bf16[16,3200]{1,0:T(8,128)(2,1)S(1)}, u32[]{:S(2)}, u32[]{:S(2)}) collective-permute-start(bf16[16,3200]{1,0:T(8,128)(2,1)S(1)} %finish.10), channel_id=1, source_target_pairs={{0,12},{1,13},{2,14},{3,15},{4,8},{5,9},{6,10},{7,11},{8,4},{9,5},... | collective-permute-start | bytes 307208 | tf_op jit(solution)/shard_map/ppermute | solution.py:347
  142.6 3.6 %collective-permute-done.64.packet.refs_6_ = bf16[16,3200]{1,0:T(8,128)(2,1)S(1)} collective-permute-done((bf16[16,3200]{1,0:T(8,128)(2,1)S(1)}, bf16[16,3200]{1,0:T(8,128)(2,1)S(1)}, u32[]{:S(2)}, u32[]{:S(2)}) %collective-permute-start.64) | collective-permute-done | bytes 102432 | tf_op jit(solution)/shard_map/ppermute | solution.py:347
  146.6 2.7 %collective-permute-start.67 = (bf16[16,3072]{1,0:T(8,128)(2,1)S(1)}, bf16[16,3072]{1,0:T(8,128)(2,1)S(1)}, u32[]{:S(2)}, u32[]{:S(2)}) collective-permute-start(bf16[16,3072]{1,0:T(8,128)(2,1)S(1)} %get-tuple-element.131.refs_0_), channel_id=1, source_target_pairs={{0,6},{1,7},{2,4},{3,5},{4,2},{5,3},{6,0},{7,1},{8,14},{9,15},{10,... | collective-permute-start | bytes 294920 | tf_op jit(solution)/shard_map/ppermute | solution.py:299
  150.2 2.8 %collective-permute-done.67.refs_3_ = bf16[16,3072]{1,0:T(8,128)(2,1)S(1)} collective-permute-done((bf16[16,3072]{1,0:T(8,128)(2,1)S(1)}, bf16[16,3072]{1,0:T(8,128)(2,1)S(1)}, u32[]{:S(2)}, u32[]{:S(2)}) %collective-permute-start.67) | collective-permute-done | bytes 98336 | tf_op jit(solution)/shard_map/ppermute | solution.py:299
  155.5 2.8 %block.11 = (f32[64,3072]{1,0:T(8,128)S(1)}, bf16[48,3072]{1,0:T(8,128)(2,1)S(1)}, bf16[16,3072]{1,0:T(8,128)(2,1)S(1)}, bf16[2,256,384]{2,1,0:T(8,128)(2,1)S(1)}) custom-call(s32[1]{0:T(128)} %bitcast.section.refs_0_, s32[2,6]{1,0:T(2,128)S(1)} %get-tuple-element.79.patch_flow, ...), custom_call_target="tpu_custom_call", output_to_operand_aliasing={{3}: (13, {})} | custom-call | flops 1207959552 | bytes 9437184 | tf_op jit(solution)/shard_map/block/pallas_call | solution.py:111
  160.1 2.2 %collective-permute-start.74 = (bf16[16,3072]{1,0:T(8,128)(2,1)S(1)}, bf16[16,3072]{1,0:T(8,128)(2,1)S(1)}, u32[]{:S(2)}, u32[]{:S(2)}) collective-permute-start(bf16[16,3072]{1,0:T(8,128)(2,1)S(1)} %split_last.11), channel_id=1, source_target_pairs={{0,6},{1,7},{2,4},{3,5},{4,2},{5,3},{6,0},{7,1},{8,14},{9,15},{10,... | collective-permute-start | bytes 294920 | tf_op jit(solution)/shard_map/ppermute | solution.py:299
  163.8 2.9 %collective-permute-done.74.refs_2_ = bf16[16,3072]{1,0:T(8,128)(2,1)S(1)} collective-permute-done((bf16[16,3072]{1,0:T(8,128)(2,1)S(1)}, bf16[16,3072]{1,0:T(8,128)(2,1)S(1)}, u32[]{:S(2)}, u32[]{:S(2)}) %collective-permute-start.74) | collective-permute-done | bytes 98336 | tf_op jit(solution)/shard_map/ppermute | solution.py:299
  168.3 2.9 %collective-permute-start.77 = (bf16[16,3200]{1,0:T(8,128)(2,1)S(1)}, bf16[16,3200]{1,0:T(8,128)(2,1)S(1)}, u32[]{:S(2)}, u32[]{:S(2)}) collective-permute-start(bf16[16,3200]{1,0:T(8,128)(2,1)S(1)} %finish.11), channel_id=1, source_target_pairs={{0,12},{1,13},{2,14},{3,15},{4,8},{5,9},{6,10},{7,11},{8,4},{9,5},... | collective-permute-start | bytes 307208 | tf_op jit(solution)/shard_map/ppermute | solution.py:347
  171.3 3.6 %collective-permute-done.77.packet = bf16[16,3200]{1,0:T(8,128)(2,1)S(1)} collective-permute-done((bf16[16,3200]{1,0:T(8,128)(2,1)S(1)}, bf16[16,3200]{1,0:T(8,128)(2,1)S(1)}, u32[]{:S(2)}, u32[]{:S(2)}) %collective-permute-start.77) | collective-permute-done | bytes 102432 | tf_op jit(solution)/shard_map/ppermute | solution.py:347
  (149 shorter events, 44.7 us)
Async XLA Ops:
  0.7 8.7 %collective-permute-start.2 = (bf16[16,3072]{1,0:T(8,128)(2,1)}, bf16[16,3072]{1,0:T(8,128)(2,1)S(1)}, u32[]{:S(2)}, u32[]{:S(2)}) collective-permute-start(bf16[16,3072]{1,0:T(8,128)(2,1)} %refs_5_.1), channel_id=1, source_target_pairs={{0,6},{1,7},{2,4},{3,5},{4,2},{5,3},{6,0},{7,1},{8,14},{9,15},{10,... | collective-permute-start | bytes 294920 | tf_op jit(solution)/shard_map/ppermute | solution.py:299
  4.7 5.4 %collective-permute-start.1 = (bf16[16,3072]{1,0:T(8,128)(2,1)}, bf16[16,3072]{1,0:T(8,128)(2,1)S(1)}, u32[]{:S(2)}, u32[]{:S(2)}) collective-permute-start(bf16[16,3072]{1,0:T(8,128)(2,1)} %refs_5_.1), channel_id=1, source_target_pairs={{0,4},{1,5},{2,6},{3,7},{4,0},{5,1},{6,2},{7,3},{8,12},{9,13},{10,... | collective-permute-start | bytes 294920 | tf_op jit(solution)/shard_map/ppermute | solution.py:299
  5.2 4.9 %collective-permute-start = (bf16[16,3072]{1,0:T(8,128)(2,1)}, bf16[16,3072]{1,0:T(8,128)(2,1)S(1)}, u32[]{:S(2)}, u32[]{:S(2)}) collective-permute-start(bf16[16,3072]{1,0:T(8,128)(2,1)} %refs_5_.1), channel_id=1, source_target_pairs={{0,2},{1,3},{2,0},{3,1},{4,6},{5,7},{6,4},{7,5},{8,10},{9,11},{10,... | collective-permute-start | bytes 294920 | tf_op jit(solution)/shard_map/ppermute | solution.py:299
  15.2 4.3 %collective-permute-start.7 = (bf16[48,3072]{1,0:T(8,128)(2,1)S(1)}, bf16[48,3072]{1,0:T(8,128)(2,1)S(1)}, u32[]{:S(2)}, u32[]{:S(2)}) collective-permute-start(bf16[48,3072]{1,0:T(8,128)(2,1)S(1)} %get-tuple-element.90), channel_id=1, source_target_pairs={{0,1},{1,0},{2,3},{3,2},{4,5},{5,4},{6,7},{7,6},{8,9},{9,8},{10,11... | collective-permute-start | bytes 884744 | tf_op jit(solution)/shard_map/ppermute | solution.py:299
  17.0 6.6 %collective-permute-start.9 = (bf16[16,3072]{1,0:T(8,128)(2,1)S(1)}, bf16[16,3072]{1,0:T(8,128)(2,1)S(1)}, u32[]{:S(2)}, u32[]{:S(2)}) collective-permute-start(bf16[16,3072]{1,0:T(8,128)(2,1)S(1)} %split_last.6), channel_id=1, source_target_pairs={{0,6},{1,7},{2,4},{3,5},{4,2},{5,3},{6,0},{7,1},{8,14},{9,15},{10,... | collective-permute-start | bytes 294920 | tf_op jit(solution)/shard_map/ppermute | solution.py:299
  19.6 5.5 %collective-permute-start.10 = (bf16[16,3072]{1,0:T(8,128)(2,1)S(1)}, bf16[16,3072]{1,0:T(8,128)(2,1)S(1)}, u32[]{:S(2)}, u32[]{:S(2)}) collective-permute-start(bf16[16,3072]{1,0:T(8,128)(2,1)S(1)} %get-tuple-element.93), channel_id=1, source_target_pairs={{0,4},{1,5},{2,6},{3,7},{4,0},{5,1},{6,2},{7,3},{8,12},{9,13},{10,... | collective-permute-start | bytes 294920 | tf_op jit(solution)/shard_map/ppermute | solution.py:299
  20.1 5.1 %collective-permute-start.11 = (bf16[16,3072]{1,0:T(8,128)(2,1)S(1)}, bf16[16,3072]{1,0:T(8,128)(2,1)S(1)}, u32[]{:S(2)}, u32[]{:S(2)}) collective-permute-start(bf16[16,3072]{1,0:T(8,128)(2,1)S(1)} %get-tuple-element.94), channel_id=1, source_target_pairs={{0,2},{1,3},{2,0},{3,1},{4,6},{5,7},{6,4},{7,5},{8,10},{9,11},{10,... | collective-permute-start | bytes 294920 | tf_op jit(solution)/shard_map/ppermute | solution.py:299
  25.3 6.9 %collective-permute-start.12 = (bf16[16,3200]{1,0:T(8,128)(2,1)S(1)}, bf16[16,3200]{1,0:T(8,128)(2,1)S(1)}, u32[]{:S(2)}, u32[]{:S(2)}) collective-permute-start(bf16[16,3200]{1,0:T(8,128)(2,1)S(1)} %finish.6), channel_id=1, source_target_pairs={{0,12},{1,13},{2,14},{3,15},{4,8},{5,9},{6,10},{7,11},{8,4},{9,5},... | collective-permute-start | bytes 307208 | tf_op jit(solution)/shard_map/ppermute | solution.py:347
  32.6 6.0 %collective-permute-start.15 = (bf16[16,3072]{1,0:T(8,128)(2,1)S(1)}, bf16[16,3072]{1,0:T(8,128)(2,1)S(1)}, u32[]{:S(2)}, u32[]{:S(2)}) collective-permute-start(bf16[16,3072]{1,0:T(8,128)(2,1)S(1)} %get-tuple-element.95.refs_0_), channel_id=1, source_target_pairs={{0,6},{1,7},{2,4},{3,5},{4,2},{5,3},{6,0},{7,1},{8,14},{9,15},{10,... | collective-permute-start | bytes 294920 | tf_op jit(solution)/shard_map/ppermute | solution.py:299
  35.3 4.7 %collective-permute-start.14 = (bf16[16,3072]{1,0:T(8,128)(2,1)S(1)}, bf16[16,3072]{1,0:T(8,128)(2,1)S(1)}, u32[]{:S(2)}, u32[]{:S(2)}) collective-permute-start(bf16[16,3072]{1,0:T(8,128)(2,1)S(1)} %get-tuple-element.95.refs_0_), channel_id=1, source_target_pairs={{0,4},{1,5},{2,6},{3,7},{4,0},{5,1},{6,2},{7,3},{8,12},{9,13},{10,... | collective-permute-start | bytes 294920 | tf_op jit(solution)/shard_map/ppermute | solution.py:299
  35.6 4.6 %collective-permute-start.13 = (bf16[16,3072]{1,0:T(8,128)(2,1)S(1)}, bf16[16,3072]{1,0:T(8,128)(2,1)S(1)}, u32[]{:S(2)}, u32[]{:S(2)}) collective-permute-start(bf16[16,3072]{1,0:T(8,128)(2,1)S(1)} %get-tuple-element.95.refs_0_), channel_id=1, source_target_pairs={{0,2},{1,3},{2,0},{3,1},{4,6},{5,7},{6,4},{7,5},{8,10},{9,11},{10,... | collective-permute-start | bytes 294920 | tf_op jit(solution)/shard_map/ppermute | solution.py:299
  36.2 4.3 %collective-permute-start.16 = (bf16[16,3072]{1,0:T(8,128)(2,1)S(1)}, bf16[16,3072]{1,0:T(8,128)(2,1)S(1)}, u32[]{:S(2)}, u32[]{:S(2)}) collective-permute-start(bf16[16,3072]{1,0:T(8,128)(2,1)S(1)} %get-tuple-element.95.refs_0_), channel_id=1, source_target_pairs={{0,1},{1,0},{2,3},{3,2},{4,5},{5,4},{6,7},{7,6},{8,9},{9,8},{10,11... | collective-permute-start | bytes 294920 | tf_op jit(solution)/shard_map/ppermute | solution.py:299
  46.1 6.5 %collective-permute-start.22 = (bf16[16,3072]{1,0:T(8,128)(2,1)S(1)}, bf16[16,3072]{1,0:T(8,128)(2,1)S(1)}, u32[]{:S(2)}, u32[]{:S(2)}) collective-permute-start(bf16[16,3072]{1,0:T(8,128)(2,1)S(1)} %split_last.7), channel_id=1, source_target_pairs={{0,6},{1,7},{2,4},{3,5},{4,2},{5,3},{6,0},{7,1},{8,14},{9,15},{10,... | collective-permute-start | bytes 294920 | tf_op jit(solution)/shard_map/ppermute | solution.py:299
  48.2 5.4 %collective-permute-start.23 = (bf16[16,3072]{1,0:T(8,128)(2,1)S(1)}, bf16[16,3072]{1,0:T(8,128)(2,1)S(1)}, u32[]{:S(2)}, u32[]{:S(2)}) collective-permute-start(bf16[16,3072]{1,0:T(8,128)(2,1)S(1)} %get-tuple-element.101), channel_id=1, source_target_pairs={{0,4},{1,5},{2,6},{3,7},{4,0},{5,1},{6,2},{7,3},{8,12},{9,13},{10,... | collective-permute-start | bytes 294920 | tf_op jit(solution)/shard_map/ppermute | solution.py:299
  48.8 5.3 %collective-permute-start.24 = (bf16[16,3072]{1,0:T(8,128)(2,1)S(1)}, bf16[16,3072]{1,0:T(8,128)(2,1)S(1)}, u32[]{:S(2)}, u32[]{:S(2)}) collective-permute-start(bf16[16,3072]{1,0:T(8,128)(2,1)S(1)} %get-tuple-element.102), channel_id=1, source_target_pairs={{0,2},{1,3},{2,0},{3,1},{4,6},{5,7},{6,4},{7,5},{8,10},{9,11},{10,... | collective-permute-start | bytes 294920 | tf_op jit(solution)/shard_map/ppermute | solution.py:299
  54.2 6.5 %collective-permute-start.25 = (bf16[16,3200]{1,0:T(8,128)(2,1)S(1)}, bf16[16,3200]{1,0:T(8,128)(2,1)S(1)}, u32[]{:S(2)}, u32[]{:S(2)}) collective-permute-start(bf16[16,3200]{1,0:T(8,128)(2,1)S(1)} %finish.7), channel_id=1, source_target_pairs={{0,12},{1,13},{2,14},{3,15},{4,8},{5,9},{6,10},{7,11},{8,4},{9,5},... | collective-permute-start | bytes 307208 | tf_op jit(solution)/shard_map/ppermute | solution.py:347
  61.2 6.4 %collective-permute-start.28 = (bf16[16,3072]{1,0:T(8,128)(2,1)S(1)}, bf16[16,3072]{1,0:T(8,128)(2,1)S(1)}, u32[]{:S(2)}, u32[]{:S(2)}) collective-permute-start(bf16[16,3072]{1,0:T(8,128)(2,1)S(1)} %get-tuple-element.104.refs_0_), channel_id=1, source_target_pairs={{0,6},{1,7},{2,4},{3,5},{4,2},{5,3},{6,0},{7,1},{8,14},{9,15},{10,... | collective-permute-start | bytes 294920 | tf_op jit(solution)/shard_map/ppermute | solution.py:299
  63.3 4.7 %collective-permute-start.27 = (bf16[16,3072]{1,0:T(8,128)(2,1)S(1)}, bf16[16,3072]{1,0:T(8,128)(2,1)S(1)}, u32[]{:S(2)}, u32[]{:S(2)}) collective-permute-start(bf16[16,3072]{1,0:T(8,128)(2,1)S(1)} %get-tuple-element.104.refs_0_), channel_id=1, source_target_pairs={{0,4},{1,5},{2,6},{3,7},{4,0},{5,1},{6,2},{7,3},{8,12},{9,13},{10,... | collective-permute-start | bytes 294920 | tf_op jit(solution)/shard_map/ppermute | solution.py:299
  63.7 4.8 %collective-permute-start.26 = (bf16[16,3072]{1,0:T(8,128)(2,1)S(1)}, bf16[16,3072]{1,0:T(8,128)(2,1)S(1)}, u32[]{:S(2)}, u32[]{:S(2)}) collective-permute-start(bf16[16,3072]{1,0:T(8,128)(2,1)S(1)} %get-tuple-element.104.refs_0_), channel_id=1, source_target_pairs={{0,2},{1,3},{2,0},{3,1},{4,6},{5,7},{6,4},{7,5},{8,10},{9,11},{10,... | collective-permute-start | bytes 294920 | tf_op jit(solution)/shard_map/ppermute | solution.py:299
  72.6 4.2 %collective-permute-start.33 = (bf16[48,3072]{1,0:T(8,128)(2,1)S(1)}, bf16[48,3072]{1,0:T(8,128)(2,1)S(1)}, u32[]{:S(2)}, u32[]{:S(2)}) collective-permute-start(bf16[48,3072]{1,0:T(8,128)(2,1)S(1)} %get-tuple-element.107), channel_id=1, source_target_pairs={{0,1},{1,0},{2,3},{3,2},{4,5},{5,4},{6,7},{7,6},{8,9},{9,8},{10,11... | collective-permute-start | bytes 884744 | tf_op jit(solution)/shard_map/ppermute | solution.py:299
  74.4 6.2 %collective-permute-start.35 = (bf16[16,3072]{1,0:T(8,128)(2,1)S(1)}, bf16[16,3072]{1,0:T(8,128)(2,1)S(1)}, u32[]{:S(2)}, u32[]{:S(2)}) collective-permute-start(bf16[16,3072]{1,0:T(8,128)(2,1)S(1)} %split_last.8), channel_id=1, source_target_pairs={{0,6},{1,7},{2,4},{3,5},{4,2},{5,3},{6,0},{7,1},{8,14},{9,15},{10,... | collective-permute-start | bytes 294920 | tf_op jit(solution)/shard_map/ppermute | solution.py:299
  76.9 5.3 %collective-permute-start.36 = (bf16[16,3072]{1,0:T(8,128)(2,1)S(1)}, bf16[16,3072]{1,0:T(8,128)(2,1)S(1)}, u32[]{:S(2)}, u32[]{:S(2)}) collective-permute-start(bf16[16,3072]{1,0:T(8,128)(2,1)S(1)} %get-tuple-element.110), channel_id=1, source_target_pairs={{0,4},{1,5},{2,6},{3,7},{4,0},{5,1},{6,2},{7,3},{8,12},{9,13},{10,... | collective-permute-start | bytes 294920 | tf_op jit(solution)/shard_map/ppermute | solution.py:299
  77.2 5.1 %collective-permute-start.37 = (bf16[16,3072]{1,0:T(8,128)(2,1)S(1)}, bf16[16,3072]{1,0:T(8,128)(2,1)S(1)}, u32[]{:S(2)}, u32[]{:S(2)}) collective-permute-start(bf16[16,3072]{1,0:T(8,128)(2,1)S(1)} %get-tuple-element.111), channel_id=1, source_target_pairs={{0,2},{1,3},{2,0},{3,1},{4,6},{5,7},{6,4},{7,5},{8,10},{9,11},{10,... | collective-permute-start | bytes 294920 | tf_op jit(solution)/shard_map/ppermute | solution.py:299
  82.4 6.5 %collective-permute-start.38 = (bf16[16,3200]{1,0:T(8,128)(2,1)S(1)}, bf16[16,3200]{1,0:T(8,128)(2,1)S(1)}, u32[]{:S(2)}, u32[]{:S(2)}) collective-permute-start(bf16[16,3200]{1,0:T(8,128)(2,1)S(1)} %finish.8), channel_id=1, source_target_pairs={{0,12},{1,13},{2,14},{3,15},{4,8},{5,9},{6,10},{7,11},{8,4},{9,5},... | collective-permute-start | bytes 307208 | tf_op jit(solution)/shard_map/ppermute | solution.py:347
  89.5 6.1 %collective-permute-start.41 = (bf16[16,3072]{1,0:T(8,128)(2,1)S(1)}, bf16[16,3072]{1,0:T(8,128)(2,1)S(1)}, u32[]{:S(2)}, u32[]{:S(2)}) collective-permute-start(bf16[16,3072]{1,0:T(8,128)(2,1)S(1)} %get-tuple-element.113.refs_0_), channel_id=1, source_target_pairs={{0,6},{1,7},{2,4},{3,5},{4,2},{5,3},{6,0},{7,1},{8,14},{9,15},{10,... | collective-permute-start | bytes 294920 | tf_op jit(solution)/shard_map/ppermute | solution.py:299
  92.5 4.6 %collective-permute-start.40 = (bf16[16,3072]{1,0:T(8,128)(2,1)S(1)}, bf16[16,3072]{1,0:T(8,128)(2,1)S(1)}, u32[]{:S(2)}, u32[]{:S(2)}) collective-permute-start(bf16[16,3072]{1,0:T(8,128)(2,1)S(1)} %get-tuple-element.113.refs_0_), channel_id=1, source_target_pairs={{0,4},{1,5},{2,6},{3,7},{4,0},{5,1},{6,2},{7,3},{8,12},{9,13},{10,... | collective-permute-start | bytes 294920 | tf_op jit(solution)/shard_map/ppermute | solution.py:299
  92.5 4.7 %collective-permute-start.39 = (bf16[16,3072]{1,0:T(8,128)(2,1)S(1)}, bf16[16,3072]{1,0:T(8,128)(2,1)S(1)}, u32[]{:S(2)}, u32[]{:S(2)}) collective-permute-start(bf16[16,3072]{1,0:T(8,128)(2,1)S(1)} %get-tuple-element.113.refs_0_), channel_id=1, source_target_pairs={{0,2},{1,3},{2,0},{3,1},{4,6},{5,7},{6,4},{7,5},{8,10},{9,11},{10,... | collective-permute-start | bytes 294920 | tf_op jit(solution)/shard_map/ppermute | solution.py:299
  93.1 4.5 %collective-permute-start.42 = (bf16[16,3072]{1,0:T(8,128)(2,1)S(1)}, bf16[16,3072]{1,0:T(8,128)(2,1)S(1)}, u32[]{:S(2)}, u32[]{:S(2)}) collective-permute-start(bf16[16,3072]{1,0:T(8,128)(2,1)S(1)} %get-tuple-element.113.refs_0_), channel_id=1, source_target_pairs={{0,1},{1,0},{2,3},{3,2},{4,5},{5,4},{6,7},{7,6},{8,9},{9,8},{10,11... | collective-permute-start | bytes 294920 | tf_op jit(solution)/shard_map/ppermute | solution.py:299
  101.3 4.4 %collective-permute-start.46 = (bf16[48,3072]{1,0:T(8,128)(2,1)S(1)}, bf16[48,3072]{1,0:T(8,128)(2,1)S(1)}, u32[]{:S(2)}, u32[]{:S(2)}) collective-permute-start(bf16[48,3072]{1,0:T(8,128)(2,1)S(1)} %get-tuple-element.116), channel_id=1, source_target_pairs={{0,1},{1,0},{2,3},{3,2},{4,5},{5,4},{6,7},{7,6},{8,9},{9,8},{10,11... | collective-permute-start | bytes 884744 | tf_op jit(solution)/shard_map/ppermute | solution.py:299
  103.2 6.5 %collective-permute-start.48 = (bf16[16,3072]{1,0:T(8,128)(2,1)S(1)}, bf16[16,3072]{1,0:T(8,128)(2,1)S(1)}, u32[]{:S(2)}, u32[]{:S(2)}) collective-permute-start(bf16[16,3072]{1,0:T(8,128)(2,1)S(1)} %split_last.9), channel_id=1, source_target_pairs={{0,6},{1,7},{2,4},{3,5},{4,2},{5,3},{6,0},{7,1},{8,14},{9,15},{10,... | collective-permute-start | bytes 294920 | tf_op jit(solution)/shard_map/ppermute | solution.py:299
  105.8 4.9 %collective-permute-start.49 = (bf16[16,3072]{1,0:T(8,128)(2,1)S(1)}, bf16[16,3072]{1,0:T(8,128)(2,1)S(1)}, u32[]{:S(2)}, u32[]{:S(2)}) collective-permute-start(bf16[16,3072]{1,0:T(8,128)(2,1)S(1)} %get-tuple-element.119), channel_id=1, source_target_pairs={{0,4},{1,5},{2,6},{3,7},{4,0},{5,1},{6,2},{7,3},{8,12},{9,13},{10,... | collective-permute-start | bytes 294920 | tf_op jit(solution)/shard_map/ppermute | solution.py:299
  105.8 5.4 %collective-permute-start.50 = (bf16[16,3072]{1,0:T(8,128)(2,1)S(1)}, bf16[16,3072]{1,0:T(8,128)(2,1)S(1)}, u32[]{:S(2)}, u32[]{:S(2)}) collective-permute-start(bf16[16,3072]{1,0:T(8,128)(2,1)S(1)} %get-tuple-element.120), channel_id=1, source_target_pairs={{0,2},{1,3},{2,0},{3,1},{4,6},{5,7},{6,4},{7,5},{8,10},{9,11},{10,... | collective-permute-start | bytes 294920 | tf_op jit(solution)/shard_map/ppermute | solution.py:299
  111.4 6.5 %collective-permute-start.51 = (bf16[16,3200]{1,0:T(8,128)(2,1)S(1)}, bf16[16,3200]{1,0:T(8,128)(2,1)S(1)}, u32[]{:S(2)}, u32[]{:S(2)}) collective-permute-start(bf16[16,3200]{1,0:T(8,128)(2,1)S(1)} %finish.9), channel_id=1, source_target_pairs={{0,12},{1,13},{2,14},{3,15},{4,8},{5,9},{6,10},{7,11},{8,4},{9,5},... | collective-permute-start | bytes 307208 | tf_op jit(solution)/shard_map/ppermute | solution.py:347
  118.3 6.6 %collective-permute-start.54 = (bf16[16,3072]{1,0:T(8,128)(2,1)S(1)}, bf16[16,3072]{1,0:T(8,128)(2,1)S(1)}, u32[]{:S(2)}, u32[]{:S(2)}) collective-permute-start(bf16[16,3072]{1,0:T(8,128)(2,1)S(1)} %get-tuple-element.122.refs_0_), channel_id=1, source_target_pairs={{0,6},{1,7},{2,4},{3,5},{4,2},{5,3},{6,0},{7,1},{8,14},{9,15},{10,... | collective-permute-start | bytes 294920 | tf_op jit(solution)/shard_map/ppermute | solution.py:299
  120.7 4.7 %collective-permute-start.53 = (bf16[16,3072]{1,0:T(8,128)(2,1)S(1)}, bf16[16,3072]{1,0:T(8,128)(2,1)S(1)}, u32[]{:S(2)}, u32[]{:S(2)}) collective-permute-start(bf16[16,3072]{1,0:T(8,128)(2,1)S(1)} %get-tuple-element.122.refs_0_), channel_id=1, source_target_pairs={{0,4},{1,5},{2,6},{3,7},{4,0},{5,1},{6,2},{7,3},{8,12},{9,13},{10,... | collective-permute-start | bytes 294920 | tf_op jit(solution)/shard_map/ppermute | solution.py:299
  120.7 5.0 %collective-permute-start.52 = (bf16[16,3072]{1,0:T(8,128)(2,1)S(1)}, bf16[16,3072]{1,0:T(8,128)(2,1)S(1)}, u32[]{:S(2)}, u32[]{:S(2)}) collective-permute-start(bf16[16,3072]{1,0:T(8,128)(2,1)S(1)} %get-tuple-element.122.refs_0_), channel_id=1, source_target_pairs={{0,2},{1,3},{2,0},{3,1},{4,6},{5,7},{6,4},{7,5},{8,10},{9,11},{10,... | collective-permute-start | bytes 294920 | tf_op jit(solution)/shard_map/ppermute | solution.py:299
  131.6 6.4 %collective-permute-start.61 = (bf16[16,3072]{1,0:T(8,128)(2,1)S(1)}, bf16[16,3072]{1,0:T(8,128)(2,1)S(1)}, u32[]{:S(2)}, u32[]{:S(2)}) collective-permute-start(bf16[16,3072]{1,0:T(8,128)(2,1)S(1)} %split_last.10), channel_id=1, source_target_pairs={{0,6},{1,7},{2,4},{3,5},{4,2},{5,3},{6,0},{7,1},{8,14},{9,15},{10,... | collective-permute-start | bytes 294920 | tf_op jit(solution)/shard_map/ppermute | solution.py:299
  134.0 5.3 %collective-permute-start.62 = (bf16[16,3072]{1,0:T(8,128)(2,1)S(1)}, bf16[16,3072]{1,0:T(8,128)(2,1)S(1)}, u32[]{:S(2)}, u32[]{:S(2)}) collective-permute-start(bf16[16,3072]{1,0:T(8,128)(2,1)S(1)} %get-tuple-element.128), channel_id=1, source_target_pairs={{0,4},{1,5},{2,6},{3,7},{4,0},{5,1},{6,2},{7,3},{8,12},{9,13},{10,... | collective-permute-start | bytes 294920 | tf_op jit(solution)/shard_map/ppermute | solution.py:299
  134.3 5.3 %collective-permute-start.63 = (bf16[16,3072]{1,0:T(8,128)(2,1)S(1)}, bf16[16,3072]{1,0:T(8,128)(2,1)S(1)}, u32[]{:S(2)}, u32[]{:S(2)}) collective-permute-start(bf16[16,3072]{1,0:T(8,128)(2,1)S(1)} %get-tuple-element.129), channel_id=1, source_target_pairs={{0,2},{1,3},{2,0},{3,1},{4,6},{5,7},{6,4},{7,5},{8,10},{9,11},{10,... | collective-permute-start | bytes 294920 | tf_op jit(solution)/shard_map/ppermute | solution.py:299
  139.7 6.5 %collective-permute-start.64 = (bf16[16,3200]{1,0:T(8,128)(2,1)S(1)}, bf16[16,3200]{1,0:T(8,128)(2,1)S(1)}, u32[]{:S(2)}, u32[]{:S(2)}) collective-permute-start(bf16[16,3200]{1,0:T(8,128)(2,1)S(1)} %finish.10), channel_id=1, source_target_pairs={{0,12},{1,13},{2,14},{3,15},{4,8},{5,9},{6,10},{7,11},{8,4},{9,5},... | collective-permute-start | bytes 307208 | tf_op jit(solution)/shard_map/ppermute | solution.py:347
  146.6 6.4 %collective-permute-start.67 = (bf16[16,3072]{1,0:T(8,128)(2,1)S(1)}, bf16[16,3072]{1,0:T(8,128)(2,1)S(1)}, u32[]{:S(2)}, u32[]{:S(2)}) collective-permute-start(bf16[16,3072]{1,0:T(8,128)(2,1)S(1)} %get-tuple-element.131.refs_0_), channel_id=1, source_target_pairs={{0,6},{1,7},{2,4},{3,5},{4,2},{5,3},{6,0},{7,1},{8,14},{9,15},{10,... | collective-permute-start | bytes 294920 | tf_op jit(solution)/shard_map/ppermute | solution.py:299
  149.3 4.8 %collective-permute-start.66 = (bf16[16,3072]{1,0:T(8,128)(2,1)S(1)}, bf16[16,3072]{1,0:T(8,128)(2,1)S(1)}, u32[]{:S(2)}, u32[]{:S(2)}) collective-permute-start(bf16[16,3072]{1,0:T(8,128)(2,1)S(1)} %get-tuple-element.131.refs_0_), channel_id=1, source_target_pairs={{0,4},{1,5},{2,6},{3,7},{4,0},{5,1},{6,2},{7,3},{8,12},{9,13},{10,... | collective-permute-start | bytes 294920 | tf_op jit(solution)/shard_map/ppermute | solution.py:299
  149.3 4.8 %collective-permute-start.65 = (bf16[16,3072]{1,0:T(8,128)(2,1)S(1)}, bf16[16,3072]{1,0:T(8,128)(2,1)S(1)}, u32[]{:S(2)}, u32[]{:S(2)}) collective-permute-start(bf16[16,3072]{1,0:T(8,128)(2,1)S(1)} %get-tuple-element.131.refs_0_), channel_id=1, source_target_pairs={{0,2},{1,3},{2,0},{3,1},{4,6},{5,7},{6,4},{7,5},{8,10},{9,11},{10,... | collective-permute-start | bytes 294920 | tf_op jit(solution)/shard_map/ppermute | solution.py:299
  150.2 4.4 %collective-permute-start.68 = (bf16[16,3072]{1,0:T(8,128)(2,1)S(1)}, bf16[16,3072]{1,0:T(8,128)(2,1)S(1)}, u32[]{:S(2)}, u32[]{:S(2)}) collective-permute-start(bf16[16,3072]{1,0:T(8,128)(2,1)S(1)} %get-tuple-element.131.refs_0_), channel_id=1, source_target_pairs={{0,1},{1,0},{2,3},{3,2},{4,5},{5,4},{6,7},{7,6},{8,9},{9,8},{10,11... | collective-permute-start | bytes 294920 | tf_op jit(solution)/shard_map/ppermute | solution.py:299
  160.1 6.6 %collective-permute-start.74 = (bf16[16,3072]{1,0:T(8,128)(2,1)S(1)}, bf16[16,3072]{1,0:T(8,128)(2,1)S(1)}, u32[]{:S(2)}, u32[]{:S(2)}) collective-permute-start(bf16[16,3072]{1,0:T(8,128)(2,1)S(1)} %split_last.11), channel_id=1, source_target_pairs={{0,6},{1,7},{2,4},{3,5},{4,2},{5,3},{6,0},{7,1},{8,14},{9,15},{10,... | collective-permute-start | bytes 294920 | tf_op jit(solution)/shard_map/ppermute | solution.py:299
  162.4 5.0 %collective-permute-start.75 = (bf16[16,3072]{1,0:T(8,128)(2,1)S(1)}, bf16[16,3072]{1,0:T(8,128)(2,1)S(1)}, u32[]{:S(2)}, u32[]{:S(2)}) collective-permute-start(bf16[16,3072]{1,0:T(8,128)(2,1)S(1)} %get-tuple-element.137), channel_id=1, source_target_pairs={{0,4},{1,5},{2,6},{3,7},{4,0},{5,1},{6,2},{7,3},{8,12},{9,13},{10,... | collective-permute-start | bytes 294920 | tf_op jit(solution)/shard_map/ppermute | solution.py:299
  162.6 5.6 %collective-permute-start.76 = (bf16[16,3072]{1,0:T(8,128)(2,1)S(1)}, bf16[16,3072]{1,0:T(8,128)(2,1)S(1)}, u32[]{:S(2)}, u32[]{:S(2)}) collective-permute-start(bf16[16,3072]{1,0:T(8,128)(2,1)S(1)} %get-tuple-element.138), channel_id=1, source_target_pairs={{0,2},{1,3},{2,0},{3,1},{4,6},{5,7},{6,4},{7,5},{8,10},{9,11},{10,... | collective-permute-start | bytes 294920 | tf_op jit(solution)/shard_map/ppermute | solution.py:299
  168.3 6.5 %collective-permute-start.77 = (bf16[16,3200]{1,0:T(8,128)(2,1)S(1)}, bf16[16,3200]{1,0:T(8,128)(2,1)S(1)}, u32[]{:S(2)}, u32[]{:S(2)}) collective-permute-start(bf16[16,3200]{1,0:T(8,128)(2,1)S(1)} %finish.11), channel_id=1, source_target_pairs={{0,12},{1,13},{2,14},{3,15},{4,8},{5,9},{6,10},{7,11},{8,4},{9,5},... | collective-permute-start | bytes 307208 | tf_op jit(solution)/shard_map/ppermute | solution.py:347
  (35 other events, 127.7 us)

commit v8 on v7

--- a/solution.py
+++ b/solution.py
@@ -65,7 +65,7 @@
     pieces, refs = refs[: 2 * CHIPS], refs[2 * CHIPS :]
     if tick == 0:
         mod, refs = refs[0], refs[1:]
-    gains, w_qkv, w_out, kv_in, kept, sent, ahead, kv, normed, mixed = refs
+    gains, w_qkv, w_out, _, kept, sent, ahead, kv, normed, mixed = refs
     part_rows, width = pieces[0].shape
     half = CHIPS * part_rows
     rows = 2 * half
@@ -77,7 +77,6 @@
             values = norm_here(section, f32(values), mod)
         normed[place * part_rows : (place + 1) * part_rows, :] = values
     start = pl.multiple_of(patch_flow[here, tick] * rows, rows)
-    kv[...] = kv_in[...]
     gain = gains[here]
     tokens = normed[...]
     columns = w_out.shape[0]
@@ -114,8 +113,8 @@
             ((half, width), jnp.float32),
             ((half - half // CHIPS, width), jnp.bfloat16),
             ((half // CHIPS, width), jnp.bfloat16),
-            (kv.shape, jnp.bfloat16),
-        ),
+        )
+        + (VMEM(kv.shape, kv.dtype),),
         in_specs=[SCALARS] * 2 + [WHOLE] * (len(args) - 2),
         out_specs=(WHOLE,) * 4,
         scratch_shapes=[

time: 176 us -> 175 us (level)
  no operation moved by 1% of the time
where the time goes in v8:
time: 175 us
  waiting for transfers between devices  79 us (45%)
  starting transfers between devices  70.5 us (40%)
  Pallas kernels  24.4 us (14%)
    ppermute x72, waiting for transfers between devices, exchange(): return lax.ppermute(value, 'section', route)  60 us
    ppermute x72, starting transfers between devices, exchange(): return lax.ppermute(value, 'section', route)  50 us
    ppermute x6, starting transfers between devices, body(): packet = lax.ppermute(packet, 'section', across if swaps else onward)  20.5 us
    ppermute x6, waiting for transfers between devices, body(): packet = lax.ppermute(packet, 'section', across if swaps else onward)  19 us
    pallas_call x6, Pallas kernels, block(): pl.pallas_call(functools.partial(block_kernel, tick), out_shape=like(((ha...  16.2 us
    pallas_call x1, Pallas kernels, load(): pl.pallas_call(functools.partial(load_kernel, count), out_shape=tuple((VM...  3.97 us
  transfers between devices with their start and end apart: 78, of which 62 were waited for; matrix products, arithmetic and copies ran while one was open for 0% of the time, Pallas kernels for 3%

profile of v8, /device:TPU:0, one launch (start us, length us, event | category | flops | bytes accessed | tf_op | source)
XLA Modules:
  0.0 174.9 jit_solution(16324913844561183607)
XLA Ops:
  0.7 4.1 %collective-permute-start.2 = (bf16[16,3072]{1,0:T(8,128)(2,1)}, bf16[16,3072]{1,0:T(8,128)(2,1)S(1)}, u32[]{:S(2)}, u32[]{:S(2)}) collective-permute-start(bf16[16,3072]{1,0:T(8,128)(2,1)} %refs_5_.1), channel_id=1, source_target_pairs={{0,6},{1,7},{2,4},{3,5},{4,2},{5,3},{6,0},{7,1},{8,14},{9,15},{10,... | collective-permute-start | bytes 294920 | tf_op jit(solution)/shard_map/ppermute | solution.py:298
  5.4 4.0 %load.1 = (bf16[3072,1152]{1,0:T(8,128)(2,1)S(1)}, bf16[384,3072]{1,0:T(8,128)(2,1)S(1)}, f32[2,2,128]{2,1,0:T(2,128)S(1)}, s32[2,6]{1,0:T(2,128)S(1)}, bf16[2,2...) custom-call(bf16[3,3072,384]{2,1,0:T(8,128)(2,1)} %refs_0_.1, bf16[384,3072]{1,0:T(8,128)(2,1)} %refs_1_.1, ...), custom_call_target="tpu_custom_call" | custom-call | bytes 19812448 | tf_op jit(solution)/shard_map/load/pallas_call | solution.py:264
  12.1 3.0 %block.6 = (f32[64,3072]{1,0:T(8,128)S(1)}, bf16[48,3072]{1,0:T(8,128)(2,1)S(1)}, bf16[16,3072]{1,0:T(8,128)(2,1)S(1)}, bf16[2,256,384]{2,1,0:T(8,128)(2,1)S(1)}) custom-call(s32[1]{0:T(128)} %bitcast.section.refs_0_, s32[2,6]{1,0:T(2,128)S(1)} %get-tuple-element.79.patch_flow, bf16[16,3072]{1,0:T(8,128)(2,1)S(1)} %copy-done.3, ...), custom_call_target="tpu_custom_call", output_to_operand_aliasing={{3}: (14, {})} | custom-call | flops 1207959552 | bytes 9437184 | tf_op jit(solution)/shard_map/block/pallas_call | solution.py:110
  16.9 2.5 %collective-permute-start.9 = (bf16[16,3072]{1,0:T(8,128)(2,1)S(1)}, bf16[16,3072]{1,0:T(8,128)(2,1)S(1)}, u32[]{:S(2)}, u32[]{:S(2)}) collective-permute-start(bf16[16,3072]{1,0:T(8,128)(2,1)S(1)} %split_last.6), channel_id=1, source_target_pairs={{0,6},{1,7},{2,4},{3,5},{4,2},{5,3},{6,0},{7,1},{8,14},{9,15},{10,... | collective-permute-start | bytes 294920 | tf_op jit(solution)/shard_map/ppermute | solution.py:298
  20.6 2.9 %collective-permute-done.9.refs_2_ = bf16[16,3072]{1,0:T(8,128)(2,1)S(1)} collective-permute-done((bf16[16,3072]{1,0:T(8,128)(2,1)S(1)}, bf16[16,3072]{1,0:T(8,128)(2,1)S(1)}, u32[]{:S(2)}, u32[]{:S(2)}) %collective-permute-start.9) | collective-permute-done | bytes 98336 | tf_op jit(solution)/shard_map/ppermute | solution.py:298
  23.5 1.5 collective-permute-done.10.refs_3_
  25.2 4.2 %collective-permute-start.12 = (bf16[16,3200]{1,0:T(8,128)(2,1)S(1)}, bf16[16,3200]{1,0:T(8,128)(2,1)S(1)}, u32[]{:S(2)}, u32[]{:S(2)}) collective-permute-start(bf16[16,3200]{1,0:T(8,128)(2,1)S(1)} %finish.6), channel_id=1, source_target_pairs={{0,12},{1,13},{2,14},{3,15},{4,8},{5,9},{6,10},{7,11},{8,4},{9,5},... | collective-permute-start | bytes 307208 | tf_op jit(solution)/shard_map/ppermute | solution.py:346
  29.4 2.7 %collective-permute-done.12.packet.refs_6_ = bf16[16,3200]{1,0:T(8,128)(2,1)S(1)} collective-permute-done((bf16[16,3200]{1,0:T(8,128)(2,1)S(1)}, bf16[16,3200]{1,0:T(8,128)(2,1)S(1)}, u32[]{:S(2)}, u32[]{:S(2)}) %collective-permute-start.12) | collective-permute-done | bytes 102432 | tf_op jit(solution)/shard_map/ppermute | solution.py:346
  32.5 2.7 %collective-permute-start.15 = (bf16[16,3072]{1,0:T(8,128)(2,1)S(1)}, bf16[16,3072]{1,0:T(8,128)(2,1)S(1)}, u32[]{:S(2)}, u32[]{:S(2)}) collective-permute-start(bf16[16,3072]{1,0:T(8,128)(2,1)S(1)} %get-tuple-element.95.refs_0_), channel_id=1, source_target_pairs={{0,6},{1,7},{2,4},{3,5},{4,2},{5,3},{6,0},{7,1},{8,14},{9,15},{10,... | collective-permute-start | bytes 294920 | tf_op jit(solution)/shard_map/ppermute | solution.py:298
  36.1 2.4 %collective-permute-done.15.refs_3_ = bf16[16,3072]{1,0:T(8,128)(2,1)S(1)} collective-permute-done((bf16[16,3072]{1,0:T(8,128)(2,1)S(1)}, bf16[16,3072]{1,0:T(8,128)(2,1)S(1)}, u32[]{:S(2)}, u32[]{:S(2)}) %collective-permute-start.15) | collective-permute-done | bytes 98336 | tf_op jit(solution)/shard_map/ppermute | solution.py:298
  38.5 1.4 collective-permute-done.14.refs_2_
  41.4 2.6 %block.7 = (f32[64,3072]{1,0:T(8,128)S(1)}, bf16[48,3072]{1,0:T(8,128)(2,1)S(1)}, bf16[16,3072]{1,0:T(8,128)(2,1)S(1)}, bf16[2,256,384]{2,1,0:T(8,128)(2,1)S(1)}) custom-call(s32[1]{0:T(128)} %bitcast.section.refs_0_, s32[2,6]{1,0:T(2,128)S(1)} %get-tuple-element.79.patch_flow, ...), custom_call_target="tpu_custom_call", output_to_operand_aliasing={{3}: (13, {})} | custom-call | flops 1207959552 | bytes 9437184 | tf_op jit(solution)/shard_map/block/pallas_call | solution.py:110
  45.9 2.0 %collective-permute-start.22 = (bf16[16,3072]{1,0:T(8,128)(2,1)S(1)}, bf16[16,3072]{1,0:T(8,128)(2,1)S(1)}, u32[]{:S(2)}, u32[]{:S(2)}) collective-permute-start(bf16[16,3072]{1,0:T(8,128)(2,1)S(1)} %split_last.7), channel_id=1, source_target_pairs={{0,6},{1,7},{2,4},{3,5},{4,2},{5,3},{6,0},{7,1},{8,14},{9,15},{10,... | collective-permute-start | bytes 294920 | tf_op jit(solution)/shard_map/ppermute | solution.py:298
  49.6 2.9 %collective-permute-done.22.refs_2_ = bf16[16,3072]{1,0:T(8,128)(2,1)S(1)} collective-permute-done((bf16[16,3072]{1,0:T(8,128)(2,1)S(1)}, bf16[16,3072]{1,0:T(8,128)(2,1)S(1)}, u32[]{:S(2)}, u32[]{:S(2)}) %collective-permute-start.22) | collective-permute-done | bytes 98336 | tf_op jit(solution)/shard_map/ppermute | solution.py:298
  54.0 3.7 %collective-permute-start.25 = (bf16[16,3200]{1,0:T(8,128)(2,1)S(1)}, bf16[16,3200]{1,0:T(8,128)(2,1)S(1)}, u32[]{:S(2)}, u32[]{:S(2)}) collective-permute-start(bf16[16,3200]{1,0:T(8,128)(2,1)S(1)} %finish.7), channel_id=1, source_target_pairs={{0,12},{1,13},{2,14},{3,15},{4,8},{5,9},{6,10},{7,11},{8,4},{9,5},... | collective-permute-start | bytes 307208 | tf_op jit(solution)/shard_map/ppermute | solution.py:346
  57.7 2.8 %collective-permute-done.25.packet.refs_6_ = bf16[16,3200]{1,0:T(8,128)(2,1)S(1)} collective-permute-done((bf16[16,3200]{1,0:T(8,128)(2,1)S(1)}, bf16[16,3200]{1,0:T(8,128)(2,1)S(1)}, u32[]{:S(2)}, u32[]{:S(2)}) %collective-permute-start.25) | collective-permute-done | bytes 102432 | tf_op jit(solution)/shard_map/ppermute | solution.py:346
  61.0 2.1 %collective-permute-start.28 = (bf16[16,3072]{1,0:T(8,128)(2,1)S(1)}, bf16[16,3072]{1,0:T(8,128)(2,1)S(1)}, u32[]{:S(2)}, u32[]{:S(2)}) collective-permute-start(bf16[16,3072]{1,0:T(8,128)(2,1)S(1)} %get-tuple-element.104.refs_0_), channel_id=1, source_target_pairs={{0,6},{1,7},{2,4},{3,5},{4,2},{5,3},{6,0},{7,1},{8,14},{9,15},{10,... | collective-permute-start | bytes 294920 | tf_op jit(solution)/shard_map/ppermute | solution.py:298
  64.5 2.9 %collective-permute-done.28.refs_3_ = bf16[16,3072]{1,0:T(8,128)(2,1)S(1)} collective-permute-done((bf16[16,3072]{1,0:T(8,128)(2,1)S(1)}, bf16[16,3072]{1,0:T(8,128)(2,1)S(1)}, u32[]{:S(2)}, u32[]{:S(2)}) %collective-permute-start.28) | collective-permute-done | bytes 98336 | tf_op jit(solution)/shard_map/ppermute | solution.py:298
  69.6 2.6 %block.8 = (f32[64,3072]{1,0:T(8,128)S(1)}, bf16[48,3072]{1,0:T(8,128)(2,1)S(1)}, bf16[16,3072]{1,0:T(8,128)(2,1)S(1)}, bf16[2,256,384]{2,1,0:T(8,128)(2,1)S(1)}) custom-call(s32[1]{0:T(128)} %bitcast.section.refs_0_, s32[2,6]{1,0:T(2,128)S(1)} %get-tuple-element.79.patch_flow, ...), custom_call_target="tpu_custom_call", output_to_operand_aliasing={{3}: (13, {})} | custom-call | flops 1207959552 | bytes 9437184 | tf_op jit(solution)/shard_map/block/pallas_call | solution.py:110
  74.0 2.4 %collective-permute-start.35 = (bf16[16,3072]{1,0:T(8,128)(2,1)S(1)}, bf16[16,3072]{1,0:T(8,128)(2,1)S(1)}, u32[]{:S(2)}, u32[]{:S(2)}) collective-permute-start(bf16[16,3072]{1,0:T(8,128)(2,1)S(1)} %split_last.8), channel_id=1, source_target_pairs={{0,6},{1,7},{2,4},{3,5},{4,2},{5,3},{6,0},{7,1},{8,14},{9,15},{10,... | collective-permute-start | bytes 294920 | tf_op jit(solution)/shard_map/ppermute | solution.py:298
  77.7 2.5 %collective-permute-done.35.refs_2_ = bf16[16,3072]{1,0:T(8,128)(2,1)S(1)} collective-permute-done((bf16[16,3072]{1,0:T(8,128)(2,1)S(1)}, bf16[16,3072]{1,0:T(8,128)(2,1)S(1)}, u32[]{:S(2)}, u32[]{:S(2)}) %collective-permute-start.35) | collective-permute-done | bytes 98336 | tf_op jit(solution)/shard_map/ppermute | solution.py:298
  80.2 1.6 collective-permute-done.36.refs_3_
  82.1 3.6 %collective-permute-start.38 = (bf16[16,3200]{1,0:T(8,128)(2,1)S(1)}, bf16[16,3200]{1,0:T(8,128)(2,1)S(1)}, u32[]{:S(2)}, u32[]{:S(2)}) collective-permute-start(bf16[16,3200]{1,0:T(8,128)(2,1)S(1)} %finish.8), channel_id=1, source_target_pairs={{0,12},{1,13},{2,14},{3,15},{4,8},{5,9},{6,10},{7,11},{8,4},{9,5},... | collective-permute-start | bytes 307208 | tf_op jit(solution)/shard_map/ppermute | solution.py:346
  85.7 2.9 %collective-permute-done.38.packet.refs_6_ = bf16[16,3200]{1,0:T(8,128)(2,1)S(1)} collective-permute-done((bf16[16,3200]{1,0:T(8,128)(2,1)S(1)}, bf16[16,3200]{1,0:T(8,128)(2,1)S(1)}, u32[]{:S(2)}, u32[]{:S(2)}) %collective-permute-start.38) | collective-permute-done | bytes 102432 | tf_op jit(solution)/shard_map/ppermute | solution.py:346
  89.2 3.0 %collective-permute-start.41 = (bf16[16,3072]{1,0:T(8,128)(2,1)S(1)}, bf16[16,3072]{1,0:T(8,128)(2,1)S(1)}, u32[]{:S(2)}, u32[]{:S(2)}) collective-permute-start(bf16[16,3072]{1,0:T(8,128)(2,1)S(1)} %get-tuple-element.113.refs_0_), channel_id=1, source_target_pairs={{0,6},{1,7},{2,4},{3,5},{4,2},{5,3},{6,0},{7,1},{8,14},{9,15},{10,... | collective-permute-start | bytes 294920 | tf_op jit(solution)/shard_map/ppermute | solution.py:298
  92.8 2.6 %collective-permute-done.41.refs_3_ = bf16[16,3072]{1,0:T(8,128)(2,1)S(1)} collective-permute-done((bf16[16,3072]{1,0:T(8,128)(2,1)S(1)}, bf16[16,3072]{1,0:T(8,128)(2,1)S(1)}, u32[]{:S(2)}, u32[]{:S(2)}) %collective-permute-start.41) | collective-permute-done | bytes 98336 | tf_op jit(solution)/shard_map/ppermute | solution.py:298
  95.4 1.4 collective-permute-done.40.refs_2_
  98.2 2.6 %block.9 = (f32[64,3072]{1,0:T(8,128)S(1)}, bf16[48,3072]{1,0:T(8,128)(2,1)S(1)}, bf16[16,3072]{1,0:T(8,128)(2,1)S(1)}, bf16[2,256,384]{2,1,0:T(8,128)(2,1)S(1)}) custom-call(s32[1]{0:T(128)} %bitcast.section.refs_0_, s32[2,6]{1,0:T(2,128)S(1)} %get-tuple-element.79.patch_flow, ...), custom_call_target="tpu_custom_call", output_to_operand_aliasing={{3}: (13, {})} | custom-call | flops 1207959552 | bytes 9437184 | tf_op jit(solution)/shard_map/block/pallas_call | solution.py:110
  102.7 2.6 %collective-permute-start.48 = (bf16[16,3072]{1,0:T(8,128)(2,1)S(1)}, bf16[16,3072]{1,0:T(8,128)(2,1)S(1)}, u32[]{:S(2)}, u32[]{:S(2)}) collective-permute-start(bf16[16,3072]{1,0:T(8,128)(2,1)S(1)} %split_last.9), channel_id=1, source_target_pairs={{0,6},{1,7},{2,4},{3,5},{4,2},{5,3},{6,0},{7,1},{8,14},{9,15},{10,... | collective-permute-start | bytes 294920 | tf_op jit(solution)/shard_map/ppermute | solution.py:298
  106.4 2.7 %collective-permute-done.48.refs_2_ = bf16[16,3072]{1,0:T(8,128)(2,1)S(1)} collective-permute-done((bf16[16,3072]{1,0:T(8,128)(2,1)S(1)}, bf16[16,3072]{1,0:T(8,128)(2,1)S(1)}, u32[]{:S(2)}, u32[]{:S(2)}) %collective-permute-start.48) | collective-permute-done | bytes 98336 | tf_op jit(solution)/shard_map/ppermute | solution.py:298
  110.9 3.1 %collective-permute-start.51 = (bf16[16,3200]{1,0:T(8,128)(2,1)S(1)}, bf16[16,3200]{1,0:T(8,128)(2,1)S(1)}, u32[]{:S(2)}, u32[]{:S(2)}) collective-permute-start(bf16[16,3200]{1,0:T(8,128)(2,1)S(1)} %finish.9), channel_id=1, source_target_pairs={{0,12},{1,13},{2,14},{3,15},{4,8},{5,9},{6,10},{7,11},{8,4},{9,5},... | collective-permute-start | bytes 307208 | tf_op jit(solution)/shard_map/ppermute | solution.py:346
  114.0 3.4 %collective-permute-done.51.packet.refs_6_ = bf16[16,3200]{1,0:T(8,128)(2,1)S(1)} collective-permute-done((bf16[16,3200]{1,0:T(8,128)(2,1)S(1)}, bf16[16,3200]{1,0:T(8,128)(2,1)S(1)}, u32[]{:S(2)}, u32[]{:S(2)}) %collective-permute-start.51) | collective-permute-done | bytes 102432 | tf_op jit(solution)/shard_map/ppermute | solution.py:346
  117.8 2.4 %collective-permute-start.54 = (bf16[16,3072]{1,0:T(8,128)(2,1)S(1)}, bf16[16,3072]{1,0:T(8,128)(2,1)S(1)}, u32[]{:S(2)}, u32[]{:S(2)}) collective-permute-start(bf16[16,3072]{1,0:T(8,128)(2,1)S(1)} %get-tuple-element.122.refs_0_), channel_id=1, source_target_pairs={{0,6},{1,7},{2,4},{3,5},{4,2},{5,3},{6,0},{7,1},{8,14},{9,15},{10,... | collective-permute-start | bytes 294920 | tf_op jit(solution)/shard_map/ppermute | solution.py:298
  121.4 3.0 %collective-permute-done.54.refs_3_ = bf16[16,3072]{1,0:T(8,128)(2,1)S(1)} collective-permute-done((bf16[16,3072]{1,0:T(8,128)(2,1)S(1)}, bf16[16,3072]{1,0:T(8,128)(2,1)S(1)}, u32[]{:S(2)}, u32[]{:S(2)}) %collective-permute-start.54) | collective-permute-done | bytes 98336 | tf_op jit(solution)/shard_map/ppermute | solution.py:298
  126.6 2.6 %block.10 = (f32[64,3072]{1,0:T(8,128)S(1)}, bf16[48,3072]{1,0:T(8,128)(2,1)S(1)}, bf16[16,3072]{1,0:T(8,128)(2,1)S(1)}, bf16[2,256,384]{2,1,0:T(8,128)(2,1)S(1)}) custom-call(s32[1]{0:T(128)} %bitcast.section.refs_0_, s32[2,6]{1,0:T(2,128)S(1)} %get-tuple-element.79.patch_flow, ...), custom_call_target="tpu_custom_call", output_to_operand_aliasing={{3}: (13, {})} | custom-call | flops 1207959552 | bytes 9437184 | tf_op jit(solution)/shard_map/block/pallas_call | solution.py:110
  131.1 2.3 %collective-permute-start.61 = (bf16[16,3072]{1,0:T(8,128)(2,1)S(1)}, bf16[16,3072]{1,0:T(8,128)(2,1)S(1)}, u32[]{:S(2)}, u32[]{:S(2)}) collective-permute-start(bf16[16,3072]{1,0:T(8,128)(2,1)S(1)} %split_last.10), channel_id=1, source_target_pairs={{0,6},{1,7},{2,4},{3,5},{4,2},{5,3},{6,0},{7,1},{8,14},{9,15},{10,... | collective-permute-start | bytes 294920 | tf_op jit(solution)/shard_map/ppermute | solution.py:298
  134.8 2.6 %collective-permute-done.61.refs_2_ = bf16[16,3072]{1,0:T(8,128)(2,1)S(1)} collective-permute-done((bf16[16,3072]{1,0:T(8,128)(2,1)S(1)}, bf16[16,3072]{1,0:T(8,128)(2,1)S(1)}, u32[]{:S(2)}, u32[]{:S(2)}) %collective-permute-start.61) | collective-permute-done | bytes 98336 | tf_op jit(solution)/shard_map/ppermute | solution.py:298
  137.4 1.2 collective-permute-done.62.refs_3_
  139.1 2.8 %collective-permute-start.64 = (bf16[16,3200]{1,0:T(8,128)(2,1)S(1)}, bf16[16,3200]{1,0:T(8,128)(2,1)S(1)}, u32[]{:S(2)}, u32[]{:S(2)}) collective-permute-start(bf16[16,3200]{1,0:T(8,128)(2,1)S(1)} %finish.10), channel_id=1, source_target_pairs={{0,12},{1,13},{2,14},{3,15},{4,8},{5,9},{6,10},{7,11},{8,4},{9,5},... | collective-permute-start | bytes 307208 | tf_op jit(solution)/shard_map/ppermute | solution.py:346
  141.9 3.7 %collective-permute-done.64.packet.refs_6_ = bf16[16,3200]{1,0:T(8,128)(2,1)S(1)} collective-permute-done((bf16[16,3200]{1,0:T(8,128)(2,1)S(1)}, bf16[16,3200]{1,0:T(8,128)(2,1)S(1)}, u32[]{:S(2)}, u32[]{:S(2)}) %collective-permute-start.64) | collective-permute-done | bytes 102432 | tf_op jit(solution)/shard_map/ppermute | solution.py:346
  146.1 2.6 %collective-permute-start.67 = (bf16[16,3072]{1,0:T(8,128)(2,1)S(1)}, bf16[16,3072]{1,0:T(8,128)(2,1)S(1)}, u32[]{:S(2)}, u32[]{:S(2)}) collective-permute-start(bf16[16,3072]{1,0:T(8,128)(2,1)S(1)} %get-tuple-element.131.refs_0_), channel_id=1, source_target_pairs={{0,6},{1,7},{2,4},{3,5},{4,2},{5,3},{6,0},{7,1},{8,14},{9,15},{10,... | collective-permute-start | bytes 294920 | tf_op jit(solution)/shard_map/ppermute | solution.py:298
  149.6 2.8 %collective-permute-done.67.refs_3_ = bf16[16,3072]{1,0:T(8,128)(2,1)S(1)} collective-permute-done((bf16[16,3072]{1,0:T(8,128)(2,1)S(1)}, bf16[16,3072]{1,0:T(8,128)(2,1)S(1)}, u32[]{:S(2)}, u32[]{:S(2)}) %collective-permute-start.67) | collective-permute-done | bytes 98336 | tf_op jit(solution)/shard_map/ppermute | solution.py:298
  154.9 2.7 %block.11 = (f32[64,3072]{1,0:T(8,128)S(1)}, bf16[48,3072]{1,0:T(8,128)(2,1)S(1)}, bf16[16,3072]{1,0:T(8,128)(2,1)S(1)}, bf16[2,256,384]{2,1,0:T(8,128)(2,1)S(1)}) custom-call(s32[1]{0:T(128)} %bitcast.section.refs_0_, s32[2,6]{1,0:T(2,128)S(1)} %get-tuple-element.79.patch_flow, ...), custom_call_target="tpu_custom_call", output_to_operand_aliasing={{3}: (13, {})} | custom-call | flops 1207959552 | bytes 9437184 | tf_op jit(solution)/shard_map/block/pallas_call | solution.py:110
  159.4 2.3 %collective-permute-start.74 = (bf16[16,3072]{1,0:T(8,128)(2,1)S(1)}, bf16[16,3072]{1,0:T(8,128)(2,1)S(1)}, u32[]{:S(2)}, u32[]{:S(2)}) collective-permute-start(bf16[16,3072]{1,0:T(8,128)(2,1)S(1)} %split_last.11), channel_id=1, source_target_pairs={{0,6},{1,7},{2,4},{3,5},{4,2},{5,3},{6,0},{7,1},{8,14},{9,15},{10,... | collective-permute-start | bytes 294920 | tf_op jit(solution)/shard_map/ppermute | solution.py:298
  161.9 1.2 collective-permute-start.76
  163.1 2.9 %collective-permute-done.74.refs_2_ = bf16[16,3072]{1,0:T(8,128)(2,1)S(1)} collective-permute-done((bf16[16,3072]{1,0:T(8,128)(2,1)S(1)}, bf16[16,3072]{1,0:T(8,128)(2,1)S(1)}, u32[]{:S(2)}, u32[]{:S(2)}) %collective-permute-start.74) | collective-permute-done | bytes 98336 | tf_op jit(solution)/shard_map/ppermute | solution.py:298
  167.5 3.0 %collective-permute-start.77 = (bf16[16,3200]{1,0:T(8,128)(2,1)S(1)}, bf16[16,3200]{1,0:T(8,128)(2,1)S(1)}, u32[]{:S(2)}, u32[]{:S(2)}) collective-permute-start(bf16[16,3200]{1,0:T(8,128)(2,1)S(1)} %finish.11), channel_id=1, source_target_pairs={{0,12},{1,13},{2,14},{3,15},{4,8},{5,9},{6,10},{7,11},{8,4},{9,5},... | collective-permute-start | bytes 307208 | tf_op jit(solution)/shard_map/ppermute | solution.py:346
  170.6 3.5 %collective-permute-done.77.packet = bf16[16,3200]{1,0:T(8,128)(2,1)S(1)} collective-permute-done((bf16[16,3200]{1,0:T(8,128)(2,1)S(1)}, bf16[16,3200]{1,0:T(8,128)(2,1)S(1)}, u32[]{:S(2)}, u32[]{:S(2)}) %collective-permute-start.77) | collective-permute-done | bytes 102432 | tf_op jit(solution)/shard_map/ppermute | solution.py:346
  (149 shorter events, 44.9 us)
Async XLA Ops:
  0.7 8.7 %collective-permute-start.2 = (bf16[16,3072]{1,0:T(8,128)(2,1)}, bf16[16,3072]{1,0:T(8,128)(2,1)S(1)}, u32[]{:S(2)}, u32[]{:S(2)}) collective-permute-start(bf16[16,3072]{1,0:T(8,128)(2,1)} %refs_5_.1), channel_id=1, source_target_pairs={{0,6},{1,7},{2,4},{3,5},{4,2},{5,3},{6,0},{7,1},{8,14},{9,15},{10,... | collective-permute-start | bytes 294920 | tf_op jit(solution)/shard_map/ppermute | solution.py:298
  4.7 5.4 %collective-permute-start.1 = (bf16[16,3072]{1,0:T(8,128)(2,1)}, bf16[16,3072]{1,0:T(8,128)(2,1)S(1)}, u32[]{:S(2)}, u32[]{:S(2)}) collective-permute-start(bf16[16,3072]{1,0:T(8,128)(2,1)} %refs_5_.1), channel_id=1, source_target_pairs={{0,4},{1,5},{2,6},{3,7},{4,0},{5,1},{6,2},{7,3},{8,12},{9,13},{10,... | collective-permute-start | bytes 294920 | tf_op jit(solution)/shard_map/ppermute | solution.py:298
  5.2 4.9 %collective-permute-start = (bf16[16,3072]{1,0:T(8,128)(2,1)}, bf16[16,3072]{1,0:T(8,128)(2,1)S(1)}, u32[]{:S(2)}, u32[]{:S(2)}) collective-permute-start(bf16[16,3072]{1,0:T(8,128)(2,1)} %refs_5_.1), channel_id=1, source_target_pairs={{0,2},{1,3},{2,0},{3,1},{4,6},{5,7},{6,4},{7,5},{8,10},{9,11},{10,... | collective-permute-start | bytes 294920 | tf_op jit(solution)/shard_map/ppermute | solution.py:298
  15.1 4.3 %collective-permute-start.7 = (bf16[48,3072]{1,0:T(8,128)(2,1)S(1)}, bf16[48,3072]{1,0:T(8,128)(2,1)S(1)}, u32[]{:S(2)}, u32[]{:S(2)}) collective-permute-start(bf16[48,3072]{1,0:T(8,128)(2,1)S(1)} %get-tuple-element.90), channel_id=1, source_target_pairs={{0,1},{1,0},{2,3},{3,2},{4,5},{5,4},{6,7},{7,6},{8,9},{9,8},{10,11... | collective-permute-start | bytes 884744 | tf_op jit(solution)/shard_map/ppermute | solution.py:298
  16.9 6.6 %collective-permute-start.9 = (bf16[16,3072]{1,0:T(8,128)(2,1)S(1)}, bf16[16,3072]{1,0:T(8,128)(2,1)S(1)}, u32[]{:S(2)}, u32[]{:S(2)}) collective-permute-start(bf16[16,3072]{1,0:T(8,128)(2,1)S(1)} %split_last.6), channel_id=1, source_target_pairs={{0,6},{1,7},{2,4},{3,5},{4,2},{5,3},{6,0},{7,1},{8,14},{9,15},{10,... | collective-permute-start | bytes 294920 | tf_op jit(solution)/shard_map/ppermute | solution.py:298
  19.5 5.5 %collective-permute-start.10 = (bf16[16,3072]{1,0:T(8,128)(2,1)S(1)}, bf16[16,3072]{1,0:T(8,128)(2,1)S(1)}, u32[]{:S(2)}, u32[]{:S(2)}) collective-permute-start(bf16[16,3072]{1,0:T(8,128)(2,1)S(1)} %get-tuple-element.93), channel_id=1, source_target_pairs={{0,4},{1,5},{2,6},{3,7},{4,0},{5,1},{6,2},{7,3},{8,12},{9,13},{10,... | collective-permute-start | bytes 294920 | tf_op jit(solution)/shard_map/ppermute | solution.py:298
  20.0 5.1 %collective-permute-start.11 = (bf16[16,3072]{1,0:T(8,128)(2,1)S(1)}, bf16[16,3072]{1,0:T(8,128)(2,1)S(1)}, u32[]{:S(2)}, u32[]{:S(2)}) collective-permute-start(bf16[16,3072]{1,0:T(8,128)(2,1)S(1)} %get-tuple-element.94), channel_id=1, source_target_pairs={{0,2},{1,3},{2,0},{3,1},{4,6},{5,7},{6,4},{7,5},{8,10},{9,11},{10,... | collective-permute-start | bytes 294920 | tf_op jit(solution)/shard_map/ppermute | solution.py:298
  25.2 6.9 %collective-permute-start.12 = (bf16[16,3200]{1,0:T(8,128)(2,1)S(1)}, bf16[16,3200]{1,0:T(8,128)(2,1)S(1)}, u32[]{:S(2)}, u32[]{:S(2)}) collective-permute-start(bf16[16,3200]{1,0:T(8,128)(2,1)S(1)} %finish.6), channel_id=1, source_target_pairs={{0,12},{1,13},{2,14},{3,15},{4,8},{5,9},{6,10},{7,11},{8,4},{9,5},... | collective-permute-start | bytes 307208 | tf_op jit(solution)/shard_map/ppermute | solution.py:346
  32.5 6.0 %collective-permute-start.15 = (bf16[16,3072]{1,0:T(8,128)(2,1)S(1)}, bf16[16,3072]{1,0:T(8,128)(2,1)S(1)}, u32[]{:S(2)}, u32[]{:S(2)}) collective-permute-start(bf16[16,3072]{1,0:T(8,128)(2,1)S(1)} %get-tuple-element.95.refs_0_), channel_id=1, source_target_pairs={{0,6},{1,7},{2,4},{3,5},{4,2},{5,3},{6,0},{7,1},{8,14},{9,15},{10,... | collective-permute-start | bytes 294920 | tf_op jit(solution)/shard_map/ppermute | solution.py:298
  35.2 4.7 %collective-permute-start.14 = (bf16[16,3072]{1,0:T(8,128)(2,1)S(1)}, bf16[16,3072]{1,0:T(8,128)(2,1)S(1)}, u32[]{:S(2)}, u32[]{:S(2)}) collective-permute-start(bf16[16,3072]{1,0:T(8,128)(2,1)S(1)} %get-tuple-element.95.refs_0_), channel_id=1, source_target_pairs={{0,4},{1,5},{2,6},{3,7},{4,0},{5,1},{6,2},{7,3},{8,12},{9,13},{10,... | collective-permute-start | bytes 294920 | tf_op jit(solution)/shard_map/ppermute | solution.py:298
  35.5 4.6 %collective-permute-start.13 = (bf16[16,3072]{1,0:T(8,128)(2,1)S(1)}, bf16[16,3072]{1,0:T(8,128)(2,1)S(1)}, u32[]{:S(2)}, u32[]{:S(2)}) collective-permute-start(bf16[16,3072]{1,0:T(8,128)(2,1)S(1)} %get-tuple-element.95.refs_0_), channel_id=1, source_target_pairs={{0,2},{1,3},{2,0},{3,1},{4,6},{5,7},{6,4},{7,5},{8,10},{9,11},{10,... | collective-permute-start | bytes 294920 | tf_op jit(solution)/shard_map/ppermute | solution.py:298
  36.1 4.3 %collective-permute-start.16 = (bf16[16,3072]{1,0:T(8,128)(2,1)S(1)}, bf16[16,3072]{1,0:T(8,128)(2,1)S(1)}, u32[]{:S(2)}, u32[]{:S(2)}) collective-permute-start(bf16[16,3072]{1,0:T(8,128)(2,1)S(1)} %get-tuple-element.95.refs_0_), channel_id=1, source_target_pairs={{0,1},{1,0},{2,3},{3,2},{4,5},{5,4},{6,7},{7,6},{8,9},{9,8},{10,11... | collective-permute-start | bytes 294920 | tf_op jit(solution)/shard_map/ppermute | solution.py:298
  45.9 6.5 %collective-permute-start.22 = (bf16[16,3072]{1,0:T(8,128)(2,1)S(1)}, bf16[16,3072]{1,0:T(8,128)(2,1)S(1)}, u32[]{:S(2)}, u32[]{:S(2)}) collective-permute-start(bf16[16,3072]{1,0:T(8,128)(2,1)S(1)} %split_last.7), channel_id=1, source_target_pairs={{0,6},{1,7},{2,4},{3,5},{4,2},{5,3},{6,0},{7,1},{8,14},{9,15},{10,... | collective-permute-start | bytes 294920 | tf_op jit(solution)/shard_map/ppermute | solution.py:298
  48.0 5.4 %collective-permute-start.23 = (bf16[16,3072]{1,0:T(8,128)(2,1)S(1)}, bf16[16,3072]{1,0:T(8,128)(2,1)S(1)}, u32[]{:S(2)}, u32[]{:S(2)}) collective-permute-start(bf16[16,3072]{1,0:T(8,128)(2,1)S(1)} %get-tuple-element.101), channel_id=1, source_target_pairs={{0,4},{1,5},{2,6},{3,7},{4,0},{5,1},{6,2},{7,3},{8,12},{9,13},{10,... | collective-permute-start | bytes 294920 | tf_op jit(solution)/shard_map/ppermute | solution.py:298
  48.6 5.3 %collective-permute-start.24 = (bf16[16,3072]{1,0:T(8,128)(2,1)S(1)}, bf16[16,3072]{1,0:T(8,128)(2,1)S(1)}, u32[]{:S(2)}, u32[]{:S(2)}) collective-permute-start(bf16[16,3072]{1,0:T(8,128)(2,1)S(1)} %get-tuple-element.102), channel_id=1, source_target_pairs={{0,2},{1,3},{2,0},{3,1},{4,6},{5,7},{6,4},{7,5},{8,10},{9,11},{10,... | collective-permute-start | bytes 294920 | tf_op jit(solution)/shard_map/ppermute | solution.py:298
  54.0 6.5 %collective-permute-start.25 = (bf16[16,3200]{1,0:T(8,128)(2,1)S(1)}, bf16[16,3200]{1,0:T(8,128)(2,1)S(1)}, u32[]{:S(2)}, u32[]{:S(2)}) collective-permute-start(bf16[16,3200]{1,0:T(8,128)(2,1)S(1)} %finish.7), channel_id=1, source_target_pairs={{0,12},{1,13},{2,14},{3,15},{4,8},{5,9},{6,10},{7,11},{8,4},{9,5},... | collective-permute-start | bytes 307208 | tf_op jit(solution)/shard_map/ppermute | solution.py:346
  61.0 6.5 %collective-permute-start.28 = (bf16[16,3072]{1,0:T(8,128)(2,1)S(1)}, bf16[16,3072]{1,0:T(8,128)(2,1)S(1)}, u32[]{:S(2)}, u32[]{:S(2)}) collective-permute-start(bf16[16,3072]{1,0:T(8,128)(2,1)S(1)} %get-tuple-element.104.refs_0_), channel_id=1, source_target_pairs={{0,6},{1,7},{2,4},{3,5},{4,2},{5,3},{6,0},{7,1},{8,14},{9,15},{10,... | collective-permute-start | bytes 294920 | tf_op jit(solution)/shard_map/ppermute | solution.py:298
  63.0 4.7 %collective-permute-start.27 = (bf16[16,3072]{1,0:T(8,128)(2,1)S(1)}, bf16[16,3072]{1,0:T(8,128)(2,1)S(1)}, u32[]{:S(2)}, u32[]{:S(2)}) collective-permute-start(bf16[16,3072]{1,0:T(8,128)(2,1)S(1)} %get-tuple-element.104.refs_0_), channel_id=1, source_target_pairs={{0,4},{1,5},{2,6},{3,7},{4,0},{5,1},{6,2},{7,3},{8,12},{9,13},{10,... | collective-permute-start | bytes 294920 | tf_op jit(solution)/shard_map/ppermute | solution.py:298
  63.4 4.8 %collective-permute-start.26 = (bf16[16,3072]{1,0:T(8,128)(2,1)S(1)}, bf16[16,3072]{1,0:T(8,128)(2,1)S(1)}, u32[]{:S(2)}, u32[]{:S(2)}) collective-permute-start(bf16[16,3072]{1,0:T(8,128)(2,1)S(1)} %get-tuple-element.104.refs_0_), channel_id=1, source_target_pairs={{0,2},{1,3},{2,0},{3,1},{4,6},{5,7},{6,4},{7,5},{8,10},{9,11},{10,... | collective-permute-start | bytes 294920 | tf_op jit(solution)/shard_map/ppermute | solution.py:298
  72.2 4.2 %collective-permute-start.33 = (bf16[48,3072]{1,0:T(8,128)(2,1)S(1)}, bf16[48,3072]{1,0:T(8,128)(2,1)S(1)}, u32[]{:S(2)}, u32[]{:S(2)}) collective-permute-start(bf16[48,3072]{1,0:T(8,128)(2,1)S(1)} %get-tuple-element.107), channel_id=1, source_target_pairs={{0,1},{1,0},{2,3},{3,2},{4,5},{5,4},{6,7},{7,6},{8,9},{9,8},{10,11... | collective-permute-start | bytes 884744 | tf_op jit(solution)/shard_map/ppermute | solution.py:298
  74.0 6.2 %collective-permute-start.35 = (bf16[16,3072]{1,0:T(8,128)(2,1)S(1)}, bf16[16,3072]{1,0:T(8,128)(2,1)S(1)}, u32[]{:S(2)}, u32[]{:S(2)}) collective-permute-start(bf16[16,3072]{1,0:T(8,128)(2,1)S(1)} %split_last.8), channel_id=1, source_target_pairs={{0,6},{1,7},{2,4},{3,5},{4,2},{5,3},{6,0},{7,1},{8,14},{9,15},{10,... | collective-permute-start | bytes 294920 | tf_op jit(solution)/shard_map/ppermute | solution.py:298
  76.5 5.3 %collective-permute-start.36 = (bf16[16,3072]{1,0:T(8,128)(2,1)S(1)}, bf16[16,3072]{1,0:T(8,128)(2,1)S(1)}, u32[]{:S(2)}, u32[]{:S(2)}) collective-permute-start(bf16[16,3072]{1,0:T(8,128)(2,1)S(1)} %get-tuple-element.110), channel_id=1, source_target_pairs={{0,4},{1,5},{2,6},{3,7},{4,0},{5,1},{6,2},{7,3},{8,12},{9,13},{10,... | collective-permute-start | bytes 294920 | tf_op jit(solution)/shard_map/ppermute | solution.py:298
  76.8 5.2 %collective-permute-start.37 = (bf16[16,3072]{1,0:T(8,128)(2,1)S(1)}, bf16[16,3072]{1,0:T(8,128)(2,1)S(1)}, u32[]{:S(2)}, u32[]{:S(2)}) collective-permute-start(bf16[16,3072]{1,0:T(8,128)(2,1)S(1)} %get-tuple-element.111), channel_id=1, source_target_pairs={{0,2},{1,3},{2,0},{3,1},{4,6},{5,7},{6,4},{7,5},{8,10},{9,11},{10,... | collective-permute-start | bytes 294920 | tf_op jit(solution)/shard_map/ppermute | solution.py:298
  82.1 6.5 %collective-permute-start.38 = (bf16[16,3200]{1,0:T(8,128)(2,1)S(1)}, bf16[16,3200]{1,0:T(8,128)(2,1)S(1)}, u32[]{:S(2)}, u32[]{:S(2)}) collective-permute-start(bf16[16,3200]{1,0:T(8,128)(2,1)S(1)} %finish.8), channel_id=1, source_target_pairs={{0,12},{1,13},{2,14},{3,15},{4,8},{5,9},{6,10},{7,11},{8,4},{9,5},... | collective-permute-start | bytes 307208 | tf_op jit(solution)/shard_map/ppermute | solution.py:346
  89.2 6.2 %collective-permute-start.41 = (bf16[16,3072]{1,0:T(8,128)(2,1)S(1)}, bf16[16,3072]{1,0:T(8,128)(2,1)S(1)}, u32[]{:S(2)}, u32[]{:S(2)}) collective-permute-start(bf16[16,3072]{1,0:T(8,128)(2,1)S(1)} %get-tuple-element.113.refs_0_), channel_id=1, source_target_pairs={{0,6},{1,7},{2,4},{3,5},{4,2},{5,3},{6,0},{7,1},{8,14},{9,15},{10,... | collective-permute-start | bytes 294920 | tf_op jit(solution)/shard_map/ppermute | solution.py:298
  92.1 4.6 %collective-permute-start.40 = (bf16[16,3072]{1,0:T(8,128)(2,1)S(1)}, bf16[16,3072]{1,0:T(8,128)(2,1)S(1)}, u32[]{:S(2)}, u32[]{:S(2)}) collective-permute-start(bf16[16,3072]{1,0:T(8,128)(2,1)S(1)} %get-tuple-element.113.refs_0_), channel_id=1, source_target_pairs={{0,4},{1,5},{2,6},{3,7},{4,0},{5,1},{6,2},{7,3},{8,12},{9,13},{10,... | collective-permute-start | bytes 294920 | tf_op jit(solution)/shard_map/ppermute | solution.py:298
  92.1 4.7 %collective-permute-start.39 = (bf16[16,3072]{1,0:T(8,128)(2,1)S(1)}, bf16[16,3072]{1,0:T(8,128)(2,1)S(1)}, u32[]{:S(2)}, u32[]{:S(2)}) collective-permute-start(bf16[16,3072]{1,0:T(8,128)(2,1)S(1)} %get-tuple-element.113.refs_0_), channel_id=1, source_target_pairs={{0,2},{1,3},{2,0},{3,1},{4,6},{5,7},{6,4},{7,5},{8,10},{9,11},{10,... | collective-permute-start | bytes 294920 | tf_op jit(solution)/shard_map/ppermute | solution.py:298
  92.8 4.5 %collective-permute-start.42 = (bf16[16,3072]{1,0:T(8,128)(2,1)S(1)}, bf16[16,3072]{1,0:T(8,128)(2,1)S(1)}, u32[]{:S(2)}, u32[]{:S(2)}) collective-permute-start(bf16[16,3072]{1,0:T(8,128)(2,1)S(1)} %get-tuple-element.113.refs_0_), channel_id=1, source_target_pairs={{0,1},{1,0},{2,3},{3,2},{4,5},{5,4},{6,7},{7,6},{8,9},{9,8},{10,11... | collective-permute-start | bytes 294920 | tf_op jit(solution)/shard_map/ppermute | solution.py:298
  100.8 4.4 %collective-permute-start.46 = (bf16[48,3072]{1,0:T(8,128)(2,1)S(1)}, bf16[48,3072]{1,0:T(8,128)(2,1)S(1)}, u32[]{:S(2)}, u32[]{:S(2)}) collective-permute-start(bf16[48,3072]{1,0:T(8,128)(2,1)S(1)} %get-tuple-element.116), channel_id=1, source_target_pairs={{0,1},{1,0},{2,3},{3,2},{4,5},{5,4},{6,7},{7,6},{8,9},{9,8},{10,11... | collective-permute-start | bytes 884744 | tf_op jit(solution)/shard_map/ppermute | solution.py:298
  102.7 6.5 %collective-permute-start.48 = (bf16[16,3072]{1,0:T(8,128)(2,1)S(1)}, bf16[16,3072]{1,0:T(8,128)(2,1)S(1)}, u32[]{:S(2)}, u32[]{:S(2)}) collective-permute-start(bf16[16,3072]{1,0:T(8,128)(2,1)S(1)} %split_last.9), channel_id=1, source_target_pairs={{0,6},{1,7},{2,4},{3,5},{4,2},{5,3},{6,0},{7,1},{8,14},{9,15},{10,... | collective-permute-start | bytes 294920 | tf_op jit(solution)/shard_map/ppermute | solution.py:298
  105.3 4.8 %collective-permute-start.49 = (bf16[16,3072]{1,0:T(8,128)(2,1)S(1)}, bf16[16,3072]{1,0:T(8,128)(2,1)S(1)}, u32[]{:S(2)}, u32[]{:S(2)}) collective-permute-start(bf16[16,3072]{1,0:T(8,128)(2,1)S(1)} %get-tuple-element.119), channel_id=1, source_target_pairs={{0,4},{1,5},{2,6},{3,7},{4,0},{5,1},{6,2},{7,3},{8,12},{9,13},{10,... | collective-permute-start | bytes 294920 | tf_op jit(solution)/shard_map/ppermute | solution.py:298
  105.4 5.4 %collective-permute-start.50 = (bf16[16,3072]{1,0:T(8,128)(2,1)S(1)}, bf16[16,3072]{1,0:T(8,128)(2,1)S(1)}, u32[]{:S(2)}, u32[]{:S(2)}) collective-permute-start(bf16[16,3072]{1,0:T(8,128)(2,1)S(1)} %get-tuple-element.120), channel_id=1, source_target_pairs={{0,2},{1,3},{2,0},{3,1},{4,6},{5,7},{6,4},{7,5},{8,10},{9,11},{10,... | collective-permute-start | bytes 294920 | tf_op jit(solution)/shard_map/ppermute | solution.py:298
  110.9 6.5 %collective-permute-start.51 = (bf16[16,3200]{1,0:T(8,128)(2,1)S(1)}, bf16[16,3200]{1,0:T(8,128)(2,1)S(1)}, u32[]{:S(2)}, u32[]{:S(2)}) collective-permute-start(bf16[16,3200]{1,0:T(8,128)(2,1)S(1)} %finish.9), channel_id=1, source_target_pairs={{0,12},{1,13},{2,14},{3,15},{4,8},{5,9},{6,10},{7,11},{8,4},{9,5},... | collective-permute-start | bytes 307208 | tf_op jit(solution)/shard_map/ppermute | solution.py:346
  117.8 6.6 %collective-permute-start.54 = (bf16[16,3072]{1,0:T(8,128)(2,1)S(1)}, bf16[16,3072]{1,0:T(8,128)(2,1)S(1)}, u32[]{:S(2)}, u32[]{:S(2)}) collective-permute-start(bf16[16,3072]{1,0:T(8,128)(2,1)S(1)} %get-tuple-element.122.refs_0_), channel_id=1, source_target_pairs={{0,6},{1,7},{2,4},{3,5},{4,2},{5,3},{6,0},{7,1},{8,14},{9,15},{10,... | collective-permute-start | bytes 294920 | tf_op jit(solution)/shard_map/ppermute | solution.py:298
  120.2 4.6 %collective-permute-start.53 = (bf16[16,3072]{1,0:T(8,128)(2,1)S(1)}, bf16[16,3072]{1,0:T(8,128)(2,1)S(1)}, u32[]{:S(2)}, u32[]{:S(2)}) collective-permute-start(bf16[16,3072]{1,0:T(8,128)(2,1)S(1)} %get-tuple-element.122.refs_0_), channel_id=1, source_target_pairs={{0,4},{1,5},{2,6},{3,7},{4,0},{5,1},{6,2},{7,3},{8,12},{9,13},{10,... | collective-permute-start | bytes 294920 | tf_op jit(solution)/shard_map/ppermute | solution.py:298
  120.2 5.1 %collective-permute-start.52 = (bf16[16,3072]{1,0:T(8,128)(2,1)S(1)}, bf16[16,3072]{1,0:T(8,128)(2,1)S(1)}, u32[]{:S(2)}, u32[]{:S(2)}) collective-permute-start(bf16[16,3072]{1,0:T(8,128)(2,1)S(1)} %get-tuple-element.122.refs_0_), channel_id=1, source_target_pairs={{0,2},{1,3},{2,0},{3,1},{4,6},{5,7},{6,4},{7,5},{8,10},{9,11},{10,... | collective-permute-start | bytes 294920 | tf_op jit(solution)/shard_map/ppermute | solution.py:298
  131.1 6.3 %collective-permute-start.61 = (bf16[16,3072]{1,0:T(8,128)(2,1)S(1)}, bf16[16,3072]{1,0:T(8,128)(2,1)S(1)}, u32[]{:S(2)}, u32[]{:S(2)}) collective-permute-start(bf16[16,3072]{1,0:T(8,128)(2,1)S(1)} %split_last.10), channel_id=1, source_target_pairs={{0,6},{1,7},{2,4},{3,5},{4,2},{5,3},{6,0},{7,1},{8,14},{9,15},{10,... | collective-permute-start | bytes 294920 | tf_op jit(solution)/shard_map/ppermute | solution.py:298
  133.5 5.2 %collective-permute-start.62 = (bf16[16,3072]{1,0:T(8,128)(2,1)S(1)}, bf16[16,3072]{1,0:T(8,128)(2,1)S(1)}, u32[]{:S(2)}, u32[]{:S(2)}) collective-permute-start(bf16[16,3072]{1,0:T(8,128)(2,1)S(1)} %get-tuple-element.128), channel_id=1, source_target_pairs={{0,4},{1,5},{2,6},{3,7},{4,0},{5,1},{6,2},{7,3},{8,12},{9,13},{10,... | collective-permute-start | bytes 294920 | tf_op jit(solution)/shard_map/ppermute | solution.py:298
  133.7 5.4 %collective-permute-start.63 = (bf16[16,3072]{1,0:T(8,128)(2,1)S(1)}, bf16[16,3072]{1,0:T(8,128)(2,1)S(1)}, u32[]{:S(2)}, u32[]{:S(2)}) collective-permute-start(bf16[16,3072]{1,0:T(8,128)(2,1)S(1)} %get-tuple-element.129), channel_id=1, source_target_pairs={{0,2},{1,3},{2,0},{3,1},{4,6},{5,7},{6,4},{7,5},{8,10},{9,11},{10,... | collective-permute-start | bytes 294920 | tf_op jit(solution)/shard_map/ppermute | solution.py:298
  139.1 6.5 %collective-permute-start.64 = (bf16[16,3200]{1,0:T(8,128)(2,1)S(1)}, bf16[16,3200]{1,0:T(8,128)(2,1)S(1)}, u32[]{:S(2)}, u32[]{:S(2)}) collective-permute-start(bf16[16,3200]{1,0:T(8,128)(2,1)S(1)} %finish.10), channel_id=1, source_target_pairs={{0,12},{1,13},{2,14},{3,15},{4,8},{5,9},{6,10},{7,11},{8,4},{9,5},... | collective-permute-start | bytes 307208 | tf_op jit(solution)/shard_map/ppermute | solution.py:346
  146.1 6.4 %collective-permute-start.67 = (bf16[16,3072]{1,0:T(8,128)(2,1)S(1)}, bf16[16,3072]{1,0:T(8,128)(2,1)S(1)}, u32[]{:S(2)}, u32[]{:S(2)}) collective-permute-start(bf16[16,3072]{1,0:T(8,128)(2,1)S(1)} %get-tuple-element.131.refs_0_), channel_id=1, source_target_pairs={{0,6},{1,7},{2,4},{3,5},{4,2},{5,3},{6,0},{7,1},{8,14},{9,15},{10,... | collective-permute-start | bytes 294920 | tf_op jit(solution)/shard_map/ppermute | solution.py:298
  148.7 4.7 %collective-permute-start.66 = (bf16[16,3072]{1,0:T(8,128)(2,1)S(1)}, bf16[16,3072]{1,0:T(8,128)(2,1)S(1)}, u32[]{:S(2)}, u32[]{:S(2)}) collective-permute-start(bf16[16,3072]{1,0:T(8,128)(2,1)S(1)} %get-tuple-element.131.refs_0_), channel_id=1, source_target_pairs={{0,4},{1,5},{2,6},{3,7},{4,0},{5,1},{6,2},{7,3},{8,12},{9,13},{10,... | collective-permute-start | bytes 294920 | tf_op jit(solution)/shard_map/ppermute | solution.py:298
  148.7 4.9 %collective-permute-start.65 = (bf16[16,3072]{1,0:T(8,128)(2,1)S(1)}, bf16[16,3072]{1,0:T(8,128)(2,1)S(1)}, u32[]{:S(2)}, u32[]{:S(2)}) collective-permute-start(bf16[16,3072]{1,0:T(8,128)(2,1)S(1)} %get-tuple-element.131.refs_0_), channel_id=1, source_target_pairs={{0,2},{1,3},{2,0},{3,1},{4,6},{5,7},{6,4},{7,5},{8,10},{9,11},{10,... | collective-permute-start | bytes 294920 | tf_op jit(solution)/shard_map/ppermute | solution.py:298
  149.6 4.3 %collective-permute-start.68 = (bf16[16,3072]{1,0:T(8,128)(2,1)S(1)}, bf16[16,3072]{1,0:T(8,128)(2,1)S(1)}, u32[]{:S(2)}, u32[]{:S(2)}) collective-permute-start(bf16[16,3072]{1,0:T(8,128)(2,1)S(1)} %get-tuple-element.131.refs_0_), channel_id=1, source_target_pairs={{0,1},{1,0},{2,3},{3,2},{4,5},{5,4},{6,7},{7,6},{8,9},{9,8},{10,11... | collective-permute-start | bytes 294920 | tf_op jit(solution)/shard_map/ppermute | solution.py:298
  159.4 6.5 %collective-permute-start.74 = (bf16[16,3072]{1,0:T(8,128)(2,1)S(1)}, bf16[16,3072]{1,0:T(8,128)(2,1)S(1)}, u32[]{:S(2)}, u32[]{:S(2)}) collective-permute-start(bf16[16,3072]{1,0:T(8,128)(2,1)S(1)} %split_last.11), channel_id=1, source_target_pairs={{0,6},{1,7},{2,4},{3,5},{4,2},{5,3},{6,0},{7,1},{8,14},{9,15},{10,... | collective-permute-start | bytes 294920 | tf_op jit(solution)/shard_map/ppermute | solution.py:298
  161.8 4.9 %collective-permute-start.75 = (bf16[16,3072]{1,0:T(8,128)(2,1)S(1)}, bf16[16,3072]{1,0:T(8,128)(2,1)S(1)}, u32[]{:S(2)}, u32[]{:S(2)}) collective-permute-start(bf16[16,3072]{1,0:T(8,128)(2,1)S(1)} %get-tuple-element.137), channel_id=1, source_target_pairs={{0,4},{1,5},{2,6},{3,7},{4,0},{5,1},{6,2},{7,3},{8,12},{9,13},{10,... | collective-permute-start | bytes 294920 | tf_op jit(solution)/shard_map/ppermute | solution.py:298
  161.9 5.6 %collective-permute-start.76 = (bf16[16,3072]{1,0:T(8,128)(2,1)S(1)}, bf16[16,3072]{1,0:T(8,128)(2,1)S(1)}, u32[]{:S(2)}, u32[]{:S(2)}) collective-permute-start(bf16[16,3072]{1,0:T(8,128)(2,1)S(1)} %get-tuple-element.138), channel_id=1, source_target_pairs={{0,2},{1,3},{2,0},{3,1},{4,6},{5,7},{6,4},{7,5},{8,10},{9,11},{10,... | collective-permute-start | bytes 294920 | tf_op jit(solution)/shard_map/ppermute | solution.py:298
  167.5 6.5 %collective-permute-start.77 = (bf16[16,3200]{1,0:T(8,128)(2,1)S(1)}, bf16[16,3200]{1,0:T(8,128)(2,1)S(1)}, u32[]{:S(2)}, u32[]{:S(2)}) collective-permute-start(bf16[16,3200]{1,0:T(8,128)(2,1)S(1)} %finish.11), channel_id=1, source_target_pairs={{0,12},{1,13},{2,14},{3,15},{4,8},{5,9},{6,10},{7,11},{8,4},{9,5},... | collective-permute-start | bytes 307208 | tf_op jit(solution)/shard_map/ppermute | solution.py:346
  (35 other events, 127.2 us)

commit v9 on v8

--- a/solution.py
+++ b/solution.py
@@ -65,20 +65,21 @@
     pieces, refs = refs[: 2 * CHIPS], refs[2 * CHIPS :]
     if tick == 0:
         mod, refs = refs[0], refs[1:]
-    gains, w_qkv, w_out, _, kept, sent, ahead, kv, normed, mixed = refs
+    gains, w_qkv, w_out, _, kept, sent, ahead, kv, mixed = refs
     part_rows, width = pieces[0].shape
     half = CHIPS * part_rows
     rows = 2 * half
     heads = w_out.shape[0] // HS
     here = section[0]
-    for place, piece in enumerate(pieces):
+    values_of = []
+    for piece in pieces:
         values = piece[...]
         if tick == 0:
             values = norm_here(section, f32(values), mod)
-        normed[place * part_rows : (place + 1) * part_rows, :] = values
+        values_of.append(values)
     start = pl.multiple_of(patch_flow[here, tick] * rows, rows)
     gain = gains[here]
-    tokens = normed[...]
+    tokens = jnp.concatenate(values_of, 0)
     columns = w_out.shape[0]
     products = dot(tokens, w_qkv[...])
     queries, keys = products[:, :columns], products[:, columns : 2 * columns]
@@ -118,7 +119,6 @@
         in_specs=[SCALARS] * 2 + [WHOLE] * (len(args) - 2),
         out_specs=(WHOLE,) * 4,
         scratch_shapes=[
-            VMEM((2 * half, width), jnp.bfloat16),
             VMEM((2 * half, columns), jnp.bfloat16),
         ],
         input_output_aliases={len(args) - 1: 3},

time: 175 us -> 175 us (level)
  no operation moved by 1% of the time
where the time goes in v9:
time: 175 us
  waiting for transfers between devices  79.1 us (45%)
  starting transfers between devices  70.5 us (40%)
  Pallas kernels  24.3 us (14%)
    ppermute x72, waiting for transfers between devices, exchange(): return lax.ppermute(value, 'section', route)  59.9 us
    ppermute x72, starting transfers between devices, exchange(): return lax.ppermute(value, 'section', route)  50.1 us
    ppermute x6, starting transfers between devices, body(): packet = lax.ppermute(packet, 'section', across if swaps else onward)  20.4 us
    ppermute x6, waiting for transfers between devices, body(): packet = lax.ppermute(packet, 'section', across if swaps else onward)  19.2 us
    pallas_call x6, Pallas kernels, block(): pl.pallas_call(functools.partial(block_kernel, tick), out_shape=like(((ha...  16.2 us
    pallas_call x1, Pallas kernels, load(): pl.pallas_call(functools.partial(load_kernel, count), out_shape=tuple((VM...  3.97 us
  transfers between devices with their start and end apart: 78, of which 62 were waited for; matrix products, arithmetic and copies ran while one was open for 0% of the time, Pallas kernels for 3%

profile of v9, /device:TPU:0, one launch (start us, length us, event | category | flops | bytes accessed | tf_op | source)
XLA Modules:
  0.0 174.9 jit_solution(2726110816889571817)
XLA Ops:
  0.7 4.1 %collective-permute-start.2 = (bf16[16,3072]{1,0:T(8,128)(2,1)}, bf16[16,3072]{1,0:T(8,128)(2,1)S(1)}, u32[]{:S(2)}, u32[]{:S(2)}) collective-permute-start(bf16[16,3072]{1,0:T(8,128)(2,1)} %refs_5_.1), channel_id=1, source_target_pairs={{0,6},{1,7},{2,4},{3,5},{4,2},{5,3},{6,0},{7,1},{8,14},{9,15},{10,... | collective-permute-start | bytes 294920 | tf_op jit(solution)/shard_map/ppermute | solution.py:298
  5.4 4.0 %load.1 = (bf16[3072,1152]{1,0:T(8,128)(2,1)S(1)}, bf16[384,3072]{1,0:T(8,128)(2,1)S(1)}, f32[2,2,128]{2,1,0:T(2,128)S(1)}, s32[2,6]{1,0:T(2,128)S(1)}, bf16[2,2...) custom-call(bf16[3,3072,384]{2,1,0:T(8,128)(2,1)} %refs_0_.1, bf16[384,3072]{1,0:T(8,128)(2,1)} %refs_1_.1, ...), custom_call_target="tpu_custom_call" | custom-call | bytes 19812448 | tf_op jit(solution)/shard_map/load/pallas_call | solution.py:264
  12.1 3.0 %block.6 = (f32[64,3072]{1,0:T(8,128)S(1)}, bf16[48,3072]{1,0:T(8,128)(2,1)S(1)}, bf16[16,3072]{1,0:T(8,128)(2,1)S(1)}, bf16[2,256,384]{2,1,0:T(8,128)(2,1)S(1)}) custom-call(s32[1]{0:T(128)} %bitcast.section.refs_0_, s32[2,6]{1,0:T(2,128)S(1)} %get-tuple-element.79.patch_flow, bf16[16,3072]{1,0:T(8,128)(2,1)S(1)} %copy-done.3, ...), custom_call_target="tpu_custom_call", output_to_operand_aliasing={{3}: (14, {})} | custom-call | flops 1207959552 | bytes 9437184 | tf_op jit(solution)/shard_map/block/pallas_call | solution.py:111
  16.9 2.5 %collective-permute-start.9 = (bf16[16,3072]{1,0:T(8,128)(2,1)S(1)}, bf16[16,3072]{1,0:T(8,128)(2,1)S(1)}, u32[]{:S(2)}, u32[]{:S(2)}) collective-permute-start(bf16[16,3072]{1,0:T(8,128)(2,1)S(1)} %split_last.6), channel_id=1, source_target_pairs={{0,6},{1,7},{2,4},{3,5},{4,2},{5,3},{6,0},{7,1},{8,14},{9,15},{10,... | collective-permute-start | bytes 294920 | tf_op jit(solution)/shard_map/ppermute | solution.py:298
  20.6 2.9 %collective-permute-done.9.refs_2_ = bf16[16,3072]{1,0:T(8,128)(2,1)S(1)} collective-permute-done((bf16[16,3072]{1,0:T(8,128)(2,1)S(1)}, bf16[16,3072]{1,0:T(8,128)(2,1)S(1)}, u32[]{:S(2)}, u32[]{:S(2)}) %collective-permute-start.9) | collective-permute-done | bytes 98336 | tf_op jit(solution)/shard_map/ppermute | solution.py:298
  23.5 1.5 collective-permute-done.10.refs_3_
  25.2 4.2 %collective-permute-start.12 = (bf16[16,3200]{1,0:T(8,128)(2,1)S(1)}, bf16[16,3200]{1,0:T(8,128)(2,1)S(1)}, u32[]{:S(2)}, u32[]{:S(2)}) collective-permute-start(bf16[16,3200]{1,0:T(8,128)(2,1)S(1)} %finish.6), channel_id=1, source_target_pairs={{0,12},{1,13},{2,14},{3,15},{4,8},{5,9},{6,10},{7,11},{8,4},{9,5},... | collective-permute-start | bytes 307208 | tf_op jit(solution)/shard_map/ppermute | solution.py:346
  29.4 2.7 %collective-permute-done.12.packet.refs_6_ = bf16[16,3200]{1,0:T(8,128)(2,1)S(1)} collective-permute-done((bf16[16,3200]{1,0:T(8,128)(2,1)S(1)}, bf16[16,3200]{1,0:T(8,128)(2,1)S(1)}, u32[]{:S(2)}, u32[]{:S(2)}) %collective-permute-start.12) | collective-permute-done | bytes 102432 | tf_op jit(solution)/shard_map/ppermute | solution.py:346
  32.5 2.7 %collective-permute-start.15 = (bf16[16,3072]{1,0:T(8,128)(2,1)S(1)}, bf16[16,3072]{1,0:T(8,128)(2,1)S(1)}, u32[]{:S(2)}, u32[]{:S(2)}) collective-permute-start(bf16[16,3072]{1,0:T(8,128)(2,1)S(1)} %get-tuple-element.95.refs_0_), channel_id=1, source_target_pairs={{0,6},{1,7},{2,4},{3,5},{4,2},{5,3},{6,0},{7,1},{8,14},{9,15},{10,... | collective-permute-start | bytes 294920 | tf_op jit(solution)/shard_map/ppermute | solution.py:298
  36.1 2.4 %collective-permute-done.15.refs_3_ = bf16[16,3072]{1,0:T(8,128)(2,1)S(1)} collective-permute-done((bf16[16,3072]{1,0:T(8,128)(2,1)S(1)}, bf16[16,3072]{1,0:T(8,128)(2,1)S(1)}, u32[]{:S(2)}, u32[]{:S(2)}) %collective-permute-start.15) | collective-permute-done | bytes 98336 | tf_op jit(solution)/shard_map/ppermute | solution.py:298
  38.5 1.4 collective-permute-done.14.refs_2_
  41.4 2.6 %block.7 = (f32[64,3072]{1,0:T(8,128)S(1)}, bf16[48,3072]{1,0:T(8,128)(2,1)S(1)}, bf16[16,3072]{1,0:T(8,128)(2,1)S(1)}, bf16[2,256,384]{2,1,0:T(8,128)(2,1)S(1)}) custom-call(s32[1]{0:T(128)} %bitcast.section.refs_0_, s32[2,6]{1,0:T(2,128)S(1)} %get-tuple-element.79.patch_flow, ...), custom_call_target="tpu_custom_call", output_to_operand_aliasing={{3}: (13, {})} | custom-call | flops 1207959552 | bytes 9437184 | tf_op jit(solution)/shard_map/block/pallas_call | solution.py:111
  44.7 1.2 collective-permute-done.21.came
  45.9 2.0 %collective-permute-start.22 = (bf16[16,3072]{1,0:T(8,128)(2,1)S(1)}, bf16[16,3072]{1,0:T(8,128)(2,1)S(1)}, u32[]{:S(2)}, u32[]{:S(2)}) collective-permute-start(bf16[16,3072]{1,0:T(8,128)(2,1)S(1)} %split_last.7), channel_id=1, source_target_pairs={{0,6},{1,7},{2,4},{3,5},{4,2},{5,3},{6,0},{7,1},{8,14},{9,15},{10,... | collective-permute-start | bytes 294920 | tf_op jit(solution)/shard_map/ppermute | solution.py:298
  49.6 2.8 %collective-permute-done.22.refs_2_ = bf16[16,3072]{1,0:T(8,128)(2,1)S(1)} collective-permute-done((bf16[16,3072]{1,0:T(8,128)(2,1)S(1)}, bf16[16,3072]{1,0:T(8,128)(2,1)S(1)}, u32[]{:S(2)}, u32[]{:S(2)}) %collective-permute-start.22) | collective-permute-done | bytes 98336 | tf_op jit(solution)/shard_map/ppermute | solution.py:298
  54.0 3.7 %collective-permute-start.25 = (bf16[16,3200]{1,0:T(8,128)(2,1)S(1)}, bf16[16,3200]{1,0:T(8,128)(2,1)S(1)}, u32[]{:S(2)}, u32[]{:S(2)}) collective-permute-start(bf16[16,3200]{1,0:T(8,128)(2,1)S(1)} %finish.7), channel_id=1, source_target_pairs={{0,12},{1,13},{2,14},{3,15},{4,8},{5,9},{6,10},{7,11},{8,4},{9,5},... | collective-permute-start | bytes 307208 | tf_op jit(solution)/shard_map/ppermute | solution.py:346
  57.8 2.8 %collective-permute-done.25.packet.refs_6_ = bf16[16,3200]{1,0:T(8,128)(2,1)S(1)} collective-permute-done((bf16[16,3200]{1,0:T(8,128)(2,1)S(1)}, bf16[16,3200]{1,0:T(8,128)(2,1)S(1)}, u32[]{:S(2)}, u32[]{:S(2)}) %collective-permute-start.25) | collective-permute-done | bytes 102432 | tf_op jit(solution)/shard_map/ppermute | solution.py:346
  61.0 2.1 %collective-permute-start.28 = (bf16[16,3072]{1,0:T(8,128)(2,1)S(1)}, bf16[16,3072]{1,0:T(8,128)(2,1)S(1)}, u32[]{:S(2)}, u32[]{:S(2)}) collective-permute-start(bf16[16,3072]{1,0:T(8,128)(2,1)S(1)} %get-tuple-element.104.refs_0_), channel_id=1, source_target_pairs={{0,6},{1,7},{2,4},{3,5},{4,2},{5,3},{6,0},{7,1},{8,14},{9,15},{10,... | collective-permute-start | bytes 294920 | tf_op jit(solution)/shard_map/ppermute | solution.py:298
  64.5 2.9 %collective-permute-done.28.refs_3_ = bf16[16,3072]{1,0:T(8,128)(2,1)S(1)} collective-permute-done((bf16[16,3072]{1,0:T(8,128)(2,1)S(1)}, bf16[16,3072]{1,0:T(8,128)(2,1)S(1)}, u32[]{:S(2)}, u32[]{:S(2)}) %collective-permute-start.28) | collective-permute-done | bytes 98336 | tf_op jit(solution)/shard_map/ppermute | solution.py:298
  69.6 2.6 %block.8 = (f32[64,3072]{1,0:T(8,128)S(1)}, bf16[48,3072]{1,0:T(8,128)(2,1)S(1)}, bf16[16,3072]{1,0:T(8,128)(2,1)S(1)}, bf16[2,256,384]{2,1,0:T(8,128)(2,1)S(1)}) custom-call(s32[1]{0:T(128)} %bitcast.section.refs_0_, s32[2,6]{1,0:T(2,128)S(1)} %get-tuple-element.79.patch_flow, ...), custom_call_target="tpu_custom_call", output_to_operand_aliasing={{3}: (13, {})} | custom-call | flops 1207959552 | bytes 9437184 | tf_op jit(solution)/shard_map/block/pallas_call | solution.py:111
  74.0 2.4 %collective-permute-start.35 = (bf16[16,3072]{1,0:T(8,128)(2,1)S(1)}, bf16[16,3072]{1,0:T(8,128)(2,1)S(1)}, u32[]{:S(2)}, u32[]{:S(2)}) collective-permute-start(bf16[16,3072]{1,0:T(8,128)(2,1)S(1)} %split_last.8), channel_id=1, source_target_pairs={{0,6},{1,7},{2,4},{3,5},{4,2},{5,3},{6,0},{7,1},{8,14},{9,15},{10,... | collective-permute-start | bytes 294920 | tf_op jit(solution)/shard_map/ppermute | solution.py:298
  77.7 2.5 %collective-permute-done.35.refs_2_ = bf16[16,3072]{1,0:T(8,128)(2,1)S(1)} collective-permute-done((bf16[16,3072]{1,0:T(8,128)(2,1)S(1)}, bf16[16,3072]{1,0:T(8,128)(2,1)S(1)}, u32[]{:S(2)}, u32[]{:S(2)}) %collective-permute-start.35) | collective-permute-done | bytes 98336 | tf_op jit(solution)/shard_map/ppermute | solution.py:298
  80.3 1.5 collective-permute-done.36.refs_3_
  82.1 3.6 %collective-permute-start.38 = (bf16[16,3200]{1,0:T(8,128)(2,1)S(1)}, bf16[16,3200]{1,0:T(8,128)(2,1)S(1)}, u32[]{:S(2)}, u32[]{:S(2)}) collective-permute-start(bf16[16,3200]{1,0:T(8,128)(2,1)S(1)} %finish.8), channel_id=1, source_target_pairs={{0,12},{1,13},{2,14},{3,15},{4,8},{5,9},{6,10},{7,11},{8,4},{9,5},... | collective-permute-start | bytes 307208 | tf_op jit(solution)/shard_map/ppermute | solution.py:346
  85.7 2.9 %collective-permute-done.38.packet.refs_6_ = bf16[16,3200]{1,0:T(8,128)(2,1)S(1)} collective-permute-done((bf16[16,3200]{1,0:T(8,128)(2,1)S(1)}, bf16[16,3200]{1,0:T(8,128)(2,1)S(1)}, u32[]{:S(2)}, u32[]{:S(2)}) %collective-permute-start.38) | collective-permute-done | bytes 102432 | tf_op jit(solution)/shard_map/ppermute | solution.py:346
  89.2 2.9 %collective-permute-start.41 = (bf16[16,3072]{1,0:T(8,128)(2,1)S(1)}, bf16[16,3072]{1,0:T(8,128)(2,1)S(1)}, u32[]{:S(2)}, u32[]{:S(2)}) collective-permute-start(bf16[16,3072]{1,0:T(8,128)(2,1)S(1)} %get-tuple-element.113.refs_0_), channel_id=1, source_target_pairs={{0,6},{1,7},{2,4},{3,5},{4,2},{5,3},{6,0},{7,1},{8,14},{9,15},{10,... | collective-permute-start | bytes 294920 | tf_op jit(solution)/shard_map/ppermute | solution.py:298
  92.8 2.6 %collective-permute-done.41.refs_3_ = bf16[16,3072]{1,0:T(8,128)(2,1)S(1)} collective-permute-done((bf16[16,3072]{1,0:T(8,128)(2,1)S(1)}, bf16[16,3072]{1,0:T(8,128)(2,1)S(1)}, u32[]{:S(2)}, u32[]{:S(2)}) %collective-permute-start.41) | collective-permute-done | bytes 98336 | tf_op jit(solution)/shard_map/ppermute | solution.py:298
  95.4 1.3 collective-permute-done.40.refs_2_
  98.2 2.6 %block.9 = (f32[64,3072]{1,0:T(8,128)S(1)}, bf16[48,3072]{1,0:T(8,128)(2,1)S(1)}, bf16[16,3072]{1,0:T(8,128)(2,1)S(1)}, bf16[2,256,384]{2,1,0:T(8,128)(2,1)S(1)}) custom-call(s32[1]{0:T(128)} %bitcast.section.refs_0_, s32[2,6]{1,0:T(2,128)S(1)} %get-tuple-element.79.patch_flow, ...), custom_call_target="tpu_custom_call", output_to_operand_aliasing={{3}: (13, {})} | custom-call | flops 1207959552 | bytes 9437184 | tf_op jit(solution)/shard_map/block/pallas_call | solution.py:111
  102.6 2.5 %collective-permute-start.48 = (bf16[16,3072]{1,0:T(8,128)(2,1)S(1)}, bf16[16,3072]{1,0:T(8,128)(2,1)S(1)}, u32[]{:S(2)}, u32[]{:S(2)}) collective-permute-start(bf16[16,3072]{1,0:T(8,128)(2,1)S(1)} %split_last.9), channel_id=1, source_target_pairs={{0,6},{1,7},{2,4},{3,5},{4,2},{5,3},{6,0},{7,1},{8,14},{9,15},{10,... | collective-permute-start | bytes 294920 | tf_op jit(solution)/shard_map/ppermute | solution.py:298
  106.4 2.7 %collective-permute-done.48.refs_2_ = bf16[16,3072]{1,0:T(8,128)(2,1)S(1)} collective-permute-done((bf16[16,3072]{1,0:T(8,128)(2,1)S(1)}, bf16[16,3072]{1,0:T(8,128)(2,1)S(1)}, u32[]{:S(2)}, u32[]{:S(2)}) %collective-permute-start.48) | collective-permute-done | bytes 98336 | tf_op jit(solution)/shard_map/ppermute | solution.py:298
  110.9 3.1 %collective-permute-start.51 = (bf16[16,3200]{1,0:T(8,128)(2,1)S(1)}, bf16[16,3200]{1,0:T(8,128)(2,1)S(1)}, u32[]{:S(2)}, u32[]{:S(2)}) collective-permute-start(bf16[16,3200]{1,0:T(8,128)(2,1)S(1)} %finish.9), channel_id=1, source_target_pairs={{0,12},{1,13},{2,14},{3,15},{4,8},{5,9},{6,10},{7,11},{8,4},{9,5},... | collective-permute-start | bytes 307208 | tf_op jit(solution)/shard_map/ppermute | solution.py:346
  114.0 3.4 %collective-permute-done.51.packet.refs_6_ = bf16[16,3200]{1,0:T(8,128)(2,1)S(1)} collective-permute-done((bf16[16,3200]{1,0:T(8,128)(2,1)S(1)}, bf16[16,3200]{1,0:T(8,128)(2,1)S(1)}, u32[]{:S(2)}, u32[]{:S(2)}) %collective-permute-start.51) | collective-permute-done | bytes 102432 | tf_op jit(solution)/shard_map/ppermute | solution.py:346
  117.8 2.4 %collective-permute-start.54 = (bf16[16,3072]{1,0:T(8,128)(2,1)S(1)}, bf16[16,3072]{1,0:T(8,128)(2,1)S(1)}, u32[]{:S(2)}, u32[]{:S(2)}) collective-permute-start(bf16[16,3072]{1,0:T(8,128)(2,1)S(1)} %get-tuple-element.122.refs_0_), channel_id=1, source_target_pairs={{0,6},{1,7},{2,4},{3,5},{4,2},{5,3},{6,0},{7,1},{8,14},{9,15},{10,... | collective-permute-start | bytes 294920 | tf_op jit(solution)/shard_map/ppermute | solution.py:298
  121.4 3.0 %collective-permute-done.54.refs_3_ = bf16[16,3072]{1,0:T(8,128)(2,1)S(1)} collective-permute-done((bf16[16,3072]{1,0:T(8,128)(2,1)S(1)}, bf16[16,3072]{1,0:T(8,128)(2,1)S(1)}, u32[]{:S(2)}, u32[]{:S(2)}) %collective-permute-start.54) | collective-permute-done | bytes 98336 | tf_op jit(solution)/shard_map/ppermute | solution.py:298
  126.7 2.6 %block.10 = (f32[64,3072]{1,0:T(8,128)S(1)}, bf16[48,3072]{1,0:T(8,128)(2,1)S(1)}, bf16[16,3072]{1,0:T(8,128)(2,1)S(1)}, bf16[2,256,384]{2,1,0:T(8,128)(2,1)S(1)}) custom-call(s32[1]{0:T(128)} %bitcast.section.refs_0_, s32[2,6]{1,0:T(2,128)S(1)} %get-tuple-element.79.patch_flow, ...), custom_call_target="tpu_custom_call", output_to_operand_aliasing={{3}: (13, {})} | custom-call | flops 1207959552 | bytes 9437184 | tf_op jit(solution)/shard_map/block/pallas_call | solution.py:111
  131.2 2.3 %collective-permute-start.61 = (bf16[16,3072]{1,0:T(8,128)(2,1)S(1)}, bf16[16,3072]{1,0:T(8,128)(2,1)S(1)}, u32[]{:S(2)}, u32[]{:S(2)}) collective-permute-start(bf16[16,3072]{1,0:T(8,128)(2,1)S(1)} %split_last.10), channel_id=1, source_target_pairs={{0,6},{1,7},{2,4},{3,5},{4,2},{5,3},{6,0},{7,1},{8,14},{9,15},{10,... | collective-permute-start | bytes 294920 | tf_op jit(solution)/shard_map/ppermute | solution.py:298
  133.6 1.2 collective-permute-start.63
  134.9 2.6 %collective-permute-done.61.refs_2_ = bf16[16,3072]{1,0:T(8,128)(2,1)S(1)} collective-permute-done((bf16[16,3072]{1,0:T(8,128)(2,1)S(1)}, bf16[16,3072]{1,0:T(8,128)(2,1)S(1)}, u32[]{:S(2)}, u32[]{:S(2)}) %collective-permute-start.61) | collective-permute-done | bytes 98336 | tf_op jit(solution)/shard_map/ppermute | solution.py:298
  139.2 2.9 %collective-permute-start.64 = (bf16[16,3200]{1,0:T(8,128)(2,1)S(1)}, bf16[16,3200]{1,0:T(8,128)(2,1)S(1)}, u32[]{:S(2)}, u32[]{:S(2)}) collective-permute-start(bf16[16,3200]{1,0:T(8,128)(2,1)S(1)} %finish.10), channel_id=1, source_target_pairs={{0,12},{1,13},{2,14},{3,15},{4,8},{5,9},{6,10},{7,11},{8,4},{9,5},... | collective-permute-start | bytes 307208 | tf_op jit(solution)/shard_map/ppermute | solution.py:346
  142.1 3.7 %collective-permute-done.64.packet.refs_6_ = bf16[16,3200]{1,0:T(8,128)(2,1)S(1)} collective-permute-done((bf16[16,3200]{1,0:T(8,128)(2,1)S(1)}, bf16[16,3200]{1,0:T(8,128)(2,1)S(1)}, u32[]{:S(2)}, u32[]{:S(2)}) %collective-permute-start.64) | collective-permute-done | bytes 102432 | tf_op jit(solution)/shard_map/ppermute | solution.py:346
  146.1 2.4 %collective-permute-start.67 = (bf16[16,3072]{1,0:T(8,128)(2,1)S(1)}, bf16[16,3072]{1,0:T(8,128)(2,1)S(1)}, u32[]{:S(2)}, u32[]{:S(2)}) collective-permute-start(bf16[16,3072]{1,0:T(8,128)(2,1)S(1)} %get-tuple-element.131.refs_0_), channel_id=1, source_target_pairs={{0,6},{1,7},{2,4},{3,5},{4,2},{5,3},{6,0},{7,1},{8,14},{9,15},{10,... | collective-permute-start | bytes 294920 | tf_op jit(solution)/shard_map/ppermute | solution.py:298
  149.7 2.7 %collective-permute-done.67.refs_3_ = bf16[16,3072]{1,0:T(8,128)(2,1)S(1)} collective-permute-done((bf16[16,3072]{1,0:T(8,128)(2,1)S(1)}, bf16[16,3072]{1,0:T(8,128)(2,1)S(1)}, u32[]{:S(2)}, u32[]{:S(2)}) %collective-permute-start.67) | collective-permute-done | bytes 98336 | tf_op jit(solution)/shard_map/ppermute | solution.py:298
  154.8 2.6 %block.11 = (f32[64,3072]{1,0:T(8,128)S(1)}, bf16[48,3072]{1,0:T(8,128)(2,1)S(1)}, bf16[16,3072]{1,0:T(8,128)(2,1)S(1)}, bf16[2,256,384]{2,1,0:T(8,128)(2,1)S(1)}) custom-call(s32[1]{0:T(128)} %bitcast.section.refs_0_, s32[2,6]{1,0:T(2,128)S(1)} %get-tuple-element.79.patch_flow, ...), custom_call_target="tpu_custom_call", output_to_operand_aliasing={{3}: (13, {})} | custom-call | flops 1207959552 | bytes 9437184 | tf_op jit(solution)/shard_map/block/pallas_call | solution.py:111
  159.3 2.1 %collective-permute-start.74 = (bf16[16,3072]{1,0:T(8,128)(2,1)S(1)}, bf16[16,3072]{1,0:T(8,128)(2,1)S(1)}, u32[]{:S(2)}, u32[]{:S(2)}) collective-permute-start(bf16[16,3072]{1,0:T(8,128)(2,1)S(1)} %split_last.11), channel_id=1, source_target_pairs={{0,6},{1,7},{2,4},{3,5},{4,2},{5,3},{6,0},{7,1},{8,14},{9,15},{10,... | collective-permute-start | bytes 294920 | tf_op jit(solution)/shard_map/ppermute | solution.py:298
  163.0 2.9 %collective-permute-done.74.refs_2_ = bf16[16,3072]{1,0:T(8,128)(2,1)S(1)} collective-permute-done((bf16[16,3072]{1,0:T(8,128)(2,1)S(1)}, bf16[16,3072]{1,0:T(8,128)(2,1)S(1)}, u32[]{:S(2)}, u32[]{:S(2)}) %collective-permute-start.74) | collective-permute-done | bytes 98336 | tf_op jit(solution)/shard_map/ppermute | solution.py:298
  167.5 2.8 %collective-permute-start.77 = (bf16[16,3200]{1,0:T(8,128)(2,1)S(1)}, bf16[16,3200]{1,0:T(8,128)(2,1)S(1)}, u32[]{:S(2)}, u32[]{:S(2)}) collective-permute-start(bf16[16,3200]{1,0:T(8,128)(2,1)S(1)} %finish.11), channel_id=1, source_target_pairs={{0,12},{1,13},{2,14},{3,15},{4,8},{5,9},{6,10},{7,11},{8,4},{9,5},... | collective-permute-start | bytes 307208 | tf_op jit(solution)/shard_map/ppermute | solution.py:346
  170.3 3.7 %collective-permute-done.77.packet = bf16[16,3200]{1,0:T(8,128)(2,1)S(1)} collective-permute-done((bf16[16,3200]{1,0:T(8,128)(2,1)S(1)}, bf16[16,3200]{1,0:T(8,128)(2,1)S(1)}, u32[]{:S(2)}, u32[]{:S(2)}) %collective-permute-start.77) | collective-permute-done | bytes 102432 | tf_op jit(solution)/shard_map/ppermute | solution.py:346
  (149 shorter events, 45.4 us)
Async XLA Ops:
  0.7 8.7 %collective-permute-start.2 = (bf16[16,3072]{1,0:T(8,128)(2,1)}, bf16[16,3072]{1,0:T(8,128)(2,1)S(1)}, u32[]{:S(2)}, u32[]{:S(2)}) collective-permute-start(bf16[16,3072]{1,0:T(8,128)(2,1)} %refs_5_.1), channel_id=1, source_target_pairs={{0,6},{1,7},{2,4},{3,5},{4,2},{5,3},{6,0},{7,1},{8,14},{9,15},{10,... | collective-permute-start | bytes 294920 | tf_op jit(solution)/shard_map/ppermute | solution.py:298
  4.7 5.4 %collective-permute-start.1 = (bf16[16,3072]{1,0:T(8,128)(2,1)}, bf16[16,3072]{1,0:T(8,128)(2,1)S(1)}, u32[]{:S(2)}, u32[]{:S(2)}) collective-permute-start(bf16[16,3072]{1,0:T(8,128)(2,1)} %refs_5_.1), channel_id=1, source_target_pairs={{0,4},{1,5},{2,6},{3,7},{4,0},{5,1},{6,2},{7,3},{8,12},{9,13},{10,... | collective-permute-start | bytes 294920 | tf_op jit(solution)/shard_map/ppermute | solution.py:298
  5.2 4.9 %collective-permute-start = (bf16[16,3072]{1,0:T(8,128)(2,1)}, bf16[16,3072]{1,0:T(8,128)(2,1)S(1)}, u32[]{:S(2)}, u32[]{:S(2)}) collective-permute-start(bf16[16,3072]{1,0:T(8,128)(2,1)} %refs_5_.1), channel_id=1, source_target_pairs={{0,2},{1,3},{2,0},{3,1},{4,6},{5,7},{6,4},{7,5},{8,10},{9,11},{10,... | collective-permute-start | bytes 294920 | tf_op jit(solution)/shard_map/ppermute | solution.py:298
  15.1 4.3 %collective-permute-start.7 = (bf16[48,3072]{1,0:T(8,128)(2,1)S(1)}, bf16[48,3072]{1,0:T(8,128)(2,1)S(1)}, u32[]{:S(2)}, u32[]{:S(2)}) collective-permute-start(bf16[48,3072]{1,0:T(8,128)(2,1)S(1)} %get-tuple-element.90), channel_id=1, source_target_pairs={{0,1},{1,0},{2,3},{3,2},{4,5},{5,4},{6,7},{7,6},{8,9},{9,8},{10,11... | collective-permute-start | bytes 884744 | tf_op jit(solution)/shard_map/ppermute | solution.py:298
  16.9 6.6 %collective-permute-start.9 = (bf16[16,3072]{1,0:T(8,128)(2,1)S(1)}, bf16[16,3072]{1,0:T(8,128)(2,1)S(1)}, u32[]{:S(2)}, u32[]{:S(2)}) collective-permute-start(bf16[16,3072]{1,0:T(8,128)(2,1)S(1)} %split_last.6), channel_id=1, source_target_pairs={{0,6},{1,7},{2,4},{3,5},{4,2},{5,3},{6,0},{7,1},{8,14},{9,15},{10,... | collective-permute-start | bytes 294920 | tf_op jit(solution)/shard_map/ppermute | solution.py:298
  19.5 5.5 %collective-permute-start.10 = (bf16[16,3072]{1,0:T(8,128)(2,1)S(1)}, bf16[16,3072]{1,0:T(8,128)(2,1)S(1)}, u32[]{:S(2)}, u32[]{:S(2)}) collective-permute-start(bf16[16,3072]{1,0:T(8,128)(2,1)S(1)} %get-tuple-element.93), channel_id=1, source_target_pairs={{0,4},{1,5},{2,6},{3,7},{4,0},{5,1},{6,2},{7,3},{8,12},{9,13},{10,... | collective-permute-start | bytes 294920 | tf_op jit(solution)/shard_map/ppermute | solution.py:298
  20.0 5.1 %collective-permute-start.11 = (bf16[16,3072]{1,0:T(8,128)(2,1)S(1)}, bf16[16,3072]{1,0:T(8,128)(2,1)S(1)}, u32[]{:S(2)}, u32[]{:S(2)}) collective-permute-start(bf16[16,3072]{1,0:T(8,128)(2,1)S(1)} %get-tuple-element.94), channel_id=1, source_target_pairs={{0,2},{1,3},{2,0},{3,1},{4,6},{5,7},{6,4},{7,5},{8,10},{9,11},{10,... | collective-permute-start | bytes 294920 | tf_op jit(solution)/shard_map/ppermute | solution.py:298
  25.2 6.9 %collective-permute-start.12 = (bf16[16,3200]{1,0:T(8,128)(2,1)S(1)}, bf16[16,3200]{1,0:T(8,128)(2,1)S(1)}, u32[]{:S(2)}, u32[]{:S(2)}) collective-permute-start(bf16[16,3200]{1,0:T(8,128)(2,1)S(1)} %finish.6), channel_id=1, source_target_pairs={{0,12},{1,13},{2,14},{3,15},{4,8},{5,9},{6,10},{7,11},{8,4},{9,5},... | collective-permute-start | bytes 307208 | tf_op jit(solution)/shard_map/ppermute | solution.py:346
  32.5 6.0 %collective-permute-start.15 = (bf16[16,3072]{1,0:T(8,128)(2,1)S(1)}, bf16[16,3072]{1,0:T(8,128)(2,1)S(1)}, u32[]{:S(2)}, u32[]{:S(2)}) collective-permute-start(bf16[16,3072]{1,0:T(8,128)(2,1)S(1)} %get-tuple-element.95.refs_0_), channel_id=1, source_target_pairs={{0,6},{1,7},{2,4},{3,5},{4,2},{5,3},{6,0},{7,1},{8,14},{9,15},{10,... | collective-permute-start | bytes 294920 | tf_op jit(solution)/shard_map/ppermute | solution.py:298
  35.2 4.7 %collective-permute-start.14 = (bf16[16,3072]{1,0:T(8,128)(2,1)S(1)}, bf16[16,3072]{1,0:T(8,128)(2,1)S(1)}, u32[]{:S(2)}, u32[]{:S(2)}) collective-permute-start(bf16[16,3072]{1,0:T(8,128)(2,1)S(1)} %get-tuple-element.95.refs_0_), channel_id=1, source_target_pairs={{0,4},{1,5},{2,6},{3,7},{4,0},{5,1},{6,2},{7,3},{8,12},{9,13},{10,... | collective-permute-start | bytes 294920 | tf_op jit(solution)/shard_map/ppermute | solution.py:298
  35.5 4.6 %collective-permute-start.13 = (bf16[16,3072]{1,0:T(8,128)(2,1)S(1)}, bf16[16,3072]{1,0:T(8,128)(2,1)S(1)}, u32[]{:S(2)}, u32[]{:S(2)}) collective-permute-start(bf16[16,3072]{1,0:T(8,128)(2,1)S(1)} %get-tuple-element.95.refs_0_), channel_id=1, source_target_pairs={{0,2},{1,3},{2,0},{3,1},{4,6},{5,7},{6,4},{7,5},{8,10},{9,11},{10,... | collective-permute-start | bytes 294920 | tf_op jit(solution)/shard_map/ppermute | solution.py:298
  36.1 4.3 %collective-permute-start.16 = (bf16[16,3072]{1,0:T(8,128)(2,1)S(1)}, bf16[16,3072]{1,0:T(8,128)(2,1)S(1)}, u32[]{:S(2)}, u32[]{:S(2)}) collective-permute-start(bf16[16,3072]{1,0:T(8,128)(2,1)S(1)} %get-tuple-element.95.refs_0_), channel_id=1, source_target_pairs={{0,1},{1,0},{2,3},{3,2},{4,5},{5,4},{6,7},{7,6},{8,9},{9,8},{10,11... | collective-permute-start | bytes 294920 | tf_op jit(solution)/shard_map/ppermute | solution.py:298
  45.9 6.5 %collective-permute-start.22 = (bf16[16,3072]{1,0:T(8,128)(2,1)S(1)}, bf16[16,3072]{1,0:T(8,128)(2,1)S(1)}, u32[]{:S(2)}, u32[]{:S(2)}) collective-permute-start(bf16[16,3072]{1,0:T(8,128)(2,1)S(1)} %split_last.7), channel_id=1, source_target_pairs={{0,6},{1,7},{2,4},{3,5},{4,2},{5,3},{6,0},{7,1},{8,14},{9,15},{10,... | collective-permute-start | bytes 294920 | tf_op jit(solution)/shard_map/ppermute | solution.py:298
  48.0 5.4 %collective-permute-start.23 = (bf16[16,3072]{1,0:T(8,128)(2,1)S(1)}, bf16[16,3072]{1,0:T(8,128)(2,1)S(1)}, u32[]{:S(2)}, u32[]{:S(2)}) collective-permute-start(bf16[16,3072]{1,0:T(8,128)(2,1)S(1)} %get-tuple-element.101), channel_id=1, source_target_pairs={{0,4},{1,5},{2,6},{3,7},{4,0},{5,1},{6,2},{7,3},{8,12},{9,13},{10,... | collective-permute-start | bytes 294920 | tf_op jit(solution)/shard_map/ppermute | solution.py:298
  48.6 5.3 %collective-permute-start.24 = (bf16[16,3072]{1,0:T(8,128)(2,1)S(1)}, bf16[16,3072]{1,0:T(8,128)(2,1)S(1)}, u32[]{:S(2)}, u32[]{:S(2)}) collective-permute-start(bf16[16,3072]{1,0:T(8,128)(2,1)S(1)} %get-tuple-element.102), channel_id=1, source_target_pairs={{0,2},{1,3},{2,0},{3,1},{4,6},{5,7},{6,4},{7,5},{8,10},{9,11},{10,... | collective-permute-start | bytes 294920 | tf_op jit(solution)/shard_map/ppermute | solution.py:298
  54.0 6.5 %collective-permute-start.25 = (bf16[16,3200]{1,0:T(8,128)(2,1)S(1)}, bf16[16,3200]{1,0:T(8,128)(2,1)S(1)}, u32[]{:S(2)}, u32[]{:S(2)}) collective-permute-start(bf16[16,3200]{1,0:T(8,128)(2,1)S(1)} %finish.7), channel_id=1, source_target_pairs={{0,12},{1,13},{2,14},{3,15},{4,8},{5,9},{6,10},{7,11},{8,4},{9,5},... | collective-permute-start | bytes 307208 | tf_op jit(solution)/shard_map/ppermute | solution.py:346
  61.0 6.5 %collective-permute-start.28 = (bf16[16,3072]{1,0:T(8,128)(2,1)S(1)}, bf16[16,3072]{1,0:T(8,128)(2,1)S(1)}, u32[]{:S(2)}, u32[]{:S(2)}) collective-permute-start(bf16[16,3072]{1,0:T(8,128)(2,1)S(1)} %get-tuple-element.104.refs_0_), channel_id=1, source_target_pairs={{0,6},{1,7},{2,4},{3,5},{4,2},{5,3},{6,0},{7,1},{8,14},{9,15},{10,... | collective-permute-start | bytes 294920 | tf_op jit(solution)/shard_map/ppermute | solution.py:298
  63.0 4.7 %collective-permute-start.27 = (bf16[16,3072]{1,0:T(8,128)(2,1)S(1)}, bf16[16,3072]{1,0:T(8,128)(2,1)S(1)}, u32[]{:S(2)}, u32[]{:S(2)}) collective-permute-start(bf16[16,3072]{1,0:T(8,128)(2,1)S(1)} %get-tuple-element.104.refs_0_), channel_id=1, source_target_pairs={{0,4},{1,5},{2,6},{3,7},{4,0},{5,1},{6,2},{7,3},{8,12},{9,13},{10,... | collective-permute-start | bytes 294920 | tf_op jit(solution)/shard_map/ppermute | solution.py:298
  63.4 4.8 %collective-permute-start.26 = (bf16[16,3072]{1,0:T(8,128)(2,1)S(1)}, bf16[16,3072]{1,0:T(8,128)(2,1)S(1)}, u32[]{:S(2)}, u32[]{:S(2)}) collective-permute-start(bf16[16,3072]{1,0:T(8,128)(2,1)S(1)} %get-tuple-element.104.refs_0_), channel_id=1, source_target_pairs={{0,2},{1,3},{2,0},{3,1},{4,6},{5,7},{6,4},{7,5},{8,10},{9,11},{10,... | collective-permute-start | bytes 294920 | tf_op jit(solution)/shard_map/ppermute | solution.py:298
  72.2 4.2 %collective-permute-start.33 = (bf16[48,3072]{1,0:T(8,128)(2,1)S(1)}, bf16[48,3072]{1,0:T(8,128)(2,1)S(1)}, u32[]{:S(2)}, u32[]{:S(2)}) collective-permute-start(bf16[48,3072]{1,0:T(8,128)(2,1)S(1)} %get-tuple-element.107), channel_id=1, source_target_pairs={{0,1},{1,0},{2,3},{3,2},{4,5},{5,4},{6,7},{7,6},{8,9},{9,8},{10,11... | collective-permute-start | bytes 884744 | tf_op jit(solution)/shard_map/ppermute | solution.py:298
  74.0 6.2 %collective-permute-start.35 = (bf16[16,3072]{1,0:T(8,128)(2,1)S(1)}, bf16[16,3072]{1,0:T(8,128)(2,1)S(1)}, u32[]{:S(2)}, u32[]{:S(2)}) collective-permute-start(bf16[16,3072]{1,0:T(8,128)(2,1)S(1)} %split_last.8), channel_id=1, source_target_pairs={{0,6},{1,7},{2,4},{3,5},{4,2},{5,3},{6,0},{7,1},{8,14},{9,15},{10,... | collective-permute-start | bytes 294920 | tf_op jit(solution)/shard_map/ppermute | solution.py:298
  76.5 5.3 %collective-permute-start.36 = (bf16[16,3072]{1,0:T(8,128)(2,1)S(1)}, bf16[16,3072]{1,0:T(8,128)(2,1)S(1)}, u32[]{:S(2)}, u32[]{:S(2)}) collective-permute-start(bf16[16,3072]{1,0:T(8,128)(2,1)S(1)} %get-tuple-element.110), channel_id=1, source_target_pairs={{0,4},{1,5},{2,6},{3,7},{4,0},{5,1},{6,2},{7,3},{8,12},{9,13},{10,... | collective-permute-start | bytes 294920 | tf_op jit(solution)/shard_map/ppermute | solution.py:298
  76.8 5.2 %collective-permute-start.37 = (bf16[16,3072]{1,0:T(8,128)(2,1)S(1)}, bf16[16,3072]{1,0:T(8,128)(2,1)S(1)}, u32[]{:S(2)}, u32[]{:S(2)}) collective-permute-start(bf16[16,3072]{1,0:T(8,128)(2,1)S(1)} %get-tuple-element.111), channel_id=1, source_target_pairs={{0,2},{1,3},{2,0},{3,1},{4,6},{5,7},{6,4},{7,5},{8,10},{9,11},{10,... | collective-permute-start | bytes 294920 | tf_op jit(solution)/shard_map/ppermute | solution.py:298
  82.1 6.5 %collective-permute-start.38 = (bf16[16,3200]{1,0:T(8,128)(2,1)S(1)}, bf16[16,3200]{1,0:T(8,128)(2,1)S(1)}, u32[]{:S(2)}, u32[]{:S(2)}) collective-permute-start(bf16[16,3200]{1,0:T(8,128)(2,1)S(1)} %finish.8), channel_id=1, source_target_pairs={{0,12},{1,13},{2,14},{3,15},{4,8},{5,9},{6,10},{7,11},{8,4},{9,5},... | collective-permute-start | bytes 307208 | tf_op jit(solution)/shard_map/ppermute | solution.py:346
  89.2 6.2 %collective-permute-start.41 = (bf16[16,3072]{1,0:T(8,128)(2,1)S(1)}, bf16[16,3072]{1,0:T(8,128)(2,1)S(1)}, u32[]{:S(2)}, u32[]{:S(2)}) collective-permute-start(bf16[16,3072]{1,0:T(8,128)(2,1)S(1)} %get-tuple-element.113.refs_0_), channel_id=1, source_target_pairs={{0,6},{1,7},{2,4},{3,5},{4,2},{5,3},{6,0},{7,1},{8,14},{9,15},{10,... | collective-permute-start | bytes 294920 | tf_op jit(solution)/shard_map/ppermute | solution.py:298
  92.1 4.6 %collective-permute-start.40 = (bf16[16,3072]{1,0:T(8,128)(2,1)S(1)}, bf16[16,3072]{1,0:T(8,128)(2,1)S(1)}, u32[]{:S(2)}, u32[]{:S(2)}) collective-permute-start(bf16[16,3072]{1,0:T(8,128)(2,1)S(1)} %get-tuple-element.113.refs_0_), channel_id=1, source_target_pairs={{0,4},{1,5},{2,6},{3,7},{4,0},{5,1},{6,2},{7,3},{8,12},{9,13},{10,... | collective-permute-start | bytes 294920 | tf_op jit(solution)/shard_map/ppermute | solution.py:298
  92.1 4.7 %collective-permute-start.39 = (bf16[16,3072]{1,0:T(8,128)(2,1)S(1)}, bf16[16,3072]{1,0:T(8,128)(2,1)S(1)}, u32[]{:S(2)}, u32[]{:S(2)}) collective-permute-start(bf16[16,3072]{1,0:T(8,128)(2,1)S(1)} %get-tuple-element.113.refs_0_), channel_id=1, source_target_pairs={{0,2},{1,3},{2,0},{3,1},{4,6},{5,7},{6,4},{7,5},{8,10},{9,11},{10,... | collective-permute-start | bytes 294920 | tf_op jit(solution)/shard_map/ppermute | solution.py:298
  92.8 4.5 %collective-permute-start.42 = (bf16[16,3072]{1,0:T(8,128)(2,1)S(1)}, bf16[16,3072]{1,0:T(8,128)(2,1)S(1)}, u32[]{:S(2)}, u32[]{:S(2)}) collective-permute-start(bf16[16,3072]{1,0:T(8,128)(2,1)S(1)} %get-tuple-element.113.refs_0_), channel_id=1, source_target_pairs={{0,1},{1,0},{2,3},{3,2},{4,5},{5,4},{6,7},{7,6},{8,9},{9,8},{10,11... | collective-permute-start | bytes 294920 | tf_op jit(solution)/shard_map/ppermute | solution.py:298
  100.8 4.4 %collective-permute-start.46 = (bf16[48,3072]{1,0:T(8,128)(2,1)S(1)}, bf16[48,3072]{1,0:T(8,128)(2,1)S(1)}, u32[]{:S(2)}, u32[]{:S(2)}) collective-permute-start(bf16[48,3072]{1,0:T(8,128)(2,1)S(1)} %get-tuple-element.116), channel_id=1, source_target_pairs={{0,1},{1,0},{2,3},{3,2},{4,5},{5,4},{6,7},{7,6},{8,9},{9,8},{10,11... | collective-permute-start | bytes 884744 | tf_op jit(solution)/shard_map/ppermute | solution.py:298
  102.6 6.5 %collective-permute-start.48 = (bf16[16,3072]{1,0:T(8,128)(2,1)S(1)}, bf16[16,3072]{1,0:T(8,128)(2,1)S(1)}, u32[]{:S(2)}, u32[]{:S(2)}) collective-permute-start(bf16[16,3072]{1,0:T(8,128)(2,1)S(1)} %split_last.9), channel_id=1, source_target_pairs={{0,6},{1,7},{2,4},{3,5},{4,2},{5,3},{6,0},{7,1},{8,14},{9,15},{10,... | collective-permute-start | bytes 294920 | tf_op jit(solution)/shard_map/ppermute | solution.py:298
  105.3 4.8 %collective-permute-start.49 = (bf16[16,3072]{1,0:T(8,128)(2,1)S(1)}, bf16[16,3072]{1,0:T(8,128)(2,1)S(1)}, u32[]{:S(2)}, u32[]{:S(2)}) collective-permute-start(bf16[16,3072]{1,0:T(8,128)(2,1)S(1)} %get-tuple-element.119), channel_id=1, source_target_pairs={{0,4},{1,5},{2,6},{3,7},{4,0},{5,1},{6,2},{7,3},{8,12},{9,13},{10,... | collective-permute-start | bytes 294920 | tf_op jit(solution)/shard_map/ppermute | solution.py:298
  105.3 5.4 %collective-permute-start.50 = (bf16[16,3072]{1,0:T(8,128)(2,1)S(1)}, bf16[16,3072]{1,0:T(8,128)(2,1)S(1)}, u32[]{:S(2)}, u32[]{:S(2)}) collective-permute-start(bf16[16,3072]{1,0:T(8,128)(2,1)S(1)} %get-tuple-element.120), channel_id=1, source_target_pairs={{0,2},{1,3},{2,0},{3,1},{4,6},{5,7},{6,4},{7,5},{8,10},{9,11},{10,... | collective-permute-start | bytes 294920 | tf_op jit(solution)/shard_map/ppermute | solution.py:298
  110.9 6.5 %collective-permute-start.51 = (bf16[16,3200]{1,0:T(8,128)(2,1)S(1)}, bf16[16,3200]{1,0:T(8,128)(2,1)S(1)}, u32[]{:S(2)}, u32[]{:S(2)}) collective-permute-start(bf16[16,3200]{1,0:T(8,128)(2,1)S(1)} %finish.9), channel_id=1, source_target_pairs={{0,12},{1,13},{2,14},{3,15},{4,8},{5,9},{6,10},{7,11},{8,4},{9,5},... | collective-permute-start | bytes 307208 | tf_op jit(solution)/shard_map/ppermute | solution.py:346
  117.8 6.5 %collective-permute-start.54 = (bf16[16,3072]{1,0:T(8,128)(2,1)S(1)}, bf16[16,3072]{1,0:T(8,128)(2,1)S(1)}, u32[]{:S(2)}, u32[]{:S(2)}) collective-permute-start(bf16[16,3072]{1,0:T(8,128)(2,1)S(1)} %get-tuple-element.122.refs_0_), channel_id=1, source_target_pairs={{0,6},{1,7},{2,4},{3,5},{4,2},{5,3},{6,0},{7,1},{8,14},{9,15},{10,... | collective-permute-start | bytes 294920 | tf_op jit(solution)/shard_map/ppermute | solution.py:298
  120.2 4.6 %collective-permute-start.53 = (bf16[16,3072]{1,0:T(8,128)(2,1)S(1)}, bf16[16,3072]{1,0:T(8,128)(2,1)S(1)}, u32[]{:S(2)}, u32[]{:S(2)}) collective-permute-start(bf16[16,3072]{1,0:T(8,128)(2,1)S(1)} %get-tuple-element.122.refs_0_), channel_id=1, source_target_pairs={{0,4},{1,5},{2,6},{3,7},{4,0},{5,1},{6,2},{7,3},{8,12},{9,13},{10,... | collective-permute-start | bytes 294920 | tf_op jit(solution)/shard_map/ppermute | solution.py:298
  120.2 5.2 %collective-permute-start.52 = (bf16[16,3072]{1,0:T(8,128)(2,1)S(1)}, bf16[16,3072]{1,0:T(8,128)(2,1)S(1)}, u32[]{:S(2)}, u32[]{:S(2)}) collective-permute-start(bf16[16,3072]{1,0:T(8,128)(2,1)S(1)} %get-tuple-element.122.refs_0_), channel_id=1, source_target_pairs={{0,2},{1,3},{2,0},{3,1},{4,6},{5,7},{6,4},{7,5},{8,10},{9,11},{10,... | collective-permute-start | bytes 294920 | tf_op jit(solution)/shard_map/ppermute | solution.py:298
  131.2 6.3 %collective-permute-start.61 = (bf16[16,3072]{1,0:T(8,128)(2,1)S(1)}, bf16[16,3072]{1,0:T(8,128)(2,1)S(1)}, u32[]{:S(2)}, u32[]{:S(2)}) collective-permute-start(bf16[16,3072]{1,0:T(8,128)(2,1)S(1)} %split_last.10), channel_id=1, source_target_pairs={{0,6},{1,7},{2,4},{3,5},{4,2},{5,3},{6,0},{7,1},{8,14},{9,15},{10,... | collective-permute-start | bytes 294920 | tf_op jit(solution)/shard_map/ppermute | solution.py:298
  133.5 5.1 %collective-permute-start.62 = (bf16[16,3072]{1,0:T(8,128)(2,1)S(1)}, bf16[16,3072]{1,0:T(8,128)(2,1)S(1)}, u32[]{:S(2)}, u32[]{:S(2)}) collective-permute-start(bf16[16,3072]{1,0:T(8,128)(2,1)S(1)} %get-tuple-element.128), channel_id=1, source_target_pairs={{0,4},{1,5},{2,6},{3,7},{4,0},{5,1},{6,2},{7,3},{8,12},{9,13},{10,... | collective-permute-start | bytes 294920 | tf_op jit(solution)/shard_map/ppermute | solution.py:298
  133.6 5.4 %collective-permute-start.63 = (bf16[16,3072]{1,0:T(8,128)(2,1)S(1)}, bf16[16,3072]{1,0:T(8,128)(2,1)S(1)}, u32[]{:S(2)}, u32[]{:S(2)}) collective-permute-start(bf16[16,3072]{1,0:T(8,128)(2,1)S(1)} %get-tuple-element.129), channel_id=1, source_target_pairs={{0,2},{1,3},{2,0},{3,1},{4,6},{5,7},{6,4},{7,5},{8,10},{9,11},{10,... | collective-permute-start | bytes 294920 | tf_op jit(solution)/shard_map/ppermute | solution.py:298
  139.2 6.5 %collective-permute-start.64 = (bf16[16,3200]{1,0:T(8,128)(2,1)S(1)}, bf16[16,3200]{1,0:T(8,128)(2,1)S(1)}, u32[]{:S(2)}, u32[]{:S(2)}) collective-permute-start(bf16[16,3200]{1,0:T(8,128)(2,1)S(1)} %finish.10), channel_id=1, source_target_pairs={{0,12},{1,13},{2,14},{3,15},{4,8},{5,9},{6,10},{7,11},{8,4},{9,5},... | collective-permute-start | bytes 307208 | tf_op jit(solution)/shard_map/ppermute | solution.py:346
  146.1 6.3 %collective-permute-start.67 = (bf16[16,3072]{1,0:T(8,128)(2,1)S(1)}, bf16[16,3072]{1,0:T(8,128)(2,1)S(1)}, u32[]{:S(2)}, u32[]{:S(2)}) collective-permute-start(bf16[16,3072]{1,0:T(8,128)(2,1)S(1)} %get-tuple-element.131.refs_0_), channel_id=1, source_target_pairs={{0,6},{1,7},{2,4},{3,5},{4,2},{5,3},{6,0},{7,1},{8,14},{9,15},{10,... | collective-permute-start | bytes 294920 | tf_op jit(solution)/shard_map/ppermute | solution.py:298
  148.5 4.8 %collective-permute-start.66 = (bf16[16,3072]{1,0:T(8,128)(2,1)S(1)}, bf16[16,3072]{1,0:T(8,128)(2,1)S(1)}, u32[]{:S(2)}, u32[]{:S(2)}) collective-permute-start(bf16[16,3072]{1,0:T(8,128)(2,1)S(1)} %get-tuple-element.131.refs_0_), channel_id=1, source_target_pairs={{0,4},{1,5},{2,6},{3,7},{4,0},{5,1},{6,2},{7,3},{8,12},{9,13},{10,... | collective-permute-start | bytes 294920 | tf_op jit(solution)/shard_map/ppermute | solution.py:298
  148.7 4.8 %collective-permute-start.65 = (bf16[16,3072]{1,0:T(8,128)(2,1)S(1)}, bf16[16,3072]{1,0:T(8,128)(2,1)S(1)}, u32[]{:S(2)}, u32[]{:S(2)}) collective-permute-start(bf16[16,3072]{1,0:T(8,128)(2,1)S(1)} %get-tuple-element.131.refs_0_), channel_id=1, source_target_pairs={{0,2},{1,3},{2,0},{3,1},{4,6},{5,7},{6,4},{7,5},{8,10},{9,11},{10,... | collective-permute-start | bytes 294920 | tf_op jit(solution)/shard_map/ppermute | solution.py:298
  149.7 4.2 %collective-permute-start.68 = (bf16[16,3072]{1,0:T(8,128)(2,1)S(1)}, bf16[16,3072]{1,0:T(8,128)(2,1)S(1)}, u32[]{:S(2)}, u32[]{:S(2)}) collective-permute-start(bf16[16,3072]{1,0:T(8,128)(2,1)S(1)} %get-tuple-element.131.refs_0_), channel_id=1, source_target_pairs={{0,1},{1,0},{2,3},{3,2},{4,5},{5,4},{6,7},{7,6},{8,9},{9,8},{10,11... | collective-permute-start | bytes 294920 | tf_op jit(solution)/shard_map/ppermute | solution.py:298
  159.3 6.6 %collective-permute-start.74 = (bf16[16,3072]{1,0:T(8,128)(2,1)S(1)}, bf16[16,3072]{1,0:T(8,128)(2,1)S(1)}, u32[]{:S(2)}, u32[]{:S(2)}) collective-permute-start(bf16[16,3072]{1,0:T(8,128)(2,1)S(1)} %split_last.11), channel_id=1, source_target_pairs={{0,6},{1,7},{2,4},{3,5},{4,2},{5,3},{6,0},{7,1},{8,14},{9,15},{10,... | collective-permute-start | bytes 294920 | tf_op jit(solution)/shard_map/ppermute | solution.py:298
  161.5 5.3 %collective-permute-start.75 = (bf16[16,3072]{1,0:T(8,128)(2,1)S(1)}, bf16[16,3072]{1,0:T(8,128)(2,1)S(1)}, u32[]{:S(2)}, u32[]{:S(2)}) collective-permute-start(bf16[16,3072]{1,0:T(8,128)(2,1)S(1)} %get-tuple-element.137), channel_id=1, source_target_pairs={{0,4},{1,5},{2,6},{3,7},{4,0},{5,1},{6,2},{7,3},{8,12},{9,13},{10,... | collective-permute-start | bytes 294920 | tf_op jit(solution)/shard_map/ppermute | solution.py:298
  162.0 5.4 %collective-permute-start.76 = (bf16[16,3072]{1,0:T(8,128)(2,1)S(1)}, bf16[16,3072]{1,0:T(8,128)(2,1)S(1)}, u32[]{:S(2)}, u32[]{:S(2)}) collective-permute-start(bf16[16,3072]{1,0:T(8,128)(2,1)S(1)} %get-tuple-element.138), channel_id=1, source_target_pairs={{0,2},{1,3},{2,0},{3,1},{4,6},{5,7},{6,4},{7,5},{8,10},{9,11},{10,... | collective-permute-start | bytes 294920 | tf_op jit(solution)/shard_map/ppermute | solution.py:298
  167.5 6.5 %collective-permute-start.77 = (bf16[16,3200]{1,0:T(8,128)(2,1)S(1)}, bf16[16,3200]{1,0:T(8,128)(2,1)S(1)}, u32[]{:S(2)}, u32[]{:S(2)}) collective-permute-start(bf16[16,3200]{1,0:T(8,128)(2,1)S(1)} %finish.11), channel_id=1, source_target_pairs={{0,12},{1,13},{2,14},{3,15},{4,8},{5,9},{6,10},{7,11},{8,4},{9,5},... | collective-permute-start | bytes 307208 | tf_op jit(solution)/shard_map/ppermute | solution.py:346
  (35 other events, 127.1 us)
